TPU v7x, 128 devices: a whole 4x4x4 slice. The times are simulated.
128 devices in a mesh: seq: 32 (over y, z, core), head: 4 (over x).
Axes of the slice: x: 4, y: 4, z: 4, core: 2. Of those that a mesh axis runs over, the one named last changes fastest.
Arguments:
- queries: bfloat16 [32768, 1024], P('seq', 'head'), may hold values from -6 to 6
- key_rows: bfloat16 [32768, 1024], P('seq', 'head'), may hold values from -6 to 6
- value_rows: bfloat16 [32768, 1024], P('seq', 'head'), may hold values from -6 to 6
- attn_out: bfloat16 [32768, 1024], P('seq', 'head'), may hold values from -6 to 6
- gate_pre: bfloat16 [32768, 1024], P('seq', 'head'), may hold values from -6 to 6
- out_grad: bfloat16 [32768, 1024], P('seq', 'head'), may hold values from -6 to 6
- segments: int32 [32768], P('seq'), may hold values from 0 to 7, never falling along the last dimension, each value on 1 to 6145 neighbouring positions
- projections: bfloat16 [4, 1024, 1024], P(None, None, 'head'), may hold values from -0.1875 to 0.1875
Outputs:
- input_grad: bfloat16 [32768, 1024], P('seq', 'head')
Inputs may be any that keep to these rules, and one draw needn't show every extreme that they name: `segments`: each user's rows are contiguous and ordered; a user has 1 to 6145 rows and one user has exactly 6145, so no user spans more than 6 + 1 = 7 shards of 1024 rows.
All inputs are finite; a program needn't handle non-finite values.
Results may differ from a plain program's by a relative error of at most 0.0064.
Values may be sent and summed in bfloat16 or wider, within the bound.
No kernel may reach another device: no remote copies, remote signals or barrier semaphores. Data moves between devices by JAX's collectives and lax.ppermute only.
A program may use at most 128 MiB of HBM per device.

v0:
```python
import jax
import jax.numpy as jnp
from jax import lax
from jax.experimental import pallas as pl
from jax.experimental.pallas import tpu as pltpu
from jax.sharding import PartitionSpec as P

HEAD_DIM = 128
ROWS = 1024
PAIR = 2 * ROWS
SEG_ROWS = 16
TILE = 512
TILES = PAIR // TILE
HALF_SCALE = 0.5 * HEAD_DIM ** (-0.5)
VMEM = pl.BlockSpec(memory_space=pltpu.VMEM)
SMEM = pl.BlockSpec(memory_space=pltpu.SMEM)
BF16, F32 = jnp.bfloat16, jnp.float32


def cost(flops, transcendentals, size):
    return pl.CostEstimate(flops=flops, transcendentals=transcendentals, bytes_accessed=size)


def params(mib):
    return pltpu.CompilerParams(vmem_limit_bytes=mib * 2**20)


def shift(block, distance):
    devices = range(lax.axis_size("seq"))
    return lax.ppermute(block, "seq", [(i, i + distance) for i in devices if i + distance in devices])


def swap(block):
    return lax.ppermute(block, "seq", [(i, i ^ 1) for i in range(lax.axis_size("seq"))])


def silu_slope(v):
    sigma = jax.nn.sigmoid(v)
    return sigma * (1.0 + v * (1.0 - sigma))


def prepare_kernel(core, q, k, v, o, gate, grad, keep, send, gate_grad):
    for slot, out in ((0, keep), (1, send)):
        head = core[0] if slot == 0 else 1 - core[0]
        cols = pl.ds(pl.multiple_of(head * HEAD_DIM, HEAD_DIM), HEAD_DIM)
        saved = o[:, cols].astype(F32)
        centred = saved - jnp.mean(saved, axis=-1, keepdims=True)
        inverse = lax.rsqrt(jnp.mean(centred * centred, axis=-1, keepdims=True) + 1e-06)
        normed = centred * inverse
        gate_in = gate[:, cols].astype(F32)
        grad_in = grad[:, cols].astype(F32)
        gate_grad[:, cols] = (grad_in * normed * silu_slope(gate_in)).astype(BF16)
        g = grad_in * jax.nn.silu(gate_in)
        attn_grad = inverse * (
            g
            - jnp.mean(g, axis=-1, keepdims=True)
            - normed * jnp.mean(g * normed, axis=-1, keepdims=True)
        )
        out[:, 0:128] = q[:, cols]
        out[:, 128:256] = attn_grad.astype(BF16)
        out[:, 256:384] = k[:, cols]
        out[:, 384:512] = v[:, cols]


def prepare(core, *arrays):
    rows = 256
    wide = pl.BlockSpec((rows, 2 * HEAD_DIM), lambda i, c: (i, 0))
    packed = pl.BlockSpec((rows, 4 * HEAD_DIM), lambda i, c: (i, 0))
    return pl.pallas_call(
        prepare_kernel,
        grid_spec=pltpu.PrefetchScalarGridSpec(
            num_scalar_prefetch=1,
            grid=(ROWS // rows,),
            in_specs=[wide] * 6,
            out_specs=[packed, packed, wide],
        ),
        out_shape=[
            jax.ShapeDtypeStruct((ROWS, 4 * HEAD_DIM), BF16),
            jax.ShapeDtypeStruct((ROWS, 4 * HEAD_DIM), BF16),
            jax.ShapeDtypeStruct((ROWS, 2 * HEAD_DIM), BF16),
        ],
        compiler_params=params(60),
        cost_estimate=cost(30 * ROWS * 256, 2 * ROWS * 256, 11 * ROWS * 512),
        name="prepare",
    )(core, *arrays)


def pairs_kernel(kind, sources, *refs):
    own, near = kind == "own", kind == "near"
    q_in, k_in = refs[:sources], refs[sources:2 * sources]
    outs = refs[2 * sources:4 * sources]
    q, k, dq, dk, dv, row_q, col_k, bound, chip, todo, w0, d0, w1, d1, sem = refs[4 * sources:]
    wide = PAIR + SEG_ROWS
    copies = []
    for i in range(sources):
        at = pl.ds(i * wide, wide)
        copies.append(pltpu.make_async_copy(q_in[i], q.at[at], sem.at[2 * i]))
        copies.append(pltpu.make_async_copy(k_in[i], k.at[at], sem.at[2 * i + 1]))
    for copy in copies:
        copy.start()
    dq[...] = jnp.zeros_like(dq)
    dk[...] = jnp.zeros_like(dk)
    dv[...] = jnp.zeros_like(dv)
    for copy in copies:
        copy.wait()
    blocks = PAIR // 256
    for i in range(sources):
        at = slice(i * wide + PAIR, (i + 1) * wide)
        users_q, users_k = q[at].astype(F32), k[at].astype(F32)
        for r in range(blocks):
            start = i * PAIR + r * 256
            row_q[:, start:start + 256] = users_q[r:r + 1]
        padded = jnp.concatenate([users_k, jnp.zeros((128 - SEG_ROWS, 256), F32)])
        for half in range(2):
            turned = jnp.transpose(padded[:, half * 128:half * 128 + 128])
            for r in range(blocks):
                start = i * PAIR + r * 256 + half * 128
                col_k[start:start + 128] = jnp.broadcast_to(turned[:, r:r + 1], (128, 128))
        for b in range(TILES):
            rows = slice(b * TILE // 256, (b + 1) * TILE // 256)
            bound[0, i * TILES + b] = jnp.min(users_q[rows])
            bound[1, i * TILES + b] = jnp.max(users_q[rows])
            bound[2, i * TILES + b] = jnp.min(users_k[rows])
            bound[3, i * TILES + b] = jnp.max(users_k[rows])
        first_q, last_q = bound[0, i * TILES], bound[1, (i + 1) * TILES - 1]
        first_k, last_k = bound[2, i * TILES], bound[3, (i + 1) * TILES - 1]
        chip[i] = (first_q == last_q).astype(jnp.int32)
        chip[2 + i] = (first_k == last_k).astype(jnp.int32)
    row_q[:, sources * PAIR:] = jnp.full((1, TILE), -1.0, F32)

    count = jnp.int32(0)
    for qs in range(sources):
        for ks in range(sources):
            for kt in range(TILES):
                here = jnp.int32(1)
                if near and (qs, ks) != (1, 1):
                    late, early = chip[qs], chip[2 + ks]
                    if (qs, ks) == (1, 0):
                        here = jnp.where(early == 0, 1, late * (1 - kt % 2))
                    else:
                        here = early * jnp.where(late == 0, 1, kt % 2)
                for qt in range(TILES):
                    if (own and qt < kt) or (near and (qs, ks) == (0, 0)):
                        continue
                    i, j = qs * TILES + qt, ks * TILES + kt
                    some = (bound[0, i] <= bound[3, j]) & (bound[1, i] >= bound[2, j])
                    todo[0, count] = i
                    todo[1, count] = j
                    todo[2, count] = i
                    count = count + some.astype(jnp.int32) * here
    for extra in range(3):
        todo[0, count + extra] = 0
        todo[1, count + extra] = 0
        todo[2, count + extra] = sources * TILES
    last = (((1,), (1,)), ((), ()))
    first = (((0,), (0,)), ((), ()))

    def rows_of(tile):
        start = tile * TILE + (tile // TILES) * SEG_ROWS
        return pl.ds(pl.multiple_of(start, SEG_ROWS), TILE), pl.ds(pl.multiple_of(tile * TILE, TILE), TILE)

    def score(n, w_out, d_out):
        qt, kt = todo[0, n], todo[1, n]
        (q_at, _), (k_at, k_flat) = rows_of(qt), rows_of(kt)
        s = lax.dot_general(k[k_at, 0:128], q[q_at, 0:128], last, preferred_element_type=F32)
        p = lax.dot_general(k[k_at, 128:256], q[q_at, 128:256], last, preferred_element_type=F32)
        mask_at = pl.ds(pl.multiple_of(todo[2, n] * TILE, TILE), TILE)
        allowed = col_k[k_flat, 0:1] == row_q[:, mask_at]
        if own:
            ahead = (qt - kt) * TILE
            allowed = allowed & (
                lax.broadcasted_iota(jnp.int32, (TILE, TILE), 1) + ahead
                >= lax.broadcasted_iota(jnp.int32, (TILE, TILE), 0)
            )
        y = jnp.where(allowed, s * HALF_SCALE, -64.0)
        t = jnp.tanh(y)
        u = 1.0 + t
        w = y * u
        d_out[...] = (p * (u + w * (1.0 - t))).astype(BF16)
        w_out[...] = w.astype(BF16)

    def gather(n, w_in, d_in):
        (q_at, q_flat), (k_at, k_flat) = rows_of(todo[0, n]), rows_of(todo[1, n])
        dv[k_flat, :] += jnp.dot(w_in[...], q[q_at, 128:256], preferred_element_type=F32)
        dk[k_flat, :] += jnp.dot(d_in[...], q[q_at, 0:128], preferred_element_type=F32)
        dq[q_flat, :] += lax.dot_general(d_in[...], k[k_at, 0:128], first, preferred_element_type=F32)

    @pl.when(count > 0)
    def _():
        score(0, w0, d0)

        def two(j, carry):
            n = 2 * j
            score(n + 1, w1, d1)
            gather(n, w0, d0)
            score(n + 2, w0, d0)
            gather(n + 1, w1, d1)
            return carry

        lax.fori_loop(0, (count + 1) // 2, two, 0)

    for i in range(sources):
        at = slice(i * PAIR, (i + 1) * PAIR)
        dq_out, dkv_out = outs[i], outs[sources + i]
        dq_out[...] = (dq[at] * HALF_SCALE).astype(dq_out.dtype)
        dkv_out[:, 0:128] = (dk[at] * HALF_SCALE).astype(dkv_out.dtype)
        dkv_out[:, 128:256] = dv[at].astype(dkv_out.dtype)


def pairs(kind, queries, keys, types, area):
    sources = len(queries)
    anywhere = pl.BlockSpec(memory_space=pl.ANY)
    rows = sources * PAIR
    slots = sources * TILES
    return pl.pallas_call(
        lambda *refs: pairs_kernel(kind, sources, *refs),
        in_specs=[anywhere] * (2 * sources),
        out_specs=[VMEM] * (2 * sources),
        out_shape=[jax.ShapeDtypeStruct((PAIR, 128), t) for t in types]
        + [jax.ShapeDtypeStruct((PAIR, 256), t) for t in types],
        scratch_shapes=[
            pltpu.VMEM((rows + sources * SEG_ROWS, 256), BF16),
            pltpu.VMEM((rows + sources * SEG_ROWS, 256), BF16),
            pltpu.VMEM((rows, 128), F32),
            pltpu.VMEM((rows, 128), F32),
            pltpu.VMEM((rows, 128), F32),
            pltpu.VMEM((1, rows + TILE), F32),
            pltpu.VMEM((rows, 128), F32),
            pltpu.SMEM((4, slots), F32),
            pltpu.SMEM((4,), jnp.int32),
            pltpu.SMEM((3, slots * slots + 4), jnp.int32),
            pltpu.VMEM((TILE, TILE), BF16),
            pltpu.VMEM((TILE, TILE), BF16),
            pltpu.VMEM((TILE, TILE), BF16),
            pltpu.VMEM((TILE, TILE), BF16),
            pltpu.SemaphoreType.DMA((2 * sources,)),
        ],
        compiler_params=params(36),
        cost_estimate=cost(20 * area * 128, area, 8 * rows * 256),
        name="pairs_" + kind,
    )(*queries, *keys)


def project_kernel(place, mine, other, gate_grad, weights, out1, out2, out3, own):
    core, x = place[0], place[1]
    a = mine[...]
    b = other[...]
    first = core == 0
    blocks = []
    for p in range(3):
        cols = slice(p * 128, (p + 1) * 128)
        blocks.append(jnp.where(first, a[:, cols], b[:, cols]))
        blocks.append(jnp.where(first, b[:, cols], a[:, cols]))
    for step, out in ((1, out1), (2, out2), (3, out3), (4, own)):
        dest = lax.rem(x + step, 4)
        ds = pl.ds(pl.multiple_of(dest * 256, 256), 256)
        acc = lax.dot_general(gate_grad[...], weights[3, ds, :], (((1,), (1,)), ((), ())),
                              preferred_element_type=F32)
        for p in range(3):
            left = jnp.concatenate([blocks[2 * p], blocks[2 * p + 1]], axis=1)
            acc += lax.dot_general(left, weights[p, ds, :], (((1,), (1,)), ((), ())),
                                   preferred_element_type=F32)
        out[...] = acc.astype(out.dtype)


def project(place, mine, other, gate_grad, weights):
    part = jax.ShapeDtypeStruct((ROWS, 256), BF16)
    return pl.pallas_call(
        project_kernel,
        in_specs=[SMEM, VMEM, VMEM, VMEM, VMEM],
        out_specs=[VMEM] * 4,
        out_shape=[part, part, part, jax.ShapeDtypeStruct((ROWS, 256), F32)],
        compiler_params=params(24),
        cost_estimate=cost(2 * ROWS * 1024 * 1024, 0, 8 * ROWS * 1024),
        name="project",
    )(place, mine, other, gate_grad, weights)


def per_device(queries, key_rows, value_rows, attn_out, gate_pre, out_grad, segments, projections):
    core = lax.axis_index("seq") % 2
    head = lax.axis_index("head")
    core_at = core.reshape(1).astype(jnp.int32)
    keep, send, gate_grad = prepare(
        core_at, queries, key_rows, value_rows, attn_out, gate_pre, out_grad
    )
    users = (segments + 1).astype(BF16)
    recv = swap(send)
    users_recv = swap(users)
    front = core == 0

    def in_order(kept, received):
        return jnp.concatenate([jnp.where(front, kept, received), jnp.where(front, received, kept)])

    seg = in_order(users, users_recv).reshape(PAIR // 256, 256)
    seg = jnp.pad(seg, ((0, SEG_ROWS - PAIR // 256), (0, 0)))
    query = jnp.concatenate([in_order(keep[:, :256], recv[:, :256]), seg])
    key = jnp.concatenate([in_order(keep[:, 256:], recv[:, 256:]), seg])
    query_next, key_prev = shift(query, -2), shift(key, 2)
    dq0, dkv0 = pairs("own", [query], [key], [F32], PAIR * PAIR // 2)
    query, query_next, key_prev, dq0 = lax.optimization_barrier((query, query_next, key_prev, dq0))
    query_far = shift(query, -6)
    dq1, dq_next, dkv1, dkv_prev = pairs(
        "near", [query, query_next], [key, key_prev], [F32, BF16], PAIR * PAIR
    )
    dkv_back, dq_back = shift(dkv_prev, -2), shift(dq_next, 2)
    query_far, dq_next = lax.optimization_barrier((query_far, dq_next))
    dq_far, dkv2 = pairs("far", [query_far], [key], [BF16], PAIR * PAIR // 4)
    far_back = shift(dq_far, 6)
    total = lambda *terms: sum(t.astype(F32) for t in terms).astype(BF16)
    dq = total(dq0, dq1, dq_back, far_back)
    dkv = total(dkv0, dkv1, dkv2, dkv_back)
    grads = jnp.concatenate([dq, dkv], axis=1)
    mine = jnp.where(front, grads[:ROWS], grads[ROWS:])
    other = swap(jnp.where(front, grads[ROWS:], grads[:ROWS]))
    place = jnp.stack([core, head]).astype(jnp.int32)
    part1, part2, part3, own = project(place, mine, other, gate_grad, projections)
    turn = lambda block, by: lax.ppermute(block, "head", [(i, (i + by) % 4) for i in range(4)])
    result = own + turn(part1, 1).astype(F32) + turn(part2, 2).astype(F32) + turn(part3, 3).astype(F32)
    return result.astype(BF16)


def solution(mesh):
    return jax.shard_map(
        per_device,
        mesh=mesh,
        in_specs=(
            P("seq", "head"),
            P("seq", "head"),
            P("seq", "head"),
            P("seq", "head"),
            P("seq", "head"),
            P("seq", "head"),
            P("seq"),
            P(None, None, "head"),
        ),
        out_specs=P("seq", "head"),
        check_vma=False,
    )
```

profile of v0, /device:TPU:16, one launch (start us, length us, event | category | flops | bytes accessed | tf_op | source)
XLA Modules:
  0.0 143.7 jit_solution(2515998988046614589)
XLA Ops:
  0.0 0.0 copy-start.2
  0.0 5.0 %prepare.1 = (bf16[1024,512]{1,0:T(8,128)(2,1)}, bf16[1024,512]{1,0:T(8,128)(2,1)}, bf16[1024,256]{1,0:T(8,128)(2,1)}) custom-call(s32[1]{0:T(128)} %bitcast.core, bf16[1024,256]{1,0:T(8,128)(2,1)} %q.1, bf16[1024,256]{1,0:T(8,128)(2,1)} %k.1, bf16[1024,256]{1,0:T(8,128)(2,1)} %v.1, bf16[1024,256]{1,0:T(8,128)(2,1)} %o.1, bf16[1024,256]{1,0:T(8,128)(2,1)} %gate.1, ...), custom_call_target="tpu_custom_call" | custom-call | flops 7864320 | bytes 5767168 | tf_op jit(solution)/shard_map/prepare/pallas_call | solution.py:69
  5.0 0.0 collective-permute-start
  5.0 0.0 copy-done.2
  5.0 0.5 collective-permute-start.1
  5.5 2.4 %collective-permute-done.1 = bf16[1024]{0:T(1024)(128)(2,1)S(1)} collective-permute-done((bf16[1024]{0:T(1024)(128)(2,1)S(1)}, bf16[1024]{0:T(1024)(128)(2,1)S(1)}, u32[]{:S(2)}, u32[]{:S(2)}) %collective-permute-start.1) | collective-permute-done | bytes 2080 | tf_op jit(solution)/shard_map/ppermute | solution.py:34
  7.9 0.0 collective-permute-done
  7.9 1.3 broadcast_select_fusion.3
  9.3 0.1 pad_maximum_fusion
  9.4 5.8 %collective-permute-start.2 = (bf16[2064,256]{1,0:T(8,128)(2,1)S(1)}, bf16[2064,256]{1,0:T(8,128)(2,1)S(1)}, u32[]{:S(2)}, u32[]{:S(2)}) collective-permute-start(bf16[2064,256]{1,0:T(8,128)(2,1)S(1)} %get-tuple-element.29.refs_0_), channel_id=1, source_target_pairs={{8,0},{12,4},{16,8},{20,12},{24,16},{28,20},{32,24},{36,28},{40,32... | collective-permute-start | bytes 3170312 | tf_op jit(solution)/shard_map/ppermute | solution.py:30
  15.3 1.9 %collective-permute-start.3 = (bf16[2064,256]{1,0:T(8,128)(2,1)S(1)}, bf16[2064,256]{1,0:T(8,128)(2,1)S(1)}, u32[]{:S(2)}, u32[]{:S(2)}) collective-permute-start(bf16[2064,256]{1,0:T(8,128)(2,1)S(1)} %get-tuple-element.51.refs_1_.refs_2_), channel_id=1, source_target_pairs={{0,8},{4,12},{8,16},{12,20},{16,24},{20,28},{24,32},{28,36},{32,40... | collective-permute-start | bytes 3170312 | tf_op jit(solution)/shard_map/ppermute | solution.py:30
  17.2 11.6 %pairs_own.1 = (f32[2048,128]{1,0:T(8,128)S(1)}, f32[2048,256]{1,0:T(8,128)S(1)}) custom-call(bf16[2064,256]{1,0:T(8,128)(2,1)S(1)} %get-tuple-element.29.refs_0_, bf16[2064,256]{1,0:T(8,128)(2,1)S(1)} %get-tuple-element.51.refs_1_.refs_2_), custom_call_target="tpu_custom_call" | custom-call | flops 5368709120 | bytes 4194304 | tf_op jit(solution)/shard_map/pairs_own/pallas_call | solution.py:215
  28.8 9.4 %collective-permute-done.2.refs_1_ = bf16[2064,256]{1,0:T(8,128)(2,1)S(1)} collective-permute-done((bf16[2064,256]{1,0:T(8,128)(2,1)S(1)}, bf16[2064,256]{1,0:T(8,128)(2,1)S(1)}, u32[]{:S(2)}, u32[]{:S(2)}) %collective-permute-start.2) | collective-permute-done | bytes 1056800 | tf_op jit(solution)/shard_map/ppermute | solution.py:30
  38.1 6.2 %collective-permute-done.3.refs_3_ = bf16[2064,256]{1,0:T(8,128)(2,1)S(1)} collective-permute-done((bf16[2064,256]{1,0:T(8,128)(2,1)S(1)}, bf16[2064,256]{1,0:T(8,128)(2,1)S(1)}, u32[]{:S(2)}, u32[]{:S(2)}) %collective-permute-start.3) | collective-permute-done | bytes 1056800 | tf_op jit(solution)/shard_map/ppermute | solution.py:30
  44.4 1.9 %collective-permute-start.5 = (bf16[2064,256]{1,0:T(8,128)(2,1)S(1)}, bf16[2064,256]{1,0:T(8,128)(2,1)S(1)}, u32[]{:S(2)}, u32[]{:S(2)}) collective-permute-start(bf16[2064,256]{1,0:T(8,128)(2,1)S(1)} %get-tuple-element.29.refs_0_), channel_id=1, source_target_pairs={{24,0},{28,4},{32,8},{36,12},{40,16},{44,20},{48,24},{52,28},{56,3... | collective-permute-start | bytes 3170312 | tf_op jit(solution)/shard_map/ppermute | solution.py:30
  46.3 6.4 %pairs_near.1 = (f32[2048,128]{1,0:T(8,128)S(1)}, bf16[2048,128]{1,0:T(8,128)(2,1)S(1)}, f32[2048,256]{1,0:T(8,128)S(1)}, bf16[2048,256]{1,0:T(8,128)(2,1)S(1)}) custom-call(bf16[2064,256]{1,0:T(8,128)(2,1)S(1)} %get-tuple-element.29.refs_0_, bf16[2064,256]{1,0:T(8,128)(2,1)S(1)} %collective-permute-done.2.refs_1_, ...), custom_call_target="tpu_custom_call" | custom-call | flops 10737418240 | bytes 8388608 | tf_op jit(solution)/shard_map/pairs_near/pallas_call | solution.py:215
  52.7 19.6 %collective-permute-start.7 = (bf16[2048,256]{1,0:T(8,128)(2,1)S(1)}, bf16[2048,256]{1,0:T(8,128)(2,1)S(1)}, u32[]{:S(2)}, u32[]{:S(2)}) collective-permute-start(bf16[2048,256]{1,0:T(8,128)(2,1)S(1)} %get-tuple-element.39), channel_id=1, source_target_pairs={{8,0},{12,4},{16,8},{20,12},{24,16},{28,20},{32,24},{36,28},{40,32... | collective-permute-start | bytes 3145736 | tf_op jit(solution)/shard_map/ppermute | solution.py:30
  72.3 1.9 %collective-permute-start.4 = (bf16[2048,128]{1,0:T(8,128)(2,1)S(1)}, bf16[2048,128]{1,0:T(8,128)(2,1)S(1)}, u32[]{:S(2)}, u32[]{:S(2)}) collective-permute-start(bf16[2048,128]{1,0:T(8,128)(2,1)S(1)} %get-tuple-element.33), channel_id=1, source_target_pairs={{0,8},{4,12},{8,16},{12,20},{16,24},{20,28},{24,32},{28,36},{32,40... | collective-permute-start | bytes 1572872 | tf_op jit(solution)/shard_map/ppermute | solution.py:30
  74.2 0.0 collective-permute-done.5.refs_0_
  74.2 5.5 %pairs_far.1 = (bf16[2048,128]{1,0:T(8,128)(2,1)S(1)}, bf16[2048,256]{1,0:T(8,128)(2,1)S(1)}) custom-call(bf16[2064,256]{1,0:T(8,128)(2,1)S(1)} %collective-permute-done.5.refs_0_, bf16[2064,256]{1,0:T(8,128)(2,1)S(1)} %get-tuple-element.51.refs_1_.refs_2_), custom_call_target="tpu_custom_call" | custom-call | flops 2684354560 | bytes 4194304 | tf_op jit(solution)/shard_map/pairs_far/pallas_call | solution.py:215
  79.8 4.3 %collective-permute-start.6 = (bf16[2048,128]{1,0:T(8,128)(2,1)S(1)}, bf16[2048,128]{1,0:T(8,128)(2,1)S(1)}, u32[]{:S(2)}, u32[]{:S(2)}) collective-permute-start(bf16[2048,128]{1,0:T(8,128)(2,1)S(1)} %get-tuple-element.35), channel_id=1, source_target_pairs={{0,24},{4,28},{8,32},{12,36},{16,40},{20,44},{24,48},{28,52},{32,5... | collective-permute-start | bytes 1572872 | tf_op jit(solution)/shard_map/ppermute | solution.py:30
  84.1 9.5 %collective-permute-done.7 = bf16[2048,256]{1,0:T(8,128)(2,1)S(1)} collective-permute-done((bf16[2048,256]{1,0:T(8,128)(2,1)S(1)}, bf16[2048,256]{1,0:T(8,128)(2,1)S(1)}, u32[]{:S(2)}, u32[]{:S(2)}) %collective-permute-start.7) | collective-permute-done | bytes 1048608 | tf_op jit(solution)/shard_map/ppermute | solution.py:30
  93.6 0.4 add_convert_fusion
  94.1 0.0 collective-permute-done.4
  94.1 11.8 %collective-permute-done.6 = bf16[2048,128]{1,0:T(8,128)(2,1)S(1)} collective-permute-done((bf16[2048,128]{1,0:T(8,128)(2,1)S(1)}, bf16[2048,128]{1,0:T(8,128)(2,1)S(1)}, u32[]{:S(2)}, u32[]{:S(2)}) %collective-permute-start.6) | collective-permute-done | bytes 524320 | tf_op jit(solution)/shard_map/ppermute | solution.py:30
  105.8 0.2 add_convert_fusion.2
  106.0 0.0 copy-start
  106.0 0.0 copy-start.1
  106.1 1.2 broadcast_select_fusion
  107.2 0.0 collective-permute-start.8
  107.3 0.1 pad_add_fusion.place
  107.3 2.5 %collective-permute-done.8.other = bf16[1024,384]{1,0:T(8,128)(2,1)} collective-permute-done((bf16[1024,384]{1,0:T(8,128)(2,1)}, bf16[1024,384]{1,0:T(8,128)(2,1)}, u32[]{:S(2)}, u32[]{:S(2)}) %collective-permute-start.8) | collective-permute-done | bytes 786464 | tf_op jit(solution)/shard_map/ppermute | solution.py:34
  109.9 0.0 copy-done
  109.9 0.0 copy-done.1
  109.9 3.5 %project.1 = (bf16[1024,256]{1,0:T(8,128)(2,1)S(1)}, bf16[1024,256]{1,0:T(8,128)(2,1)S(1)}, bf16[1024,256]{1,0:T(8,128)(2,1)S(1)}, f32[1024,256]{1,0:T(8,128)S(1)}) custom-call(s32[2]{0:T(128)S(1)} %pad_add_fusion.place, bf16[1024,384]{1,0:T(8,128)(2,1)S(1)} %get-tuple-element.50.mine, bf16[1024,384]{1,0:T(8,128)(2,1)} %collective-permute-done.8.other, ...), custom_call_target="tpu_custom_call" | custom-call | flops 2147483648 | bytes 8388608 | tf_op jit(solution)/shard_map/project/pallas_call | solution.py:268
  113.4 2.8 %collective-permute-start.11 = (bf16[1024,256]{1,0:T(8,128)(2,1)S(1)}, bf16[1024,256]{1,0:T(8,128)(2,1)S(1)}, u32[]{:S(2)}, u32[]{:S(2)}) collective-permute-start(bf16[1024,256]{1,0:T(8,128)(2,1)S(1)} %get-tuple-element.44), channel_id=1, source_target_pairs={{0,3},{1,0},{2,1},{3,2},{4,7},{5,4},{6,5},{7,6},{8,11},{9,8},{10,9... | collective-permute-start | bytes 1572872 | tf_op jit(solution)/shard_map/ppermute | solution.py:317
  116.2 0.8 collective-permute-start.10
  117.0 0.9 collective-permute-start.9
  117.9 21.1 %collective-permute-done.11 = bf16[1024,256]{1,0:T(8,128)(2,1)S(1)} collective-permute-done((bf16[1024,256]{1,0:T(8,128)(2,1)S(1)}, bf16[1024,256]{1,0:T(8,128)(2,1)S(1)}, u32[]{:S(2)}, u32[]{:S(2)}) %collective-permute-start.11) | collective-permute-done | bytes 524320 | tf_op jit(solution)/shard_map/ppermute | solution.py:317
  139.0 0.0 collective-permute-done.10
  139.0 3.7 %collective-permute-done.9 = bf16[1024,256]{1,0:T(8,128)(2,1)S(1)} collective-permute-done((bf16[1024,256]{1,0:T(8,128)(2,1)S(1)}, bf16[1024,256]{1,0:T(8,128)(2,1)S(1)}, u32[]{:S(2)}, u32[]{:S(2)}) %collective-permute-start.9) | collective-permute-done | bytes 524320 | tf_op jit(solution)/shard_map/ppermute | solution.py:317
  142.7 1.0 add_convert_fusion.1
  (5 shorter events, 0.0 us)
Async XLA Ops:
  0.0 5.0 %copy-start.2 = (s32[1024]{0:T(1024)S(1)}, s32[1024]{0:T(1024)}, u32[]{:S(2)}) copy-start(s32[1024]{0:T(1024)} %param.14) | copy-start | bytes 12292
  5.0 2.9 %collective-permute-start = (bf16[1024,512]{1,0:T(8,128)(2,1)}, bf16[1024,512]{1,0:T(8,128)(2,1)S(1)}, u32[]{:S(2)}, u32[]{:S(2)}) collective-permute-start(bf16[1024,512]{1,0:T(8,128)(2,1)} %get-tuple-element.26), channel_id=1, source_target_pairs={{0,4},{4,0},{8,12},{12,8},{16,20},{20,16},{24,28},{28,24},{32,36},... | collective-permute-start | bytes 3145736 | tf_op jit(solution)/shard_map/ppermute | solution.py:34
  5.0 2.8 %collective-permute-start.1 = (bf16[1024]{0:T(1024)(128)(2,1)S(1)}, bf16[1024]{0:T(1024)(128)(2,1)S(1)}, u32[]{:S(2)}, u32[]{:S(2)}) collective-permute-start(bf16[1024]{0:T(1024)(128)(2,1)S(1)} %add_convert_fusion.3), channel_id=1, source_target_pairs={{0,4},{4,0},{8,12},{12,8},{16,20},{20,16},{24,28},{28,24},{32,36},... | collective-permute-start | bytes 6152 | tf_op jit(solution)/shard_map/ppermute | solution.py:34
  9.4 28.7 %collective-permute-start.2 = (bf16[2064,256]{1,0:T(8,128)(2,1)S(1)}, bf16[2064,256]{1,0:T(8,128)(2,1)S(1)}, u32[]{:S(2)}, u32[]{:S(2)}) collective-permute-start(bf16[2064,256]{1,0:T(8,128)(2,1)S(1)} %get-tuple-element.29.refs_0_), channel_id=1, source_target_pairs={{8,0},{12,4},{16,8},{20,12},{24,16},{28,20},{32,24},{36,28},{40,32... | collective-permute-start | bytes 3170312 | tf_op jit(solution)/shard_map/ppermute | solution.py:30
  15.3 29.1 %collective-permute-start.3 = (bf16[2064,256]{1,0:T(8,128)(2,1)S(1)}, bf16[2064,256]{1,0:T(8,128)(2,1)S(1)}, u32[]{:S(2)}, u32[]{:S(2)}) collective-permute-start(bf16[2064,256]{1,0:T(8,128)(2,1)S(1)} %get-tuple-element.51.refs_1_.refs_2_), channel_id=1, source_target_pairs={{0,8},{4,12},{8,16},{12,20},{16,24},{20,28},{24,32},{28,36},{32,40... | collective-permute-start | bytes 3170312 | tf_op jit(solution)/shard_map/ppermute | solution.py:30
  44.4 29.9 %collective-permute-start.5 = (bf16[2064,256]{1,0:T(8,128)(2,1)S(1)}, bf16[2064,256]{1,0:T(8,128)(2,1)S(1)}, u32[]{:S(2)}, u32[]{:S(2)}) collective-permute-start(bf16[2064,256]{1,0:T(8,128)(2,1)S(1)} %get-tuple-element.29.refs_0_), channel_id=1, source_target_pairs={{24,0},{28,4},{32,8},{36,12},{40,16},{44,20},{48,24},{52,28},{56,3... | collective-permute-start | bytes 3170312 | tf_op jit(solution)/shard_map/ppermute | solution.py:30
  52.7 41.0 %collective-permute-start.7 = (bf16[2048,256]{1,0:T(8,128)(2,1)S(1)}, bf16[2048,256]{1,0:T(8,128)(2,1)S(1)}, u32[]{:S(2)}, u32[]{:S(2)}) collective-permute-start(bf16[2048,256]{1,0:T(8,128)(2,1)S(1)} %get-tuple-element.39), channel_id=1, source_target_pairs={{8,0},{12,4},{16,8},{20,12},{24,16},{28,20},{32,24},{36,28},{40,32... | collective-permute-start | bytes 3145736 | tf_op jit(solution)/shard_map/ppermute | solution.py:30
  72.3 21.8 %collective-permute-start.4 = (bf16[2048,128]{1,0:T(8,128)(2,1)S(1)}, bf16[2048,128]{1,0:T(8,128)(2,1)S(1)}, u32[]{:S(2)}, u32[]{:S(2)}) collective-permute-start(bf16[2048,128]{1,0:T(8,128)(2,1)S(1)} %get-tuple-element.33), channel_id=1, source_target_pairs={{0,8},{4,12},{8,16},{12,20},{16,24},{20,28},{24,32},{28,36},{32,40... | collective-permute-start | bytes 1572872 | tf_op jit(solution)/shard_map/ppermute | solution.py:30
  79.8 26.1 %collective-permute-start.6 = (bf16[2048,128]{1,0:T(8,128)(2,1)S(1)}, bf16[2048,128]{1,0:T(8,128)(2,1)S(1)}, u32[]{:S(2)}, u32[]{:S(2)}) collective-permute-start(bf16[2048,128]{1,0:T(8,128)(2,1)S(1)} %get-tuple-element.35), channel_id=1, source_target_pairs={{0,24},{4,28},{8,32},{12,36},{16,40},{20,44},{24,48},{28,52},{32,5... | collective-permute-start | bytes 1572872 | tf_op jit(solution)/shard_map/ppermute | solution.py:30
  106.0 3.8 %copy-start = (bf16[4,1024,256]{2,1,0:T(8,128)(2,1)S(1)}, bf16[4,1024,256]{2,1,0:T(8,128)(2,1)}, u32[]{:S(2)}) copy-start(bf16[4,1024,256]{2,1,0:T(8,128)(2,1)} %weights.1) | copy-start | bytes 6291460
  106.0 3.8 %copy-start.1 = (bf16[1024,256]{1,0:T(8,128)(2,1)S(1)}, bf16[1024,256]{1,0:T(8,128)(2,1)}, u32[]{:S(2)}) copy-start(bf16[1024,256]{1,0:T(8,128)(2,1)} %get-tuple-element.40.gate_grad) | copy-start | bytes 1572868
  107.2 2.6 %collective-permute-start.8 = (bf16[1024,384]{1,0:T(8,128)(2,1)}, bf16[1024,384]{1,0:T(8,128)(2,1)}, u32[]{:S(2)}, u32[]{:S(2)}) collective-permute-start(bf16[1024,384]{1,0:T(8,128)(2,1)} %get-tuple-element.49), channel_id=1, source_target_pairs={{0,4},{4,0},{8,12},{12,8},{16,20},{20,16},{24,28},{28,24},{32,36},... | collective-permute-start | bytes 2359304 | tf_op jit(solution)/shard_map/ppermute | solution.py:34
  113.4 25.6 %collective-permute-start.11 = (bf16[1024,256]{1,0:T(8,128)(2,1)S(1)}, bf16[1024,256]{1,0:T(8,128)(2,1)S(1)}, u32[]{:S(2)}, u32[]{:S(2)}) collective-permute-start(bf16[1024,256]{1,0:T(8,128)(2,1)S(1)} %get-tuple-element.44), channel_id=1, source_target_pairs={{0,3},{1,0},{2,1},{3,2},{4,7},{5,4},{6,5},{7,6},{8,11},{9,8},{10,9... | collective-permute-start | bytes 1572872 | tf_op jit(solution)/shard_map/ppermute | solution.py:317
  116.2 22.8 %collective-permute-start.10 = (bf16[1024,256]{1,0:T(8,128)(2,1)S(1)}, bf16[1024,256]{1,0:T(8,128)(2,1)S(1)}, u32[]{:S(2)}, u32[]{:S(2)}) collective-permute-start(bf16[1024,256]{1,0:T(8,128)(2,1)S(1)} %get-tuple-element.43), channel_id=1, source_target_pairs={{0,2},{1,3},{2,0},{3,1},{4,6},{5,7},{6,4},{7,5},{8,10},{9,11},{10,... | collective-permute-start | bytes 1572872 | tf_op jit(solution)/shard_map/ppermute | solution.py:317
  117.0 25.6 %collective-permute-start.9 = (bf16[1024,256]{1,0:T(8,128)(2,1)S(1)}, bf16[1024,256]{1,0:T(8,128)(2,1)S(1)}, u32[]{:S(2)}, u32[]{:S(2)}) collective-permute-start(bf16[1024,256]{1,0:T(8,128)(2,1)S(1)} %get-tuple-element.42), channel_id=1, source_target_pairs={{0,1},{1,2},{2,3},{3,0},{4,5},{5,6},{6,7},{7,4},{8,9},{9,10},{10,1... | collective-permute-start | bytes 1572872 | tf_op jit(solution)/shard_map/ppermute | solution.py:317
where the time goes:
time: 146 us; the launch traced here: 144 us
  waiting for transfers between devices  66.5 us (46%)
  starting transfers between devices  40.5 us (28%)
  Pallas kernels  32 us (22%)
  other arithmetic  4.45 us (3%)
    ppermute x6, waiting for transfers between devices, shift(): lax.ppermute(block, 'seq', [(i, i + distance) for i in devices if i + dis...  36.9 us
    ppermute x6, starting transfers between devices, shift(): lax.ppermute(block, 'seq', [(i, i + distance) for i in devices if i + dis...  35.5 us
    ppermute x3, waiting for transfers between devices, per_device(): lax.ppermute(block, 'head', [(i, (i + by) % 4) for i in range(4)])  24.8 us
    pallas_call x3, Pallas kernels, pairs(): pl.pallas_call(lambda *refs: pairs_kernel(kind, sources, *refs), in_specs...  23.4 us
    pallas_call x1, Pallas kernels, prepare(): pl.pallas_call(prepare_kernel, grid_spec=pltpu.PrefetchScalarGridSpec(num...  5.01 us
    ppermute x3, waiting for transfers between devices, swap(): lax.ppermute(block, 'seq', [(i, i ^ 1) for i in range(lax.axis_size('seq'...  4.89 us
    ppermute x3, starting transfers between devices, per_device(): lax.ppermute(block, 'head', [(i, (i + by) % 4) for i in range(4)])  4.5 us
    pallas_call x1, Pallas kernels, project(): pl.pallas_call(project_kernel, in_specs=[SMEM, VMEM, VMEM, VMEM, VMEM], o...  3.52 us
  transfers between devices with their start and end apart: 12, of which 8 were waited for; matrix products, arithmetic and copies ran while one was open for 0% of the time, Pallas kernels for 16%

commit v1 on v0

--- a/solution.py
+++ b/solution.py
@@ -85,11 +85,11 @@
     )(core, *arrays)
 
 
-def pairs_kernel(kind, sources, *refs):
-    own, near = kind == "own", kind == "near"
+def pairs_kernel(own, *refs):
+    sources = 1
     q_in, k_in = refs[:sources], refs[sources:2 * sources]
     outs = refs[2 * sources:4 * sources]
-    q, k, dq, dk, dv, row_q, col_k, bound, chip, todo, w0, d0, w1, d1, sem = refs[4 * sources:]
+    q, k, dq, dk, dv, row_q, col_k, bound, todo, w0, d0, w1, d1, sem = refs[4 * sources:]
     wide = PAIR + SEG_ROWS
     copies = []
     for i in range(sources):
@@ -122,32 +122,21 @@
             bound[1, i * TILES + b] = jnp.max(users_q[rows])
             bound[2, i * TILES + b] = jnp.min(users_k[rows])
             bound[3, i * TILES + b] = jnp.max(users_k[rows])
-        first_q, last_q = bound[0, i * TILES], bound[1, (i + 1) * TILES - 1]
-        first_k, last_k = bound[2, i * TILES], bound[3, (i + 1) * TILES - 1]
-        chip[i] = (first_q == last_q).astype(jnp.int32)
-        chip[2 + i] = (first_k == last_k).astype(jnp.int32)
     row_q[:, sources * PAIR:] = jnp.full((1, TILE), -1.0, F32)
 
     count = jnp.int32(0)
     for qs in range(sources):
         for ks in range(sources):
             for kt in range(TILES):
-                here = jnp.int32(1)
-                if near and (qs, ks) != (1, 1):
-                    late, early = chip[qs], chip[2 + ks]
-                    if (qs, ks) == (1, 0):
-                        here = jnp.where(early == 0, 1, late * (1 - kt % 2))
-                    else:
-                        here = early * jnp.where(late == 0, 1, kt % 2)
                 for qt in range(TILES):
-                    if (own and qt < kt) or (near and (qs, ks) == (0, 0)):
+                    if own and qt < kt:
                         continue
                     i, j = qs * TILES + qt, ks * TILES + kt
                     some = (bound[0, i] <= bound[3, j]) & (bound[1, i] >= bound[2, j])
                     todo[0, count] = i
                     todo[1, count] = j
                     todo[2, count] = i
-                    count = count + some.astype(jnp.int32) * here
+                    count = count + some.astype(jnp.int32)
     for extra in range(3):
         todo[0, count + extra] = 0
         todo[1, count + extra] = 0
@@ -207,73 +196,95 @@
         dkv_out[:, 128:256] = dv[at].astype(dkv_out.dtype)
 
 
-def pairs(kind, queries, keys, types, area):
-    sources = len(queries)
-    anywhere = pl.BlockSpec(memory_space=pl.ANY)
-    rows = sources * PAIR
-    slots = sources * TILES
+def pairs(name, query, key, kind, area):
+    anywhere = pl.BlockSpec(memory_space=pltpu.HBM)
     return pl.pallas_call(
-        lambda *refs: pairs_kernel(kind, sources, *refs),
-        in_specs=[anywhere] * (2 * sources),
-        out_specs=[VMEM] * (2 * sources),
-        out_shape=[jax.ShapeDtypeStruct((PAIR, 128), t) for t in types]
-        + [jax.ShapeDtypeStruct((PAIR, 256), t) for t in types],
+        lambda *refs: pairs_kernel(name == "pairs_own", *refs),
+        in_specs=[anywhere] * 2,
+        out_specs=[VMEM] * 2,
+        out_shape=[jax.ShapeDtypeStruct((PAIR, 128), kind), jax.ShapeDtypeStruct((PAIR, 256), kind)],
         scratch_shapes=[
-            pltpu.VMEM((rows + sources * SEG_ROWS, 256), BF16),
-            pltpu.VMEM((rows + sources * SEG_ROWS, 256), BF16),
-            pltpu.VMEM((rows, 128), F32),
-            pltpu.VMEM((rows, 128), F32),
-            pltpu.VMEM((rows, 128), F32),
-            pltpu.VMEM((1, rows + TILE), F32),
-            pltpu.VMEM((rows, 128), F32),
-            pltpu.SMEM((4, slots), F32),
-            pltpu.SMEM((4,), jnp.int32),
-            pltpu.SMEM((3, slots * slots + 4), jnp.int32),
+            pltpu.VMEM((PAIR + SEG_ROWS, 256), BF16),
+            pltpu.VMEM((PAIR + SEG_ROWS, 256), BF16),
+            pltpu.VMEM((PAIR, 128), F32),
+            pltpu.VMEM((PAIR, 128), F32),
+            pltpu.VMEM((PAIR, 128), F32),
+            pltpu.VMEM((1, PAIR + TILE), F32),
+            pltpu.VMEM((PAIR, 128), F32),
+            pltpu.SMEM((4, TILES), F32),
+            pltpu.SMEM((3, TILES * TILES + 4), jnp.int32),
             pltpu.VMEM((TILE, TILE), BF16),
             pltpu.VMEM((TILE, TILE), BF16),
             pltpu.VMEM((TILE, TILE), BF16),
             pltpu.VMEM((TILE, TILE), BF16),
-            pltpu.SemaphoreType.DMA((2 * sources,)),
+            pltpu.SemaphoreType.DMA((2,)),
         ],
-        compiler_params=params(36),
-        cost_estimate=cost(20 * area * 128, area, 8 * rows * 256),
-        name="pairs_" + kind,
-    )(*queries, *keys)
-
-
-def project_kernel(place, mine, other, gate_grad, weights, out1, out2, out3, own):
+        compiler_params=params(28),
+        cost_estimate=cost(20 * area * 128, area, 8 * PAIR * 256),
+        name=name,
+    )(query, key)
+
+
+def collect_kernel(place, mine, other, dq_same, dq_cross, dkv_same, dkv_cross, gate_grad, weights,
+                   left, low, high):
     core, x = place[0], place[1]
-    a = mine[...]
-    b = other[...]
-    first = core == 0
-    blocks = []
+    front = core == 0
     for p in range(3):
         cols = slice(p * 128, (p + 1) * 128)
-        blocks.append(jnp.where(first, a[:, cols], b[:, cols]))
-        blocks.append(jnp.where(first, b[:, cols], a[:, cols]))
-    for step, out in ((1, out1), (2, out2), (3, out3), (4, own)):
-        dest = lax.rem(x + step, 4)
-        ds = pl.ds(pl.multiple_of(dest * 256, 256), 256)
-        acc = lax.dot_general(gate_grad[...], weights[3, ds, :], (((1,), (1,)), ((), ())),
-                              preferred_element_type=F32)
-        for p in range(3):
-            left = jnp.concatenate([blocks[2 * p], blocks[2 * p + 1]], axis=1)
-            acc += lax.dot_general(left, weights[p, ds, :], (((1,), (1,)), ((), ())),
-                                   preferred_element_type=F32)
-        out[...] = acc.astype(out.dtype)
-
-
-def project(place, mine, other, gate_grad, weights):
-    part = jax.ShapeDtypeStruct((ROWS, 256), BF16)
+        same, cross = (dq_same, dq_cross) if p == 0 else (dkv_same, dkv_cross)
+        part = slice(max(p - 1, 0) * 128, max(p - 1, 0) * 128 + 128)
+        a = (mine[:, cols] + same[:, part].astype(F32)).astype(BF16)
+        b = (other[:, cols].astype(F32) + cross[:, part].astype(F32)).astype(BF16)
+        left[:, p * 256:p * 256 + 128] = jnp.where(front, a, b)
+        left[:, p * 256 + 128:p * 256 + 256] = jnp.where(front, b, a)
+    left[:, 768:1024] = gate_grad[...]
+    far = head_block(left, weights, lax.rem(x + 2, 4)).astype(BF16)
+    low[...] = far[:ROWS // 2]
+    high[...] = far[ROWS // 2:]
+
+
+def head_block(left, weights, dest):
+    ds = pl.ds(pl.multiple_of(dest * 256, 256), 256)
+    acc = None
+    for p in range(4):
+        term = lax.dot_general(
+            left[:, p * 256:p * 256 + 256], weights[p, ds, :], (((1,), (1,)), ((), ())),
+            preferred_element_type=F32,
+        )
+        acc = term if acc is None else acc + term
+    return acc
+
+
+def project_kernel(place, left, weights, after, before, own):
+    x = place[1]
+    after[...] = head_block(left, weights, lax.rem(x + 1, 4))
+    before[...] = head_block(left, weights, lax.rem(x + 3, 4))
+    own[...] = head_block(left, weights, x)
+
+
+def collect(place, *arrays):
+    half = jax.ShapeDtypeStruct((ROWS // 2, 256), BF16)
+    return pl.pallas_call(
+        collect_kernel,
+        in_specs=[SMEM] + [VMEM] * 8,
+        out_specs=[VMEM] * 3,
+        out_shape=[jax.ShapeDtypeStruct((ROWS, 1024), BF16), half, half],
+        compiler_params=params(24),
+        cost_estimate=cost(2 * ROWS * 1024 * 256, 0, 8 * ROWS * 1024),
+        name="collect",
+    )(place, *arrays)
+
+
+def project(place, left, weights):
     return pl.pallas_call(
         project_kernel,
-        in_specs=[SMEM, VMEM, VMEM, VMEM, VMEM],
-        out_specs=[VMEM] * 4,
-        out_shape=[part, part, part, jax.ShapeDtypeStruct((ROWS, 256), F32)],
+        in_specs=[SMEM, VMEM, VMEM],
+        out_specs=[VMEM] * 3,
+        out_shape=[jax.ShapeDtypeStruct((ROWS, 256), F32)] * 3,
         compiler_params=params(24),
-        cost_estimate=cost(2 * ROWS * 1024 * 1024, 0, 8 * ROWS * 1024),
+        cost_estimate=cost(2 * ROWS * 1024 * 768, 0, 8 * ROWS * 1024),
         name="project",
-    )(place, mine, other, gate_grad, weights)
+    )(place, left, weights)
 
 
 def per_device(queries, key_rows, value_rows, attn_out, gate_pre, out_grad, segments, projections):
@@ -296,27 +307,46 @@
     query = jnp.concatenate([in_order(keep[:, :256], recv[:, :256]), seg])
     key = jnp.concatenate([in_order(keep[:, 256:], recv[:, 256:]), seg])
     query_next, key_prev = shift(query, -2), shift(key, 2)
-    dq0, dkv0 = pairs("own", [query], [key], [F32], PAIR * PAIR // 2)
-    query, query_next, key_prev, dq0 = lax.optimization_barrier((query, query_next, key_prev, dq0))
-    query_far = shift(query, -6)
-    dq1, dq_next, dkv1, dkv_prev = pairs(
-        "near", [query, query_next], [key, key_prev], [F32, BF16], PAIR * PAIR
+    dq0, dkv0 = pairs("pairs_own", query, key, F32, PAIR * PAIR // 2)
+    query_next, key_prev, dq0 = lax.optimization_barrier((query_next, key_prev, dq0))
+    query_far = shift(query_next, -2)
+    dq2, dkv2 = pairs("pairs_two", query_next, key_prev, BF16, PAIR * PAIR // 2)
+    query_far, dq2 = lax.optimization_barrier((query_far, dq2))
+    dq3, dkv3 = pairs("pairs_three", query_far, key_prev, BF16, PAIR * PAIR // 8)
+
+    def total(*terms):
+        return sum(t.astype(F32) for t in terms)
+
+    def halves(block):
+        return jnp.where(front, block[:ROWS], block[ROWS:]), jnp.where(front, block[ROWS:], block[:ROWS])
+
+    def give(block, distance):
+        same, cross = halves(block.astype(BF16))
+        devices = range(lax.axis_size("seq"))
+        route = [(i, (i + distance) ^ 1) for i in devices if i + distance in devices]
+        return shift(same, distance), lax.ppermute(cross, "seq", route)
+
+    dkv_same, dkv_cross = give(total(dkv2, dkv3), -2)
+    dq3_next = shift(dq3, 2)
+    query_next, key, dkv3, dq3 = lax.optimization_barrier((query_next, key, dkv3, dq3))
+    dq1, dkv1 = pairs("pairs_one", query_next, key, BF16, PAIR * PAIR)
+    dq_same, dq_cross = give(total(dq1, dq2, dq3_next), 2)
+    mine, other = halves(jnp.concatenate([dq0, total(dkv0, dkv1)], axis=1))
+    other = swap(other.astype(BF16))
+    place = jnp.stack([core, head]).astype(jnp.int32)
+    left, low, high = collect(
+        place, mine, other, dq_same, dq_cross, dkv_same, dkv_cross, gate_grad, projections
     )
-    dkv_back, dq_back = shift(dkv_prev, -2), shift(dq_next, 2)
-    query_far, dq_next = lax.optimization_barrier((query_far, dq_next))
-    dq_far, dkv2 = pairs("far", [query_far], [key], [BF16], PAIR * PAIR // 4)
-    far_back = shift(dq_far, 6)
-    total = lambda *terms: sum(t.astype(F32) for t in terms).astype(BF16)
-    dq = total(dq0, dq1, dq_back, far_back)
-    dkv = total(dkv0, dkv1, dkv2, dkv_back)
-    grads = jnp.concatenate([dq, dkv], axis=1)
-    mine = jnp.where(front, grads[:ROWS], grads[ROWS:])
-    other = swap(jnp.where(front, grads[ROWS:], grads[:ROWS]))
-    place = jnp.stack([core, head]).astype(jnp.int32)
-    part1, part2, part3, own = project(place, mine, other, gate_grad, projections)
-    turn = lambda block, by: lax.ppermute(block, "head", [(i, (i + by) % 4) for i in range(4)])
-    result = own + turn(part1, 1).astype(F32) + turn(part2, 2).astype(F32) + turn(part3, 3).astype(F32)
-    return result.astype(BF16)
+
+    def turn(block, by):
+        return lax.ppermute(block, "head", [(i, (i + by) % 4) for i in range(4)])
+
+    low, high = turn(low, 1), turn(high, -1)
+    after, before, result = project(place, left, projections)
+    half = ROWS // 2
+    after = jnp.concatenate([after[:half] + low.astype(F32), after[half:]]).astype(BF16)
+    before = jnp.concatenate([before[:half], before[half:] + high.astype(F32)]).astype(BF16)
+    return total(result, turn(after, 1), turn(before, -1)).astype(BF16)
 
 
 def solution(mesh):

time: 146 us -> 154 us (1.055)
  Pallas kernels: 32 us -> 49.4 us
  waiting for transfers between devices: 66.5 us -> 58.7 us
  starting transfers between devices: 40.5 us -> 37.1 us
  local copies, waits for them, and re-layouts: 0.04 us -> 2.29 us
    ppermute x6, starting transfers between devices: 35.5 us -> 17.6 us  [shift(): lax.ppermute(block, 'seq', [(i, i + distance) for i in devices if i + dis...]
    pallas_call x4 -> x6, Pallas kernels: 27 us -> 44.3 us  [the longest x4 40.5 us: pairs(): pl.pallas_call(lambda *refs: pairs_kernel(name == 'pairs_own', *refs), in...]
    ppermute x3 -> x6, starting transfers between devices: 4.5 us -> 17.1 us  [the longest x2 10.4 us: give(): return (shift(same, distance), lax.ppermute(cross, 'seq', route))]
    ppermute x6, waiting for transfers between devices: 36.9 us -> 31.3 us  [shift(): lax.ppermute(block, 'seq', [(i, i + distance) for i in devices if i + dis...]
    ppermute x3, waiting for transfers between devices: 4.89 us -> 2.36 us  [swap(): lax.ppermute(block, 'seq', [(i, i ^ 1) for i in range(lax.axis_size('seq'...]
    unnamed x6 -> x14, local copies, waits for them, and re-layouts: 0.02 us -> 2.21 us
    ppermute x3, starting transfers between devices: 0.51 us -> 2.41 us  [swap(): lax.ppermute(block, 'seq', [(i, i ^ 1) for i in range(lax.axis_size('seq'...]
    ppermute x3 -> x6, waiting for transfers between devices: 24.8 us -> 25.1 us  [the longest x4 16.8 us: turn(): return lax.ppermute(block, 'head', [(i, (i + by) % 4) for i in range(4)])]
  transfers between devices with their start and end apart: 12 -> 15, of which waited for: 8 -> 9; matrix products, arithmetic and copies ran while one was open for 0% -> 1% of each run, Pallas kernels for 16% -> 27%
where the time goes in v1:
time: 154 us; the launch traced here: 152 us
  waiting for transfers between devices  58.7 us (38%)
  Pallas kernels  49.4 us (32%)
  starting transfers between devices  37.1 us (24%)
  other arithmetic  3.94 us (3%)
  local copies, waits for them, and re-layouts  2.29 us (1%)
    pallas_call x4, Pallas kernels, pairs(): pl.pallas_call(lambda *refs: pairs_kernel(name == 'pairs_own', *refs), in...  40.5 us
    ppermute x6, waiting for transfers between devices, shift(): lax.ppermute(block, 'seq', [(i, i + distance) for i in devices if i + dis...  31.3 us
    ppermute x6, starting transfers between devices, shift(): lax.ppermute(block, 'seq', [(i, i + distance) for i in devices if i + dis...  17.6 us
    ppermute x4, waiting for transfers between devices, turn(): return lax.ppermute(block, 'head', [(i, (i + by) % 4) for i in range(4)])  16.8 us
    ppermute x2, starting transfers between devices, give(): return (shift(same, distance), lax.ppermute(cross, 'seq', route))  10.4 us
    ppermute x2, waiting for transfers between devices, give(): return (shift(same, distance), lax.ppermute(cross, 'seq', route))  8.25 us
    ppermute x4, starting transfers between devices, turn(): return lax.ppermute(block, 'head', [(i, (i + by) % 4) for i in range(4)])  6.67 us
    pallas_call x1, Pallas kernels, prepare(): pl.pallas_call(prepare_kernel, grid_spec=pltpu.PrefetchScalarGridSpec(num...  5.01 us
  transfers between devices with their start and end apart: 15, of which 9 were waited for; matrix products, arithmetic and copies ran while one was open for 1% of the time, Pallas kernels for 27%

profile of v1, /device:TPU:16, one launch (start us, length us, event | category | flops | bytes accessed | tf_op | source)
XLA Modules:
  0.0 151.7 jit_solution(4944256510390166161)
XLA Ops:
  0.0 0.0 copy-start.6
  0.0 5.0 %prepare.1 = (bf16[1024,512]{1,0:T(8,128)(2,1)}, bf16[1024,512]{1,0:T(8,128)(2,1)}, bf16[1024,256]{1,0:T(8,128)(2,1)}) custom-call(s32[1]{0:T(128)} %bitcast.core, bf16[1024,256]{1,0:T(8,128)(2,1)} %q.1, bf16[1024,256]{1,0:T(8,128)(2,1)} %k.1, bf16[1024,256]{1,0:T(8,128)(2,1)} %v.1, bf16[1024,256]{1,0:T(8,128)(2,1)} %o.1, bf16[1024,256]{1,0:T(8,128)(2,1)} %gate.1, ...), custom_call_target="tpu_custom_call" | custom-call | flops 7864320 | bytes 5767168 | tf_op jit(solution)/shard_map/prepare/pallas_call | solution.py:69
  5.0 0.0 collective-permute-start
  5.0 0.0 copy-done.6
  5.1 0.5 collective-permute-start.1
  5.5 2.4 %collective-permute-done.1 = bf16[1024]{0:T(1024)(128)(2,1)S(1)} collective-permute-done((bf16[1024]{0:T(1024)(128)(2,1)S(1)}, bf16[1024]{0:T(1024)(128)(2,1)S(1)}, u32[]{:S(2)}, u32[]{:S(2)}) %collective-permute-start.1) | collective-permute-done | bytes 2080 | tf_op jit(solution)/shard_map/ppermute | solution.py:34
  7.9 0.0 collective-permute-done
  7.9 1.3 broadcast_select_fusion.4
  9.3 0.1 pad_maximum_fusion.1
  9.4 0.0 copy-start.1
  9.4 5.8 %collective-permute-start.2 = (bf16[2064,256]{1,0:T(8,128)(2,1)S(1)}, bf16[2064,256]{1,0:T(8,128)(2,1)}, u32[]{:S(2)}, u32[]{:S(2)}) collective-permute-start(bf16[2064,256]{1,0:T(8,128)(2,1)S(1)} %get-tuple-element.62.refs_0_), channel_id=1, source_target_pairs={{8,0},{12,4},{16,8},{20,12},{24,16},{28,20},{32,24},{36,28},{40,32... | collective-permute-start | bytes 3170312 | tf_op jit(solution)/shard_map/ppermute | solution.py:30
  15.3 1.9 %collective-permute-start.3 = (bf16[2064,256]{1,0:T(8,128)(2,1)S(1)}, bf16[2064,256]{1,0:T(8,128)(2,1)S(1)}, u32[]{:S(2)}, u32[]{:S(2)}) collective-permute-start(bf16[2064,256]{1,0:T(8,128)(2,1)S(1)} %get-tuple-element.41.refs_1_), channel_id=1, source_target_pairs={{0,8},{4,12},{8,16},{12,20},{16,24},{20,28},{24,32},{28,36},{32,40... | collective-permute-start | bytes 3170312 | tf_op jit(solution)/shard_map/ppermute | solution.py:30
  17.2 11.6 %pairs_own.1 = (f32[2048,128]{1,0:T(8,128)S(1)}, f32[2048,256]{1,0:T(8,128)S(1)}) custom-call(bf16[2064,256]{1,0:T(8,128)(2,1)S(1)} %get-tuple-element.62.refs_0_, bf16[2064,256]{1,0:T(8,128)(2,1)S(1)} %get-tuple-element.41.refs_1_), custom_call_target="tpu_custom_call" | custom-call | flops 5368709120 | bytes 4194304 | tf_op jit(solution)/shard_map/pairs_own/pallas_call | solution.py:201
  28.8 0.0 copy-done.1
  28.8 9.4 %collective-permute-done.2.refs_0_ = bf16[2064,256]{1,0:T(8,128)(2,1)} collective-permute-done((bf16[2064,256]{1,0:T(8,128)(2,1)S(1)}, bf16[2064,256]{1,0:T(8,128)(2,1)}, u32[]{:S(2)}, u32[]{:S(2)}) %collective-permute-start.2) | collective-permute-done | bytes 1056800 | tf_op jit(solution)/shard_map/ppermute | solution.py:30
  38.2 6.2 %collective-permute-done.3.refs_1_ = bf16[2064,256]{1,0:T(8,128)(2,1)S(1)} collective-permute-done((bf16[2064,256]{1,0:T(8,128)(2,1)S(1)}, bf16[2064,256]{1,0:T(8,128)(2,1)S(1)}, u32[]{:S(2)}, u32[]{:S(2)}) %collective-permute-start.3) | collective-permute-done | bytes 1056800 | tf_op jit(solution)/shard_map/ppermute | solution.py:30
  44.4 0.0 copy-start.4
  44.4 1.0 copy-done.4
  45.4 1.9 %collective-permute-start.4 = (bf16[2064,256]{1,0:T(8,128)(2,1)}, bf16[2064,256]{1,0:T(8,128)(2,1)}, u32[]{:S(2)}, u32[]{:S(2)}) collective-permute-start(bf16[2064,256]{1,0:T(8,128)(2,1)} %collective-permute-done.2.refs_0_), channel_id=1, source_target_pairs={{8,0},{12,4},{16,8},{20,12},{24,16},{28,20},{32,24},{36,28},{40,32... | collective-permute-start | bytes 3170312 | tf_op jit(solution)/shard_map/ppermute | solution.py:30
  47.3 0.0 copy-start.5
  47.3 1.2 copy-done.5
  48.5 13.5 %pairs_two.1 = (bf16[2048,128]{1,0:T(8,128)(2,1)S(1)}, bf16[2048,256]{1,0:T(8,128)(2,1)S(1)}) custom-call(bf16[2064,256]{1,0:T(8,128)(2,1)} %collective-permute-done.2.refs_0_, bf16[2064,256]{1,0:T(8,128)(2,1)S(1)} %copy-done.5), custom_call_target="tpu_custom_call" | custom-call | flops 5368709120 | bytes 4194304 | tf_op jit(solution)/shard_map/pairs_two/pallas_call | solution.py:201
  62.0 9.8 %collective-permute-done.4.refs_0_ = bf16[2064,256]{1,0:T(8,128)(2,1)} collective-permute-done((bf16[2064,256]{1,0:T(8,128)(2,1)}, bf16[2064,256]{1,0:T(8,128)(2,1)}, u32[]{:S(2)}, u32[]{:S(2)}) %collective-permute-start.4) | collective-permute-done | bytes 1056800 | tf_op jit(solution)/shard_map/ppermute | solution.py:30
  71.8 2.0 %pairs_three.1 = (bf16[2048,128]{1,0:T(8,128)(2,1)S(1)}, bf16[2048,256]{1,0:T(8,128)(2,1)S(1)}) custom-call(bf16[2064,256]{1,0:T(8,128)(2,1)} %collective-permute-done.4.refs_0_, bf16[2064,256]{1,0:T(8,128)(2,1)S(1)} %copy-done.5), custom_call_target="tpu_custom_call" | custom-call | flops 1342177280 | bytes 4194304 | tf_op jit(solution)/shard_map/pairs_three/pallas_call | solution.py:201
  73.8 2.1 %collective-permute-start.6 = (bf16[2048,128]{1,0:T(8,128)(2,1)S(1)}, bf16[2048,128]{1,0:T(8,128)(2,1)S(1)}, u32[]{:S(2)}, u32[]{:S(2)}) collective-permute-start(bf16[2048,128]{1,0:T(8,128)(2,1)S(1)} %get-tuple-element.39), channel_id=1, source_target_pairs={{0,8},{4,12},{8,16},{12,20},{16,24},{20,28},{24,32},{28,36},{32,40... | collective-permute-start | bytes 1572872 | tf_op jit(solution)/shard_map/ppermute | solution.py:30
  75.9 0.3 add_convert_fusion
  76.2 0.0 copy-start.2
  76.2 0.1 broadcast_select_fusion.1
  76.3 8.5 %collective-permute-start.10 = (bf16[1024,256]{1,0:T(8,128)(2,1)S(1)}, bf16[1024,256]{1,0:T(8,128)(2,1)S(1)}, u32[]{:S(2)}, u32[]{:S(2)}) collective-permute-start(bf16[1024,256]{1,0:T(8,128)(2,1)S(1)} %get-tuple-element.57), channel_id=1, source_target_pairs={{8,4},{12,0},{16,12},{20,8},{24,20},{28,16},{32,28},{36,24},{40,36... | collective-permute-start | bytes 1572872 | tf_op jit(solution)/shard_map/ppermute | solution.py:327
  84.8 3.9 %collective-permute-start.9 = (bf16[1024,256]{1,0:T(8,128)(2,1)S(1)}, bf16[1024,256]{1,0:T(8,128)(2,1)S(1)}, u32[]{:S(2)}, u32[]{:S(2)}) collective-permute-start(bf16[1024,256]{1,0:T(8,128)(2,1)S(1)} %get-tuple-element.58), channel_id=1, source_target_pairs={{8,0},{12,4},{16,8},{20,12},{24,16},{28,20},{32,24},{36,28},{40,32... | collective-permute-start | bytes 1572872 | tf_op jit(solution)/shard_map/ppermute | solution.py:30
  88.7 0.0 copy-done.2
  88.7 13.5 %pairs_one.1 = (bf16[2048,128]{1,0:T(8,128)(2,1)S(1)}, bf16[2048,256]{1,0:T(8,128)(2,1)S(1)}) custom-call(bf16[2064,256]{1,0:T(8,128)(2,1)} %collective-permute-done.2.refs_0_, bf16[2064,256]{1,0:T(8,128)(2,1)S(1)} %copy-done.2), custom_call_target="tpu_custom_call" | custom-call | flops 10737418240 | bytes 4194304 | tf_op jit(solution)/shard_map/pairs_one/pallas_call | solution.py:201
  102.2 0.2 convert_add_fusion
  102.4 0.2 select_convert_fusion
  102.6 1.9 %collective-permute-start.5 = (bf16[1024,384]{1,0:T(8,128)(2,1)S(1)}, bf16[1024,384]{1,0:T(8,128)(2,1)S(1)}, u32[]{:S(2)}, u32[]{:S(2)}) collective-permute-start(bf16[1024,384]{1,0:T(8,128)(2,1)S(1)} %select_convert_fusion), channel_id=1, source_target_pairs={{0,4},{4,0},{8,12},{12,8},{16,20},{20,16},{24,28},{28,24},{32,36},... | collective-permute-start | bytes 2359304 | tf_op jit(solution)/shard_map/ppermute | solution.py:34
  104.5 0.0 collective-permute-done.6
  104.5 0.2 add_convert_fusion.2
  104.8 1.9 %collective-permute-start.8 = (bf16[1024,128]{1,0:T(8,128)(2,1)S(1)}, bf16[1024,128]{1,0:T(8,128)(2,1)S(1)}, u32[]{:S(2)}, u32[]{:S(2)}) collective-permute-start(bf16[1024,128]{1,0:T(8,128)(2,1)S(1)} %get-tuple-element.59), channel_id=1, source_target_pairs={{0,12},{4,8},{8,20},{12,16},{16,28},{20,24},{24,36},{28,32},{32,44... | collective-permute-start | bytes 786440 | tf_op jit(solution)/shard_map/ppermute | solution.py:327
  106.7 1.9 %collective-permute-start.7 = (bf16[1024,128]{1,0:T(8,128)(2,1)S(1)}, bf16[1024,128]{1,0:T(8,128)(2,1)S(1)}, u32[]{:S(2)}, u32[]{:S(2)}) collective-permute-start(bf16[1024,128]{1,0:T(8,128)(2,1)S(1)} %get-tuple-element.60), channel_id=1, source_target_pairs={{0,8},{4,12},{8,16},{12,20},{16,24},{20,28},{24,32},{28,36},{32,40... | collective-permute-start | bytes 786440 | tf_op jit(solution)/shard_map/ppermute | solution.py:30
  108.7 0.1 pad_add_fusion.place
  108.7 0.0 copy-start
  108.7 0.0 copy-start.3
  108.7 0.2 broadcast_select_fusion.mine
  108.9 0.0 collective-permute-done.10.dkv_cross
  108.9 0.0 collective-permute-done.9.dkv_same
  109.0 8.2 %collective-permute-done.8.dq_cross = bf16[1024,128]{1,0:T(8,128)(2,1)S(1)} collective-permute-done((bf16[1024,128]{1,0:T(8,128)(2,1)S(1)}, bf16[1024,128]{1,0:T(8,128)(2,1)S(1)}, u32[]{:S(2)}, u32[]{:S(2)}) %collective-permute-start.8) | collective-permute-done | bytes 262176 | tf_op jit(solution)/shard_map/ppermute | solution.py:327
  117.2 5.9 %collective-permute-done.7.dq_same = bf16[1024,128]{1,0:T(8,128)(2,1)S(1)} collective-permute-done((bf16[1024,128]{1,0:T(8,128)(2,1)S(1)}, bf16[1024,128]{1,0:T(8,128)(2,1)S(1)}, u32[]{:S(2)}, u32[]{:S(2)}) %collective-permute-start.7) | collective-permute-done | bytes 262176 | tf_op jit(solution)/shard_map/ppermute | solution.py:30
  123.1 0.0 collective-permute-done.5.other
  123.1 0.0 copy-done
  123.1 0.0 copy-done.3
  123.1 1.5 collect.1
  124.6 2.8 %collective-permute-start.13 = (bf16[512,256]{1,0:T(8,128)(2,1)S(1)}, bf16[512,256]{1,0:T(8,128)(2,1)S(1)}, u32[]{:S(2)}, u32[]{:S(2)}) collective-permute-start(bf16[512,256]{1,0:T(8,128)(2,1)S(1)} %get-tuple-element.52), channel_id=1, source_target_pairs={{0,3},{1,0},{2,1},{3,2},{4,7},{5,4},{6,5},{7,6},{8,11},{9,8},{10,9... | collective-permute-start | bytes 786440 | tf_op jit(solution)/shard_map/ppermute | solution.py:342
  127.4 0.0 collective-permute-start.11
  127.5 2.4 %project.1 = (f32[1024,256]{1,0:T(8,128)S(1)}, f32[1024,256]{1,0:T(8,128)S(1)}, f32[1024,256]{1,0:T(8,128)S(1)}) custom-call(s32[2]{0:T(128)S(1)} %pad_add_fusion.place, bf16[1024,1024]{1,0:T(8,128)(2,1)S(1)} %get-tuple-element.47.left, bf16[4,1024,256]{2,1,0:T(8,128)(2,1)S(1)} %copy-done), custom_call_target="tpu_custom_call" | custom-call | flops 1610612736 | bytes 8388608 | tf_op jit(solution)/shard_map/project/pallas_call | solution.py:279
  129.9 3.1 %collective-permute-done.13 = bf16[512,256]{1,0:T(8,128)(2,1)S(1)} collective-permute-done((bf16[512,256]{1,0:T(8,128)(2,1)S(1)}, bf16[512,256]{1,0:T(8,128)(2,1)S(1)}, u32[]{:S(2)}, u32[]{:S(2)}) %collective-permute-start.13) | collective-permute-done | bytes 262176 | tf_op jit(solution)/shard_map/ppermute | solution.py:342
  133.0 0.1 add_convert_fusion.3
  133.1 3.8 %collective-permute-start.14 = (bf16[1024,256]{1,0:T(8,128)(2,1)S(1)}, bf16[1024,256]{1,0:T(8,128)(2,1)S(1)}, u32[]{:S(2)}, u32[]{:S(2)}) collective-permute-start(bf16[1024,256]{1,0:T(8,128)(2,1)S(1)} %pad_maximum_fusion.4), channel_id=1, source_target_pairs={{0,3},{1,0},{2,1},{3,2},{4,7},{5,4},{6,5},{7,6},{8,11},{9,8},{10,9... | collective-permute-start | bytes 1572872 | tf_op jit(solution)/shard_map/ppermute | solution.py:342
  136.9 0.0 collective-permute-done.11
  136.9 0.1 add_convert_fusion.4
  137.0 0.1 collective-permute-start.12
  137.1 10.1 %collective-permute-done.14 = bf16[1024,256]{1,0:T(8,128)(2,1)S(1)} collective-permute-done((bf16[1024,256]{1,0:T(8,128)(2,1)S(1)}, bf16[1024,256]{1,0:T(8,128)(2,1)S(1)}, u32[]{:S(2)}, u32[]{:S(2)}) %collective-permute-start.14) | collective-permute-done | bytes 524320 | tf_op jit(solution)/shard_map/ppermute | solution.py:342
  147.2 3.6 %collective-permute-done.12 = bf16[1024,256]{1,0:T(8,128)(2,1)S(1)} collective-permute-done((bf16[1024,256]{1,0:T(8,128)(2,1)S(1)}, bf16[1024,256]{1,0:T(8,128)(2,1)S(1)}, u32[]{:S(2)}, u32[]{:S(2)}) %collective-permute-start.12) | collective-permute-done | bytes 524320 | tf_op jit(solution)/shard_map/ppermute | solution.py:342
  150.8 1.0 add_convert_fusion.1
  (10 shorter events, 0.2 us)
Async XLA Ops:
  0.0 5.0 %copy-start.6 = (s32[1024]{0:T(1024)S(1)}, s32[1024]{0:T(1024)}, u32[]{:S(2)}) copy-start(s32[1024]{0:T(1024)} %param.14) | copy-start | bytes 12292
  5.0 2.9 %collective-permute-start = (bf16[1024,512]{1,0:T(8,128)(2,1)}, bf16[1024,512]{1,0:T(8,128)(2,1)S(1)}, u32[]{:S(2)}, u32[]{:S(2)}) collective-permute-start(bf16[1024,512]{1,0:T(8,128)(2,1)} %get-tuple-element.30), channel_id=1, source_target_pairs={{0,4},{4,0},{8,12},{12,8},{16,20},{20,16},{24,28},{28,24},{32,36},... | collective-permute-start | bytes 3145736 | tf_op jit(solution)/shard_map/ppermute | solution.py:34
  5.1 2.8 %collective-permute-start.1 = (bf16[1024]{0:T(1024)(128)(2,1)S(1)}, bf16[1024]{0:T(1024)(128)(2,1)S(1)}, u32[]{:S(2)}, u32[]{:S(2)}) collective-permute-start(bf16[1024]{0:T(1024)(128)(2,1)S(1)} %add_convert_fusion.5), channel_id=1, source_target_pairs={{0,4},{4,0},{8,12},{12,8},{16,20},{20,16},{24,28},{28,24},{32,36},... | collective-permute-start | bytes 6152 | tf_op jit(solution)/shard_map/ppermute | solution.py:34
  9.4 19.3 %copy-start.1 = (bf16[2064,256]{1,0:T(8,128)(2,1)}, bf16[2064,256]{1,0:T(8,128)(2,1)S(1)}, u32[]{:S(2)}) copy-start(bf16[2064,256]{1,0:T(8,128)(2,1)S(1)} %get-tuple-element.41.refs_1_) | copy-start | bytes 3170308
  9.4 28.7 %collective-permute-start.2 = (bf16[2064,256]{1,0:T(8,128)(2,1)S(1)}, bf16[2064,256]{1,0:T(8,128)(2,1)}, u32[]{:S(2)}, u32[]{:S(2)}) collective-permute-start(bf16[2064,256]{1,0:T(8,128)(2,1)S(1)} %get-tuple-element.62.refs_0_), channel_id=1, source_target_pairs={{8,0},{12,4},{16,8},{20,12},{24,16},{28,20},{32,24},{36,28},{40,32... | collective-permute-start | bytes 3170312 | tf_op jit(solution)/shard_map/ppermute | solution.py:30
  15.3 29.1 %collective-permute-start.3 = (bf16[2064,256]{1,0:T(8,128)(2,1)S(1)}, bf16[2064,256]{1,0:T(8,128)(2,1)S(1)}, u32[]{:S(2)}, u32[]{:S(2)}) collective-permute-start(bf16[2064,256]{1,0:T(8,128)(2,1)S(1)} %get-tuple-element.41.refs_1_), channel_id=1, source_target_pairs={{0,8},{4,12},{8,16},{12,20},{16,24},{20,28},{24,32},{28,36},{32,40... | collective-permute-start | bytes 3170312 | tf_op jit(solution)/shard_map/ppermute | solution.py:30
  44.4 1.0 copy-start.4
  45.4 26.4 %collective-permute-start.4 = (bf16[2064,256]{1,0:T(8,128)(2,1)}, bf16[2064,256]{1,0:T(8,128)(2,1)}, u32[]{:S(2)}, u32[]{:S(2)}) collective-permute-start(bf16[2064,256]{1,0:T(8,128)(2,1)} %collective-permute-done.2.refs_0_), channel_id=1, source_target_pairs={{8,0},{12,4},{16,8},{20,12},{24,16},{28,20},{32,24},{36,28},{40,32... | collective-permute-start | bytes 3170312 | tf_op jit(solution)/shard_map/ppermute | solution.py:30
  47.3 1.2 copy-start.5
  73.8 30.8 %collective-permute-start.6 = (bf16[2048,128]{1,0:T(8,128)(2,1)S(1)}, bf16[2048,128]{1,0:T(8,128)(2,1)S(1)}, u32[]{:S(2)}, u32[]{:S(2)}) collective-permute-start(bf16[2048,128]{1,0:T(8,128)(2,1)S(1)} %get-tuple-element.39), channel_id=1, source_target_pairs={{0,8},{4,12},{8,16},{12,20},{16,24},{20,28},{24,32},{28,36},{32,40... | collective-permute-start | bytes 1572872 | tf_op jit(solution)/shard_map/ppermute | solution.py:30
  76.2 12.5 %copy-start.2 = (bf16[2064,256]{1,0:T(8,128)(2,1)S(1)}, bf16[2064,256]{1,0:T(8,128)(2,1)}, u32[]{:S(2)}) copy-start(bf16[2064,256]{1,0:T(8,128)(2,1)} %copy-done.1) | copy-start | bytes 3170308
  76.3 32.7 %collective-permute-start.10 = (bf16[1024,256]{1,0:T(8,128)(2,1)S(1)}, bf16[1024,256]{1,0:T(8,128)(2,1)S(1)}, u32[]{:S(2)}, u32[]{:S(2)}) collective-permute-start(bf16[1024,256]{1,0:T(8,128)(2,1)S(1)} %get-tuple-element.57), channel_id=1, source_target_pairs={{8,4},{12,0},{16,12},{20,8},{24,20},{28,16},{32,28},{36,24},{40,36... | collective-permute-start | bytes 1572872 | tf_op jit(solution)/shard_map/ppermute | solution.py:327
  84.8 24.2 %collective-permute-start.9 = (bf16[1024,256]{1,0:T(8,128)(2,1)S(1)}, bf16[1024,256]{1,0:T(8,128)(2,1)S(1)}, u32[]{:S(2)}, u32[]{:S(2)}) collective-permute-start(bf16[1024,256]{1,0:T(8,128)(2,1)S(1)} %get-tuple-element.58), channel_id=1, source_target_pairs={{8,0},{12,4},{16,8},{20,12},{24,16},{28,20},{32,24},{36,28},{40,32... | collective-permute-start | bytes 1572872 | tf_op jit(solution)/shard_map/ppermute | solution.py:30
  102.6 20.5 %collective-permute-start.5 = (bf16[1024,384]{1,0:T(8,128)(2,1)S(1)}, bf16[1024,384]{1,0:T(8,128)(2,1)S(1)}, u32[]{:S(2)}, u32[]{:S(2)}) collective-permute-start(bf16[1024,384]{1,0:T(8,128)(2,1)S(1)} %select_convert_fusion), channel_id=1, source_target_pairs={{0,4},{4,0},{8,12},{12,8},{16,20},{20,16},{24,28},{28,24},{32,36},... | collective-permute-start | bytes 2359304 | tf_op jit(solution)/shard_map/ppermute | solution.py:34
  104.8 12.4 %collective-permute-start.8 = (bf16[1024,128]{1,0:T(8,128)(2,1)S(1)}, bf16[1024,128]{1,0:T(8,128)(2,1)S(1)}, u32[]{:S(2)}, u32[]{:S(2)}) collective-permute-start(bf16[1024,128]{1,0:T(8,128)(2,1)S(1)} %get-tuple-element.59), channel_id=1, source_target_pairs={{0,12},{4,8},{8,20},{12,16},{16,28},{20,24},{24,36},{28,32},{32,44... | collective-permute-start | bytes 786440 | tf_op jit(solution)/shard_map/ppermute | solution.py:327
  106.7 16.4 %collective-permute-start.7 = (bf16[1024,128]{1,0:T(8,128)(2,1)S(1)}, bf16[1024,128]{1,0:T(8,128)(2,1)S(1)}, u32[]{:S(2)}, u32[]{:S(2)}) collective-permute-start(bf16[1024,128]{1,0:T(8,128)(2,1)S(1)} %get-tuple-element.60), channel_id=1, source_target_pairs={{0,8},{4,12},{8,16},{12,20},{16,24},{20,28},{24,32},{28,36},{32,40... | collective-permute-start | bytes 786440 | tf_op jit(solution)/shard_map/ppermute | solution.py:30
  108.7 14.4 %copy-start = (bf16[4,1024,256]{2,1,0:T(8,128)(2,1)S(1)}, bf16[4,1024,256]{2,1,0:T(8,128)(2,1)}, u32[]{:S(2)}) copy-start(bf16[4,1024,256]{2,1,0:T(8,128)(2,1)} %weights.3) | copy-start | bytes 6291460
  108.7 14.4 %copy-start.3 = (bf16[1024,256]{1,0:T(8,128)(2,1)S(1)}, bf16[1024,256]{1,0:T(8,128)(2,1)}, u32[]{:S(2)}) copy-start(bf16[1024,256]{1,0:T(8,128)(2,1)} %get-tuple-element.46.gate_grad) | copy-start | bytes 1572868
  124.6 8.4 %collective-permute-start.13 = (bf16[512,256]{1,0:T(8,128)(2,1)S(1)}, bf16[512,256]{1,0:T(8,128)(2,1)S(1)}, u32[]{:S(2)}, u32[]{:S(2)}) collective-permute-start(bf16[512,256]{1,0:T(8,128)(2,1)S(1)} %get-tuple-element.52), channel_id=1, source_target_pairs={{0,3},{1,0},{2,1},{3,2},{4,7},{5,4},{6,5},{7,6},{8,11},{9,8},{10,9... | collective-permute-start | bytes 786440 | tf_op jit(solution)/shard_map/ppermute | solution.py:342
  127.4 9.4 %collective-permute-start.11 = (bf16[512,256]{1,0:T(8,128)(2,1)S(1)}, bf16[512,256]{1,0:T(8,128)(2,1)S(1)}, u32[]{:S(2)}, u32[]{:S(2)}) collective-permute-start(bf16[512,256]{1,0:T(8,128)(2,1)S(1)} %get-tuple-element.50), channel_id=1, source_target_pairs={{0,1},{1,2},{2,3},{3,0},{4,5},{5,6},{6,7},{7,4},{8,9},{9,10},{10,1... | collective-permute-start | bytes 786440 | tf_op jit(solution)/shard_map/ppermute | solution.py:342
  133.1 14.1 %collective-permute-start.14 = (bf16[1024,256]{1,0:T(8,128)(2,1)S(1)}, bf16[1024,256]{1,0:T(8,128)(2,1)S(1)}, u32[]{:S(2)}, u32[]{:S(2)}) collective-permute-start(bf16[1024,256]{1,0:T(8,128)(2,1)S(1)} %pad_maximum_fusion.4), channel_id=1, source_target_pairs={{0,3},{1,0},{2,1},{3,2},{4,7},{5,4},{6,5},{7,6},{8,11},{9,8},{10,9... | collective-permute-start | bytes 1572872 | tf_op jit(solution)/shard_map/ppermute | solution.py:342
  137.0 13.8 %collective-permute-start.12 = (bf16[1024,256]{1,0:T(8,128)(2,1)S(1)}, bf16[1024,256]{1,0:T(8,128)(2,1)S(1)}, u32[]{:S(2)}, u32[]{:S(2)}) collective-permute-start(bf16[1024,256]{1,0:T(8,128)(2,1)S(1)} %pad_maximum_fusion.3), channel_id=1, source_target_pairs={{0,1},{1,2},{2,3},{3,0},{4,5},{5,6},{6,7},{7,4},{8,9},{9,10},{10,1... | collective-permute-start | bytes 1572872 | tf_op jit(solution)/shard_map/ppermute | solution.py:342

commit v2 on v1

--- a/solution.py
+++ b/solution.py
@@ -4,6 +4,7 @@
 from jax.experimental import pallas as pl
 from jax.experimental.pallas import tpu as pltpu
 from jax.sharding import PartitionSpec as P
+
 
 HEAD_DIM = 128
 ROWS = 1024
@@ -221,20 +222,19 @@
         ],
         compiler_params=params(28),
         cost_estimate=cost(20 * area * 128, area, 8 * PAIR * 256),
-        name=name,
     )(query, key)
 
 
-def collect_kernel(place, mine, other, dq_same, dq_cross, dkv_same, dkv_cross, gate_grad, weights,
+def collect_kernel(place, mine, other, far_same, far_cross, gate_grad, weights,
                    left, low, high):
     core, x = place[0], place[1]
     front = core == 0
     for p in range(3):
         cols = slice(p * 128, (p + 1) * 128)
-        same, cross = (dq_same, dq_cross) if p == 0 else (dkv_same, dkv_cross)
-        part = slice(max(p - 1, 0) * 128, max(p - 1, 0) * 128 + 128)
-        a = (mine[:, cols] + same[:, part].astype(F32)).astype(BF16)
-        b = (other[:, cols].astype(F32) + cross[:, part].astype(F32)).astype(BF16)
+        a, b = mine[:, cols], other[:, cols].astype(F32)
+        if p == 0:
+            a, b = a + far_same[...].astype(F32), b + far_cross[...].astype(F32)
+        a, b = a.astype(BF16), b.astype(BF16)
         left[:, p * 256:p * 256 + 128] = jnp.where(front, a, b)
         left[:, p * 256 + 128:p * 256 + 256] = jnp.where(front, b, a)
     left[:, 768:1024] = gate_grad[...]
@@ -266,7 +266,7 @@
     half = jax.ShapeDtypeStruct((ROWS // 2, 256), BF16)
     return pl.pallas_call(
         collect_kernel,
-        in_specs=[SMEM] + [VMEM] * 8,
+        in_specs=[SMEM] + [VMEM] * 6,
         out_specs=[VMEM] * 3,
         out_shape=[jax.ShapeDtypeStruct((ROWS, 1024), BF16), half, half],
         compiler_params=params(24),
@@ -287,7 +287,7 @@
     )(place, left, weights)
 
 
-def per_device(queries, key_rows, value_rows, attn_out, gate_pre, out_grad, segments, projections):
+def compute(queries, key_rows, value_rows, attn_out, gate_pre, out_grad, segments, projections):
     core = lax.axis_index("seq") % 2
     head = lax.axis_index("head")
     core_at = core.reshape(1).astype(jnp.int32)
@@ -306,13 +306,11 @@
     seg = jnp.pad(seg, ((0, SEG_ROWS - PAIR // 256), (0, 0)))
     query = jnp.concatenate([in_order(keep[:, :256], recv[:, :256]), seg])
     key = jnp.concatenate([in_order(keep[:, 256:], recv[:, 256:]), seg])
-    query_next, key_prev = shift(query, -2), shift(key, 2)
+    query_next = shift(query, -2)
+    key_prev = shift(key, 2)
     dq0, dkv0 = pairs("pairs_own", query, key, F32, PAIR * PAIR // 2)
-    query_next, key_prev, dq0 = lax.optimization_barrier((query_next, key_prev, dq0))
-    query_far = shift(query_next, -2)
-    dq2, dkv2 = pairs("pairs_two", query_next, key_prev, BF16, PAIR * PAIR // 2)
-    query_far, dq2 = lax.optimization_barrier((query_far, dq2))
-    dq3, dkv3 = pairs("pairs_three", query_far, key_prev, BF16, PAIR * PAIR // 8)
+    query, query_next, key_prev, dq0 = lax.optimization_barrier((query, query_next, key_prev, dq0))
+    query_far = shift(query, -6)
 
     def total(*terms):
         return sum(t.astype(F32) for t in terms)
@@ -320,23 +318,22 @@
     def halves(block):
         return jnp.where(front, block[:ROWS], block[ROWS:]), jnp.where(front, block[ROWS:], block[:ROWS])
 
-    def give(block, distance):
-        same, cross = halves(block.astype(BF16))
-        devices = range(lax.axis_size("seq"))
-        route = [(i, (i + distance) ^ 1) for i in devices if i + distance in devices]
-        return shift(same, distance), lax.ppermute(cross, "seq", route)
-
-    dkv_same, dkv_cross = give(total(dkv2, dkv3), -2)
-    dq3_next = shift(dq3, 2)
-    query_next, key, dkv3, dq3 = lax.optimization_barrier((query_next, key, dkv3, dq3))
+    dq2, dkv2 = pairs("pairs_two", query_next, key_prev, BF16, PAIR * PAIR // 2)
+    dkv_back = shift(dkv2, -2)
+    query_next, dq2 = lax.optimization_barrier((query_next, dq2))
     dq1, dkv1 = pairs("pairs_one", query_next, key, BF16, PAIR * PAIR)
-    dq_same, dq_cross = give(total(dq1, dq2, dq3_next), 2)
-    mine, other = halves(jnp.concatenate([dq0, total(dkv0, dkv1)], axis=1))
+    dq_back = shift(total(dq1, dq2).astype(BF16), 2)
+    query_far, dq1 = lax.optimization_barrier((query_far, dq1))
+    dq3, dkv3 = pairs("pairs_three", query_far, key, BF16, PAIR * PAIR // 8)
+    same, cross = halves(dq3)
+    route = [(i, (i + 6) ^ 1) for i in range(lax.axis_size("seq") - 6)]
+    far_same = shift(same, 6)
+    far_cross = lax.ppermute(cross, "seq", route)
+    grads = jnp.concatenate([total(dq0, dq_back), total(dkv0, dkv1, dkv3, dkv_back)], axis=1)
+    mine, other = halves(grads)
     other = swap(other.astype(BF16))
     place = jnp.stack([core, head]).astype(jnp.int32)
-    left, low, high = collect(
-        place, mine, other, dq_same, dq_cross, dkv_same, dkv_cross, gate_grad, projections
-    )
+    left, low, high = collect(place, mine, other, far_same, far_cross, gate_grad, projections)
 
     def turn(block, by):
         return lax.ppermute(block, "head", [(i, (i + by) % 4) for i in range(4)])
@@ -350,19 +347,11 @@
 
 
 def solution(mesh):
+    split = P("seq", "head")
     return jax.shard_map(
-        per_device,
+        compute,
         mesh=mesh,
-        in_specs=(
-            P("seq", "head"),
-            P("seq", "head"),
-            P("seq", "head"),
-            P("seq", "head"),
-            P("seq", "head"),
-            P("seq", "head"),
-            P("seq"),
-            P(None, None, "head"),
-        ),
-        out_specs=P("seq", "head"),
+        in_specs=(split,) * 6 + (P("seq"), P(None, None, "head")),
+        out_specs=split,
         check_vma=False,
     )

time: 154 us -> 152 us (0.987); the launches traced: 152 us -> 152 us
  Pallas kernels: 49.4 us -> 43.2 us
  waiting for transfers between devices: 58.7 us -> 63.4 us
  starting transfers between devices: 37.1 us -> 40 us
  local copies, waits for them, and re-layouts: 2.29 us -> 0.1 us
    ppermute x6, starting transfers between devices: 17.6 us -> 28.7 us  [shift(): lax.ppermute(block, 'seq', [(i, i + distance) for i in devices if i + dis...]
    ppermute x6, waiting for transfers between devices: 31.3 us -> 40.5 us  [shift(): lax.ppermute(block, 'seq', [(i, i + distance) for i in devices if i + dis...]
    ppermute x2 -> x1, starting transfers between devices: 10.4 us -> 4.13 us  [compute(): far_cross = lax.ppermute(cross, 'seq', route)]
    pallas_call x4, Pallas kernels: 40.5 us -> 34.5 us  [pairs(): pl.pallas_call(lambda *refs: pairs_kernel(name == 'pairs_own', *refs), in...]
    ppermute x2 -> x1, waiting for transfers between devices: 8.25 us -> 4.49 us  [compute(): far_cross = lax.ppermute(cross, 'seq', route)]
    unnamed x14 -> x10, local copies, waits for them, and re-layouts: 2.21 us -> 0.02 us
    ppermute x3, starting transfers between devices: 2.41 us -> 0.49 us  [swap(): lax.ppermute(block, 'seq', [(i, i ^ 1) for i in range(lax.axis_size('seq'...]
  transfers between devices with their start and end apart: 15 -> 14, of which waited for: 9 -> 10; matrix products, arithmetic and copies ran while one was open for 1% -> 1% of each run, Pallas kernels for 27% -> 24%
where the time goes in v2:
time: 152 us
  waiting for transfers between devices  63.4 us (42%)
  Pallas kernels  43.2 us (28%)
  starting transfers between devices  40 us (26%)
  other arithmetic  4.9 us (3%)
    ppermute x6, waiting for transfers between devices, shift(): lax.ppermute(block, 'seq', [(i, i + distance) for i in devices if i + dis...  40.5 us
    pallas_call x4, Pallas kernels, pairs(): pl.pallas_call(lambda *refs: pairs_kernel(name == 'pairs_own', *refs), in...  34.5 us
    ppermute x6, starting transfers between devices, shift(): lax.ppermute(block, 'seq', [(i, i + distance) for i in devices if i + dis...  28.7 us
    ppermute x4, waiting for transfers between devices, turn(): return lax.ppermute(block, 'head', [(i, (i + by) % 4) for i in range(4)])  16 us
    ppermute x4, starting transfers between devices, turn(): return lax.ppermute(block, 'head', [(i, (i + by) % 4) for i in range(4)])  6.66 us
    pallas_call x1, Pallas kernels, prepare(): pl.pallas_call(prepare_kernel, grid_spec=pltpu.PrefetchScalarGridSpec(num...  5.01 us
    ppermute x1, waiting for transfers between devices, compute(): far_cross = lax.ppermute(cross, 'seq', route)  4.49 us
    ppermute x1, starting transfers between devices, compute(): far_cross = lax.ppermute(cross, 'seq', route)  4.13 us
  transfers between devices with their start and end apart: 14, of which 10 were waited for; matrix products, arithmetic and copies ran while one was open for 1% of the time, Pallas kernels for 24%

profile of v2, /device:TPU:16, one launch (start us, length us, event | category | flops | bytes accessed | tf_op | source)
XLA Modules:
  0.0 151.8 jit_solution(3151327411726655129)
XLA Ops:
  0.0 0.0 copy-start.4
  0.0 5.0 %prepare.1 = (bf16[1024,512]{1,0:T(8,128)(2,1)}, bf16[1024,512]{1,0:T(8,128)(2,1)}, bf16[1024,256]{1,0:T(8,128)(2,1)}) custom-call(s32[1]{0:T(128)} %bitcast.core, bf16[1024,256]{1,0:T(8,128)(2,1)} %q.1, bf16[1024,256]{1,0:T(8,128)(2,1)} %k.1, bf16[1024,256]{1,0:T(8,128)(2,1)} %v.1, bf16[1024,256]{1,0:T(8,128)(2,1)} %o.1, bf16[1024,256]{1,0:T(8,128)(2,1)} %gate.1, ...), custom_call_target="tpu_custom_call" | custom-call | flops 7864320 | bytes 5767168 | tf_op jit(solution)/shard_map/prepare/pallas_call | solution.py:70
  5.0 0.0 collective-permute-start
  5.0 0.0 copy-done.4
  5.0 0.5 collective-permute-start.1
  5.5 2.4 %collective-permute-done.1 = bf16[1024]{0:T(1024)(128)(2,1)S(1)} collective-permute-done((bf16[1024]{0:T(1024)(128)(2,1)S(1)}, bf16[1024]{0:T(1024)(128)(2,1)S(1)}, u32[]{:S(2)}, u32[]{:S(2)}) %collective-permute-start.1) | collective-permute-done | bytes 2080 | tf_op jit(solution)/shard_map/ppermute | solution.py:35
  7.9 0.0 collective-permute-done
  7.9 1.3 broadcast_select_fusion.2
  9.3 0.1 pad_maximum_fusion.1
  9.4 5.8 %collective-permute-start.2 = (bf16[2064,256]{1,0:T(8,128)(2,1)S(1)}, bf16[2064,256]{1,0:T(8,128)(2,1)S(1)}, u32[]{:S(2)}, u32[]{:S(2)}) collective-permute-start(bf16[2064,256]{1,0:T(8,128)(2,1)S(1)} %get-tuple-element.41.refs_0_), channel_id=1, source_target_pairs={{8,0},{12,4},{16,8},{20,12},{24,16},{28,20},{32,24},{36,28},{40,32... | collective-permute-start | bytes 3170312 | tf_op jit(solution)/shard_map/ppermute | solution.py:31
  15.3 1.9 %collective-permute-start.3 = (bf16[2064,256]{1,0:T(8,128)(2,1)S(1)}, bf16[2064,256]{1,0:T(8,128)(2,1)S(1)}, u32[]{:S(2)}, u32[]{:S(2)}) collective-permute-start(bf16[2064,256]{1,0:T(8,128)(2,1)S(1)} %get-tuple-element.59.refs_1_), channel_id=1, source_target_pairs={{0,8},{4,12},{8,16},{12,20},{16,24},{20,28},{24,32},{28,36},{32,40... | collective-permute-start | bytes 3170312 | tf_op jit(solution)/shard_map/ppermute | solution.py:31
  17.2 11.6 %shard_map.82 = (f32[2048,128]{1,0:T(8,128)S(1)}, f32[2048,256]{1,0:T(8,128)S(1)}) custom-call(bf16[2064,256]{1,0:T(8,128)(2,1)S(1)} %get-tuple-element.41.refs_0_, bf16[2064,256]{1,0:T(8,128)(2,1)S(1)} %get-tuple-element.59.refs_1_), custom_call_target="tpu_custom_call" | custom-call | flops 5368709120 | bytes 4194304 | tf_op jit(solution)/shard_map/pallas_call | solution.py:202
  28.8 9.4 %collective-permute-done.2.refs_0_ = bf16[2064,256]{1,0:T(8,128)(2,1)S(1)} collective-permute-done((bf16[2064,256]{1,0:T(8,128)(2,1)S(1)}, bf16[2064,256]{1,0:T(8,128)(2,1)S(1)}, u32[]{:S(2)}, u32[]{:S(2)}) %collective-permute-start.2) | collective-permute-done | bytes 1056800 | tf_op jit(solution)/shard_map/ppermute | solution.py:31
  38.1 6.2 %collective-permute-done.3.refs_1_ = bf16[2064,256]{1,0:T(8,128)(2,1)S(1)} collective-permute-done((bf16[2064,256]{1,0:T(8,128)(2,1)S(1)}, bf16[2064,256]{1,0:T(8,128)(2,1)S(1)}, u32[]{:S(2)}, u32[]{:S(2)}) %collective-permute-start.3) | collective-permute-done | bytes 1056800 | tf_op jit(solution)/shard_map/ppermute | solution.py:31
  44.4 1.9 %collective-permute-start.5 = (bf16[2064,256]{1,0:T(8,128)(2,1)S(1)}, bf16[2064,256]{1,0:T(8,128)(2,1)S(1)}, u32[]{:S(2)}, u32[]{:S(2)}) collective-permute-start(bf16[2064,256]{1,0:T(8,128)(2,1)S(1)} %get-tuple-element.41.refs_0_), channel_id=1, source_target_pairs={{24,0},{28,4},{32,8},{36,12},{40,16},{44,20},{48,24},{52,28},{56,3... | collective-permute-start | bytes 3170312 | tf_op jit(solution)/shard_map/ppermute | solution.py:31
  46.3 1.1 shard_map.83
  47.4 16.4 %shard_map.84 = (bf16[2048,128]{1,0:T(8,128)(2,1)S(1)}, bf16[2048,256]{1,0:T(8,128)(2,1)S(1)}) custom-call(bf16[2064,256]{1,0:T(8,128)(2,1)S(1)} %collective-permute-done.2.refs_0_, bf16[2064,256]{1,0:T(8,128)(2,1)S(1)} %get-tuple-element.59.refs_1_), custom_call_target="tpu_custom_call" | custom-call | flops 10737418240 | bytes 4194304 | tf_op jit(solution)/shard_map/pallas_call | solution.py:202
  63.9 0.1 add_convert_fusion.1
  64.0 15.2 %collective-permute-start.4 = (bf16[2048,128]{1,0:T(8,128)(2,1)S(1)}, bf16[2048,128]{1,0:T(8,128)(2,1)S(1)}, u32[]{:S(2)}, u32[]{:S(2)}) collective-permute-start(bf16[2048,128]{1,0:T(8,128)(2,1)S(1)} %add_convert_fusion.1), channel_id=1, source_target_pairs={{0,8},{4,12},{8,16},{12,20},{16,24},{20,28},{24,32},{28,36},{32,40... | collective-permute-start | bytes 1572872 | tf_op jit(solution)/shard_map/ppermute | solution.py:31
  79.2 1.9 %collective-permute-start.6 = (bf16[2048,256]{1,0:T(8,128)(2,1)S(1)}, bf16[2048,256]{1,0:T(8,128)(2,1)S(1)}, u32[]{:S(2)}, u32[]{:S(2)}) collective-permute-start(bf16[2048,256]{1,0:T(8,128)(2,1)S(1)} %get-tuple-element.44), channel_id=1, source_target_pairs={{8,0},{12,4},{16,8},{20,12},{24,16},{28,20},{32,24},{36,28},{40,32... | collective-permute-start | bytes 3145736 | tf_op jit(solution)/shard_map/ppermute | solution.py:31
  81.2 8.7 %collective-permute-done.4 = bf16[2048,128]{1,0:T(8,128)(2,1)S(1)} collective-permute-done((bf16[2048,128]{1,0:T(8,128)(2,1)S(1)}, bf16[2048,128]{1,0:T(8,128)(2,1)S(1)}, u32[]{:S(2)}, u32[]{:S(2)}) %collective-permute-start.4) | collective-permute-done | bytes 524320 | tf_op jit(solution)/shard_map/ppermute | solution.py:31
  89.9 0.1 convert_add_fusion.1
  89.9 0.0 copy-start.2
  90.0 0.0 collective-permute-done.5.refs_0_
  90.0 5.3 %shard_map.85 = (bf16[2048,128]{1,0:T(8,128)(2,1)S(1)}, bf16[2048,256]{1,0:T(8,128)(2,1)S(1)}) custom-call(bf16[2064,256]{1,0:T(8,128)(2,1)S(1)} %collective-permute-done.5.refs_0_, bf16[2064,256]{1,0:T(8,128)(2,1)S(1)} %get-tuple-element.59.refs_1_), custom_call_target="tpu_custom_call" | custom-call | flops 1342177280 | bytes 4194304 | tf_op jit(solution)/shard_map/pallas_call | solution.py:202
  95.3 9.9 %collective-permute-done.6 = bf16[2048,256]{1,0:T(8,128)(2,1)S(1)} collective-permute-done((bf16[2048,256]{1,0:T(8,128)(2,1)S(1)}, bf16[2048,256]{1,0:T(8,128)(2,1)S(1)}, u32[]{:S(2)}, u32[]{:S(2)}) %collective-permute-start.6) | collective-permute-done | bytes 1048608 | tf_op jit(solution)/shard_map/ppermute | solution.py:31
  105.2 0.6 convert_add_fusion
  105.8 0.0 copy-done.2
  105.8 1.1 select_convert_fusion
  106.9 0.0 collective-permute-start.7
  106.9 0.0 copy-start.3
  106.9 4.1 %collective-permute-start.9 = (bf16[1024,128]{1,0:T(8,128)(2,1)S(1)}, bf16[1024,128]{1,0:T(8,128)(2,1)S(1)}, u32[]{:S(2)}, u32[]{:S(2)}) collective-permute-start(bf16[1024,128]{1,0:T(8,128)(2,1)S(1)} %get-tuple-element.57), channel_id=1, source_target_pairs={{0,28},{4,24},{8,36},{12,32},{16,44},{20,40},{24,52},{28,48},{32,6... | collective-permute-start | bytes 786440 | tf_op jit(solution)/shard_map/ppermute | solution.py:331
  111.1 1.9 %collective-permute-start.8 = (bf16[1024,128]{1,0:T(8,128)(2,1)S(1)}, bf16[1024,128]{1,0:T(8,128)(2,1)S(1)}, u32[]{:S(2)}, u32[]{:S(2)}) collective-permute-start(bf16[1024,128]{1,0:T(8,128)(2,1)S(1)} %get-tuple-element.58), channel_id=1, source_target_pairs={{0,24},{4,28},{8,32},{12,36},{16,40},{20,44},{24,48},{28,52},{32,5... | collective-permute-start | bytes 786440 | tf_op jit(solution)/shard_map/ppermute | solution.py:31
  113.0 0.1 pad_add_fusion.place
  113.1 0.0 copy-done.3
  113.1 0.0 copy-start
  113.1 0.0 copy-start.1
  113.1 0.2 broadcast_select_fusion.mine
  113.3 4.5 %collective-permute-done.9.far_cross = bf16[1024,128]{1,0:T(8,128)(2,1)S(1)} collective-permute-done((bf16[1024,128]{1,0:T(8,128)(2,1)S(1)}, bf16[1024,128]{1,0:T(8,128)(2,1)S(1)}, u32[]{:S(2)}, u32[]{:S(2)}) %collective-permute-start.9) | collective-permute-done | bytes 262176 | tf_op jit(solution)/shard_map/ppermute | solution.py:331
  117.8 6.3 %collective-permute-done.8.far_same = bf16[1024,128]{1,0:T(8,128)(2,1)S(1)} collective-permute-done((bf16[1024,128]{1,0:T(8,128)(2,1)S(1)}, bf16[1024,128]{1,0:T(8,128)(2,1)S(1)}, u32[]{:S(2)}, u32[]{:S(2)}) %collective-permute-start.8) | collective-permute-done | bytes 262176 | tf_op jit(solution)/shard_map/ppermute | solution.py:31
  124.1 0.0 collective-permute-done.7.other
  124.1 0.0 copy-done
  124.1 0.0 copy-done.1
  124.1 1.3 collect.1
  125.4 2.8 %collective-permute-start.12 = (bf16[512,256]{1,0:T(8,128)(2,1)S(1)}, bf16[512,256]{1,0:T(8,128)(2,1)S(1)}, u32[]{:S(2)}, u32[]{:S(2)}) collective-permute-start(bf16[512,256]{1,0:T(8,128)(2,1)S(1)} %get-tuple-element.52), channel_id=1, source_target_pairs={{0,3},{1,0},{2,1},{3,2},{4,7},{5,4},{6,5},{7,6},{8,11},{9,8},{10,9... | collective-permute-start | bytes 786440 | tf_op jit(solution)/shard_map/ppermute | solution.py:339
  128.3 0.0 collective-permute-start.10
  128.3 2.4 %project.1 = (f32[1024,256]{1,0:T(8,128)S(1)}, f32[1024,256]{1,0:T(8,128)S(1)}, f32[1024,256]{1,0:T(8,128)S(1)}) custom-call(s32[2]{0:T(128)S(1)} %pad_add_fusion.place, bf16[1024,1024]{1,0:T(8,128)(2,1)S(1)} %get-tuple-element.47.left, bf16[4,1024,256]{2,1,0:T(8,128)(2,1)S(1)} %copy-done), custom_call_target="tpu_custom_call" | custom-call | flops 1610612736 | bytes 8388608 | tf_op jit(solution)/shard_map/project/pallas_call | solution.py:279
  130.7 2.7 %collective-permute-done.12 = bf16[512,256]{1,0:T(8,128)(2,1)S(1)} collective-permute-done((bf16[512,256]{1,0:T(8,128)(2,1)S(1)}, bf16[512,256]{1,0:T(8,128)(2,1)S(1)}, u32[]{:S(2)}, u32[]{:S(2)}) %collective-permute-start.12) | collective-permute-done | bytes 262176 | tf_op jit(solution)/shard_map/ppermute | solution.py:339
  133.4 0.1 add_convert_fusion.2
  133.5 3.8 %collective-permute-start.13 = (bf16[1024,256]{1,0:T(8,128)(2,1)S(1)}, bf16[1024,256]{1,0:T(8,128)(2,1)S(1)}, u32[]{:S(2)}, u32[]{:S(2)}) collective-permute-start(bf16[1024,256]{1,0:T(8,128)(2,1)S(1)} %pad_maximum_fusion.4), channel_id=1, source_target_pairs={{0,3},{1,0},{2,1},{3,2},{4,7},{5,4},{6,5},{7,6},{8,11},{9,8},{10,9... | collective-permute-start | bytes 1572872 | tf_op jit(solution)/shard_map/ppermute | solution.py:339
  137.3 0.0 collective-permute-done.10
  137.3 0.1 add_convert_fusion.3
  137.4 0.1 collective-permute-start.11
  137.5 9.7 %collective-permute-done.13 = bf16[1024,256]{1,0:T(8,128)(2,1)S(1)} collective-permute-done((bf16[1024,256]{1,0:T(8,128)(2,1)S(1)}, bf16[1024,256]{1,0:T(8,128)(2,1)S(1)}, u32[]{:S(2)}, u32[]{:S(2)}) %collective-permute-start.13) | collective-permute-done | bytes 524320 | tf_op jit(solution)/shard_map/ppermute | solution.py:339
  147.2 3.6 %collective-permute-done.11 = bf16[1024,256]{1,0:T(8,128)(2,1)S(1)} collective-permute-done((bf16[1024,256]{1,0:T(8,128)(2,1)S(1)}, bf16[1024,256]{1,0:T(8,128)(2,1)S(1)}, u32[]{:S(2)}, u32[]{:S(2)}) %collective-permute-start.11) | collective-permute-done | bytes 524320 | tf_op jit(solution)/shard_map/ppermute | solution.py:339
  150.8 1.0 add_convert_fusion
  (10 shorter events, 0.2 us)
Async XLA Ops:
  0.0 5.0 %copy-start.4 = (s32[1024]{0:T(1024)S(1)}, s32[1024]{0:T(1024)}, u32[]{:S(2)}) copy-start(s32[1024]{0:T(1024)} %param.14) | copy-start | bytes 12292
  5.0 2.9 %collective-permute-start = (bf16[1024,512]{1,0:T(8,128)(2,1)}, bf16[1024,512]{1,0:T(8,128)(2,1)S(1)}, u32[]{:S(2)}, u32[]{:S(2)}) collective-permute-start(bf16[1024,512]{1,0:T(8,128)(2,1)} %get-tuple-element.30), channel_id=1, source_target_pairs={{0,4},{4,0},{8,12},{12,8},{16,20},{20,16},{24,28},{28,24},{32,36},... | collective-permute-start | bytes 3145736 | tf_op jit(solution)/shard_map/ppermute | solution.py:35
  5.0 2.8 %collective-permute-start.1 = (bf16[1024]{0:T(1024)(128)(2,1)S(1)}, bf16[1024]{0:T(1024)(128)(2,1)S(1)}, u32[]{:S(2)}, u32[]{:S(2)}) collective-permute-start(bf16[1024]{0:T(1024)(128)(2,1)S(1)} %add_convert_fusion.4), channel_id=1, source_target_pairs={{0,4},{4,0},{8,12},{12,8},{16,20},{20,16},{24,28},{28,24},{32,36},... | collective-permute-start | bytes 6152 | tf_op jit(solution)/shard_map/ppermute | solution.py:35
  9.4 28.7 %collective-permute-start.2 = (bf16[2064,256]{1,0:T(8,128)(2,1)S(1)}, bf16[2064,256]{1,0:T(8,128)(2,1)S(1)}, u32[]{:S(2)}, u32[]{:S(2)}) collective-permute-start(bf16[2064,256]{1,0:T(8,128)(2,1)S(1)} %get-tuple-element.41.refs_0_), channel_id=1, source_target_pairs={{8,0},{12,4},{16,8},{20,12},{24,16},{28,20},{32,24},{36,28},{40,32... | collective-permute-start | bytes 3170312 | tf_op jit(solution)/shard_map/ppermute | solution.py:31
  15.3 29.1 %collective-permute-start.3 = (bf16[2064,256]{1,0:T(8,128)(2,1)S(1)}, bf16[2064,256]{1,0:T(8,128)(2,1)S(1)}, u32[]{:S(2)}, u32[]{:S(2)}) collective-permute-start(bf16[2064,256]{1,0:T(8,128)(2,1)S(1)} %get-tuple-element.59.refs_1_), channel_id=1, source_target_pairs={{0,8},{4,12},{8,16},{12,20},{16,24},{20,28},{24,32},{28,36},{32,40... | collective-permute-start | bytes 3170312 | tf_op jit(solution)/shard_map/ppermute | solution.py:31
  44.4 45.6 %collective-permute-start.5 = (bf16[2064,256]{1,0:T(8,128)(2,1)S(1)}, bf16[2064,256]{1,0:T(8,128)(2,1)S(1)}, u32[]{:S(2)}, u32[]{:S(2)}) collective-permute-start(bf16[2064,256]{1,0:T(8,128)(2,1)S(1)} %get-tuple-element.41.refs_0_), channel_id=1, source_target_pairs={{24,0},{28,4},{32,8},{36,12},{40,16},{44,20},{48,24},{52,28},{56,3... | collective-permute-start | bytes 3170312 | tf_op jit(solution)/shard_map/ppermute | solution.py:31
  64.0 25.8 %collective-permute-start.4 = (bf16[2048,128]{1,0:T(8,128)(2,1)S(1)}, bf16[2048,128]{1,0:T(8,128)(2,1)S(1)}, u32[]{:S(2)}, u32[]{:S(2)}) collective-permute-start(bf16[2048,128]{1,0:T(8,128)(2,1)S(1)} %add_convert_fusion.1), channel_id=1, source_target_pairs={{0,8},{4,12},{8,16},{12,20},{16,24},{20,28},{24,32},{28,36},{32,40... | collective-permute-start | bytes 1572872 | tf_op jit(solution)/shard_map/ppermute | solution.py:31
  79.2 26.0 %collective-permute-start.6 = (bf16[2048,256]{1,0:T(8,128)(2,1)S(1)}, bf16[2048,256]{1,0:T(8,128)(2,1)S(1)}, u32[]{:S(2)}, u32[]{:S(2)}) collective-permute-start(bf16[2048,256]{1,0:T(8,128)(2,1)S(1)} %get-tuple-element.44), channel_id=1, source_target_pairs={{8,0},{12,4},{16,8},{20,12},{24,16},{28,20},{32,24},{36,28},{40,32... | collective-permute-start | bytes 3145736 | tf_op jit(solution)/shard_map/ppermute | solution.py:31
  89.9 15.9 %copy-start.2 = (f32[2048,128]{1,0:T(8,128)}, f32[2048,128]{1,0:T(8,128)S(1)}, u32[]{:S(2)}) copy-start(f32[2048,128]{1,0:T(8,128)S(1)} %convert_add_fusion.1) | copy-start | bytes 3145732
  106.9 17.2 %collective-permute-start.7 = (bf16[1024,384]{1,0:T(8,128)(2,1)}, bf16[1024,384]{1,0:T(8,128)(2,1)S(1)}, u32[]{:S(2)}, u32[]{:S(2)}) collective-permute-start(bf16[1024,384]{1,0:T(8,128)(2,1)} %select_convert_fusion), channel_id=1, source_target_pairs={{0,4},{4,0},{8,12},{12,8},{16,20},{20,16},{24,28},{28,24},{32,36},... | collective-permute-start | bytes 2359304 | tf_op jit(solution)/shard_map/ppermute | solution.py:35
  106.9 6.2 %copy-start.3 = (f32[2048,128]{1,0:T(8,128)S(1)}, f32[2048,128]{1,0:T(8,128)}, u32[]{:S(2)}) copy-start(f32[2048,128]{1,0:T(8,128)} %copy-done.2) | copy-start | bytes 3145732
  106.9 10.8 %collective-permute-start.9 = (bf16[1024,128]{1,0:T(8,128)(2,1)S(1)}, bf16[1024,128]{1,0:T(8,128)(2,1)S(1)}, u32[]{:S(2)}, u32[]{:S(2)}) collective-permute-start(bf16[1024,128]{1,0:T(8,128)(2,1)S(1)} %get-tuple-element.57), channel_id=1, source_target_pairs={{0,28},{4,24},{8,36},{12,32},{16,44},{20,40},{24,52},{28,48},{32,6... | collective-permute-start | bytes 786440 | tf_op jit(solution)/shard_map/ppermute | solution.py:331
  111.1 13.0 %collective-permute-start.8 = (bf16[1024,128]{1,0:T(8,128)(2,1)S(1)}, bf16[1024,128]{1,0:T(8,128)(2,1)S(1)}, u32[]{:S(2)}, u32[]{:S(2)}) collective-permute-start(bf16[1024,128]{1,0:T(8,128)(2,1)S(1)} %get-tuple-element.58), channel_id=1, source_target_pairs={{0,24},{4,28},{8,32},{12,36},{16,40},{20,44},{24,48},{28,52},{32,5... | collective-permute-start | bytes 786440 | tf_op jit(solution)/shard_map/ppermute | solution.py:31
  113.1 11.0 %copy-start = (bf16[4,1024,256]{2,1,0:T(8,128)(2,1)S(1)}, bf16[4,1024,256]{2,1,0:T(8,128)(2,1)}, u32[]{:S(2)}) copy-start(bf16[4,1024,256]{2,1,0:T(8,128)(2,1)} %weights.3) | copy-start | bytes 6291460
  113.1 11.0 %copy-start.1 = (bf16[1024,256]{1,0:T(8,128)(2,1)S(1)}, bf16[1024,256]{1,0:T(8,128)(2,1)}, u32[]{:S(2)}) copy-start(bf16[1024,256]{1,0:T(8,128)(2,1)} %get-tuple-element.46.gate_grad) | copy-start | bytes 1572868
  125.4 8.0 %collective-permute-start.12 = (bf16[512,256]{1,0:T(8,128)(2,1)S(1)}, bf16[512,256]{1,0:T(8,128)(2,1)S(1)}, u32[]{:S(2)}, u32[]{:S(2)}) collective-permute-start(bf16[512,256]{1,0:T(8,128)(2,1)S(1)} %get-tuple-element.52), channel_id=1, source_target_pairs={{0,3},{1,0},{2,1},{3,2},{4,7},{5,4},{6,5},{7,6},{8,11},{9,8},{10,9... | collective-permute-start | bytes 786440 | tf_op jit(solution)/shard_map/ppermute | solution.py:339
  128.3 9.0 %collective-permute-start.10 = (bf16[512,256]{1,0:T(8,128)(2,1)S(1)}, bf16[512,256]{1,0:T(8,128)(2,1)S(1)}, u32[]{:S(2)}, u32[]{:S(2)}) collective-permute-start(bf16[512,256]{1,0:T(8,128)(2,1)S(1)} %get-tuple-element.50), channel_id=1, source_target_pairs={{0,1},{1,2},{2,3},{3,0},{4,5},{5,6},{6,7},{7,4},{8,9},{9,10},{10,1... | collective-permute-start | bytes 786440 | tf_op jit(solution)/shard_map/ppermute | solution.py:339
  133.5 13.7 %collective-permute-start.13 = (bf16[1024,256]{1,0:T(8,128)(2,1)S(1)}, bf16[1024,256]{1,0:T(8,128)(2,1)S(1)}, u32[]{:S(2)}, u32[]{:S(2)}) collective-permute-start(bf16[1024,256]{1,0:T(8,128)(2,1)S(1)} %pad_maximum_fusion.4), channel_id=1, source_target_pairs={{0,3},{1,0},{2,1},{3,2},{4,7},{5,4},{6,5},{7,6},{8,11},{9,8},{10,9... | collective-permute-start | bytes 1572872 | tf_op jit(solution)/shard_map/ppermute | solution.py:339
  137.4 13.4 %collective-permute-start.11 = (bf16[1024,256]{1,0:T(8,128)(2,1)S(1)}, bf16[1024,256]{1,0:T(8,128)(2,1)S(1)}, u32[]{:S(2)}, u32[]{:S(2)}) collective-permute-start(bf16[1024,256]{1,0:T(8,128)(2,1)S(1)} %pad_maximum_fusion.3), channel_id=1, source_target_pairs={{0,1},{1,2},{2,3},{3,0},{4,5},{5,6},{6,7},{7,4},{8,9},{9,10},{10,1... | collective-permute-start | bytes 1572872 | tf_op jit(solution)/shard_map/ppermute | solution.py:339

commit v3 on v2

v3 whole, which is shorter than its diff:
```python
import jax
import jax.numpy as jnp
from jax import lax
from jax.experimental import pallas as pl
from jax.experimental.pallas import tpu as pltpu
from jax.sharding import PartitionSpec as P


HEAD_DIM = 128
ROWS = 1024
PAIR = 2 * ROWS
SEG_ROWS = 16
TILE = 512
TILES = PAIR // TILE
HALF_SCALE = 0.5 * HEAD_DIM ** (-0.5)
VMEM = pl.BlockSpec(memory_space=pltpu.VMEM)
SMEM = pl.BlockSpec(memory_space=pltpu.SMEM)
BF16, F32 = jnp.bfloat16, jnp.float32


def cost(flops, transcendentals, size):
    return pl.CostEstimate(flops=flops, transcendentals=transcendentals, bytes_accessed=size)


def params(mib):
    return pltpu.CompilerParams(vmem_limit_bytes=mib * 2**20)


def shift(block, distance):
    devices = range(lax.axis_size("seq"))
    return lax.ppermute(block, "seq", [(i, i + distance) for i in devices if i + distance in devices])


def swap(block):
    return lax.ppermute(block, "seq", [(i, i ^ 1) for i in range(lax.axis_size("seq"))])


def silu_slope(v):
    sigma = jax.nn.sigmoid(v)
    return sigma * (1.0 + v * (1.0 - sigma))


def split_kernel(core, k, v, keep, send):
    for slot, out in ((0, keep), (1, send)):
        head = core[0] if slot == 0 else 1 - core[0]
        cols = pl.ds(pl.multiple_of(head * HEAD_DIM, HEAD_DIM), HEAD_DIM)
        out[:, 0:128] = k[:, cols]
        out[:, 128:256] = v[:, cols]


def prepare_kernel(core, q, o, gate, grad, keep, send, gate_grad):
    for slot, out in ((0, keep), (1, send)):
        head = core[0] if slot == 0 else 1 - core[0]
        cols = pl.ds(pl.multiple_of(head * HEAD_DIM, HEAD_DIM), HEAD_DIM)
        saved = o[:, cols].astype(F32)
        centred = saved - jnp.mean(saved, axis=-1, keepdims=True)
        inverse = lax.rsqrt(jnp.mean(centred * centred, axis=-1, keepdims=True) + 1e-06)
        normed = centred * inverse
        gate_in = gate[:, cols].astype(F32)
        grad_in = grad[:, cols].astype(F32)
        gate_grad[:, cols] = (grad_in * normed * silu_slope(gate_in)).astype(BF16)
        g = grad_in * jax.nn.silu(gate_in)
        attn_grad = inverse * (
            g
            - jnp.mean(g, axis=-1, keepdims=True)
            - normed * jnp.mean(g * normed, axis=-1, keepdims=True)
        )
        out[:, 0:128] = q[:, cols]
        out[:, 128:256] = attn_grad.astype(BF16)


def by_rows(kernel, outputs, core, *arrays):
    rows = 256
    wide = pl.BlockSpec((rows, 2 * HEAD_DIM), lambda i, c: (i, 0))
    return pl.pallas_call(
        kernel,
        grid_spec=pltpu.PrefetchScalarGridSpec(
            num_scalar_prefetch=1,
            grid=(ROWS // rows,),
            in_specs=[wide] * len(arrays),
            out_specs=[wide] * outputs,
        ),
        out_shape=[jax.ShapeDtypeStruct((ROWS, 2 * HEAD_DIM), BF16)] * outputs,
        compiler_params=params(60),
        cost_estimate=cost(30 * ROWS * 256, 2 * ROWS * 256, 8 * ROWS * 512),
    )(core, *arrays)


def pairs_kernel(own, parts, tiles, *refs):
    q_in, k_in, dq_out, dkv_out = refs[:len(parts)], refs[len(parts)], refs[len(parts) + 1], refs[len(parts) + 2]
    q, k, dq, dk, dv, row_q, col_k, bound, todo, w0, d0, w1, d1, sem = refs[len(parts) + 3:]
    copies = [pltpu.make_async_copy(k_in, k, sem.at[0])]
    for ref, moves in zip(q_in, parts):
        for source, target, size in moves:
            copies.append(
                pltpu.make_async_copy(
                    ref.at[pl.ds(source, size)], q.at[pl.ds(target, size)], sem.at[len(copies)]
                )
            )
    for copy in copies:
        copy.start()
    dq[...] = jnp.zeros_like(dq)
    dk[...] = jnp.zeros_like(dk)
    dv[...] = jnp.zeros_like(dv)
    for copy in copies:
        copy.wait()
    blocks = PAIR // 256
    users_q, users_k = q[PAIR:].astype(F32), k[PAIR:].astype(F32)
    padded = jnp.concatenate([users_k, jnp.zeros((128 - SEG_ROWS, 256), F32)])
    for half in range(2):
        turned = jnp.transpose(padded[:, half * 128:half * 128 + 128])
        for r in range(blocks):
            start = r * 256 + half * 128
            col_k[start:start + 128] = jnp.broadcast_to(turned[:, r:r + 1], (128, 128))
    for r in range(blocks):
        row_q[:, r * 256:(r + 1) * 256] = users_q[r:r + 1]
    row_q[:, PAIR:] = jnp.full((1, TILE), -1.0, F32)
    for b in range(TILES):
        rows = slice(b * TILE // 256, (b + 1) * TILE // 256)
        bound[0, b] = jnp.min(users_q[rows])
        bound[1, b] = jnp.max(users_q[rows])
        bound[2, b] = jnp.min(users_k[rows])
        bound[3, b] = jnp.max(users_k[rows])

    count = jnp.int32(0)
    for kt in range(TILES):
        for qt in tiles:
            if own and qt < kt:
                continue
            some = (bound[0, qt] <= bound[3, kt]) & (bound[1, qt] >= bound[2, kt])
            todo[0, count] = qt
            todo[1, count] = kt
            todo[2, count] = qt
            count = count + some.astype(jnp.int32)
    for extra in range(3):
        todo[0, count + extra] = tiles[0]
        todo[1, count + extra] = 0
        todo[2, count + extra] = TILES
    last = (((1,), (1,)), ((), ()))
    first = (((0,), (0,)), ((), ()))

    def rows_of(tile):
        return pl.ds(pl.multiple_of(tile * TILE, TILE), TILE)

    def score(n, w_out, d_out):
        qt, kt = todo[0, n], todo[1, n]
        q_at, k_at = rows_of(qt), rows_of(kt)
        s = lax.dot_general(k[k_at, 0:128], q[q_at, 0:128], last, preferred_element_type=F32)
        p = lax.dot_general(k[k_at, 128:256], q[q_at, 128:256], last, preferred_element_type=F32)
        allowed = col_k[k_at, 0:1] == row_q[:, rows_of(todo[2, n])]
        if own:
            ahead = (qt - kt) * TILE
            allowed = allowed & (
                lax.broadcasted_iota(jnp.int32, (TILE, TILE), 1) + ahead
                >= lax.broadcasted_iota(jnp.int32, (TILE, TILE), 0)
            )
        y = jnp.where(allowed, s * HALF_SCALE, -64.0)
        t = jnp.tanh(y)
        u = 1.0 + t
        w = y * u
        d_out[...] = (p * (u + w * (1.0 - t))).astype(BF16)
        w_out[...] = w.astype(BF16)

    def gather(n, w_in, d_in):
        q_at, k_at = rows_of(todo[0, n]), rows_of(todo[1, n])
        dv[k_at, :] += jnp.dot(w_in[...], q[q_at, 128:256], preferred_element_type=F32)
        dk[k_at, :] += jnp.dot(d_in[...], q[q_at, 0:128], preferred_element_type=F32)
        dq[q_at, :] += lax.dot_general(d_in[...], k[k_at, 0:128], first, preferred_element_type=F32)

    @pl.when(count > 0)
    def _():
        score(0, w0, d0)

        def two(j, carry):
            n = 2 * j
            score(n + 1, w1, d1)
            gather(n, w0, d0)
            score(n + 2, w0, d0)
            gather(n + 1, w1, d1)
            return carry

        lax.fori_loop(0, (count + 1) // 2, two, 0)

    at = slice(tiles[0] * TILE, (tiles[-1] + 1) * TILE)
    dq_out[...] = (dq[at] * HALF_SCALE).astype(dq_out.dtype)
    dkv_out[:, 0:128] = (dk[...] * HALF_SCALE).astype(dkv_out.dtype)
    dkv_out[:, 128:256] = dv[...].astype(dkv_out.dtype)


WHOLE = [(0, 0, PAIR + SEG_ROWS)]
EARLY = [(0, 0, ROWS), (ROWS, PAIR, SEG_ROWS)]
USERS_ONLY = [(ROWS, PAIR, SEG_ROWS)]
LATE = [(0, ROWS, ROWS)]


def pairs(name, queries, parts, key, kind, tiles, area):
    anywhere = pl.BlockSpec(memory_space=pl.ANY)
    return pl.pallas_call(
        lambda *refs: pairs_kernel(name == "pairs_own", parts, tiles, *refs),
        in_specs=[anywhere] * (len(queries) + 1),
        out_specs=[VMEM] * 2,
        out_shape=[
            jax.ShapeDtypeStruct((len(tiles) * TILE, 128), kind),
            jax.ShapeDtypeStruct((PAIR, 256), kind),
        ],
        scratch_shapes=[
            pltpu.VMEM((PAIR + SEG_ROWS, 256), BF16),
            pltpu.VMEM((PAIR + SEG_ROWS, 256), BF16),
            pltpu.VMEM((PAIR, 128), F32),
            pltpu.VMEM((PAIR, 128), F32),
            pltpu.VMEM((PAIR, 128), F32),
            pltpu.VMEM((1, PAIR + TILE), F32),
            pltpu.VMEM((PAIR, 128), F32),
            pltpu.SMEM((4, TILES), F32),
            pltpu.SMEM((3, TILES * TILES + 4), jnp.int32),
            pltpu.VMEM((TILE, TILE), BF16),
            pltpu.VMEM((TILE, TILE), BF16),
            pltpu.VMEM((TILE, TILE), BF16),
            pltpu.VMEM((TILE, TILE), BF16),
            pltpu.SemaphoreType.DMA((4,)),
        ],
        compiler_params=params(28),
        cost_estimate=cost(20 * area * 128, area, 8 * PAIR * 256),
    )(*queries, key)


def collect_kernel(place, mine, other, back_same, back_cross, far_same, far_cross, gate_grad, weights,
                   left, low, high):
    core, x = place[0], place[1]
    front = core == 0
    for p in range(3):
        cols = slice(p * 128, (p + 1) * 128)
        a, b = mine[:, cols], other[:, cols].astype(F32)
        if p == 0:
            a = a + back_same[...].astype(F32) + far_same[...].astype(F32)
            b = b + back_cross[...].astype(F32) + far_cross[...].astype(F32)
        a, b = a.astype(BF16), b.astype(BF16)
        left[:, p * 256:p * 256 + 128] = jnp.where(front, a, b)
        left[:, p * 256 + 128:p * 256 + 256] = jnp.where(front, b, a)
    left[:, 768:1024] = gate_grad[...]
    far = head_block(left, weights, lax.rem(x + 2, 4)).astype(BF16)
    low[...] = far[:ROWS // 2]
    high[...] = far[ROWS // 2:]


def head_block(left, weights, dest):
    ds = pl.ds(pl.multiple_of(dest * 256, 256), 256)
    acc = None
    for p in range(4):
        term = lax.dot_general(
            left[:, p * 256:p * 256 + 256], weights[p, ds, :], (((1,), (1,)), ((), ())),
            preferred_element_type=F32,
        )
        acc = term if acc is None else acc + term
    return acc


def project_kernel(place, left, weights, after, before, own):
    x = place[1]
    after[...] = head_block(left, weights, lax.rem(x + 1, 4))
    before[...] = head_block(left, weights, lax.rem(x + 3, 4))
    own[...] = head_block(left, weights, x)


def collect(place, *arrays):
    half = jax.ShapeDtypeStruct((ROWS // 2, 256), BF16)
    return pl.pallas_call(
        collect_kernel,
        in_specs=[SMEM] + [VMEM] * 8,
        out_specs=[VMEM] * 3,
        out_shape=[jax.ShapeDtypeStruct((ROWS, 1024), BF16), half, half],
        compiler_params=params(24),
        cost_estimate=cost(2 * ROWS * 1024 * 256, 0, 8 * ROWS * 1024),
        name="collect",
    )(place, *arrays)


def project(place, left, weights):
    return pl.pallas_call(
        project_kernel,
        in_specs=[SMEM, VMEM, VMEM],
        out_specs=[VMEM] * 3,
        out_shape=[jax.ShapeDtypeStruct((ROWS, 256), F32)] * 3,
        compiler_params=params(24),
        cost_estimate=cost(2 * ROWS * 1024 * 768, 0, 8 * ROWS * 1024),
        name="project",
    )(place, left, weights)


def compute(queries, key_rows, value_rows, attn_out, gate_pre, out_grad, segments, projections):
    core = lax.axis_index("seq") % 2
    head = lax.axis_index("head")
    front = core == 0
    core_at = core.reshape(1).astype(jnp.int32)

    def in_order(kept, received):
        return jnp.where(front, kept, received), jnp.where(front, received, kept)

    def total(*terms):
        return sum(t.astype(F32) for t in terms)

    def halves(block):
        return in_order(block[:ROWS], block[ROWS:])

    def give(same, cross, distance):
        devices = range(lax.axis_size("seq") - distance)
        same = shift(same, distance)
        cross = lax.ppermute(cross, "seq", [(i, (i + distance) ^ 1) for i in devices])
        return same, cross

    users = (segments + 1).astype(BF16)
    users_recv = swap(users)
    kv_keep, kv_send = by_rows(split_kernel, 2, core_at, key_rows, value_rows)
    kv_recv = swap(kv_send)
    keep, send, gate_grad = by_rows(
        prepare_kernel, 3, core_at, queries, attn_out, gate_pre, out_grad
    )
    recv = swap(send)
    seg = jnp.concatenate(in_order(users, users_recv)).reshape(PAIR // 256, 256)
    seg = jnp.pad(seg, ((0, SEG_ROWS - PAIR // 256), (0, 0)))
    key = jnp.concatenate([*in_order(kv_keep, kv_recv), seg])
    key_prev = shift(key, 2)
    recv, key, seg = lax.optimization_barrier((recv, key, seg))
    low_rows, high_rows = in_order(keep, recv)
    next_a = shift(jnp.concatenate([low_rows, seg]), -2)
    next_b = shift(high_rows, -2)
    query = jnp.concatenate([low_rows, high_rows, seg])
    every, early, late = (0, 1, 2, 3), (0, 1), (2, 3)
    area = PAIR * PAIR
    dq0, dkv0 = pairs("pairs_own", [query], [WHOLE], key, F32, every, area // 2)
    next_a, dq0 = lax.optimization_barrier((next_a, dq0))
    dq1a, dkv1a = pairs("pairs_one", [next_a], [EARLY], key, BF16, early, area // 2)
    query, next_a, next_b, key_prev, dq1a = lax.optimization_barrier(
        (query, next_a, next_b, key_prev, dq1a)
    )
    query_far = shift(query, -6)
    dq2, dkv2 = pairs(
        "pairs_two", [next_a, next_b], [EARLY, LATE], key_prev, BF16, every, area // 2
    )
    dkv_back = shift(dkv2, -2)
    next_b, dq2 = lax.optimization_barrier((next_b, dq2))
    dq1b, dkv1b = pairs(
        "pairs_one", [next_a, next_b], [USERS_ONLY, LATE], key, BF16, late, area // 2
    )
    back = in_order(total(dq1a, dq2[:ROWS]).astype(BF16), total(dq1b, dq2[ROWS:]).astype(BF16))
    back_same, back_cross = give(*back, 2)
    query_far, dq1b = lax.optimization_barrier((query_far, dq1b))
    dq3, dkv3 = pairs("pairs_three", [query_far], [WHOLE], key, BF16, every, area // 8)
    far_same, far_cross = give(*halves(dq3), 6)
    grads = jnp.concatenate([dq0, total(dkv0, dkv1a, dkv1b, dkv3, dkv_back)], axis=1)
    mine, other = halves(grads)
    other = swap(other.astype(BF16))
    place = jnp.stack([core, head]).astype(jnp.int32)
    left, low, high = collect(
        place, mine, other, back_same, back_cross, far_same, far_cross, gate_grad, projections
    )

    def turn(block, by):
        return lax.ppermute(block, "head", [(i, (i + by) % 4) for i in range(4)])

    low, high = turn(low, 1), turn(high, -1)
    after, before, result = project(place, left, projections)
    half = ROWS // 2
    after = jnp.concatenate([after[:half] + low.astype(F32), after[half:]]).astype(BF16)
    before = jnp.concatenate([before[:half], before[half:] + high.astype(F32)]).astype(BF16)
    return total(result, turn(after, 1), turn(before, -1)).astype(BF16)


def solution(mesh):
    split = P("seq", "head")
    return jax.shard_map(
        compute,
        mesh=mesh,
        in_specs=(split,) * 6 + (P("seq"), P(None, None, "head")),
        out_specs=split,
        check_vma=False,
    )
```

time: 152 us -> 149 us (0.980)
  the two profiles are of different devices: /device:TPU:16 before, /device:TPU:88 now
where the time goes in v3:
time: 149 us
  waiting for transfers between devices  67.8 us (46%)
  starting transfers between devices  42.9 us (29%)
  Pallas kernels  32.5 us (22%)
  other arithmetic  4.64 us (3%)
    ppermute x7, waiting for transfers between devices, shift(): lax.ppermute(block, 'seq', [(i, i + distance) for i in devices if i + dis...  36.5 us
    ppermute x7, starting transfers between devices, shift(): lax.ppermute(block, 'seq', [(i, i + distance) for i in devices if i + dis...  32.4 us
    pallas_call x5, Pallas kernels, pairs(): pl.pallas_call(lambda *refs: pairs_kernel(name == 'pairs_own', parts, til...  20.8 us
    ppermute x4, waiting for transfers between devices, turn(): return lax.ppermute(block, 'head', [(i, (i + by) % 4) for i in range(4)])  17 us
    ppermute x2, waiting for transfers between devices, give(): cross = lax.ppermute(cross, 'seq', [(i, i + distance ^ 1) for i in devices])  14.2 us
    pallas_call x2, Pallas kernels, by_rows(): pl.pallas_call(kernel, grid_spec=pltpu.PrefetchScalarGridSpec(num_scalar_...  7.9 us
    ppermute x4, starting transfers between devices, turn(): return lax.ppermute(block, 'head', [(i, (i + by) % 4) for i in range(4)])  6.66 us
    ppermute x2, starting transfers between devices, give(): cross = lax.ppermute(cross, 'seq', [(i, i + distance ^ 1) for i in devices])  3.34 us
  transfers between devices with their start and end apart: 17, of which 11 were waited for; matrix products, arithmetic and copies ran while one was open for 1% of the time, Pallas kernels for 19%

profile of v3, /device:TPU:88, one launch (start us, length us, event | category | flops | bytes accessed | tf_op | source)
XLA Modules:
  0.0 148.6 jit_solution(7960720087799838759)
XLA Ops:
  0.0 3.5 %shard_map.83 = (bf16[1024,256]{1,0:T(8,128)(2,1)}, bf16[1024,256]{1,0:T(8,128)(2,1)}) custom-call(s32[1]{0:T(128)} %bitcast.core, bf16[1024,256]{1,0:T(8,128)(2,1)} %k.1, bf16[1024,256]{1,0:T(8,128)(2,1)} %v.1), custom_call_target="tpu_custom_call" | custom-call | flops 7864320 | bytes 4194304 | tf_op jit(solution)/shard_map/pallas_call | solution.py:75
  3.5 0.0 collective-permute-start.1
  3.5 0.8 add_convert_fusion.5
  4.2 0.4 collective-permute-start.2
  4.7 4.4 %shard_map.82 = (bf16[1024,256]{1,0:T(8,128)(2,1)}, bf16[1024,256]{1,0:T(8,128)(2,1)}, bf16[1024,256]{1,0:T(8,128)(2,1)}) custom-call(s32[1]{0:T(128)} %bitcast.core, bf16[1024,256]{1,0:T(8,128)(2,1)} %q.1, bf16[1024,256]{1,0:T(8,128)(2,1)} %o.1, bf16[1024,256]{1,0:T(8,128)(2,1)} %gate.1, bf16[1024,256]{1,0:T(8,128)(2,1)} %grad.1), custom_call_target="tpu_custom_call" | custom-call | flops 7864320 | bytes 4194304 | tf_op jit(solution)/shard_map/pallas_call | solution.py:75
  9.1 0.1 collective-permute-start
  9.2 0.0 collective-permute-done.2
  9.2 0.0 copy-done.6
  9.2 0.0 collective-permute-done.1
  9.2 0.0 copy-done.5
  9.2 0.1 broadcast_select_fusion.4
  9.3 0.0 copy-start.4
  9.3 0.1 pad_maximum_fusion.1.refs_1_.refs_2_
  9.4 3.7 %collective-permute-start.5 = (bf16[2064,256]{1,0:T(8,128)(2,1)S(1)}, bf16[2064,256]{1,0:T(8,128)(2,1)S(1)}, u32[]{:S(2)}, u32[]{:S(2)}) collective-permute-start(bf16[2064,256]{1,0:T(8,128)(2,1)S(1)} %pad_maximum_fusion.1.refs_1_.refs_2_), channel_id=1, source_target_pairs={{0,8},{4,12},{8,16},{12,20},{16,24},{20,28},{24,32},{28,36},{32,40... | collective-permute-start | bytes 3170312 | tf_op jit(solution)/shard_map/ppermute | solution.py:31
  13.1 0.0 collective-permute-done
  13.1 0.0 copy-done.4
  13.1 0.1 broadcast_select_fusion.2
  13.2 2.3 %collective-permute-start.3 = (bf16[1040,256]{1,0:T(8,128)(2,1)S(1)}, bf16[1040,256]{1,0:T(8,128)(2,1)S(1)}, u32[]{:S(2)}, u32[]{:S(2)}) collective-permute-start(bf16[1040,256]{1,0:T(8,128)(2,1)S(1)} %pad_maximum_fusion.3), channel_id=1, source_target_pairs={{8,0},{12,4},{16,8},{20,12},{24,16},{28,20},{32,24},{36,28},{40,32... | collective-permute-start | bytes 1597448 | tf_op jit(solution)/shard_map/ppermute | solution.py:31
  15.6 0.1 pad_maximum_fusion.2.refs_0_
  15.6 2.0 %collective-permute-start.4 = (bf16[1024,256]{1,0:T(8,128)(2,1)S(1)}, bf16[1024,256]{1,0:T(8,128)(2,1)S(1)}, u32[]{:S(2)}, u32[]{:S(2)}) collective-permute-start(bf16[1024,256]{1,0:T(8,128)(2,1)S(1)} %get-tuple-element.76), channel_id=1, source_target_pairs={{8,0},{12,4},{16,8},{20,12},{24,16},{28,20},{32,24},{36,28},{40,32... | collective-permute-start | bytes 1572872 | tf_op jit(solution)/shard_map/ppermute | solution.py:31
  17.7 11.5 %shard_map.84 = (f32[2048,128]{1,0:T(8,128)S(1)}, f32[2048,256]{1,0:T(8,128)S(1)}) custom-call(bf16[2064,256]{1,0:T(8,128)(2,1)S(1)} %pad_maximum_fusion.2.refs_0_, bf16[2064,256]{1,0:T(8,128)(2,1)S(1)} %pad_maximum_fusion.1.refs_1_.refs_2_), custom_call_target="tpu_custom_call" | custom-call | flops 5368709120 | bytes 4194304 | tf_op jit(solution)/shard_map/pallas_call | solution.py:198
  29.2 0.9 collective-permute-done.3.refs_0_
  30.1 3.4 %shard_map.85 = (bf16[1024,128]{1,0:T(8,128)(2,1)S(1)}, bf16[2048,256]{1,0:T(8,128)(2,1)S(1)}) custom-call(bf16[1040,256]{1,0:T(8,128)(2,1)S(1)} %collective-permute-done.3.refs_0_, bf16[2064,256]{1,0:T(8,128)(2,1)S(1)} %pad_maximum_fusion.1.refs_1_.refs_2_), custom_call_target="tpu_custom_call" | custom-call | flops 5368709120 | bytes 4194304 | tf_op jit(solution)/shard_map/pallas_call | solution.py:198
  33.5 7.0 %collective-permute-done.4.refs_1_ = bf16[1024,256]{1,0:T(8,128)(2,1)S(1)} collective-permute-done((bf16[1024,256]{1,0:T(8,128)(2,1)S(1)}, bf16[1024,256]{1,0:T(8,128)(2,1)S(1)}, u32[]{:S(2)}, u32[]{:S(2)}) %collective-permute-start.4) | collective-permute-done | bytes 524320 | tf_op jit(solution)/shard_map/ppermute | solution.py:31
  40.5 0.0 collective-permute-done.5.refs_2_
  40.5 4.5 %collective-permute-start.6 = (bf16[2064,256]{1,0:T(8,128)(2,1)S(1)}, bf16[2064,256]{1,0:T(8,128)(2,1)S(1)}, u32[]{:S(2)}, u32[]{:S(2)}) collective-permute-start(bf16[2064,256]{1,0:T(8,128)(2,1)S(1)} %pad_maximum_fusion.2.refs_0_), channel_id=1, source_target_pairs={{24,0},{28,4},{32,8},{36,12},{40,16},{44,20},{48,24},{52,28},{56,3... | collective-permute-start | bytes 3170312 | tf_op jit(solution)/shard_map/ppermute | solution.py:31
  45.1 1.3 shard_map.86
  46.4 16.6 %collective-permute-start.7 = (bf16[2048,256]{1,0:T(8,128)(2,1)S(1)}, bf16[2048,256]{1,0:T(8,128)(2,1)S(1)}, u32[]{:S(2)}, u32[]{:S(2)}) collective-permute-start(bf16[2048,256]{1,0:T(8,128)(2,1)S(1)} %get-tuple-element.62), channel_id=1, source_target_pairs={{8,0},{12,4},{16,8},{20,12},{24,16},{28,20},{32,24},{36,28},{40,32... | collective-permute-start | bytes 3145736 | tf_op jit(solution)/shard_map/ppermute | solution.py:31
  63.1 3.4 %shard_map.87 = (bf16[1024,128]{1,0:T(8,128)(2,1)S(1)}, bf16[2048,256]{1,0:T(8,128)(2,1)S(1)}) custom-call(bf16[1040,256]{1,0:T(8,128)(2,1)S(1)} %collective-permute-done.3.refs_0_, bf16[1024,256]{1,0:T(8,128)(2,1)S(1)} %collective-permute-done.4.refs_1_, bf16[2064,256]{1,0:T(8,128)(2,1)S(1)} %pad_maximum_fusion.1.refs_1_.refs_2_), custom_call_target="tpu_custom_call" | custom-call | flops 5368709120 | bytes 4194304 | tf_op jit(solution)/shard_map/pallas_call | solution.py:198
  66.5 0.8 collective-permute-done.6.refs_0_
  67.4 1.1 shard_map.88
  68.5 16.2 %collective-permute-done.7 = bf16[2048,256]{1,0:T(8,128)(2,1)S(1)} collective-permute-done((bf16[2048,256]{1,0:T(8,128)(2,1)S(1)}, bf16[2048,256]{1,0:T(8,128)(2,1)S(1)}, u32[]{:S(2)}, u32[]{:S(2)}) %collective-permute-start.7) | collective-permute-done | bytes 1048608 | tf_op jit(solution)/shard_map/ppermute | solution.py:31
  84.7 0.7 convert_add_fusion
  85.3 0.0 copy-start.2
  85.3 1.2 select_convert_fusion
  86.5 0.3 copy-done.2
  86.9 0.0 collective-permute-start.8
  86.9 0.2 broadcast_select_fusion.7
  87.1 2.1 %collective-permute-start.10 = (bf16[1024,128]{1,0:T(8,128)(2,1)S(1)}, bf16[1024,128]{1,0:T(8,128)(2,1)S(1)}, u32[]{:S(2)}, u32[]{:S(2)}) collective-permute-start(bf16[1024,128]{1,0:T(8,128)(2,1)S(1)} %get-tuple-element.73), channel_id=1, source_target_pairs={{0,12},{4,8},{8,20},{12,16},{16,28},{20,24},{24,36},{28,32},{32,44... | collective-permute-start | bytes 786440 | tf_op jit(solution)/shard_map/ppermute | solution.py:308
  89.1 1.9 %collective-permute-start.9 = (bf16[1024,128]{1,0:T(8,128)(2,1)S(1)}, bf16[1024,128]{1,0:T(8,128)(2,1)S(1)}, u32[]{:S(2)}, u32[]{:S(2)}) collective-permute-start(bf16[1024,128]{1,0:T(8,128)(2,1)S(1)} %get-tuple-element.74), channel_id=1, source_target_pairs={{0,8},{4,12},{8,16},{12,20},{16,24},{20,28},{24,32},{28,36},{32,40... | collective-permute-start | bytes 786440 | tf_op jit(solution)/shard_map/ppermute | solution.py:31
  91.1 1.3 collective-permute-start.12
  92.4 1.3 collective-permute-start.11
  93.7 0.1 pad_add_fusion.place
  93.8 0.0 copy-done.3
  93.8 0.2 broadcast_select_fusion.mine
  94.0 4.4 %collective-permute-done.10.back_cross = bf16[1024,128]{1,0:T(8,128)(2,1)S(1)} collective-permute-done((bf16[1024,128]{1,0:T(8,128)(2,1)S(1)}, bf16[1024,128]{1,0:T(8,128)(2,1)S(1)}, u32[]{:S(2)}, u32[]{:S(2)}) %collective-permute-start.10) | collective-permute-done | bytes 262176 | tf_op jit(solution)/shard_map/ppermute | solution.py:308
  98.4 5.8 %collective-permute-done.9.back_same = bf16[1024,128]{1,0:T(8,128)(2,1)S(1)} collective-permute-done((bf16[1024,128]{1,0:T(8,128)(2,1)S(1)}, bf16[1024,128]{1,0:T(8,128)(2,1)S(1)}, u32[]{:S(2)}, u32[]{:S(2)}) %collective-permute-start.9) | collective-permute-done | bytes 262176 | tf_op jit(solution)/shard_map/ppermute | solution.py:31
  104.2 9.8 %collective-permute-done.12.far_cross = bf16[1024,128]{1,0:T(8,128)(2,1)S(1)} collective-permute-done((bf16[1024,128]{1,0:T(8,128)(2,1)S(1)}, bf16[1024,128]{1,0:T(8,128)(2,1)S(1)}, u32[]{:S(2)}, u32[]{:S(2)}) %collective-permute-start.12) | collective-permute-done | bytes 262176 | tf_op jit(solution)/shard_map/ppermute | solution.py:308
  114.0 5.8 %collective-permute-done.11.far_same = bf16[1024,128]{1,0:T(8,128)(2,1)S(1)} collective-permute-done((bf16[1024,128]{1,0:T(8,128)(2,1)S(1)}, bf16[1024,128]{1,0:T(8,128)(2,1)S(1)}, u32[]{:S(2)}, u32[]{:S(2)}) %collective-permute-start.11) | collective-permute-done | bytes 262176 | tf_op jit(solution)/shard_map/ppermute | solution.py:31
  119.8 0.0 collective-permute-done.8.other
  119.8 0.0 copy-done
  119.8 1.4 collect.1
  121.2 2.8 %collective-permute-start.15 = (bf16[512,256]{1,0:T(8,128)(2,1)S(1)}, bf16[512,256]{1,0:T(8,128)(2,1)S(1)}, u32[]{:S(2)}, u32[]{:S(2)}) collective-permute-start(bf16[512,256]{1,0:T(8,128)(2,1)S(1)} %get-tuple-element.72), channel_id=1, source_target_pairs={{0,3},{1,0},{2,1},{3,2},{4,7},{5,4},{6,5},{7,6},{8,11},{9,8},{10,9... | collective-permute-start | bytes 786440 | tf_op jit(solution)/shard_map/ppermute | solution.py:359
  124.1 0.0 collective-permute-start.13
  124.1 2.4 %project.1 = (f32[1024,256]{1,0:T(8,128)S(1)}, f32[1024,256]{1,0:T(8,128)S(1)}, f32[1024,256]{1,0:T(8,128)S(1)}) custom-call(s32[2]{0:T(128)S(1)} %pad_add_fusion.place, bf16[1024,1024]{1,0:T(8,128)(2,1)S(1)} %get-tuple-element.67.left, bf16[4,1024,256]{2,1,0:T(8,128)(2,1)S(1)} %copy-done), custom_call_target="tpu_custom_call" | custom-call | flops 1610612736 | bytes 8388608 | tf_op jit(solution)/shard_map/project/pallas_call | solution.py:279
  126.5 3.2 %collective-permute-done.15 = bf16[512,256]{1,0:T(8,128)(2,1)S(1)} collective-permute-done((bf16[512,256]{1,0:T(8,128)(2,1)S(1)}, bf16[512,256]{1,0:T(8,128)(2,1)S(1)}, u32[]{:S(2)}, u32[]{:S(2)}) %collective-permute-start.15) | collective-permute-done | bytes 262176 | tf_op jit(solution)/shard_map/ppermute | solution.py:359
  129.7 0.1 add_convert_fusion.1
  129.8 3.8 %collective-permute-start.16 = (bf16[1024,256]{1,0:T(8,128)(2,1)S(1)}, bf16[1024,256]{1,0:T(8,128)(2,1)S(1)}, u32[]{:S(2)}, u32[]{:S(2)}) collective-permute-start(bf16[1024,256]{1,0:T(8,128)(2,1)S(1)} %pad_maximum_fusion.5), channel_id=1, source_target_pairs={{0,3},{1,0},{2,1},{3,2},{4,7},{5,4},{6,5},{7,6},{8,11},{9,8},{10,9... | collective-permute-start | bytes 1572872 | tf_op jit(solution)/shard_map/ppermute | solution.py:359
  133.6 0.0 collective-permute-done.13
  133.6 0.1 add_convert_fusion.2
  133.7 0.1 collective-permute-start.14
  133.8 10.2 %collective-permute-done.16 = bf16[1024,256]{1,0:T(8,128)(2,1)S(1)} collective-permute-done((bf16[1024,256]{1,0:T(8,128)(2,1)S(1)}, bf16[1024,256]{1,0:T(8,128)(2,1)S(1)}, u32[]{:S(2)}, u32[]{:S(2)}) %collective-permute-start.16) | collective-permute-done | bytes 524320 | tf_op jit(solution)/shard_map/ppermute | solution.py:359
  144.0 3.6 %collective-permute-done.14 = bf16[1024,256]{1,0:T(8,128)(2,1)S(1)} collective-permute-done((bf16[1024,256]{1,0:T(8,128)(2,1)S(1)}, bf16[1024,256]{1,0:T(8,128)(2,1)S(1)}, u32[]{:S(2)}, u32[]{:S(2)}) %collective-permute-start.14) | collective-permute-done | bytes 524320 | tf_op jit(solution)/shard_map/ppermute | solution.py:359
  147.6 1.0 add_convert_fusion
  (16 shorter events, 0.3 us)
Async XLA Ops:
  0.0 9.2 %copy-start.6 = (s32[1024]{0:T(1024)S(1)}, s32[1024]{0:T(1024)}, u32[]{:S(2)}) copy-start(s32[1024]{0:T(1024)} %param.14) | copy-start | bytes 12292
  3.5 5.8 %copy-start.5 = (bf16[1024,256]{1,0:T(8,128)(2,1)S(1)}, bf16[1024,256]{1,0:T(8,128)(2,1)}, u32[]{:S(2)}) copy-start(bf16[1024,256]{1,0:T(8,128)(2,1)} %get-tuple-element.41) | copy-start | bytes 1572868
  3.5 5.8 %collective-permute-start.1 = (bf16[1024,256]{1,0:T(8,128)(2,1)}, bf16[1024,256]{1,0:T(8,128)(2,1)S(1)}, u32[]{:S(2)}, u32[]{:S(2)}) collective-permute-start(bf16[1024,256]{1,0:T(8,128)(2,1)} %get-tuple-element.42), channel_id=1, source_target_pairs={{0,4},{4,0},{8,12},{12,8},{16,20},{20,16},{24,28},{28,24},{32,36},... | collective-permute-start | bytes 1572872 | tf_op jit(solution)/shard_map/ppermute | solution.py:35
  4.2 5.0 %collective-permute-start.2 = (bf16[1024]{0:T(1024)(128)(2,1)S(1)}, bf16[1024]{0:T(1024)(128)(2,1)S(1)}, u32[]{:S(2)}, u32[]{:S(2)}) collective-permute-start(bf16[1024]{0:T(1024)(128)(2,1)S(1)} %add_convert_fusion.5), channel_id=1, source_target_pairs={{0,4},{4,0},{8,12},{12,8},{16,20},{20,16},{24,28},{28,24},{32,36},... | collective-permute-start | bytes 6152 | tf_op jit(solution)/shard_map/ppermute | solution.py:35
  9.1 4.0 %collective-permute-start = (bf16[1024,256]{1,0:T(8,128)(2,1)}, bf16[1024,256]{1,0:T(8,128)(2,1)S(1)}, u32[]{:S(2)}, u32[]{:S(2)}) collective-permute-start(bf16[1024,256]{1,0:T(8,128)(2,1)} %get-tuple-element.40), channel_id=1, source_target_pairs={{0,4},{4,0},{8,12},{12,8},{16,20},{20,16},{24,28},{28,24},{32,36},... | collective-permute-start | bytes 1572872 | tf_op jit(solution)/shard_map/ppermute | solution.py:35
  9.3 3.8 %copy-start.4 = (bf16[1024,256]{1,0:T(8,128)(2,1)S(1)}, bf16[1024,256]{1,0:T(8,128)(2,1)}, u32[]{:S(2)}) copy-start(bf16[1024,256]{1,0:T(8,128)(2,1)} %get-tuple-element.39) | copy-start | bytes 1572868
  9.4 31.1 %collective-permute-start.5 = (bf16[2064,256]{1,0:T(8,128)(2,1)S(1)}, bf16[2064,256]{1,0:T(8,128)(2,1)S(1)}, u32[]{:S(2)}, u32[]{:S(2)}) collective-permute-start(bf16[2064,256]{1,0:T(8,128)(2,1)S(1)} %pad_maximum_fusion.1.refs_1_.refs_2_), channel_id=1, source_target_pairs={{0,8},{4,12},{8,16},{12,20},{16,24},{20,28},{24,32},{28,36},{32,40... | collective-permute-start | bytes 3170312 | tf_op jit(solution)/shard_map/ppermute | solution.py:31
  13.2 16.9 %collective-permute-start.3 = (bf16[1040,256]{1,0:T(8,128)(2,1)S(1)}, bf16[1040,256]{1,0:T(8,128)(2,1)S(1)}, u32[]{:S(2)}, u32[]{:S(2)}) collective-permute-start(bf16[1040,256]{1,0:T(8,128)(2,1)S(1)} %pad_maximum_fusion.3), channel_id=1, source_target_pairs={{8,0},{12,4},{16,8},{20,12},{24,16},{28,20},{32,24},{36,28},{40,32... | collective-permute-start | bytes 1597448 | tf_op jit(solution)/shard_map/ppermute | solution.py:31
  15.6 24.9 %collective-permute-start.4 = (bf16[1024,256]{1,0:T(8,128)(2,1)S(1)}, bf16[1024,256]{1,0:T(8,128)(2,1)S(1)}, u32[]{:S(2)}, u32[]{:S(2)}) collective-permute-start(bf16[1024,256]{1,0:T(8,128)(2,1)S(1)} %get-tuple-element.76), channel_id=1, source_target_pairs={{8,0},{12,4},{16,8},{20,12},{24,16},{28,20},{32,24},{36,28},{40,32... | collective-permute-start | bytes 1572872 | tf_op jit(solution)/shard_map/ppermute | solution.py:31
  40.5 26.8 %collective-permute-start.6 = (bf16[2064,256]{1,0:T(8,128)(2,1)S(1)}, bf16[2064,256]{1,0:T(8,128)(2,1)S(1)}, u32[]{:S(2)}, u32[]{:S(2)}) collective-permute-start(bf16[2064,256]{1,0:T(8,128)(2,1)S(1)} %pad_maximum_fusion.2.refs_0_), channel_id=1, source_target_pairs={{24,0},{28,4},{32,8},{36,12},{40,16},{44,20},{48,24},{52,28},{56,3... | collective-permute-start | bytes 3170312 | tf_op jit(solution)/shard_map/ppermute | solution.py:31
  46.4 38.2 %collective-permute-start.7 = (bf16[2048,256]{1,0:T(8,128)(2,1)S(1)}, bf16[2048,256]{1,0:T(8,128)(2,1)S(1)}, u32[]{:S(2)}, u32[]{:S(2)}) collective-permute-start(bf16[2048,256]{1,0:T(8,128)(2,1)S(1)} %get-tuple-element.62), channel_id=1, source_target_pairs={{8,0},{12,4},{16,8},{20,12},{24,16},{28,20},{32,24},{36,28},{40,32... | collective-permute-start | bytes 3145736 | tf_op jit(solution)/shard_map/ppermute | solution.py:31
  85.3 1.6 %copy-start.2 = (f32[2048,256]{1,0:T(8,128)}, f32[2048,256]{1,0:T(8,128)S(1)}, u32[]{:S(2)}) copy-start(f32[2048,256]{1,0:T(8,128)S(1)} %convert_add_fusion) | copy-start | bytes 6291460
  86.9 32.9 %collective-permute-start.8 = (bf16[1024,384]{1,0:T(8,128)(2,1)}, bf16[1024,384]{1,0:T(8,128)(2,1)S(1)}, u32[]{:S(2)}, u32[]{:S(2)}) collective-permute-start(bf16[1024,384]{1,0:T(8,128)(2,1)} %select_convert_fusion), channel_id=1, source_target_pairs={{0,4},{4,0},{8,12},{12,8},{16,20},{20,16},{24,28},{28,24},{32,36},... | collective-permute-start | bytes 2359304 | tf_op jit(solution)/shard_map/ppermute | solution.py:35
  86.9 6.9 %copy-start.3 = (f32[2048,256]{1,0:T(8,128)S(1)}, f32[2048,256]{1,0:T(8,128)}, u32[]{:S(2)}) copy-start(f32[2048,256]{1,0:T(8,128)} %copy-done.2) | copy-start | bytes 6291460
  87.1 11.3 %collective-permute-start.10 = (bf16[1024,128]{1,0:T(8,128)(2,1)S(1)}, bf16[1024,128]{1,0:T(8,128)(2,1)S(1)}, u32[]{:S(2)}, u32[]{:S(2)}) collective-permute-start(bf16[1024,128]{1,0:T(8,128)(2,1)S(1)} %get-tuple-element.73), channel_id=1, source_target_pairs={{0,12},{4,8},{8,20},{12,16},{16,28},{20,24},{24,36},{28,32},{32,44... | collective-permute-start | bytes 786440 | tf_op jit(solution)/shard_map/ppermute | solution.py:308
  89.1 15.0 %collective-permute-start.9 = (bf16[1024,128]{1,0:T(8,128)(2,1)S(1)}, bf16[1024,128]{1,0:T(8,128)(2,1)S(1)}, u32[]{:S(2)}, u32[]{:S(2)}) collective-permute-start(bf16[1024,128]{1,0:T(8,128)(2,1)S(1)} %get-tuple-element.74), channel_id=1, source_target_pairs={{0,8},{4,12},{8,16},{12,20},{16,24},{20,28},{24,32},{28,36},{32,40... | collective-permute-start | bytes 786440 | tf_op jit(solution)/shard_map/ppermute | solution.py:31
  91.1 22.9 %collective-permute-start.12 = (bf16[1024,128]{1,0:T(8,128)(2,1)S(1)}, bf16[1024,128]{1,0:T(8,128)(2,1)S(1)}, u32[]{:S(2)}, u32[]{:S(2)}) collective-permute-start(bf16[1024,128]{1,0:T(8,128)(2,1)S(1)} %get-tuple-element.79), channel_id=1, source_target_pairs={{0,28},{4,24},{8,36},{12,32},{16,44},{20,40},{24,52},{28,48},{32,6... | collective-permute-start | bytes 786440 | tf_op jit(solution)/shard_map/ppermute | solution.py:308
  92.4 27.4 %collective-permute-start.11 = (bf16[1024,128]{1,0:T(8,128)(2,1)S(1)}, bf16[1024,128]{1,0:T(8,128)(2,1)S(1)}, u32[]{:S(2)}, u32[]{:S(2)}) collective-permute-start(bf16[1024,128]{1,0:T(8,128)(2,1)S(1)} %get-tuple-element.80), channel_id=1, source_target_pairs={{0,24},{4,28},{8,32},{12,36},{16,40},{20,44},{24,48},{28,52},{32,5... | collective-permute-start | bytes 786440 | tf_op jit(solution)/shard_map/ppermute | solution.py:31
  93.8 26.0 %copy-start = (bf16[4,1024,256]{2,1,0:T(8,128)(2,1)S(1)}, bf16[4,1024,256]{2,1,0:T(8,128)(2,1)}, u32[]{:S(2)}) copy-start(bf16[4,1024,256]{2,1,0:T(8,128)(2,1)} %weights.3) | copy-start | bytes 6291460
  93.8 26.0 %copy-start.1 = (bf16[1024,256]{1,0:T(8,128)(2,1)S(1)}, bf16[1024,256]{1,0:T(8,128)(2,1)}, u32[]{:S(2)}) copy-start(bf16[1024,256]{1,0:T(8,128)(2,1)} %get-tuple-element.66.gate_grad) | copy-start | bytes 1572868
  121.2 8.5 %collective-permute-start.15 = (bf16[512,256]{1,0:T(8,128)(2,1)S(1)}, bf16[512,256]{1,0:T(8,128)(2,1)S(1)}, u32[]{:S(2)}, u32[]{:S(2)}) collective-permute-start(bf16[512,256]{1,0:T(8,128)(2,1)S(1)} %get-tuple-element.72), channel_id=1, source_target_pairs={{0,3},{1,0},{2,1},{3,2},{4,7},{5,4},{6,5},{7,6},{8,11},{9,8},{10,9... | collective-permute-start | bytes 786440 | tf_op jit(solution)/shard_map/ppermute | solution.py:359
  124.1 9.5 %collective-permute-start.13 = (bf16[512,256]{1,0:T(8,128)(2,1)S(1)}, bf16[512,256]{1,0:T(8,128)(2,1)S(1)}, u32[]{:S(2)}, u32[]{:S(2)}) collective-permute-start(bf16[512,256]{1,0:T(8,128)(2,1)S(1)} %get-tuple-element.70), channel_id=1, source_target_pairs={{0,1},{1,2},{2,3},{3,0},{4,5},{5,6},{6,7},{7,4},{8,9},{9,10},{10,1... | collective-permute-start | bytes 786440 | tf_op jit(solution)/shard_map/ppermute | solution.py:359
  129.8 14.2 %collective-permute-start.16 = (bf16[1024,256]{1,0:T(8,128)(2,1)S(1)}, bf16[1024,256]{1,0:T(8,128)(2,1)S(1)}, u32[]{:S(2)}, u32[]{:S(2)}) collective-permute-start(bf16[1024,256]{1,0:T(8,128)(2,1)S(1)} %pad_maximum_fusion.5), channel_id=1, source_target_pairs={{0,3},{1,0},{2,1},{3,2},{4,7},{5,4},{6,5},{7,6},{8,11},{9,8},{10,9... | collective-permute-start | bytes 1572872 | tf_op jit(solution)/shard_map/ppermute | solution.py:359
  133.7 13.9 %collective-permute-start.14 = (bf16[1024,256]{1,0:T(8,128)(2,1)S(1)}, bf16[1024,256]{1,0:T(8,128)(2,1)S(1)}, u32[]{:S(2)}, u32[]{:S(2)}) collective-permute-start(bf16[1024,256]{1,0:T(8,128)(2,1)S(1)} %pad_maximum_fusion.4), channel_id=1, source_target_pairs={{0,1},{1,2},{2,3},{3,0},{4,5},{5,6},{6,7},{7,4},{8,9},{9,10},{10,1... | collective-permute-start | bytes 1572872 | tf_op jit(solution)/shard_map/ppermute | solution.py:359

commit v4 on v3

--- a/solution.py
+++ b/solution.py
@@ -26,26 +26,27 @@
     return pltpu.CompilerParams(vmem_limit_bytes=mib * 2**20)
 
 
+def move(block, target):
+    devices = range(lax.axis_size("seq"))
+    route = [(i, target(i)) for i in devices if target(i) in devices]
+    return lax.ppermute(block, "seq", route)
+
+
 def shift(block, distance):
-    devices = range(lax.axis_size("seq"))
-    return lax.ppermute(block, "seq", [(i, i + distance) for i in devices if i + distance in devices])
+    return move(block, lambda i: i + distance)
 
 
 def swap(block):
     return lax.ppermute(block, "seq", [(i, i ^ 1) for i in range(lax.axis_size("seq"))])
+
+
+def total(*terms):
+    return sum(t.astype(F32) for t in terms)
 
 
 def silu_slope(v):
     sigma = jax.nn.sigmoid(v)
     return sigma * (1.0 + v * (1.0 - sigma))
-
-
-def split_kernel(core, k, v, keep, send):
-    for slot, out in ((0, keep), (1, send)):
-        head = core[0] if slot == 0 else 1 - core[0]
-        cols = pl.ds(pl.multiple_of(head * HEAD_DIM, HEAD_DIM), HEAD_DIM)
-        out[:, 0:128] = k[:, cols]
-        out[:, 128:256] = v[:, cols]
 
 
 def prepare_kernel(core, q, o, gate, grad, keep, send, gate_grad):
@@ -189,8 +190,6 @@
 
 WHOLE = [(0, 0, PAIR + SEG_ROWS)]
 EARLY = [(0, 0, ROWS), (ROWS, PAIR, SEG_ROWS)]
-USERS_ONLY = [(ROWS, PAIR, SEG_ROWS)]
-LATE = [(0, ROWS, ROWS)]
 
 
 def pairs(name, queries, parts, key, kind, tiles, area):
@@ -224,16 +223,19 @@
     )(*queries, key)
 
 
-def collect_kernel(place, mine, other, back_same, back_cross, far_same, far_cross, gate_grad, weights,
-                   left, low, high):
+def collect_kernel(place, mine, other, back_same, back_cross, far_same, far_cross, two_same, two_cross,
+                   key_same, key_cross, gate_grad, weights, left, low, high):
     core, x = place[0], place[1]
     front = core == 0
     for p in range(3):
         cols = slice(p * 128, (p + 1) * 128)
         a, b = mine[:, cols], other[:, cols].astype(F32)
         if p == 0:
-            a = a + back_same[...].astype(F32) + far_same[...].astype(F32)
-            b = b + back_cross[...].astype(F32) + far_cross[...].astype(F32)
+            a = a + total(back_same[...], far_same[...], two_same[...])
+            b = b + total(back_cross[...], far_cross[...], two_cross[...])
+        else:
+            part = slice((p - 1) * 128, p * 128)
+            a, b = a + key_same[:, part].astype(F32), b + key_cross[:, part].astype(F32)
         a, b = a.astype(BF16), b.astype(BF16)
         left[:, p * 256:p * 256 + 128] = jnp.where(front, a, b)
         left[:, p * 256 + 128:p * 256 + 256] = jnp.where(front, b, a)
@@ -266,7 +268,7 @@
     half = jax.ShapeDtypeStruct((ROWS // 2, 256), BF16)
     return pl.pallas_call(
         collect_kernel,
-        in_specs=[SMEM] + [VMEM] * 8,
+        in_specs=[SMEM] + [VMEM] * 12,
         out_specs=[VMEM] * 3,
         out_shape=[jax.ShapeDtypeStruct((ROWS, 1024), BF16), half, half],
         compiler_params=params(24),
@@ -296,21 +298,22 @@
     def in_order(kept, received):
         return jnp.where(front, kept, received), jnp.where(front, received, kept)
 
-    def total(*terms):
-        return sum(t.astype(F32) for t in terms)
-
     def halves(block):
         return in_order(block[:ROWS], block[ROWS:])
 
-    def give(same, cross, distance):
-        devices = range(lax.axis_size("seq") - distance)
-        same = shift(same, distance)
-        cross = lax.ppermute(cross, "seq", [(i, (i + distance) ^ 1) for i in devices])
+    def give(same, cross, target):
+        same = move(same, target)
+        cross = move(cross, lambda i: target(i) ^ 1)
         return same, cross
+
+    def by_head(block):
+        return in_order(block[:, :HEAD_DIM], block[:, HEAD_DIM:])
 
     users = (segments + 1).astype(BF16)
     users_recv = swap(users)
-    kv_keep, kv_send = by_rows(split_kernel, 2, core_at, key_rows, value_rows)
+    kv_keep, kv_send = (
+        jnp.concatenate(pair, axis=1) for pair in zip(by_head(key_rows), by_head(value_rows))
+    )
     kv_recv = swap(kv_send)
     keep, send, gate_grad = by_rows(
         prepare_kernel, 3, core_at, queries, attn_out, gate_pre, out_grad
@@ -319,40 +322,46 @@
     seg = jnp.concatenate(in_order(users, users_recv)).reshape(PAIR // 256, 256)
     seg = jnp.pad(seg, ((0, SEG_ROWS - PAIR // 256), (0, 0)))
     key = jnp.concatenate([*in_order(kv_keep, kv_recv), seg])
-    key_prev = shift(key, 2)
+    odd = lambda i: i % 2 == 1
+    key_prev = move(key, lambda i: -1 if odd(i) else i + 2)
     recv, key, seg = lax.optimization_barrier((recv, key, seg))
     low_rows, high_rows = in_order(keep, recv)
     next_a = shift(jnp.concatenate([low_rows, seg]), -2)
     next_b = shift(high_rows, -2)
     query = jnp.concatenate([low_rows, high_rows, seg])
+    query_far = shift(query, -6)
     every, early, late = (0, 1, 2, 3), (0, 1), (2, 3)
     area = PAIR * PAIR
     dq0, dkv0 = pairs("pairs_own", [query], [WHOLE], key, F32, every, area // 2)
     next_a, dq0 = lax.optimization_barrier((next_a, dq0))
     dq1a, dkv1a = pairs("pairs_one", [next_a], [EARLY], key, BF16, early, area // 2)
-    query, next_a, next_b, key_prev, dq1a = lax.optimization_barrier(
-        (query, next_a, next_b, key_prev, dq1a)
-    )
-    query_far = shift(query, -6)
-    dq2, dkv2 = pairs(
-        "pairs_two", [next_a, next_b], [EARLY, LATE], key_prev, BF16, every, area // 2
-    )
-    dkv_back = shift(dkv2, -2)
-    next_b, dq2 = lax.optimization_barrier((next_b, dq2))
-    dq1b, dkv1b = pairs(
-        "pairs_one", [next_a, next_b], [USERS_ONLY, LATE], key, BF16, late, area // 2
-    )
-    back = in_order(total(dq1a, dq2[:ROWS]).astype(BF16), total(dq1b, dq2[ROWS:]).astype(BF16))
-    back_same, back_cross = give(*back, 2)
+    next_a, next_b, dq1a = lax.optimization_barrier((next_a, next_b, dq1a))
+    query_next = jnp.concatenate([next_a[:ROWS], next_b, next_a[ROWS:]])
+    query_two = move(query_next, lambda i: i - 2 if odd(i) else -1)
+    dq1b, dkv1b = pairs("pairs_one", [query_next], [WHOLE], key, BF16, late, area // 2)
+    back_same, back_cross = give(*in_order(dq1a, dq1b), lambda i: i + 2)
     query_far, dq1b = lax.optimization_barrier((query_far, dq1b))
     dq3, dkv3 = pairs("pairs_three", [query_far], [WHOLE], key, BF16, every, area // 8)
-    far_same, far_cross = give(*halves(dq3), 6)
-    grads = jnp.concatenate([dq0, total(dkv0, dkv1a, dkv1b, dkv3, dkv_back)], axis=1)
-    mine, other = halves(grads)
+    far_same, far_cross = give(*halves(dq3), lambda i: i + 6)
+    query_two, key_prev, dkv3 = lax.optimization_barrier((query_two, key_prev, dkv3))
+    dq2, dkv2 = pairs(
+        "pairs_two",
+        [jnp.where(front, query_next, query_two)],
+        [WHOLE],
+        jnp.where(front, key_prev, key),
+        BF16,
+        every,
+        area // 2,
+    )
+    key_same, key_cross = give(*halves(dkv2), lambda i: -9 if odd(i) else i - 2)
+    two_same, two_cross = give(*halves(dq2), lambda i: i + 4 if odd(i) else i + 2)
+    dkv = total(dkv0, dkv1a, dkv1b, dkv3, jnp.where(front, jnp.zeros_like(dkv2), dkv2))
+    mine, other = halves(jnp.concatenate([dq0, dkv], axis=1))
     other = swap(other.astype(BF16))
     place = jnp.stack([core, head]).astype(jnp.int32)
     left, low, high = collect(
-        place, mine, other, back_same, back_cross, far_same, far_cross, gate_grad, projections
+        place, mine, other, back_same, back_cross, far_same, far_cross, two_same, two_cross,
+        key_same, key_cross, gate_grad, projections,
     )
 
     def turn(block, by):

time: 149 us -> 146 us (0.980)
  the two profiles are of different devices: /device:TPU:88 before, /device:TPU:8 now
where the time goes in v4:
time: 146 us
  starting transfers between devices  63.4 us (43%)
  waiting for transfers between devices  37.1 us (25%)
  Pallas kernels  33.9 us (23%)
  other arithmetic  9.14 us (6%)
  local copies, waits for them, and re-layouts  1.9 us (1%)
    ppermute x13, starting transfers between devices, move(): return lax.ppermute(block, 'seq', route)  46.4 us
    pallas_call x5, Pallas kernels, pairs(): pl.pallas_call(lambda *refs: pairs_kernel(name == 'pairs_own', parts, til...  24.9 us
    ppermute x13, waiting for transfers between devices, move(): return lax.ppermute(block, 'seq', route)  20.1 us
    ppermute x4, waiting for transfers between devices, turn(): return lax.ppermute(block, 'head', [(i, (i + by) % 4) for i in range(4)])  17 us
    ppermute x4, starting transfers between devices, swap(): lax.ppermute(block, 'seq', [(i, i ^ 1) for i in range(lax.axis_size('seq'...  10.3 us
    ppermute x4, starting transfers between devices, turn(): return lax.ppermute(block, 'head', [(i, (i + by) % 4) for i in range(4)])  6.66 us
    select_n x9, other arithmetic, in_order(): return (jnp.where(front, kept, received), jnp.where(front, received, kept))  5.38 us
    pallas_call x1, Pallas kernels, by_rows(): pl.pallas_call(kernel, grid_spec=pltpu.PrefetchScalarGridSpec(num_scalar_...  4.46 us
  transfers between devices with their start and end apart: 21, of which 7 were waited for; matrix products, arithmetic and copies ran while one was open for 5% of the time, Pallas kernels for 22%

profile of v4, /device:TPU:8, one launch (start us, length us, event | category | flops | bytes accessed | tf_op | source)
XLA Modules:
  0.0 145.9 jit_solution(10980926332498864856)
XLA Ops:
  0.0 1.3 broadcast_select_fusion.17
  1.3 0.1 pad_maximum_fusion.6
  1.3 0.1 collective-permute-start.1
  1.5 0.5 collective-permute-start.2
  1.9 4.5 %shard_map.82 = (bf16[1024,256]{1,0:T(8,128)(2,1)}, bf16[1024,256]{1,0:T(8,128)(2,1)}, bf16[1024,256]{1,0:T(8,128)(2,1)}) custom-call(s32[1]{0:T(128)} %bitcast.core, bf16[1024,256]{1,0:T(8,128)(2,1)} %q.1, bf16[1024,256]{1,0:T(8,128)(2,1)} %o.1, bf16[1024,256]{1,0:T(8,128)(2,1)} %gate.1, bf16[1024,256]{1,0:T(8,128)(2,1)} %grad.1), custom_call_target="tpu_custom_call" | custom-call | flops 7864320 | bytes 4194304 | tf_op jit(solution)/shard_map/pallas_call | solution.py:76
  6.4 0.1 collective-permute-start
  6.5 0.0 collective-permute-done.2
  6.6 0.0 collective-permute-done.1
  6.6 0.2 broadcast_select_fusion.8
  6.8 0.0 copy-start.7
  6.8 0.1 pad_maximum_fusion.1.refs_1_
  6.9 4.0 %collective-permute-start.6 = (bf16[2064,256]{1,0:T(8,128)(2,1)S(1)}, bf16[2064,256]{1,0:T(8,128)(2,1)S(1)}, u32[]{:S(2)}, u32[]{:S(2)}) collective-permute-start(bf16[2064,256]{1,0:T(8,128)(2,1)S(1)} %pad_maximum_fusion.1.refs_1_), channel_id=1, source_target_pairs={{0,8},{8,16},{16,24},{24,32},{32,40},{40,48},{48,56},{56,64},{64,7... | collective-permute-start | bytes 3170312 | tf_op jit(solution)/shard_map/ppermute | solution.py:32
  10.9 0.1 broadcast_select_fusion.5
  11.0 4.1 %collective-permute-start.3 = (bf16[1040,256]{1,0:T(8,128)(2,1)S(1)}, bf16[1040,256]{1,0:T(8,128)(2,1)S(1)}, u32[]{:S(2)}, u32[]{:S(2)}) collective-permute-start(bf16[1040,256]{1,0:T(8,128)(2,1)S(1)} %pad_maximum_fusion.4), channel_id=1, source_target_pairs={{8,0},{12,4},{16,8},{20,12},{24,16},{28,20},{32,24},{36,28},{40,32... | collective-permute-start | bytes 1597448 | tf_op jit(solution)/shard_map/ppermute | solution.py:32
  15.1 0.1 pad_maximum_fusion.2.refs_0_
  15.2 3.7 %collective-permute-start.4 = (bf16[1024,256]{1,0:T(8,128)(2,1)S(1)}, bf16[1024,256]{1,0:T(8,128)(2,1)S(1)}, u32[]{:S(2)}, u32[]{:S(2)}) collective-permute-start(bf16[1024,256]{1,0:T(8,128)(2,1)S(1)} %get-tuple-element.69), channel_id=1, source_target_pairs={{8,0},{12,4},{16,8},{20,12},{24,16},{28,20},{32,24},{36,28},{40,32... | collective-permute-start | bytes 1572872 | tf_op jit(solution)/shard_map/ppermute | solution.py:32
  18.9 1.9 %collective-permute-start.7 = (bf16[2064,256]{1,0:T(8,128)(2,1)S(1)}, bf16[2064,256]{1,0:T(8,128)(2,1)S(1)}, u32[]{:S(2)}, u32[]{:S(2)}) collective-permute-start(bf16[2064,256]{1,0:T(8,128)(2,1)S(1)} %pad_maximum_fusion.2.refs_0_), channel_id=1, source_target_pairs={{24,0},{28,4},{32,8},{36,12},{40,16},{44,20},{48,24},{52,28},{56,3... | collective-permute-start | bytes 3170312 | tf_op jit(solution)/shard_map/ppermute | solution.py:32
  20.9 9.6 %shard_map.83 = (f32[2048,128]{1,0:T(8,128)S(1)}, f32[2048,256]{1,0:T(8,128)S(1)}) custom-call(bf16[2064,256]{1,0:T(8,128)(2,1)S(1)} %pad_maximum_fusion.2.refs_0_, bf16[2064,256]{1,0:T(8,128)(2,1)S(1)} %pad_maximum_fusion.1.refs_1_), custom_call_target="tpu_custom_call" | custom-call | flops 5368709120 | bytes 4194304 | tf_op jit(solution)/shard_map/pallas_call | solution.py:197
  30.4 0.0 collective-permute-done.3.refs_0_
  30.4 5.2 %shard_map.84 = (bf16[1024,128]{1,0:T(8,128)(2,1)S(1)}, bf16[2048,256]{1,0:T(8,128)(2,1)S(1)}) custom-call(bf16[1040,256]{1,0:T(8,128)(2,1)S(1)} %collective-permute-done.3.refs_0_, bf16[2064,256]{1,0:T(8,128)(2,1)S(1)} %pad_maximum_fusion.1.refs_1_), custom_call_target="tpu_custom_call" | custom-call | flops 5368709120 | bytes 4194304 | tf_op jit(solution)/shard_map/pallas_call | solution.py:197
  35.7 3.1 %collective-permute-done.4 = bf16[1024,256]{1,0:T(8,128)(2,1)S(1)} collective-permute-done((bf16[1024,256]{1,0:T(8,128)(2,1)S(1)}, bf16[1024,256]{1,0:T(8,128)(2,1)S(1)}, u32[]{:S(2)}, u32[]{:S(2)}) %collective-permute-start.4) | collective-permute-done | bytes 524320 | tf_op jit(solution)/shard_map/ppermute | solution.py:32
  38.9 0.1 pad_maximum_fusion.3.refs_0_
  39.0 0.7 collective-permute-start.5
  39.7 5.4 %shard_map.85 = (bf16[1024,128]{1,0:T(8,128)(2,1)S(1)}, bf16[2048,256]{1,0:T(8,128)(2,1)S(1)}) custom-call(bf16[2064,256]{1,0:T(8,128)(2,1)S(1)} %pad_maximum_fusion.3.refs_0_, bf16[2064,256]{1,0:T(8,128)(2,1)S(1)} %pad_maximum_fusion.1.refs_1_), custom_call_target="tpu_custom_call" | custom-call | flops 5368709120 | bytes 4194304 | tf_op jit(solution)/shard_map/pallas_call | solution.py:197
  45.2 7.9 %collective-permute-start.10 = (bf16[1024,128]{1,0:T(8,128)(2,1)S(1)}, bf16[1024,128]{1,0:T(8,128)(2,1)S(1)}, u32[]{:S(2)}, u32[]{:S(2)}) collective-permute-start(bf16[1024,128]{1,0:T(8,128)(2,1)S(1)} %get-tuple-element.77), channel_id=1, source_target_pairs={{0,12},{4,8},{8,20},{12,16},{16,28},{20,24},{24,36},{28,32},{32,44... | collective-permute-start | bytes 786440 | tf_op jit(solution)/shard_map/ppermute | solution.py:32
  53.1 2.2 %collective-permute-start.9 = (bf16[1024,128]{1,0:T(8,128)(2,1)S(1)}, bf16[1024,128]{1,0:T(8,128)(2,1)S(1)}, u32[]{:S(2)}, u32[]{:S(2)}) collective-permute-start(bf16[1024,128]{1,0:T(8,128)(2,1)S(1)} %get-tuple-element.78), channel_id=1, source_target_pairs={{0,8},{4,12},{8,16},{12,20},{16,24},{20,28},{24,32},{28,36},{32,40... | collective-permute-start | bytes 786440 | tf_op jit(solution)/shard_map/ppermute | solution.py:32
  55.3 6.2 %collective-permute-done.7.refs_0_ = bf16[2064,256]{1,0:T(8,128)(2,1)S(1)} collective-permute-done((bf16[2064,256]{1,0:T(8,128)(2,1)S(1)}, bf16[2064,256]{1,0:T(8,128)(2,1)S(1)}, u32[]{:S(2)}, u32[]{:S(2)}) %collective-permute-start.7) | collective-permute-done | bytes 1056800 | tf_op jit(solution)/shard_map/ppermute | solution.py:32
  61.5 3.5 %shard_map.86 = (bf16[2048,128]{1,0:T(8,128)(2,1)S(1)}, bf16[2048,256]{1,0:T(8,128)(2,1)S(1)}) custom-call(bf16[2064,256]{1,0:T(8,128)(2,1)S(1)} %collective-permute-done.7.refs_0_, bf16[2064,256]{1,0:T(8,128)(2,1)S(1)} %pad_maximum_fusion.1.refs_1_), custom_call_target="tpu_custom_call" | custom-call | flops 1342177280 | bytes 4194304 | tf_op jit(solution)/shard_map/pallas_call | solution.py:197
  65.1 0.8 broadcast_select_fusion.11
  65.9 1.9 %collective-permute-start.12 = (bf16[1024,128]{1,0:T(8,128)(2,1)}, bf16[1024,128]{1,0:T(8,128)(2,1)}, u32[]{:S(2)}, u32[]{:S(2)}) collective-permute-start(bf16[1024,128]{1,0:T(8,128)(2,1)} %get-tuple-element.75), channel_id=1, source_target_pairs={{0,28},{4,24},{8,36},{12,32},{16,44},{20,40},{24,52},{28,48},{32,6... | collective-permute-start | bytes 786440 | tf_op jit(solution)/shard_map/ppermute | solution.py:32
  67.8 0.0 collective-permute-done.6
  67.8 1.9 %collective-permute-start.11 = (bf16[1024,128]{1,0:T(8,128)(2,1)}, bf16[1024,128]{1,0:T(8,128)(2,1)}, u32[]{:S(2)}, u32[]{:S(2)}) collective-permute-start(bf16[1024,128]{1,0:T(8,128)(2,1)} %get-tuple-element.76), channel_id=1, source_target_pairs={{0,24},{4,28},{8,32},{12,36},{16,40},{20,44},{24,48},{28,52},{32,5... | collective-permute-start | bytes 786440 | tf_op jit(solution)/shard_map/ppermute | solution.py:32
  69.8 0.0 collective-permute-done.5
  69.8 0.1 broadcast_select_fusion.refs_1_
  69.9 0.3 broadcast_select_fusion.1.refs_0_
  70.2 1.1 shard_map.87
  71.3 0.6 convert_add_fusion
  72.0 1.2 select_convert_fusion
  73.2 0.3 copy-done.6
  73.5 9.6 %collective-permute-start.8 = (bf16[1024,384]{1,0:T(8,128)(2,1)}, bf16[1024,384]{1,0:T(8,128)(2,1)S(1)}, u32[]{:S(2)}, u32[]{:S(2)}) collective-permute-start(bf16[1024,384]{1,0:T(8,128)(2,1)} %select_convert_fusion), channel_id=1, source_target_pairs={{0,4},{4,0},{8,12},{12,8},{16,20},{20,16},{24,28},{28,24},{32,36},... | collective-permute-start | bytes 2359304 | tf_op jit(solution)/shard_map/ppermute | solution.py:40
  83.1 1.0 broadcast_select_fusion.3
  84.1 0.7 copy-done.2
  84.9 6.5 %collective-permute-start.16 = (bf16[1024,256]{1,0:T(8,128)(2,1)}, bf16[1024,256]{1,0:T(8,128)(2,1)S(1)}, u32[]{:S(2)}, u32[]{:S(2)}) collective-permute-start(bf16[1024,256]{1,0:T(8,128)(2,1)} %get-tuple-element.67), channel_id=1, source_target_pairs={{8,4},{16,12},{24,20},{32,28},{40,36},{48,44},{56,52},{64,60},{72,... | collective-permute-start | bytes 1572872 | tf_op jit(solution)/shard_map/ppermute | solution.py:32
  91.4 0.7 copy-done.4
  92.1 7.7 %collective-permute-start.15 = (bf16[1024,256]{1,0:T(8,128)(2,1)}, bf16[1024,256]{1,0:T(8,128)(2,1)S(1)}, u32[]{:S(2)}, u32[]{:S(2)}) collective-permute-start(bf16[1024,256]{1,0:T(8,128)(2,1)} %get-tuple-element.68), channel_id=1, source_target_pairs={{8,0},{16,8},{24,16},{32,24},{40,32},{48,40},{56,48},{64,56},{72,6... | collective-permute-start | bytes 1572872 | tf_op jit(solution)/shard_map/ppermute | solution.py:32
  99.8 0.0 collective-permute-done.12.far_cross
  99.8 1.9 %collective-permute-start.14 = (bf16[1024,128]{1,0:T(8,128)(2,1)S(1)}, bf16[1024,128]{1,0:T(8,128)(2,1)S(1)}, u32[]{:S(2)}, u32[]{:S(2)}) collective-permute-start(bf16[1024,128]{1,0:T(8,128)(2,1)S(1)} %get-tuple-element.73), channel_id=1, source_target_pairs={{0,12},{4,16},{8,20},{12,24},{16,28},{20,32},{24,36},{28,40},{32,4... | collective-permute-start | bytes 786440 | tf_op jit(solution)/shard_map/ppermute | solution.py:32
  101.8 1.9 %collective-permute-start.13 = (bf16[1024,128]{1,0:T(8,128)(2,1)S(1)}, bf16[1024,128]{1,0:T(8,128)(2,1)S(1)}, u32[]{:S(2)}, u32[]{:S(2)}) collective-permute-start(bf16[1024,128]{1,0:T(8,128)(2,1)S(1)} %get-tuple-element.74), channel_id=1, source_target_pairs={{0,8},{4,20},{8,16},{12,28},{16,24},{20,36},{24,32},{28,44},{32,40... | collective-permute-start | bytes 786440 | tf_op jit(solution)/shard_map/ppermute | solution.py:32
  103.7 0.1 pad_add_fusion.place
  103.8 1.9 %broadcast_select_fusion.2.mine = f32[1024,384]{1,0:T(8,128)S(1)} fusion(pred[]{:T(512)S(6)} %eq.5, f32[2048,256]{1,0:T(8,128)} %copy-done.6, f32[2048,128]{1,0:T(8,128)S(1)} %get-tuple-element.42), kind=kLoop, calls=%fused_computation.12 | loop fusion | flops 1179648 | bytes 4718593 | tf_op jit(solution)/shard_map/jit(_where)/select_n | solution.py:299
  105.7 5.8 %collective-permute-done.14.two_cross = bf16[1024,128]{1,0:T(8,128)(2,1)S(1)} collective-permute-done((bf16[1024,128]{1,0:T(8,128)(2,1)S(1)}, bf16[1024,128]{1,0:T(8,128)(2,1)S(1)}, u32[]{:S(2)}, u32[]{:S(2)}) %collective-permute-start.14) | collective-permute-done | bytes 262176 | tf_op jit(solution)/shard_map/ppermute | solution.py:32
  111.5 4.9 %collective-permute-done.13.two_same = bf16[1024,128]{1,0:T(8,128)(2,1)S(1)} collective-permute-done((bf16[1024,128]{1,0:T(8,128)(2,1)S(1)}, bf16[1024,128]{1,0:T(8,128)(2,1)S(1)}, u32[]{:S(2)}, u32[]{:S(2)}) %collective-permute-start.13) | collective-permute-done | bytes 262176 | tf_op jit(solution)/shard_map/ppermute | solution.py:32
  116.4 2.2 %collect.1 = (bf16[1024,1024]{1,0:T(8,128)(2,1)S(1)}, bf16[512,256]{1,0:T(8,128)(2,1)S(1)}, bf16[512,256]{1,0:T(8,128)(2,1)S(1)}) custom-call(s32[2]{0:T(128)S(1)} %pad_add_fusion.place, f32[1024,384]{1,0:T(8,128)S(1)} %broadcast_select_fusion.2.mine, bf16[1024,384]{1,0:T(8,128)(2,1)S(1)} %collective-permute-done.8.other, bf16[1024,128]{1,0:T(8,128)(2,1)S(1)} %copy-done.5, ...), custom_call_target="tpu_custom_call" | custom-call | flops 536870912 | bytes 8388608 | tf_op jit(solution)/shard_map/collect/pallas_call | solution.py:269
  118.6 2.8 %collective-permute-start.19 = (bf16[512,256]{1,0:T(8,128)(2,1)S(1)}, bf16[512,256]{1,0:T(8,128)(2,1)S(1)}, u32[]{:S(2)}, u32[]{:S(2)}) collective-permute-start(bf16[512,256]{1,0:T(8,128)(2,1)S(1)} %get-tuple-element.66), channel_id=1, source_target_pairs={{0,3},{1,0},{2,1},{3,2},{4,7},{5,4},{6,5},{7,6},{8,11},{9,8},{10,9... | collective-permute-start | bytes 786440 | tf_op jit(solution)/shard_map/ppermute | solution.py:368
  121.4 0.0 collective-permute-start.17
  121.4 2.4 %project.1 = (f32[1024,256]{1,0:T(8,128)S(1)}, f32[1024,256]{1,0:T(8,128)S(1)}, f32[1024,256]{1,0:T(8,128)S(1)}) custom-call(s32[2]{0:T(128)S(1)} %pad_add_fusion.place, bf16[1024,1024]{1,0:T(8,128)(2,1)S(1)} %get-tuple-element.61.left, bf16[4,1024,256]{2,1,0:T(8,128)(2,1)S(1)} %copy-done), custom_call_target="tpu_custom_call" | custom-call | flops 1610612736 | bytes 8388608 | tf_op jit(solution)/shard_map/project/pallas_call | solution.py:281
  123.9 3.2 %collective-permute-done.19 = bf16[512,256]{1,0:T(8,128)(2,1)S(1)} collective-permute-done((bf16[512,256]{1,0:T(8,128)(2,1)S(1)}, bf16[512,256]{1,0:T(8,128)(2,1)S(1)}, u32[]{:S(2)}, u32[]{:S(2)}) %collective-permute-start.19) | collective-permute-done | bytes 262176 | tf_op jit(solution)/shard_map/ppermute | solution.py:368
  127.1 0.1 add_convert_fusion.1
  127.2 3.8 %collective-permute-start.20 = (bf16[1024,256]{1,0:T(8,128)(2,1)S(1)}, bf16[1024,256]{1,0:T(8,128)(2,1)S(1)}, u32[]{:S(2)}, u32[]{:S(2)}) collective-permute-start(bf16[1024,256]{1,0:T(8,128)(2,1)S(1)} %pad_maximum_fusion.8), channel_id=1, source_target_pairs={{0,3},{1,0},{2,1},{3,2},{4,7},{5,4},{6,5},{7,6},{8,11},{9,8},{10,9... | collective-permute-start | bytes 1572872 | tf_op jit(solution)/shard_map/ppermute | solution.py:368
  131.0 0.1 add_convert_fusion.2
  131.1 0.1 collective-permute-start.18
  131.1 10.2 %collective-permute-done.20 = bf16[1024,256]{1,0:T(8,128)(2,1)S(1)} collective-permute-done((bf16[1024,256]{1,0:T(8,128)(2,1)S(1)}, bf16[1024,256]{1,0:T(8,128)(2,1)S(1)}, u32[]{:S(2)}, u32[]{:S(2)}) %collective-permute-start.20) | collective-permute-done | bytes 524320 | tf_op jit(solution)/shard_map/ppermute | solution.py:368
  141.4 3.6 %collective-permute-done.18 = bf16[1024,256]{1,0:T(8,128)(2,1)S(1)} collective-permute-done((bf16[1024,256]{1,0:T(8,128)(2,1)S(1)}, bf16[1024,256]{1,0:T(8,128)(2,1)S(1)}, u32[]{:S(2)}, u32[]{:S(2)}) %collective-permute-start.18) | collective-permute-done | bytes 524320 | tf_op jit(solution)/shard_map/ppermute | solution.py:368
  144.9 0.9 add_convert_fusion
  (36 shorter events, 0.4 us)
Async XLA Ops:
  0.0 1.4 copy-start.8
  1.3 5.2 %collective-permute-start.1 = (bf16[1024,256]{1,0:T(8,128)(2,1)S(1)}, bf16[1024,256]{1,0:T(8,128)(2,1)S(1)}, u32[]{:S(2)}, u32[]{:S(2)}) collective-permute-start(bf16[1024,256]{1,0:T(8,128)(2,1)S(1)} %pad_maximum_fusion.6), channel_id=1, source_target_pairs={{0,4},{4,0},{8,12},{12,8},{16,20},{20,16},{24,28},{28,24},{32,36},... | collective-permute-start | bytes 1572872 | tf_op jit(solution)/shard_map/ppermute | solution.py:40
  1.5 5.1 %collective-permute-start.2 = (bf16[1024]{0:T(1024)(128)(2,1)S(1)}, bf16[1024]{0:T(1024)(128)(2,1)S(1)}, u32[]{:S(2)}, u32[]{:S(2)}) collective-permute-start(bf16[1024]{0:T(1024)(128)(2,1)S(1)} %add_convert_fusion.3), channel_id=1, source_target_pairs={{0,4},{4,0},{8,12},{12,8},{16,20},{20,16},{24,28},{28,24},{32,36},... | collective-permute-start | bytes 6152 | tf_op jit(solution)/shard_map/ppermute | solution.py:40
  6.4 4.5 %collective-permute-start = (bf16[1024,256]{1,0:T(8,128)(2,1)}, bf16[1024,256]{1,0:T(8,128)(2,1)S(1)}, u32[]{:S(2)}, u32[]{:S(2)}) collective-permute-start(bf16[1024,256]{1,0:T(8,128)(2,1)} %get-tuple-element.37), channel_id=1, source_target_pairs={{0,4},{4,0},{8,12},{12,8},{16,20},{20,16},{24,28},{28,24},{32,36},... | collective-permute-start | bytes 1572872 | tf_op jit(solution)/shard_map/ppermute | solution.py:40
  6.8 4.1 %copy-start.7 = (bf16[1024,256]{1,0:T(8,128)(2,1)S(1)}, bf16[1024,256]{1,0:T(8,128)(2,1)}, u32[]{:S(2)}) copy-start(bf16[1024,256]{1,0:T(8,128)(2,1)} %get-tuple-element.36) | copy-start | bytes 1572868
  6.9 60.9 %collective-permute-start.6 = (bf16[2064,256]{1,0:T(8,128)(2,1)S(1)}, bf16[2064,256]{1,0:T(8,128)(2,1)S(1)}, u32[]{:S(2)}, u32[]{:S(2)}) collective-permute-start(bf16[2064,256]{1,0:T(8,128)(2,1)S(1)} %pad_maximum_fusion.1.refs_1_), channel_id=1, source_target_pairs={{0,8},{8,16},{16,24},{24,32},{32,40},{40,48},{48,56},{56,64},{64,7... | collective-permute-start | bytes 3170312 | tf_op jit(solution)/shard_map/ppermute | solution.py:32
  11.0 19.4 %collective-permute-start.3 = (bf16[1040,256]{1,0:T(8,128)(2,1)S(1)}, bf16[1040,256]{1,0:T(8,128)(2,1)S(1)}, u32[]{:S(2)}, u32[]{:S(2)}) collective-permute-start(bf16[1040,256]{1,0:T(8,128)(2,1)S(1)} %pad_maximum_fusion.4), channel_id=1, source_target_pairs={{8,0},{12,4},{16,8},{20,12},{24,16},{28,20},{32,24},{36,28},{40,32... | collective-permute-start | bytes 1597448 | tf_op jit(solution)/shard_map/ppermute | solution.py:32
  15.2 23.6 %collective-permute-start.4 = (bf16[1024,256]{1,0:T(8,128)(2,1)S(1)}, bf16[1024,256]{1,0:T(8,128)(2,1)S(1)}, u32[]{:S(2)}, u32[]{:S(2)}) collective-permute-start(bf16[1024,256]{1,0:T(8,128)(2,1)S(1)} %get-tuple-element.69), channel_id=1, source_target_pairs={{8,0},{12,4},{16,8},{20,12},{24,16},{28,20},{32,24},{36,28},{40,32... | collective-permute-start | bytes 1572872 | tf_op jit(solution)/shard_map/ppermute | solution.py:32
  18.9 42.6 %collective-permute-start.7 = (bf16[2064,256]{1,0:T(8,128)(2,1)S(1)}, bf16[2064,256]{1,0:T(8,128)(2,1)S(1)}, u32[]{:S(2)}, u32[]{:S(2)}) collective-permute-start(bf16[2064,256]{1,0:T(8,128)(2,1)S(1)} %pad_maximum_fusion.2.refs_0_), channel_id=1, source_target_pairs={{24,0},{28,4},{32,8},{36,12},{40,16},{44,20},{48,24},{52,28},{56,3... | collective-permute-start | bytes 3170312 | tf_op jit(solution)/shard_map/ppermute | solution.py:32
  39.0 30.8 %collective-permute-start.5 = (bf16[2064,256]{1,0:T(8,128)(2,1)S(1)}, bf16[2064,256]{1,0:T(8,128)(2,1)S(1)}, u32[]{:S(2)}, u32[]{:S(2)}) collective-permute-start(bf16[2064,256]{1,0:T(8,128)(2,1)S(1)} %pad_maximum_fusion.3.refs_0_), channel_id=1, source_target_pairs={{12,4},{20,12},{28,20},{36,28},{44,36},{52,44},{60,52},{68,60},{76... | collective-permute-start | bytes 3170312 | tf_op jit(solution)/shard_map/ppermute | solution.py:32
  45.2 39.0 %collective-permute-start.10 = (bf16[1024,128]{1,0:T(8,128)(2,1)S(1)}, bf16[1024,128]{1,0:T(8,128)(2,1)S(1)}, u32[]{:S(2)}, u32[]{:S(2)}) collective-permute-start(bf16[1024,128]{1,0:T(8,128)(2,1)S(1)} %get-tuple-element.77), channel_id=1, source_target_pairs={{0,12},{4,8},{8,20},{12,16},{16,28},{20,24},{24,36},{28,32},{32,44... | collective-permute-start | bytes 786440 | tf_op jit(solution)/shard_map/ppermute | solution.py:32
  53.1 38.2 %collective-permute-start.9 = (bf16[1024,128]{1,0:T(8,128)(2,1)S(1)}, bf16[1024,128]{1,0:T(8,128)(2,1)S(1)}, u32[]{:S(2)}, u32[]{:S(2)}) collective-permute-start(bf16[1024,128]{1,0:T(8,128)(2,1)S(1)} %get-tuple-element.78), channel_id=1, source_target_pairs={{0,8},{4,12},{8,16},{12,20},{16,24},{20,28},{24,32},{28,36},{32,40... | collective-permute-start | bytes 786440 | tf_op jit(solution)/shard_map/ppermute | solution.py:32
  65.9 33.9 %collective-permute-start.12 = (bf16[1024,128]{1,0:T(8,128)(2,1)}, bf16[1024,128]{1,0:T(8,128)(2,1)}, u32[]{:S(2)}, u32[]{:S(2)}) collective-permute-start(bf16[1024,128]{1,0:T(8,128)(2,1)} %get-tuple-element.75), channel_id=1, source_target_pairs={{0,28},{4,24},{8,36},{12,32},{16,44},{20,40},{24,52},{28,48},{32,6... | collective-permute-start | bytes 786440 | tf_op jit(solution)/shard_map/ppermute | solution.py:32
  67.8 33.9 %collective-permute-start.11 = (bf16[1024,128]{1,0:T(8,128)(2,1)}, bf16[1024,128]{1,0:T(8,128)(2,1)}, u32[]{:S(2)}, u32[]{:S(2)}) collective-permute-start(bf16[1024,128]{1,0:T(8,128)(2,1)} %get-tuple-element.76), channel_id=1, source_target_pairs={{0,24},{4,28},{8,32},{12,36},{16,40},{20,44},{24,48},{28,52},{32,5... | collective-permute-start | bytes 786440 | tf_op jit(solution)/shard_map/ppermute | solution.py:32
  72.0 1.6 %copy-start.6 = (f32[2048,256]{1,0:T(8,128)}, f32[2048,256]{1,0:T(8,128)S(1)}, u32[]{:S(2)}) copy-start(f32[2048,256]{1,0:T(8,128)S(1)} %convert_add_fusion) | copy-start | bytes 6291460
  73.5 42.9 %collective-permute-start.8 = (bf16[1024,384]{1,0:T(8,128)(2,1)}, bf16[1024,384]{1,0:T(8,128)(2,1)S(1)}, u32[]{:S(2)}, u32[]{:S(2)}) collective-permute-start(bf16[1024,384]{1,0:T(8,128)(2,1)} %select_convert_fusion), channel_id=1, source_target_pairs={{0,4},{4,0},{8,12},{12,8},{16,20},{20,16},{24,28},{28,24},{32,36},... | collective-permute-start | bytes 2359304 | tf_op jit(solution)/shard_map/ppermute | solution.py:40
  84.1 0.7 copy-start.2
  84.9 31.5 %collective-permute-start.16 = (bf16[1024,256]{1,0:T(8,128)(2,1)}, bf16[1024,256]{1,0:T(8,128)(2,1)S(1)}, u32[]{:S(2)}, u32[]{:S(2)}) collective-permute-start(bf16[1024,256]{1,0:T(8,128)(2,1)} %get-tuple-element.67), channel_id=1, source_target_pairs={{8,4},{16,12},{24,20},{32,28},{40,36},{48,44},{56,52},{64,60},{72,... | collective-permute-start | bytes 1572872 | tf_op jit(solution)/shard_map/ppermute | solution.py:32
  91.4 0.7 copy-start.4
  92.1 24.3 %collective-permute-start.15 = (bf16[1024,256]{1,0:T(8,128)(2,1)}, bf16[1024,256]{1,0:T(8,128)(2,1)S(1)}, u32[]{:S(2)}, u32[]{:S(2)}) collective-permute-start(bf16[1024,256]{1,0:T(8,128)(2,1)} %get-tuple-element.68), channel_id=1, source_target_pairs={{8,0},{16,8},{24,16},{32,24},{40,32},{48,40},{56,48},{64,56},{72,6... | collective-permute-start | bytes 1572872 | tf_op jit(solution)/shard_map/ppermute | solution.py:32
  99.8 11.6 %collective-permute-start.14 = (bf16[1024,128]{1,0:T(8,128)(2,1)S(1)}, bf16[1024,128]{1,0:T(8,128)(2,1)S(1)}, u32[]{:S(2)}, u32[]{:S(2)}) collective-permute-start(bf16[1024,128]{1,0:T(8,128)(2,1)S(1)} %get-tuple-element.73), channel_id=1, source_target_pairs={{0,12},{4,16},{8,20},{12,24},{16,28},{20,32},{24,36},{28,40},{32,4... | collective-permute-start | bytes 786440 | tf_op jit(solution)/shard_map/ppermute | solution.py:32
  101.8 14.6 %collective-permute-start.13 = (bf16[1024,128]{1,0:T(8,128)(2,1)S(1)}, bf16[1024,128]{1,0:T(8,128)(2,1)S(1)}, u32[]{:S(2)}, u32[]{:S(2)}) collective-permute-start(bf16[1024,128]{1,0:T(8,128)(2,1)S(1)} %get-tuple-element.74), channel_id=1, source_target_pairs={{0,8},{4,20},{8,16},{12,28},{16,24},{20,36},{24,32},{28,44},{32,40... | collective-permute-start | bytes 786440 | tf_op jit(solution)/shard_map/ppermute | solution.py:32
  103.8 12.6 %copy-start = (bf16[4,1024,256]{2,1,0:T(8,128)(2,1)S(1)}, bf16[4,1024,256]{2,1,0:T(8,128)(2,1)}, u32[]{:S(2)}) copy-start(bf16[4,1024,256]{2,1,0:T(8,128)(2,1)} %weights.3) | copy-start | bytes 6291460
  103.8 12.6 %copy-start.1 = (bf16[1024,256]{1,0:T(8,128)(2,1)S(1)}, bf16[1024,256]{1,0:T(8,128)(2,1)}, u32[]{:S(2)}) copy-start(bf16[1024,256]{1,0:T(8,128)(2,1)} %get-tuple-element.60.gate_grad) | copy-start | bytes 1572868
  103.8 12.6 %copy-start.3 = (bf16[1024,128]{1,0:T(8,128)(2,1)S(1)}, bf16[1024,128]{1,0:T(8,128)(2,1)}, u32[]{:S(2)}) copy-start(bf16[1024,128]{1,0:T(8,128)(2,1)} %copy-done.2) | copy-start | bytes 786436
  103.8 12.6 %copy-start.5 = (bf16[1024,128]{1,0:T(8,128)(2,1)S(1)}, bf16[1024,128]{1,0:T(8,128)(2,1)}, u32[]{:S(2)}) copy-start(bf16[1024,128]{1,0:T(8,128)(2,1)} %copy-done.4) | copy-start | bytes 786436
  118.6 8.5 %collective-permute-start.19 = (bf16[512,256]{1,0:T(8,128)(2,1)S(1)}, bf16[512,256]{1,0:T(8,128)(2,1)S(1)}, u32[]{:S(2)}, u32[]{:S(2)}) collective-permute-start(bf16[512,256]{1,0:T(8,128)(2,1)S(1)} %get-tuple-element.66), channel_id=1, source_target_pairs={{0,3},{1,0},{2,1},{3,2},{4,7},{5,4},{6,5},{7,6},{8,11},{9,8},{10,9... | collective-permute-start | bytes 786440 | tf_op jit(solution)/shard_map/ppermute | solution.py:368
  121.4 9.5 %collective-permute-start.17 = (bf16[512,256]{1,0:T(8,128)(2,1)S(1)}, bf16[512,256]{1,0:T(8,128)(2,1)S(1)}, u32[]{:S(2)}, u32[]{:S(2)}) collective-permute-start(bf16[512,256]{1,0:T(8,128)(2,1)S(1)} %get-tuple-element.64), channel_id=1, source_target_pairs={{0,1},{1,2},{2,3},{3,0},{4,5},{5,6},{6,7},{7,4},{8,9},{9,10},{10,1... | collective-permute-start | bytes 786440 | tf_op jit(solution)/shard_map/ppermute | solution.py:368
  127.2 14.2 %collective-permute-start.20 = (bf16[1024,256]{1,0:T(8,128)(2,1)S(1)}, bf16[1024,256]{1,0:T(8,128)(2,1)S(1)}, u32[]{:S(2)}, u32[]{:S(2)}) collective-permute-start(bf16[1024,256]{1,0:T(8,128)(2,1)S(1)} %pad_maximum_fusion.8), channel_id=1, source_target_pairs={{0,3},{1,0},{2,1},{3,2},{4,7},{5,4},{6,5},{7,6},{8,11},{9,8},{10,9... | collective-permute-start | bytes 1572872 | tf_op jit(solution)/shard_map/ppermute | solution.py:368
  131.1 13.9 %collective-permute-start.18 = (bf16[1024,256]{1,0:T(8,128)(2,1)S(1)}, bf16[1024,256]{1,0:T(8,128)(2,1)S(1)}, u32[]{:S(2)}, u32[]{:S(2)}) collective-permute-start(bf16[1024,256]{1,0:T(8,128)(2,1)S(1)} %pad_maximum_fusion.7), channel_id=1, source_target_pairs={{0,1},{1,2},{2,3},{3,0},{4,5},{5,6},{6,7},{7,4},{8,9},{9,10},{10,1... | collective-permute-start | bytes 1572872 | tf_op jit(solution)/shard_map/ppermute | solution.py:368

commit v5 on v4

--- a/solution.py
+++ b/solution.py
@@ -88,8 +88,8 @@
 
 
 def pairs_kernel(own, parts, tiles, *refs):
-    q_in, k_in, dq_out, dkv_out = refs[:len(parts)], refs[len(parts)], refs[len(parts) + 1], refs[len(parts) + 2]
-    q, k, dq, dk, dv, row_q, col_k, bound, todo, w0, d0, w1, d1, sem = refs[len(parts) + 3:]
+    core, q_in, k_in = refs[0], refs[1:1 + len(parts)], refs[1 + len(parts)]
+    *outs, q, k, dq, dk, dv, row_q, col_k, bound, todo, w0, d0, w1, d1, sem = refs[2 + len(parts):]
     copies = [pltpu.make_async_copy(k_in, k, sem.at[0])]
     for ref, moves in zip(q_in, parts):
         for source, target, size in moves:
@@ -182,26 +182,33 @@
 
         lax.fori_loop(0, (count + 1) // 2, two, 0)
 
-    at = slice(tiles[0] * TILE, (tiles[-1] + 1) * TILE)
-    dq_out[...] = (dq[at] * HALF_SCALE).astype(dq_out.dtype)
-    dkv_out[:, 0:128] = (dk[...] * HALF_SCALE).astype(dkv_out.dtype)
-    dkv_out[:, 128:256] = dv[...].astype(dkv_out.dtype)
+    for out, half in zip(outs[-2:], (core[0], 1 - core[0])):
+        at = pl.ds(pl.multiple_of(half * ROWS, ROWS), ROWS)
+        out[:, 0:128] = (dk[at, :] * HALF_SCALE).astype(out.dtype)
+        out[:, 128:256] = dv[at, :].astype(out.dtype)
+    if len(tiles) == TILES:
+        for out, half in zip(outs[:2], (core[0], 1 - core[0])):
+            at = pl.ds(pl.multiple_of(half * ROWS, ROWS), ROWS)
+            out[...] = (dq[at, :] * HALF_SCALE).astype(out.dtype)
+    else:
+        out, at = outs[0], slice(tiles[0] * TILE, (tiles[-1] + 1) * TILE)
+        out[...] = (dq[at] * HALF_SCALE).astype(out.dtype)
 
 
 WHOLE = [(0, 0, PAIR + SEG_ROWS)]
 EARLY = [(0, 0, ROWS), (ROWS, PAIR, SEG_ROWS)]
-
-
-def pairs(name, queries, parts, key, kind, tiles, area):
+USERS_ONLY = [(ROWS, PAIR, SEG_ROWS)]
+LATE = [(0, ROWS, ROWS)]
+
+
+def pairs(name, core, queries, parts, key, kind, tiles, area):
     anywhere = pl.BlockSpec(memory_space=pl.ANY)
     return pl.pallas_call(
         lambda *refs: pairs_kernel(name == "pairs_own", parts, tiles, *refs),
-        in_specs=[anywhere] * (len(queries) + 1),
-        out_specs=[VMEM] * 2,
-        out_shape=[
-            jax.ShapeDtypeStruct((len(tiles) * TILE, 128), kind),
-            jax.ShapeDtypeStruct((PAIR, 256), kind),
-        ],
+        in_specs=[SMEM] + [anywhere] * (len(queries) + 1),
+        out_specs=[VMEM] * (len(tiles) * TILE // ROWS + 2),
+        out_shape=[jax.ShapeDtypeStruct((ROWS, 128), kind)] * (len(tiles) * TILE // ROWS)
+        + [jax.ShapeDtypeStruct((ROWS, 256), kind)] * 2,
         scratch_shapes=[
             pltpu.VMEM((PAIR + SEG_ROWS, 256), BF16),
             pltpu.VMEM((PAIR + SEG_ROWS, 256), BF16),
@@ -220,22 +227,23 @@
         ],
         compiler_params=params(28),
         cost_estimate=cost(20 * area * 128, area, 8 * PAIR * 256),
-    )(*queries, key)
-
-
-def collect_kernel(place, mine, other, back_same, back_cross, far_same, far_cross, two_same, two_cross,
-                   key_same, key_cross, gate_grad, weights, left, low, high):
+    )(core, *queries, key)
+
+
+def collect_kernel(place, dq, dkv, other, back_same, back_cross, far_same, far_cross, key_same, key_cross,
+                   gate_grad, weights,
+                   left, low, high):
     core, x = place[0], place[1]
     front = core == 0
     for p in range(3):
         cols = slice(p * 128, (p + 1) * 128)
-        a, b = mine[:, cols], other[:, cols].astype(F32)
+        b = other[:, cols].astype(F32)
         if p == 0:
-            a = a + total(back_same[...], far_same[...], two_same[...])
-            b = b + total(back_cross[...], far_cross[...], two_cross[...])
+            a = dq[...] + total(back_same[...], far_same[...])
+            b = b + total(back_cross[...], far_cross[...])
         else:
             part = slice((p - 1) * 128, p * 128)
-            a, b = a + key_same[:, part].astype(F32), b + key_cross[:, part].astype(F32)
+            a, b = dkv[:, part] + key_same[:, part].astype(F32), b + key_cross[:, part].astype(F32)
         a, b = a.astype(BF16), b.astype(BF16)
         left[:, p * 256:p * 256 + 128] = jnp.where(front, a, b)
         left[:, p * 256 + 128:p * 256 + 256] = jnp.where(front, b, a)
@@ -268,7 +276,7 @@
     half = jax.ShapeDtypeStruct((ROWS // 2, 256), BF16)
     return pl.pallas_call(
         collect_kernel,
-        in_specs=[SMEM] + [VMEM] * 12,
+        in_specs=[SMEM] + [VMEM] * 11,
         out_specs=[VMEM] * 3,
         out_shape=[jax.ShapeDtypeStruct((ROWS, 1024), BF16), half, half],
         compiler_params=params(24),
@@ -298,9 +306,6 @@
     def in_order(kept, received):
         return jnp.where(front, kept, received), jnp.where(front, received, kept)
 
-    def halves(block):
-        return in_order(block[:ROWS], block[ROWS:])
-
     def give(same, cross, target):
         same = move(same, target)
         cross = move(cross, lambda i: target(i) ^ 1)
@@ -322,46 +327,45 @@
     seg = jnp.concatenate(in_order(users, users_recv)).reshape(PAIR // 256, 256)
     seg = jnp.pad(seg, ((0, SEG_ROWS - PAIR // 256), (0, 0)))
     key = jnp.concatenate([*in_order(kv_keep, kv_recv), seg])
-    odd = lambda i: i % 2 == 1
-    key_prev = move(key, lambda i: -1 if odd(i) else i + 2)
+    key_prev = shift(key, 2)
     recv, key, seg = lax.optimization_barrier((recv, key, seg))
     low_rows, high_rows = in_order(keep, recv)
     next_a = shift(jnp.concatenate([low_rows, seg]), -2)
     next_b = shift(high_rows, -2)
     query = jnp.concatenate([low_rows, high_rows, seg])
-    query_far = shift(query, -6)
     every, early, late = (0, 1, 2, 3), (0, 1), (2, 3)
     area = PAIR * PAIR
-    dq0, dkv0 = pairs("pairs_own", [query], [WHOLE], key, F32, every, area // 2)
+    dq0, dq0_other, *dkv0 = pairs(
+        "pairs_own", core_at, [query], [WHOLE], key, F32, every, area // 2
+    )
     next_a, dq0 = lax.optimization_barrier((next_a, dq0))
-    dq1a, dkv1a = pairs("pairs_one", [next_a], [EARLY], key, BF16, early, area // 2)
-    next_a, next_b, dq1a = lax.optimization_barrier((next_a, next_b, dq1a))
-    query_next = jnp.concatenate([next_a[:ROWS], next_b, next_a[ROWS:]])
-    query_two = move(query_next, lambda i: i - 2 if odd(i) else -1)
-    dq1b, dkv1b = pairs("pairs_one", [query_next], [WHOLE], key, BF16, late, area // 2)
-    back_same, back_cross = give(*in_order(dq1a, dq1b), lambda i: i + 2)
+    dq1a, *dkv1a = pairs("pairs_one", core_at, [next_a], [EARLY], key, BF16, early, area // 2)
+    query, next_a, next_b, key_prev, dq1a = lax.optimization_barrier(
+        (query, next_a, next_b, key_prev, dq1a)
+    )
+    query_far = shift(query, -6)
+    dq2_same, dq2_cross, *dkv2 = pairs(
+        "pairs_two", core_at, [next_a, next_b], [EARLY, LATE], key_prev, BF16, every, area // 2
+    )
+    key_same, key_cross = give(*dkv2, lambda i: i - 2)
+    next_b, dq2_same = lax.optimization_barrier((next_b, dq2_same))
+    dq1b, *dkv1b = pairs(
+        "pairs_one", core_at, [next_a, next_b], [USERS_ONLY, LATE], key, BF16, late, area // 2
+    )
+    same, cross = in_order(dq1a, dq1b)
+    same, cross = total(same, dq2_same).astype(BF16), total(cross, dq2_cross).astype(BF16)
+    back_same, back_cross = give(same, cross, lambda i: i + 2)
     query_far, dq1b = lax.optimization_barrier((query_far, dq1b))
-    dq3, dkv3 = pairs("pairs_three", [query_far], [WHOLE], key, BF16, every, area // 8)
-    far_same, far_cross = give(*halves(dq3), lambda i: i + 6)
-    query_two, key_prev, dkv3 = lax.optimization_barrier((query_two, key_prev, dkv3))
-    dq2, dkv2 = pairs(
-        "pairs_two",
-        [jnp.where(front, query_next, query_two)],
-        [WHOLE],
-        jnp.where(front, key_prev, key),
-        BF16,
-        every,
-        area // 2,
-    )
-    key_same, key_cross = give(*halves(dkv2), lambda i: -9 if odd(i) else i - 2)
-    two_same, two_cross = give(*halves(dq2), lambda i: i + 4 if odd(i) else i + 2)
-    dkv = total(dkv0, dkv1a, dkv1b, dkv3, jnp.where(front, jnp.zeros_like(dkv2), dkv2))
-    mine, other = halves(jnp.concatenate([dq0, dkv], axis=1))
-    other = swap(other.astype(BF16))
+    dq3_same, dq3_cross, *dkv3 = pairs(
+        "pairs_three", core_at, [query_far], [WHOLE], key, BF16, every, area // 8
+    )
+    far_same, far_cross = give(dq3_same, dq3_cross, lambda i: i + 6)
+    mine, other = (total(*terms) for terms in zip(dkv0, dkv1a, dkv1b, dkv3))
+    other = swap(jnp.concatenate([dq0_other, other], axis=1).astype(BF16))
     place = jnp.stack([core, head]).astype(jnp.int32)
     left, low, high = collect(
-        place, mine, other, back_same, back_cross, far_same, far_cross, two_same, two_cross,
-        key_same, key_cross, gate_grad, projections,
+        place, dq0, mine, other, back_same, back_cross, far_same, far_cross, key_same, key_cross,
+        gate_grad, projections,
     )
 
     def turn(block, by):

time: 146 us -> 152 us (1.041)
  the two profiles are of different devices: /device:TPU:8 before, /device:TPU:16 now
where the time goes in v5:
time: 152 us; the launch traced here: 149 us
  waiting for transfers between devices  56.1 us (37%)
  Pallas kernels  45.8 us (30%)
  starting transfers between devices  37.9 us (25%)
  other arithmetic  6.99 us (5%)
  local copies, waits for them, and re-layouts  1.59 us (1%)
    ppermute x10, waiting for transfers between devices, move(): return lax.ppermute(block, 'seq', route)  38.6 us
    pallas_call x5, Pallas kernels, pairs(): pl.pallas_call(lambda *refs: pairs_kernel(name == 'pairs_own', parts, til...  36.9 us
    ppermute x10, starting transfers between devices, move(): return lax.ppermute(block, 'seq', route)  30.6 us
    ppermute x4, waiting for transfers between devices, turn(): return lax.ppermute(block, 'head', [(i, (i + by) % 4) for i in range(4)])  17.5 us
    ppermute x4, starting transfers between devices, turn(): return lax.ppermute(block, 'head', [(i, (i + by) % 4) for i in range(4)])  6.67 us
    pallas_call x1, Pallas kernels, by_rows(): pl.pallas_call(kernel, grid_spec=pltpu.PrefetchScalarGridSpec(num_scalar_...  4.45 us
  transfers between devices with their start and end apart: 18, of which 8 were waited for; matrix products, arithmetic and copies ran while one was open for 2% of the time, Pallas kernels for 26%

profile of v5, /device:TPU:16, one launch (start us, length us, event | category | flops | bytes accessed | tf_op | source)
XLA Modules:
  0.0 148.8 jit_solution(17411168046179703127)
XLA Ops:
  0.0 1.3 broadcast_select_fusion.6
  1.3 0.1 pad_maximum_fusion.5
  1.3 0.1 collective-permute-start.1
  1.5 0.5 collective-permute-start.2
  1.9 4.5 %shard_map.82 = (bf16[1024,256]{1,0:T(8,128)(2,1)}, bf16[1024,256]{1,0:T(8,128)(2,1)}, bf16[1024,256]{1,0:T(8,128)(2,1)}) custom-call(s32[1]{0:T(128)} %bitcast.core.refs_0_, bf16[1024,256]{1,0:T(8,128)(2,1)} %q.1, bf16[1024,256]{1,0:T(8,128)(2,1)} %o.1, bf16[1024,256]{1,0:T(8,128)(2,1)} %gate.1, bf16[1024,256]{1,0:T(8,128)(2,1)} %grad.1), custom_call_target="tpu_custom_call" | custom-call | flops 7864320 | bytes 4194304 | tf_op jit(solution)/shard_map/pallas_call | solution.py:76
  6.4 0.1 collective-permute-start
  6.5 0.0 collective-permute-done.2
  6.6 0.0 collective-permute-done.1
  6.6 0.2 broadcast_select_fusion.3
  6.8 0.0 copy-start.7
  6.8 0.1 pad_maximum_fusion.refs_2_.refs_3_
  6.9 4.0 %collective-permute-start.5 = (bf16[2064,256]{1,0:T(8,128)(2,1)S(1)}, bf16[2064,256]{1,0:T(8,128)(2,1)S(1)}, u32[]{:S(2)}, u32[]{:S(2)}) collective-permute-start(bf16[2064,256]{1,0:T(8,128)(2,1)S(1)} %pad_maximum_fusion.refs_2_.refs_3_), channel_id=1, source_target_pairs={{0,8},{4,12},{8,16},{12,20},{16,24},{20,28},{24,32},{28,36},{32,40... | collective-permute-start | bytes 3170312 | tf_op jit(solution)/shard_map/ppermute | solution.py:32
  10.8 0.0 collective-permute-done
  10.9 0.1 broadcast_select_fusion
  11.0 4.1 %collective-permute-start.3 = (bf16[1040,256]{1,0:T(8,128)(2,1)S(1)}, bf16[1040,256]{1,0:T(8,128)(2,1)S(1)}, u32[]{:S(2)}, u32[]{:S(2)}) collective-permute-start(bf16[1040,256]{1,0:T(8,128)(2,1)S(1)} %pad_maximum_fusion.3), channel_id=1, source_target_pairs={{8,0},{12,4},{16,8},{20,12},{24,16},{28,20},{32,24},{36,28},{40,32... | collective-permute-start | bytes 1597448 | tf_op jit(solution)/shard_map/ppermute | solution.py:32
  15.1 0.1 pad_maximum_fusion.1.refs_1_
  15.2 3.7 %collective-permute-start.4 = (bf16[1024,256]{1,0:T(8,128)(2,1)S(1)}, bf16[1024,256]{1,0:T(8,128)(2,1)S(1)}, u32[]{:S(2)}, u32[]{:S(2)}) collective-permute-start(bf16[1024,256]{1,0:T(8,128)(2,1)S(1)} %get-tuple-element.85), channel_id=1, source_target_pairs={{8,0},{12,4},{16,8},{20,12},{24,16},{28,20},{32,24},{36,28},{40,32... | collective-permute-start | bytes 1572872 | tf_op jit(solution)/shard_map/ppermute | solution.py:32
  18.9 11.5 %shard_map.83 = (f32[1024,128]{1,0:T(8,128)S(1)}, f32[1024,128]{1,0:T(8,128)S(1)}, f32[1024,256]{1,0:T(8,128)S(1)}, f32[1024,256]{1,0:T(8,128)S(1)}) custom-call(s32[1]{0:T(128)} %bitcast.core.refs_0_, bf16[2064,256]{1,0:T(8,128)(2,1)S(1)} %pad_maximum_fusion.1.refs_1_, bf16[2064,256]{1,0:T(8,128)(2,1)S(1)} %pad_maximum_fusion.refs_2_.refs_3_), custom_call_target="tpu_custom_call" | custom-call | flops 5368709120 | bytes 4194304 | tf_op jit(solution)/shard_map/pallas_call | solution.py:206
  30.5 0.0 collective-permute-done.3.refs_1_
  30.5 8.9 %shard_map.84 = (bf16[1024,128]{1,0:T(8,128)(2,1)S(1)}, bf16[1024,256]{1,0:T(8,128)(2,1)S(1)}, bf16[1024,256]{1,0:T(8,128)(2,1)S(1)}) custom-call(s32[1]{0:T(128)} %bitcast.core.refs_0_, bf16[1040,256]{1,0:T(8,128)(2,1)S(1)} %collective-permute-done.3.refs_1_, bf16[2064,256]{1,0:T(8,128)(2,1)S(1)} %pad_maximum_fusion.refs_2_.refs_3_), custom_call_target="tpu_custom_call" | custom-call | flops 5368709120 | bytes 4194304 | tf_op jit(solution)/shard_map/pallas_call | solution.py:206
  39.4 0.8 copy-done.2
  40.1 0.0 collective-permute-done.4.refs_2_
  40.1 0.0 collective-permute-done.5.refs_3_
  40.1 2.0 %collective-permute-start.6 = (bf16[2064,256]{1,0:T(8,128)(2,1)S(1)}, bf16[2064,256]{1,0:T(8,128)(2,1)S(1)}, u32[]{:S(2)}, u32[]{:S(2)}) collective-permute-start(bf16[2064,256]{1,0:T(8,128)(2,1)S(1)} %pad_maximum_fusion.1.refs_1_), channel_id=1, source_target_pairs={{24,0},{28,4},{32,8},{36,12},{40,16},{44,20},{48,24},{52,28},{56,3... | collective-permute-start | bytes 3170312 | tf_op jit(solution)/shard_map/ppermute | solution.py:32
  42.2 2.3 %shard_map.85 = (bf16[1024,128]{1,0:T(8,128)(2,1)S(1)}, bf16[1024,128]{1,0:T(8,128)(2,1)S(1)}, bf16[1024,256]{1,0:T(8,128)(2,1)}, bf16[1024,256]{1,0:T(8,128)(2,1)}) custom-call(s32[1]{0:T(128)} %bitcast.core.refs_0_, bf16[1040,256]{1,0:T(8,128)(2,1)S(1)} %collective-permute-done.3.refs_1_, bf16[1024,256]{1,0:T(8,128)(2,1)S(1)} %collective-permute-done.4.refs_2_, ...), custom_call_target="tpu_custom_call" | custom-call | flops 5368709120 | bytes 4194304 | tf_op jit(solution)/shard_map/pallas_call | solution.py:206
  44.5 8.9 %shard_map.86 = (bf16[1024,128]{1,0:T(8,128)(2,1)S(1)}, bf16[1024,256]{1,0:T(8,128)(2,1)S(1)}, bf16[1024,256]{1,0:T(8,128)(2,1)S(1)}) custom-call(s32[1]{0:T(128)} %bitcast.core.refs_0_, bf16[1040,256]{1,0:T(8,128)(2,1)S(1)} %collective-permute-done.3.refs_1_, bf16[1024,256]{1,0:T(8,128)(2,1)S(1)} %collective-permute-done.4.refs_2_, ...), custom_call_target="tpu_custom_call" | custom-call | flops 5368709120 | bytes 4194304 | tf_op jit(solution)/shard_map/pallas_call | solution.py:206
  53.4 14.7 %collective-permute-done.6.refs_1_ = bf16[2064,256]{1,0:T(8,128)(2,1)S(1)} collective-permute-done((bf16[2064,256]{1,0:T(8,128)(2,1)S(1)}, bf16[2064,256]{1,0:T(8,128)(2,1)S(1)}, u32[]{:S(2)}, u32[]{:S(2)}) %collective-permute-start.6) | collective-permute-done | bytes 1056800 | tf_op jit(solution)/shard_map/ppermute | solution.py:32
  68.0 5.4 %shard_map.87 = (bf16[1024,128]{1,0:T(8,128)(2,1)S(1)}, bf16[1024,128]{1,0:T(8,128)(2,1)S(1)}, bf16[1024,256]{1,0:T(8,128)(2,1)S(1)}, bf16[1024,256]{1,0:T(8,128)(2,1)S(1)}) custom-call(s32[1]{0:T(128)} %bitcast.core.refs_0_, bf16[2064,256]{1,0:T(8,128)(2,1)S(1)} %collective-permute-done.6.refs_1_, bf16[2064,256]{1,0:T(8,128)(2,1)S(1)} %pad_maximum_fusion.refs_2_.refs_3_), custom_call_target="tpu_custom_call" | custom-call | flops 1342177280 | bytes 4194304 | tf_op jit(solution)/shard_map/pallas_call | solution.py:206
  73.4 0.0 copy-start.4
  73.4 0.3 add_convert_fusion.1
  73.7 0.5 copy-done.4
  74.2 0.1 copy-done.5
  74.3 0.1 copy-done.6
  74.4 1.0 pad_maximum_fusion.2
  75.4 0.0 collective-permute-start.7
  75.4 1.0 add_convert_fusion.4
  76.3 1.9 %collective-permute-start.9 = (bf16[1024,128]{1,0:T(8,128)(2,1)}, bf16[1024,128]{1,0:T(8,128)(2,1)}, u32[]{:S(2)}, u32[]{:S(2)}) collective-permute-start(bf16[1024,128]{1,0:T(8,128)(2,1)} %get-tuple-element.89), channel_id=1, source_target_pairs={{0,12},{4,8},{8,20},{12,16},{16,28},{20,24},{24,36},{28,32},{32,44... | collective-permute-start | bytes 786440 | tf_op jit(solution)/shard_map/ppermute | solution.py:32
  78.2 1.9 %collective-permute-start.8 = (bf16[1024,128]{1,0:T(8,128)(2,1)}, bf16[1024,128]{1,0:T(8,128)(2,1)}, u32[]{:S(2)}, u32[]{:S(2)}) collective-permute-start(bf16[1024,128]{1,0:T(8,128)(2,1)} %get-tuple-element.90), channel_id=1, source_target_pairs={{0,8},{4,12},{8,16},{12,20},{16,24},{20,28},{24,32},{28,36},{32,40... | collective-permute-start | bytes 786440 | tf_op jit(solution)/shard_map/ppermute | solution.py:32
  80.2 6.1 %collective-permute-start.12 = (bf16[1024,256]{1,0:T(8,128)(2,1)}, bf16[1024,256]{1,0:T(8,128)(2,1)S(1)}, u32[]{:S(2)}, u32[]{:S(2)}) collective-permute-start(bf16[1024,256]{1,0:T(8,128)(2,1)} %get-tuple-element.76), channel_id=1, source_target_pairs={{8,0},{12,4},{16,8},{20,12},{24,16},{28,20},{32,24},{36,28},{40,32... | collective-permute-start | bytes 1572872 | tf_op jit(solution)/shard_map/ppermute | solution.py:32
  86.3 3.0 %collective-permute-start.13 = (bf16[1024,256]{1,0:T(8,128)(2,1)}, bf16[1024,256]{1,0:T(8,128)(2,1)S(1)}, u32[]{:S(2)}, u32[]{:S(2)}) collective-permute-start(bf16[1024,256]{1,0:T(8,128)(2,1)} %get-tuple-element.77), channel_id=1, source_target_pairs={{8,4},{12,0},{16,12},{20,8},{24,20},{28,16},{32,28},{36,24},{40,36... | collective-permute-start | bytes 1572872 | tf_op jit(solution)/shard_map/ppermute | solution.py:32
  89.3 0.1 pad_add_fusion.place
  89.4 0.0 collective-permute-done.9.back_cross
  89.4 1.9 %collective-permute-start.10 = (bf16[1024,128]{1,0:T(8,128)(2,1)}, bf16[1024,128]{1,0:T(8,128)(2,1)S(1)}, u32[]{:S(2)}, u32[]{:S(2)}) collective-permute-start(bf16[1024,128]{1,0:T(8,128)(2,1)} %copy-done.6), channel_id=1, source_target_pairs={{0,24},{4,28},{8,32},{12,36},{16,40},{20,44},{24,48},{28,52},{32,5... | collective-permute-start | bytes 786440 | tf_op jit(solution)/shard_map/ppermute | solution.py:32
  91.3 4.2 %collective-permute-done.8.back_same = bf16[1024,128]{1,0:T(8,128)(2,1)} collective-permute-done((bf16[1024,128]{1,0:T(8,128)(2,1)}, bf16[1024,128]{1,0:T(8,128)(2,1)}, u32[]{:S(2)}, u32[]{:S(2)}) %collective-permute-start.8) | collective-permute-done | bytes 262176 | tf_op jit(solution)/shard_map/ppermute | solution.py:32
  95.5 1.9 %collective-permute-start.11 = (bf16[1024,128]{1,0:T(8,128)(2,1)}, bf16[1024,128]{1,0:T(8,128)(2,1)S(1)}, u32[]{:S(2)}, u32[]{:S(2)}) collective-permute-start(bf16[1024,128]{1,0:T(8,128)(2,1)} %copy-done.5), channel_id=1, source_target_pairs={{0,28},{4,24},{8,36},{12,32},{16,44},{20,40},{24,52},{28,48},{32,6... | collective-permute-start | bytes 786440 | tf_op jit(solution)/shard_map/ppermute | solution.py:32
  97.5 0.0 copy-start
  97.5 1.7 %convert_add_fusion.dkv = f32[1024,256]{1,0:T(8,128)S(1)} fusion(bf16[1024,256]{1,0:T(8,128)(2,1)} %copy-done.4, bf16[1024,256]{1,0:T(8,128)(2,1)} %copy-done.3, f32[1024,256]{1,0:T(8,128)S(1)} %get-tuple-element.52, bf16[1024,256]{1,0:T(8,128)(2,1)} %copy-done.2), kind=kLoop, calls=%fused_computation.4 | loop fusion | flops 1572864 | bytes 3670016 | tf_op jit(solution)/shard_map/add | solution.py:44
  99.2 9.1 %collective-permute-done.12.key_same = bf16[1024,256]{1,0:T(8,128)(2,1)S(1)} collective-permute-done((bf16[1024,256]{1,0:T(8,128)(2,1)}, bf16[1024,256]{1,0:T(8,128)(2,1)S(1)}, u32[]{:S(2)}, u32[]{:S(2)}) %collective-permute-start.12) | collective-permute-done | bytes 524320 | tf_op jit(solution)/shard_map/ppermute | solution.py:32
  108.3 10.3 %collective-permute-done.13.key_cross = bf16[1024,256]{1,0:T(8,128)(2,1)S(1)} collective-permute-done((bf16[1024,256]{1,0:T(8,128)(2,1)}, bf16[1024,256]{1,0:T(8,128)(2,1)S(1)}, u32[]{:S(2)}, u32[]{:S(2)}) %collective-permute-start.13) | collective-permute-done | bytes 524320 | tf_op jit(solution)/shard_map/ppermute | solution.py:32
  118.6 0.0 collective-permute-done.10.far_same
  118.6 0.3 collective-permute-done.11.far_cross
  118.9 0.0 collective-permute-done.7.other
  118.9 2.1 %collect.1 = (bf16[1024,1024]{1,0:T(8,128)(2,1)S(1)}, bf16[512,256]{1,0:T(8,128)(2,1)S(1)}, bf16[512,256]{1,0:T(8,128)(2,1)S(1)}) custom-call(s32[2]{0:T(128)S(1)} %pad_add_fusion.place, f32[1024,128]{1,0:T(8,128)S(1)} %get-tuple-element.51.dq, f32[1024,256]{1,0:T(8,128)S(1)} %convert_add_fusion.dkv, bf16[1024,384]{1,0:T(8,128)(2,1)S(1)} %collective-permute-done.7.other, ...), custom_call_target="tpu_custom_call" | custom-call | flops 536870912 | bytes 8388608 | tf_op jit(solution)/shard_map/collect/pallas_call | solution.py:277
  121.0 2.8 %collective-permute-start.16 = (bf16[512,256]{1,0:T(8,128)(2,1)S(1)}, bf16[512,256]{1,0:T(8,128)(2,1)S(1)}, u32[]{:S(2)}, u32[]{:S(2)}) collective-permute-start(bf16[512,256]{1,0:T(8,128)(2,1)S(1)} %get-tuple-element.84), channel_id=1, source_target_pairs={{0,3},{1,0},{2,1},{3,2},{4,7},{5,4},{6,5},{7,6},{8,11},{9,8},{10,9... | collective-permute-start | bytes 786440 | tf_op jit(solution)/shard_map/ppermute | solution.py:372
  123.8 0.0 collective-permute-start.14
  123.8 2.4 %project.1 = (f32[1024,256]{1,0:T(8,128)S(1)}, f32[1024,256]{1,0:T(8,128)S(1)}, f32[1024,256]{1,0:T(8,128)S(1)}) custom-call(s32[2]{0:T(128)S(1)} %pad_add_fusion.place, bf16[1024,1024]{1,0:T(8,128)(2,1)S(1)} %get-tuple-element.79.left, bf16[4,1024,256]{2,1,0:T(8,128)(2,1)S(1)} %copy-done), custom_call_target="tpu_custom_call" | custom-call | flops 1610612736 | bytes 8388608 | tf_op jit(solution)/shard_map/project/pallas_call | solution.py:289
  126.3 3.5 %collective-permute-done.16 = bf16[512,256]{1,0:T(8,128)(2,1)S(1)} collective-permute-done((bf16[512,256]{1,0:T(8,128)(2,1)S(1)}, bf16[512,256]{1,0:T(8,128)(2,1)S(1)}, u32[]{:S(2)}, u32[]{:S(2)}) %collective-permute-start.16) | collective-permute-done | bytes 262176 | tf_op jit(solution)/shard_map/ppermute | solution.py:372
  129.7 0.1 add_convert_fusion.2
  129.8 3.8 %collective-permute-start.17 = (bf16[1024,256]{1,0:T(8,128)(2,1)S(1)}, bf16[1024,256]{1,0:T(8,128)(2,1)S(1)}, u32[]{:S(2)}, u32[]{:S(2)}) collective-permute-start(bf16[1024,256]{1,0:T(8,128)(2,1)S(1)} %pad_maximum_fusion.7), channel_id=1, source_target_pairs={{0,3},{1,0},{2,1},{3,2},{4,7},{5,4},{6,5},{7,6},{8,11},{9,8},{10,9... | collective-permute-start | bytes 1572872 | tf_op jit(solution)/shard_map/ppermute | solution.py:372
  133.6 0.1 add_convert_fusion.3
  133.7 0.1 collective-permute-start.15
  133.8 10.5 %collective-permute-done.17 = bf16[1024,256]{1,0:T(8,128)(2,1)S(1)} collective-permute-done((bf16[1024,256]{1,0:T(8,128)(2,1)S(1)}, bf16[1024,256]{1,0:T(8,128)(2,1)S(1)}, u32[]{:S(2)}, u32[]{:S(2)}) %collective-permute-start.17) | collective-permute-done | bytes 524320 | tf_op jit(solution)/shard_map/ppermute | solution.py:372
  144.2 3.6 %collective-permute-done.15 = bf16[1024,256]{1,0:T(8,128)(2,1)S(1)} collective-permute-done((bf16[1024,256]{1,0:T(8,128)(2,1)S(1)}, bf16[1024,256]{1,0:T(8,128)(2,1)S(1)}, u32[]{:S(2)}, u32[]{:S(2)}) %collective-permute-start.15) | collective-permute-done | bytes 524320 | tf_op jit(solution)/shard_map/ppermute | solution.py:372
  147.8 1.0 add_convert_fusion
  (23 shorter events, 0.3 us)
Async XLA Ops:
  0.0 1.4 copy-start.8
  1.3 5.2 %collective-permute-start.1 = (bf16[1024,256]{1,0:T(8,128)(2,1)S(1)}, bf16[1024,256]{1,0:T(8,128)(2,1)S(1)}, u32[]{:S(2)}, u32[]{:S(2)}) collective-permute-start(bf16[1024,256]{1,0:T(8,128)(2,1)S(1)} %pad_maximum_fusion.5), channel_id=1, source_target_pairs={{0,4},{4,0},{8,12},{12,8},{16,20},{20,16},{24,28},{28,24},{32,36},... | collective-permute-start | bytes 1572872 | tf_op jit(solution)/shard_map/ppermute | solution.py:40
  1.5 5.0 %collective-permute-start.2 = (bf16[1024]{0:T(1024)(128)(2,1)S(1)}, bf16[1024]{0:T(1024)(128)(2,1)S(1)}, u32[]{:S(2)}, u32[]{:S(2)}) collective-permute-start(bf16[1024]{0:T(1024)(128)(2,1)S(1)} %add_convert_fusion.6), channel_id=1, source_target_pairs={{0,4},{4,0},{8,12},{12,8},{16,20},{20,16},{24,28},{28,24},{32,36},... | collective-permute-start | bytes 6152 | tf_op jit(solution)/shard_map/ppermute | solution.py:40
  6.4 4.5 %collective-permute-start = (bf16[1024,256]{1,0:T(8,128)(2,1)}, bf16[1024,256]{1,0:T(8,128)(2,1)S(1)}, u32[]{:S(2)}, u32[]{:S(2)}) collective-permute-start(bf16[1024,256]{1,0:T(8,128)(2,1)} %get-tuple-element.46), channel_id=1, source_target_pairs={{0,4},{4,0},{8,12},{12,8},{16,20},{20,16},{24,28},{28,24},{32,36},... | collective-permute-start | bytes 1572872 | tf_op jit(solution)/shard_map/ppermute | solution.py:40
  6.8 4.1 %copy-start.7 = (bf16[1024,256]{1,0:T(8,128)(2,1)S(1)}, bf16[1024,256]{1,0:T(8,128)(2,1)}, u32[]{:S(2)}) copy-start(bf16[1024,256]{1,0:T(8,128)(2,1)} %get-tuple-element.45) | copy-start | bytes 1572868
  6.9 33.3 %collective-permute-start.5 = (bf16[2064,256]{1,0:T(8,128)(2,1)S(1)}, bf16[2064,256]{1,0:T(8,128)(2,1)S(1)}, u32[]{:S(2)}, u32[]{:S(2)}) collective-permute-start(bf16[2064,256]{1,0:T(8,128)(2,1)S(1)} %pad_maximum_fusion.refs_2_.refs_3_), channel_id=1, source_target_pairs={{0,8},{4,12},{8,16},{12,20},{16,24},{20,28},{24,32},{28,36},{32,40... | collective-permute-start | bytes 3170312 | tf_op jit(solution)/shard_map/ppermute | solution.py:32
  11.0 19.5 %collective-permute-start.3 = (bf16[1040,256]{1,0:T(8,128)(2,1)S(1)}, bf16[1040,256]{1,0:T(8,128)(2,1)S(1)}, u32[]{:S(2)}, u32[]{:S(2)}) collective-permute-start(bf16[1040,256]{1,0:T(8,128)(2,1)S(1)} %pad_maximum_fusion.3), channel_id=1, source_target_pairs={{8,0},{12,4},{16,8},{20,12},{24,16},{28,20},{32,24},{36,28},{40,32... | collective-permute-start | bytes 1597448 | tf_op jit(solution)/shard_map/ppermute | solution.py:32
  15.2 24.9 %collective-permute-start.4 = (bf16[1024,256]{1,0:T(8,128)(2,1)S(1)}, bf16[1024,256]{1,0:T(8,128)(2,1)S(1)}, u32[]{:S(2)}, u32[]{:S(2)}) collective-permute-start(bf16[1024,256]{1,0:T(8,128)(2,1)S(1)} %get-tuple-element.85), channel_id=1, source_target_pairs={{8,0},{12,4},{16,8},{20,12},{24,16},{28,20},{32,24},{36,28},{40,32... | collective-permute-start | bytes 1572872 | tf_op jit(solution)/shard_map/ppermute | solution.py:32
  39.3 0.8 copy-start.2
  40.1 27.9 %collective-permute-start.6 = (bf16[2064,256]{1,0:T(8,128)(2,1)S(1)}, bf16[2064,256]{1,0:T(8,128)(2,1)S(1)}, u32[]{:S(2)}, u32[]{:S(2)}) collective-permute-start(bf16[2064,256]{1,0:T(8,128)(2,1)S(1)} %pad_maximum_fusion.1.refs_1_), channel_id=1, source_target_pairs={{24,0},{28,4},{32,8},{36,12},{40,16},{44,20},{48,24},{52,28},{56,3... | collective-permute-start | bytes 3170312 | tf_op jit(solution)/shard_map/ppermute | solution.py:32
  53.4 20.0 %copy-start.3 = (bf16[1024,256]{1,0:T(8,128)(2,1)}, bf16[1024,256]{1,0:T(8,128)(2,1)S(1)}, u32[]{:S(2)}) copy-start(bf16[1024,256]{1,0:T(8,128)(2,1)S(1)} %get-tuple-element.61) | copy-start | bytes 1572868
  73.4 0.8 copy-start.4
  73.4 0.8 copy-start.5
  73.4 1.0 copy-start.6
  75.4 43.5 %collective-permute-start.7 = (bf16[1024,384]{1,0:T(8,128)(2,1)}, bf16[1024,384]{1,0:T(8,128)(2,1)S(1)}, u32[]{:S(2)}, u32[]{:S(2)}) collective-permute-start(bf16[1024,384]{1,0:T(8,128)(2,1)} %pad_maximum_fusion.2), channel_id=1, source_target_pairs={{0,4},{4,0},{8,12},{12,8},{16,20},{20,16},{24,28},{28,24},{32,36},... | collective-permute-start | bytes 2359304 | tf_op jit(solution)/shard_map/ppermute | solution.py:40
  76.3 13.1 %collective-permute-start.9 = (bf16[1024,128]{1,0:T(8,128)(2,1)}, bf16[1024,128]{1,0:T(8,128)(2,1)}, u32[]{:S(2)}, u32[]{:S(2)}) collective-permute-start(bf16[1024,128]{1,0:T(8,128)(2,1)} %get-tuple-element.89), channel_id=1, source_target_pairs={{0,12},{4,8},{8,20},{12,16},{16,28},{20,24},{24,36},{28,32},{32,44... | collective-permute-start | bytes 786440 | tf_op jit(solution)/shard_map/ppermute | solution.py:32
  78.2 17.3 %collective-permute-start.8 = (bf16[1024,128]{1,0:T(8,128)(2,1)}, bf16[1024,128]{1,0:T(8,128)(2,1)}, u32[]{:S(2)}, u32[]{:S(2)}) collective-permute-start(bf16[1024,128]{1,0:T(8,128)(2,1)} %get-tuple-element.90), channel_id=1, source_target_pairs={{0,8},{4,12},{8,16},{12,20},{16,24},{20,28},{24,32},{28,36},{32,40... | collective-permute-start | bytes 786440 | tf_op jit(solution)/shard_map/ppermute | solution.py:32
  80.2 28.1 %collective-permute-start.12 = (bf16[1024,256]{1,0:T(8,128)(2,1)}, bf16[1024,256]{1,0:T(8,128)(2,1)S(1)}, u32[]{:S(2)}, u32[]{:S(2)}) collective-permute-start(bf16[1024,256]{1,0:T(8,128)(2,1)} %get-tuple-element.76), channel_id=1, source_target_pairs={{8,0},{12,4},{16,8},{20,12},{24,16},{28,20},{32,24},{36,28},{40,32... | collective-permute-start | bytes 1572872 | tf_op jit(solution)/shard_map/ppermute | solution.py:32
  86.3 32.3 %collective-permute-start.13 = (bf16[1024,256]{1,0:T(8,128)(2,1)}, bf16[1024,256]{1,0:T(8,128)(2,1)S(1)}, u32[]{:S(2)}, u32[]{:S(2)}) collective-permute-start(bf16[1024,256]{1,0:T(8,128)(2,1)} %get-tuple-element.77), channel_id=1, source_target_pairs={{8,4},{12,0},{16,12},{20,8},{24,20},{28,16},{32,28},{36,24},{40,36... | collective-permute-start | bytes 1572872 | tf_op jit(solution)/shard_map/ppermute | solution.py:32
  89.4 29.2 %collective-permute-start.10 = (bf16[1024,128]{1,0:T(8,128)(2,1)}, bf16[1024,128]{1,0:T(8,128)(2,1)S(1)}, u32[]{:S(2)}, u32[]{:S(2)}) collective-permute-start(bf16[1024,128]{1,0:T(8,128)(2,1)} %copy-done.6), channel_id=1, source_target_pairs={{0,24},{4,28},{8,32},{12,36},{16,40},{20,44},{24,48},{28,52},{32,5... | collective-permute-start | bytes 786440 | tf_op jit(solution)/shard_map/ppermute | solution.py:32
  95.5 23.4 %collective-permute-start.11 = (bf16[1024,128]{1,0:T(8,128)(2,1)}, bf16[1024,128]{1,0:T(8,128)(2,1)S(1)}, u32[]{:S(2)}, u32[]{:S(2)}) collective-permute-start(bf16[1024,128]{1,0:T(8,128)(2,1)} %copy-done.5), channel_id=1, source_target_pairs={{0,28},{4,24},{8,36},{12,32},{16,44},{20,40},{24,52},{28,48},{32,6... | collective-permute-start | bytes 786440 | tf_op jit(solution)/shard_map/ppermute | solution.py:32
  97.5 21.5 %copy-start = (bf16[4,1024,256]{2,1,0:T(8,128)(2,1)S(1)}, bf16[4,1024,256]{2,1,0:T(8,128)(2,1)}, u32[]{:S(2)}) copy-start(bf16[4,1024,256]{2,1,0:T(8,128)(2,1)} %weights.3) | copy-start | bytes 6291460
  97.5 21.4 %copy-start.1 = (bf16[1024,256]{1,0:T(8,128)(2,1)S(1)}, bf16[1024,256]{1,0:T(8,128)(2,1)}, u32[]{:S(2)}) copy-start(bf16[1024,256]{1,0:T(8,128)(2,1)} %get-tuple-element.78.gate_grad) | copy-start | bytes 1572868
  121.0 8.7 %collective-permute-start.16 = (bf16[512,256]{1,0:T(8,128)(2,1)S(1)}, bf16[512,256]{1,0:T(8,128)(2,1)S(1)}, u32[]{:S(2)}, u32[]{:S(2)}) collective-permute-start(bf16[512,256]{1,0:T(8,128)(2,1)S(1)} %get-tuple-element.84), channel_id=1, source_target_pairs={{0,3},{1,0},{2,1},{3,2},{4,7},{5,4},{6,5},{7,6},{8,11},{9,8},{10,9... | collective-permute-start | bytes 786440 | tf_op jit(solution)/shard_map/ppermute | solution.py:372
  123.8 9.8 %collective-permute-start.14 = (bf16[512,256]{1,0:T(8,128)(2,1)S(1)}, bf16[512,256]{1,0:T(8,128)(2,1)S(1)}, u32[]{:S(2)}, u32[]{:S(2)}) collective-permute-start(bf16[512,256]{1,0:T(8,128)(2,1)S(1)} %get-tuple-element.82), channel_id=1, source_target_pairs={{0,1},{1,2},{2,3},{3,0},{4,5},{5,6},{6,7},{7,4},{8,9},{9,10},{10,1... | collective-permute-start | bytes 786440 | tf_op jit(solution)/shard_map/ppermute | solution.py:372
  129.8 14.4 %collective-permute-start.17 = (bf16[1024,256]{1,0:T(8,128)(2,1)S(1)}, bf16[1024,256]{1,0:T(8,128)(2,1)S(1)}, u32[]{:S(2)}, u32[]{:S(2)}) collective-permute-start(bf16[1024,256]{1,0:T(8,128)(2,1)S(1)} %pad_maximum_fusion.7), channel_id=1, source_target_pairs={{0,3},{1,0},{2,1},{3,2},{4,7},{5,4},{6,5},{7,6},{8,11},{9,8},{10,9... | collective-permute-start | bytes 1572872 | tf_op jit(solution)/shard_map/ppermute | solution.py:372
  133.7 14.1 %collective-permute-start.15 = (bf16[1024,256]{1,0:T(8,128)(2,1)S(1)}, bf16[1024,256]{1,0:T(8,128)(2,1)S(1)}, u32[]{:S(2)}, u32[]{:S(2)}) collective-permute-start(bf16[1024,256]{1,0:T(8,128)(2,1)S(1)} %pad_maximum_fusion.6), channel_id=1, source_target_pairs={{0,1},{1,2},{2,3},{3,0},{4,5},{5,6},{6,7},{7,4},{8,9},{9,10},{10,1... | collective-permute-start | bytes 1572872 | tf_op jit(solution)/shard_map/ppermute | solution.py:372

commit v6 on v5

--- a/solution.py
+++ b/solution.py
@@ -338,28 +338,26 @@
     dq0, dq0_other, *dkv0 = pairs(
         "pairs_own", core_at, [query], [WHOLE], key, F32, every, area // 2
     )
-    next_a, dq0 = lax.optimization_barrier((next_a, dq0))
+    query, next_a, dq0 = lax.optimization_barrier((query, next_a, dq0))
+    query_far = shift(query, -6)
     dq1a, *dkv1a = pairs("pairs_one", core_at, [next_a], [EARLY], key, BF16, early, area // 2)
-    query, next_a, next_b, key_prev, dq1a = lax.optimization_barrier(
-        (query, next_a, next_b, key_prev, dq1a)
-    )
-    query_far = shift(query, -6)
+    next_a, next_b, key_prev, dq1a = lax.optimization_barrier((next_a, next_b, key_prev, dq1a))
     dq2_same, dq2_cross, *dkv2 = pairs(
         "pairs_two", core_at, [next_a, next_b], [EARLY, LATE], key_prev, BF16, every, area // 2
     )
     key_same, key_cross = give(*dkv2, lambda i: i - 2)
-    next_b, dq2_same = lax.optimization_barrier((next_b, dq2_same))
+    query_far, dq2_same = lax.optimization_barrier((query_far, dq2_same))
+    dq3_same, dq3_cross, *dkv3 = pairs(
+        "pairs_three", core_at, [query_far], [WHOLE], key, BF16, every, area // 8
+    )
+    far_same, far_cross = give(dq3_same, dq3_cross, lambda i: i + 6)
+    next_b, dq3_same = lax.optimization_barrier((next_b, dq3_same))
     dq1b, *dkv1b = pairs(
         "pairs_one", core_at, [next_a, next_b], [USERS_ONLY, LATE], key, BF16, late, area // 2
     )
     same, cross = in_order(dq1a, dq1b)
     same, cross = total(same, dq2_same).astype(BF16), total(cross, dq2_cross).astype(BF16)
     back_same, back_cross = give(same, cross, lambda i: i + 2)
-    query_far, dq1b = lax.optimization_barrier((query_far, dq1b))
-    dq3_same, dq3_cross, *dkv3 = pairs(
-        "pairs_three", core_at, [query_far], [WHOLE], key, BF16, every, area // 8
-    )
-    far_same, far_cross = give(dq3_same, dq3_cross, lambda i: i + 6)
     mine, other = (total(*terms) for terms in zip(dkv0, dkv1a, dkv1b, dkv3))
     other = swap(jnp.concatenate([dq0_other, other], axis=1).astype(BF16))
     place = jnp.stack([core, head]).astype(jnp.int32)

time: 152 us -> 153 us (level)
  the two profiles are of different devices: /device:TPU:16 before, /device:TPU:72 now
where the time goes in v6:
time: 153 us; the launch traced here: 152 us
  starting transfers between devices  58.9 us (38%)
  waiting for transfers between devices  49.9 us (33%)
  Pallas kernels  33.8 us (22%)
  other arithmetic  5.94 us (4%)
  local copies, waits for them, and re-layouts  3.06 us (2%)
    ppermute x10, starting transfers between devices, move(): return lax.ppermute(block, 'seq', route)  51.5 us
    ppermute x10, waiting for transfers between devices, move(): return lax.ppermute(block, 'seq', route)  32 us
    pallas_call x5, Pallas kernels, pairs(): pl.pallas_call(lambda *refs: pairs_kernel(name == 'pairs_own', parts, til...  25.4 us
    ppermute x4, waiting for transfers between devices, turn(): return lax.ppermute(block, 'head', [(i, (i + by) % 4) for i in range(4)])  17.9 us
    ppermute x4, starting transfers between devices, turn(): return lax.ppermute(block, 'head', [(i, (i + by) % 4) for i in range(4)])  6.66 us
    pallas_call x1, Pallas kernels, by_rows(): pl.pallas_call(kernel, grid_spec=pltpu.PrefetchScalarGridSpec(num_scalar_...  4.48 us
  transfers between devices with their start and end apart: 18, of which 9 were waited for; matrix products, arithmetic and copies ran while one was open for 2% of the time, Pallas kernels for 21%

profile of v6, /device:TPU:72, one launch (start us, length us, event | category | flops | bytes accessed | tf_op | source)
XLA Modules:
  0.0 152.1 jit_solution(167618337701410784)
XLA Ops:
  0.0 1.3 broadcast_select_fusion.6
  1.3 0.1 pad_maximum_fusion.5
  1.3 0.1 collective-permute-start.1
  1.5 0.5 collective-permute-start.2
  1.9 4.5 %shard_map.82 = (bf16[1024,256]{1,0:T(8,128)(2,1)}, bf16[1024,256]{1,0:T(8,128)(2,1)}, bf16[1024,256]{1,0:T(8,128)(2,1)}) custom-call(s32[1]{0:T(128)} %bitcast.core.refs_0_, bf16[1024,256]{1,0:T(8,128)(2,1)} %q.1, bf16[1024,256]{1,0:T(8,128)(2,1)} %o.1, bf16[1024,256]{1,0:T(8,128)(2,1)} %gate.1, bf16[1024,256]{1,0:T(8,128)(2,1)} %grad.1), custom_call_target="tpu_custom_call" | custom-call | flops 7864320 | bytes 4194304 | tf_op jit(solution)/shard_map/pallas_call | solution.py:76
  6.4 0.1 collective-permute-start
  6.5 0.0 collective-permute-done.2
  6.6 0.0 collective-permute-done.1
  6.6 0.2 broadcast_select_fusion.3
  6.8 0.0 copy-start.14
  6.8 0.1 pad_maximum_fusion.refs_2_.refs_3_
  6.9 3.7 %collective-permute-start.5 = (bf16[2064,256]{1,0:T(8,128)(2,1)S(1)}, bf16[2064,256]{1,0:T(8,128)(2,1)S(1)}, u32[]{:S(2)}, u32[]{:S(2)}) collective-permute-start(bf16[2064,256]{1,0:T(8,128)(2,1)S(1)} %pad_maximum_fusion.refs_2_.refs_3_), channel_id=1, source_target_pairs={{0,8},{4,12},{8,16},{12,20},{16,24},{20,28},{24,32},{28,36},{32,40... | collective-permute-start | bytes 3170312 | tf_op jit(solution)/shard_map/ppermute | solution.py:32
  10.6 0.0 collective-permute-done
  10.6 0.1 broadcast_select_fusion.1
  10.7 2.3 %collective-permute-start.3 = (bf16[1040,256]{1,0:T(8,128)(2,1)S(1)}, bf16[1040,256]{1,0:T(8,128)(2,1)S(1)}, u32[]{:S(2)}, u32[]{:S(2)}) collective-permute-start(bf16[1040,256]{1,0:T(8,128)(2,1)S(1)} %pad_maximum_fusion.3), channel_id=1, source_target_pairs={{8,0},{12,4},{16,8},{20,12},{24,16},{28,20},{32,24},{36,28},{40,32... | collective-permute-start | bytes 1597448 | tf_op jit(solution)/shard_map/ppermute | solution.py:32
  13.0 0.1 pad_maximum_fusion.1.refs_1_
  13.1 11.5 %shard_map.83 = (f32[1024,128]{1,0:T(8,128)S(1)}, f32[1024,128]{1,0:T(8,128)S(1)}, f32[1024,256]{1,0:T(8,128)S(1)}, f32[1024,256]{1,0:T(8,128)S(1)}) custom-call(s32[1]{0:T(128)} %bitcast.core.refs_0_, bf16[2064,256]{1,0:T(8,128)(2,1)S(1)} %pad_maximum_fusion.1.refs_1_, bf16[2064,256]{1,0:T(8,128)(2,1)S(1)} %pad_maximum_fusion.refs_2_.refs_3_), custom_call_target="tpu_custom_call" | custom-call | flops 5368709120 | bytes 4194304 | tf_op jit(solution)/shard_map/pallas_call | solution.py:206
  24.6 2.1 %collective-permute-done.3.refs_1_ = bf16[1040,256]{1,0:T(8,128)(2,1)S(1)} collective-permute-done((bf16[1040,256]{1,0:T(8,128)(2,1)S(1)}, bf16[1040,256]{1,0:T(8,128)(2,1)S(1)}, u32[]{:S(2)}, u32[]{:S(2)}) %collective-permute-start.3) | collective-permute-done | bytes 532512 | tf_op jit(solution)/shard_map/ppermute | solution.py:32
  26.7 4.2 %collective-permute-start.6 = (bf16[2064,256]{1,0:T(8,128)(2,1)S(1)}, bf16[2064,256]{1,0:T(8,128)(2,1)S(1)}, u32[]{:S(2)}, u32[]{:S(2)}) collective-permute-start(bf16[2064,256]{1,0:T(8,128)(2,1)S(1)} %pad_maximum_fusion.1.refs_1_), channel_id=1, source_target_pairs={{24,0},{28,4},{32,8},{36,12},{40,16},{44,20},{48,24},{52,28},{56,3... | collective-permute-start | bytes 3170312 | tf_op jit(solution)/shard_map/ppermute | solution.py:32
  30.9 1.9 %collective-permute-start.4 = (bf16[1024,256]{1,0:T(8,128)(2,1)S(1)}, bf16[1024,256]{1,0:T(8,128)(2,1)S(1)}, u32[]{:S(2)}, u32[]{:S(2)}) collective-permute-start(bf16[1024,256]{1,0:T(8,128)(2,1)S(1)} %get-tuple-element.86), channel_id=1, source_target_pairs={{8,0},{12,4},{16,8},{20,12},{24,16},{28,20},{32,24},{36,28},{40,32... | collective-permute-start | bytes 1572872 | tf_op jit(solution)/shard_map/ppermute | solution.py:32
  32.9 5.2 %shard_map.84 = (bf16[1024,128]{1,0:T(8,128)(2,1)S(1)}, bf16[1024,256]{1,0:T(8,128)(2,1)S(1)}, bf16[1024,256]{1,0:T(8,128)(2,1)S(1)}) custom-call(s32[1]{0:T(128)} %bitcast.core.refs_0_, bf16[1040,256]{1,0:T(8,128)(2,1)S(1)} %collective-permute-done.3.refs_1_, bf16[2064,256]{1,0:T(8,128)(2,1)S(1)} %pad_maximum_fusion.refs_2_.refs_3_), custom_call_target="tpu_custom_call" | custom-call | flops 5368709120 | bytes 4194304 | tf_op jit(solution)/shard_map/pallas_call | solution.py:206
  38.2 0.8 copy-done.2
  38.9 0.7 copy-done.8
  39.7 6.1 %collective-permute-done.4.refs_2_ = bf16[1024,256]{1,0:T(8,128)(2,1)S(1)} collective-permute-done((bf16[1024,256]{1,0:T(8,128)(2,1)S(1)}, bf16[1024,256]{1,0:T(8,128)(2,1)S(1)}, u32[]{:S(2)}, u32[]{:S(2)}) %collective-permute-start.4) | collective-permute-done | bytes 524320 | tf_op jit(solution)/shard_map/ppermute | solution.py:32
  45.7 11.5 %collective-permute-done.5.refs_3_ = bf16[2064,256]{1,0:T(8,128)(2,1)S(1)} collective-permute-done((bf16[2064,256]{1,0:T(8,128)(2,1)S(1)}, bf16[2064,256]{1,0:T(8,128)(2,1)S(1)}, u32[]{:S(2)}, u32[]{:S(2)}) %collective-permute-start.5) | collective-permute-done | bytes 1056800 | tf_op jit(solution)/shard_map/ppermute | solution.py:32
  57.2 6.5 %shard_map.85 = (bf16[1024,128]{1,0:T(8,128)(2,1)S(1)}, bf16[1024,128]{1,0:T(8,128)(2,1)S(1)}, bf16[1024,256]{1,0:T(8,128)(2,1)}, bf16[1024,256]{1,0:T(8,128)(2,1)}) custom-call(s32[1]{0:T(128)} %bitcast.core.refs_0_, bf16[1040,256]{1,0:T(8,128)(2,1)S(1)} %collective-permute-done.3.refs_1_, bf16[1024,256]{1,0:T(8,128)(2,1)S(1)} %collective-permute-done.4.refs_2_, ...), custom_call_target="tpu_custom_call" | custom-call | flops 5368709120 | bytes 4194304 | tf_op jit(solution)/shard_map/pallas_call | solution.py:206
  63.8 5.6 %collective-permute-start.12 = (bf16[1024,256]{1,0:T(8,128)(2,1)}, bf16[1024,256]{1,0:T(8,128)(2,1)S(1)}, u32[]{:S(2)}, u32[]{:S(2)}) collective-permute-start(bf16[1024,256]{1,0:T(8,128)(2,1)} %get-tuple-element.76), channel_id=1, source_target_pairs={{8,0},{12,4},{16,8},{20,12},{24,16},{28,20},{32,24},{36,28},{40,32... | collective-permute-start | bytes 1572872 | tf_op jit(solution)/shard_map/ppermute | solution.py:32
  69.4 1.9 %collective-permute-start.13 = (bf16[1024,256]{1,0:T(8,128)(2,1)}, bf16[1024,256]{1,0:T(8,128)(2,1)S(1)}, u32[]{:S(2)}, u32[]{:S(2)}) collective-permute-start(bf16[1024,256]{1,0:T(8,128)(2,1)} %get-tuple-element.77), channel_id=1, source_target_pairs={{8,4},{12,0},{16,12},{20,8},{24,20},{28,16},{32,28},{36,24},{40,36... | collective-permute-start | bytes 1572872 | tf_op jit(solution)/shard_map/ppermute | solution.py:32
  71.3 0.0 collective-permute-done.6.refs_1_
  71.3 1.1 shard_map.86
  72.5 0.0 copy-start.4
  72.5 0.8 copy-done.4
  73.3 1.0 shard_map.87
  74.4 0.2 add_convert_fusion.1
  74.6 0.6 copy-done.6
  75.2 0.1 copy-done.11
  75.3 1.0 pad_maximum_fusion.2
  76.3 0.1 collective-permute-start.7
  76.4 0.1 pad_add_fusion.place
  76.5 18.1 %collective-permute-start.10 = (bf16[1024,128]{1,0:T(8,128)(2,1)}, bf16[1024,128]{1,0:T(8,128)(2,1)S(1)}, u32[]{:S(2)}, u32[]{:S(2)}) collective-permute-start(bf16[1024,128]{1,0:T(8,128)(2,1)} %copy-done.12), channel_id=1, source_target_pairs={{0,24},{4,28},{8,32},{12,36},{16,40},{20,44},{24,48},{28,52},{32,5... | collective-permute-start | bytes 786440 | tf_op jit(solution)/shard_map/ppermute | solution.py:32
  94.5 1.4 add_convert_fusion.4
  95.9 1.9 %collective-permute-start.9 = (bf16[1024,128]{1,0:T(8,128)(2,1)S(1)}, bf16[1024,128]{1,0:T(8,128)(2,1)S(1)}, u32[]{:S(2)}, u32[]{:S(2)}) collective-permute-start(bf16[1024,128]{1,0:T(8,128)(2,1)S(1)} %get-tuple-element.89), channel_id=1, source_target_pairs={{0,12},{4,8},{8,20},{12,16},{16,28},{20,24},{24,36},{28,32},{32,44... | collective-permute-start | bytes 786440 | tf_op jit(solution)/shard_map/ppermute | solution.py:32
  97.8 0.0 collective-permute-done.12.key_same
  97.8 3.2 %collective-permute-start.8 = (bf16[1024,128]{1,0:T(8,128)(2,1)S(1)}, bf16[1024,128]{1,0:T(8,128)(2,1)S(1)}, u32[]{:S(2)}, u32[]{:S(2)}) collective-permute-start(bf16[1024,128]{1,0:T(8,128)(2,1)S(1)} %get-tuple-element.90), channel_id=1, source_target_pairs={{0,8},{4,12},{8,16},{12,20},{16,24},{20,28},{24,32},{28,36},{32,40... | collective-permute-start | bytes 786440 | tf_op jit(solution)/shard_map/ppermute | solution.py:32
  101.1 0.0 collective-permute-done.13.key_cross
  101.1 8.6 %collective-permute-start.11 = (bf16[1024,128]{1,0:T(8,128)(2,1)}, bf16[1024,128]{1,0:T(8,128)(2,1)S(1)}, u32[]{:S(2)}, u32[]{:S(2)}) collective-permute-start(bf16[1024,128]{1,0:T(8,128)(2,1)} %copy-done.13), channel_id=1, source_target_pairs={{0,28},{4,24},{8,36},{12,32},{16,44},{20,40},{24,52},{28,48},{32,6... | collective-permute-start | bytes 786440 | tf_op jit(solution)/shard_map/ppermute | solution.py:32
  109.8 0.0 copy-start
  109.8 0.2 convert_add_fusion.dkv
  110.0 0.5 collective-permute-done.9.back_cross
  110.6 6.3 %collective-permute-done.8.back_same = bf16[1024,128]{1,0:T(8,128)(2,1)S(1)} collective-permute-done((bf16[1024,128]{1,0:T(8,128)(2,1)S(1)}, bf16[1024,128]{1,0:T(8,128)(2,1)S(1)}, u32[]{:S(2)}, u32[]{:S(2)}) %collective-permute-start.8) | collective-permute-done | bytes 262176 | tf_op jit(solution)/shard_map/ppermute | solution.py:32
  116.9 5.4 %collective-permute-done.11.far_cross = bf16[1024,128]{1,0:T(8,128)(2,1)S(1)} collective-permute-done((bf16[1024,128]{1,0:T(8,128)(2,1)}, bf16[1024,128]{1,0:T(8,128)(2,1)S(1)}, u32[]{:S(2)}, u32[]{:S(2)}) %collective-permute-start.11) | collective-permute-done | bytes 262176 | tf_op jit(solution)/shard_map/ppermute | solution.py:32
  122.3 0.0 collective-permute-done.10.far_same
  122.3 1.5 %collect.1 = (bf16[1024,1024]{1,0:T(8,128)(2,1)S(1)}, bf16[512,256]{1,0:T(8,128)(2,1)S(1)}, bf16[512,256]{1,0:T(8,128)(2,1)S(1)}) custom-call(s32[2]{0:T(128)S(1)} %pad_add_fusion.place, f32[1024,128]{1,0:T(8,128)S(1)} %get-tuple-element.51.dq, f32[1024,256]{1,0:T(8,128)S(1)} %convert_add_fusion.dkv, bf16[1024,384]{1,0:T(8,128)(2,1)S(1)} %collective-permute-done.7.other, ...), custom_call_target="tpu_custom_call" | custom-call | flops 536870912 | bytes 8388608 | tf_op jit(solution)/shard_map/collect/pallas_call | solution.py:277
  123.9 2.8 %collective-permute-start.16 = (bf16[512,256]{1,0:T(8,128)(2,1)S(1)}, bf16[512,256]{1,0:T(8,128)(2,1)S(1)}, u32[]{:S(2)}, u32[]{:S(2)}) collective-permute-start(bf16[512,256]{1,0:T(8,128)(2,1)S(1)} %get-tuple-element.84), channel_id=1, source_target_pairs={{0,3},{1,0},{2,1},{3,2},{4,7},{5,4},{6,5},{7,6},{8,11},{9,8},{10,9... | collective-permute-start | bytes 786440 | tf_op jit(solution)/shard_map/ppermute | solution.py:370
  126.7 2.4 %project.1 = (f32[1024,256]{1,0:T(8,128)S(1)}, f32[1024,256]{1,0:T(8,128)S(1)}, f32[1024,256]{1,0:T(8,128)S(1)}) custom-call(s32[2]{0:T(128)S(1)} %pad_add_fusion.place, bf16[1024,1024]{1,0:T(8,128)(2,1)S(1)} %get-tuple-element.79.left, bf16[4,1024,256]{2,1,0:T(8,128)(2,1)S(1)} %copy-done), custom_call_target="tpu_custom_call" | custom-call | flops 1610612736 | bytes 8388608 | tf_op jit(solution)/shard_map/project/pallas_call | solution.py:289
  129.1 3.7 %collective-permute-done.16 = bf16[512,256]{1,0:T(8,128)(2,1)S(1)} collective-permute-done((bf16[512,256]{1,0:T(8,128)(2,1)S(1)}, bf16[512,256]{1,0:T(8,128)(2,1)S(1)}, u32[]{:S(2)}, u32[]{:S(2)}) %collective-permute-start.16) | collective-permute-done | bytes 262176 | tf_op jit(solution)/shard_map/ppermute | solution.py:370
  132.8 0.1 add_convert_fusion.2
  132.9 3.8 %collective-permute-start.17 = (bf16[1024,256]{1,0:T(8,128)(2,1)S(1)}, bf16[1024,256]{1,0:T(8,128)(2,1)S(1)}, u32[]{:S(2)}, u32[]{:S(2)}) collective-permute-start(bf16[1024,256]{1,0:T(8,128)(2,1)S(1)} %pad_maximum_fusion.7), channel_id=1, source_target_pairs={{0,3},{1,0},{2,1},{3,2},{4,7},{5,4},{6,5},{7,6},{8,11},{9,8},{10,9... | collective-permute-start | bytes 1572872 | tf_op jit(solution)/shard_map/ppermute | solution.py:370
  136.7 0.0 collective-permute-done.14
  136.7 0.1 add_convert_fusion.3
  136.8 0.1 collective-permute-start.15
  136.9 10.7 %collective-permute-done.17 = bf16[1024,256]{1,0:T(8,128)(2,1)S(1)} collective-permute-done((bf16[1024,256]{1,0:T(8,128)(2,1)S(1)}, bf16[1024,256]{1,0:T(8,128)(2,1)S(1)}, u32[]{:S(2)}, u32[]{:S(2)}) %collective-permute-start.17) | collective-permute-done | bytes 524320 | tf_op jit(solution)/shard_map/ppermute | solution.py:370
  147.6 3.6 %collective-permute-done.15 = bf16[1024,256]{1,0:T(8,128)(2,1)S(1)} collective-permute-done((bf16[1024,256]{1,0:T(8,128)(2,1)S(1)}, bf16[1024,256]{1,0:T(8,128)(2,1)S(1)}, u32[]{:S(2)}, u32[]{:S(2)}) %collective-permute-start.15) | collective-permute-done | bytes 524320 | tf_op jit(solution)/shard_map/ppermute | solution.py:370
  151.2 0.9 add_convert_fusion
  (37 shorter events, 0.3 us)
Async XLA Ops:
  0.0 1.4 copy-start.15
  1.3 5.2 %collective-permute-start.1 = (bf16[1024,256]{1,0:T(8,128)(2,1)S(1)}, bf16[1024,256]{1,0:T(8,128)(2,1)S(1)}, u32[]{:S(2)}, u32[]{:S(2)}) collective-permute-start(bf16[1024,256]{1,0:T(8,128)(2,1)S(1)} %pad_maximum_fusion.5), channel_id=1, source_target_pairs={{0,4},{4,0},{8,12},{12,8},{16,20},{20,16},{24,28},{28,24},{32,36},... | collective-permute-start | bytes 1572872 | tf_op jit(solution)/shard_map/ppermute | solution.py:40
  1.5 5.1 %collective-permute-start.2 = (bf16[1024]{0:T(1024)(128)(2,1)S(1)}, bf16[1024]{0:T(1024)(128)(2,1)S(1)}, u32[]{:S(2)}, u32[]{:S(2)}) collective-permute-start(bf16[1024]{0:T(1024)(128)(2,1)S(1)} %add_convert_fusion.6), channel_id=1, source_target_pairs={{0,4},{4,0},{8,12},{12,8},{16,20},{20,16},{24,28},{28,24},{32,36},... | collective-permute-start | bytes 6152 | tf_op jit(solution)/shard_map/ppermute | solution.py:40
  6.4 4.2 %collective-permute-start = (bf16[1024,256]{1,0:T(8,128)(2,1)}, bf16[1024,256]{1,0:T(8,128)(2,1)S(1)}, u32[]{:S(2)}, u32[]{:S(2)}) collective-permute-start(bf16[1024,256]{1,0:T(8,128)(2,1)} %get-tuple-element.46), channel_id=1, source_target_pairs={{0,4},{4,0},{8,12},{12,8},{16,20},{20,16},{24,28},{28,24},{32,36},... | collective-permute-start | bytes 1572872 | tf_op jit(solution)/shard_map/ppermute | solution.py:40
  6.8 3.8 %copy-start.14 = (bf16[1024,256]{1,0:T(8,128)(2,1)S(1)}, bf16[1024,256]{1,0:T(8,128)(2,1)}, u32[]{:S(2)}) copy-start(bf16[1024,256]{1,0:T(8,128)(2,1)} %get-tuple-element.45) | copy-start | bytes 1572868
  6.9 50.3 %collective-permute-start.5 = (bf16[2064,256]{1,0:T(8,128)(2,1)S(1)}, bf16[2064,256]{1,0:T(8,128)(2,1)S(1)}, u32[]{:S(2)}, u32[]{:S(2)}) collective-permute-start(bf16[2064,256]{1,0:T(8,128)(2,1)S(1)} %pad_maximum_fusion.refs_2_.refs_3_), channel_id=1, source_target_pairs={{0,8},{4,12},{8,16},{12,20},{16,24},{20,28},{24,32},{28,36},{32,40... | collective-permute-start | bytes 3170312 | tf_op jit(solution)/shard_map/ppermute | solution.py:32
  10.7 16.0 %collective-permute-start.3 = (bf16[1040,256]{1,0:T(8,128)(2,1)S(1)}, bf16[1040,256]{1,0:T(8,128)(2,1)S(1)}, u32[]{:S(2)}, u32[]{:S(2)}) collective-permute-start(bf16[1040,256]{1,0:T(8,128)(2,1)S(1)} %pad_maximum_fusion.3), channel_id=1, source_target_pairs={{8,0},{12,4},{16,8},{20,12},{24,16},{28,20},{32,24},{36,28},{40,32... | collective-permute-start | bytes 1597448 | tf_op jit(solution)/shard_map/ppermute | solution.py:32
  26.7 44.6 %collective-permute-start.6 = (bf16[2064,256]{1,0:T(8,128)(2,1)S(1)}, bf16[2064,256]{1,0:T(8,128)(2,1)S(1)}, u32[]{:S(2)}, u32[]{:S(2)}) collective-permute-start(bf16[2064,256]{1,0:T(8,128)(2,1)S(1)} %pad_maximum_fusion.1.refs_1_), channel_id=1, source_target_pairs={{24,0},{28,4},{32,8},{36,12},{40,16},{44,20},{48,24},{52,28},{56,3... | collective-permute-start | bytes 3170312 | tf_op jit(solution)/shard_map/ppermute | solution.py:32
  30.9 14.8 %collective-permute-start.4 = (bf16[1024,256]{1,0:T(8,128)(2,1)S(1)}, bf16[1024,256]{1,0:T(8,128)(2,1)S(1)}, u32[]{:S(2)}, u32[]{:S(2)}) collective-permute-start(bf16[1024,256]{1,0:T(8,128)(2,1)S(1)} %get-tuple-element.86), channel_id=1, source_target_pairs={{8,0},{12,4},{16,8},{20,12},{24,16},{28,20},{32,24},{36,28},{40,32... | collective-permute-start | bytes 1572872 | tf_op jit(solution)/shard_map/ppermute | solution.py:32
  38.1 0.8 copy-start.2
  38.9 0.7 copy-start.8
  63.7 8.8 %copy-start.9 = (bf16[1024,128]{1,0:T(8,128)(2,1)}, bf16[1024,128]{1,0:T(8,128)(2,1)S(1)}, u32[]{:S(2)}) copy-start(bf16[1024,128]{1,0:T(8,128)(2,1)S(1)} %get-tuple-element.73) | copy-start | bytes 786436
  63.7 8.8 %copy-start.10 = (bf16[1024,128]{1,0:T(8,128)(2,1)}, bf16[1024,128]{1,0:T(8,128)(2,1)S(1)}, u32[]{:S(2)}) copy-start(bf16[1024,128]{1,0:T(8,128)(2,1)S(1)} %get-tuple-element.74) | copy-start | bytes 786436
  63.8 34.1 %collective-permute-start.12 = (bf16[1024,256]{1,0:T(8,128)(2,1)}, bf16[1024,256]{1,0:T(8,128)(2,1)S(1)}, u32[]{:S(2)}, u32[]{:S(2)}) collective-permute-start(bf16[1024,256]{1,0:T(8,128)(2,1)} %get-tuple-element.76), channel_id=1, source_target_pairs={{8,0},{12,4},{16,8},{20,12},{24,16},{28,20},{32,24},{36,28},{40,32... | collective-permute-start | bytes 1572872 | tf_op jit(solution)/shard_map/ppermute | solution.py:32
  69.4 31.7 %collective-permute-start.13 = (bf16[1024,256]{1,0:T(8,128)(2,1)}, bf16[1024,256]{1,0:T(8,128)(2,1)S(1)}, u32[]{:S(2)}, u32[]{:S(2)}) collective-permute-start(bf16[1024,256]{1,0:T(8,128)(2,1)} %get-tuple-element.77), channel_id=1, source_target_pairs={{8,4},{12,0},{16,12},{20,8},{24,20},{28,16},{32,28},{36,24},{40,36... | collective-permute-start | bytes 1572872 | tf_op jit(solution)/shard_map/ppermute | solution.py:32
  72.5 0.8 copy-start.4
  73.3 1.0 copy-start.12
  73.3 1.0 copy-start.13
  74.4 0.8 copy-start.6
  74.4 0.9 copy-start.11
  76.3 46.0 %collective-permute-start.7 = (bf16[1024,384]{1,0:T(8,128)(2,1)}, bf16[1024,384]{1,0:T(8,128)(2,1)S(1)}, u32[]{:S(2)}, u32[]{:S(2)}) collective-permute-start(bf16[1024,384]{1,0:T(8,128)(2,1)} %pad_maximum_fusion.2), channel_id=1, source_target_pairs={{0,4},{4,0},{8,12},{12,8},{16,20},{20,16},{24,28},{28,24},{32,36},... | collective-permute-start | bytes 2359304 | tf_op jit(solution)/shard_map/ppermute | solution.py:40
  76.4 33.3 %copy-start.3 = (bf16[1024,256]{1,0:T(8,128)(2,1)S(1)}, bf16[1024,256]{1,0:T(8,128)(2,1)}, u32[]{:S(2)}) copy-start(bf16[1024,256]{1,0:T(8,128)(2,1)} %copy-done.2) | copy-start | bytes 1572868
  76.4 33.3 %copy-start.5 = (bf16[1024,256]{1,0:T(8,128)(2,1)S(1)}, bf16[1024,256]{1,0:T(8,128)(2,1)}, u32[]{:S(2)}) copy-start(bf16[1024,256]{1,0:T(8,128)(2,1)} %copy-done.4) | copy-start | bytes 1572868
  76.4 33.3 %copy-start.7 = (bf16[1024,256]{1,0:T(8,128)(2,1)S(1)}, bf16[1024,256]{1,0:T(8,128)(2,1)}, u32[]{:S(2)}) copy-start(bf16[1024,256]{1,0:T(8,128)(2,1)} %copy-done.6) | copy-start | bytes 1572868
  76.5 45.8 %collective-permute-start.10 = (bf16[1024,128]{1,0:T(8,128)(2,1)}, bf16[1024,128]{1,0:T(8,128)(2,1)S(1)}, u32[]{:S(2)}, u32[]{:S(2)}) collective-permute-start(bf16[1024,128]{1,0:T(8,128)(2,1)} %copy-done.12), channel_id=1, source_target_pairs={{0,24},{4,28},{8,32},{12,36},{16,40},{20,44},{24,48},{28,52},{32,5... | collective-permute-start | bytes 786440 | tf_op jit(solution)/shard_map/ppermute | solution.py:32
  95.9 14.7 %collective-permute-start.9 = (bf16[1024,128]{1,0:T(8,128)(2,1)S(1)}, bf16[1024,128]{1,0:T(8,128)(2,1)S(1)}, u32[]{:S(2)}, u32[]{:S(2)}) collective-permute-start(bf16[1024,128]{1,0:T(8,128)(2,1)S(1)} %get-tuple-element.89), channel_id=1, source_target_pairs={{0,12},{4,8},{8,20},{12,16},{16,28},{20,24},{24,36},{28,32},{32,44... | collective-permute-start | bytes 786440 | tf_op jit(solution)/shard_map/ppermute | solution.py:32
  97.8 19.0 %collective-permute-start.8 = (bf16[1024,128]{1,0:T(8,128)(2,1)S(1)}, bf16[1024,128]{1,0:T(8,128)(2,1)S(1)}, u32[]{:S(2)}, u32[]{:S(2)}) collective-permute-start(bf16[1024,128]{1,0:T(8,128)(2,1)S(1)} %get-tuple-element.90), channel_id=1, source_target_pairs={{0,8},{4,12},{8,16},{12,20},{16,24},{20,28},{24,32},{28,36},{32,40... | collective-permute-start | bytes 786440 | tf_op jit(solution)/shard_map/ppermute | solution.py:32
  101.1 21.2 %collective-permute-start.11 = (bf16[1024,128]{1,0:T(8,128)(2,1)}, bf16[1024,128]{1,0:T(8,128)(2,1)S(1)}, u32[]{:S(2)}, u32[]{:S(2)}) collective-permute-start(bf16[1024,128]{1,0:T(8,128)(2,1)} %copy-done.13), channel_id=1, source_target_pairs={{0,28},{4,24},{8,36},{12,32},{16,44},{20,40},{24,52},{28,48},{32,6... | collective-permute-start | bytes 786440 | tf_op jit(solution)/shard_map/ppermute | solution.py:32
  109.8 12.6 %copy-start = (bf16[4,1024,256]{2,1,0:T(8,128)(2,1)S(1)}, bf16[4,1024,256]{2,1,0:T(8,128)(2,1)}, u32[]{:S(2)}) copy-start(bf16[4,1024,256]{2,1,0:T(8,128)(2,1)} %weights.3) | copy-start | bytes 6291460
  109.8 12.6 %copy-start.1 = (bf16[1024,256]{1,0:T(8,128)(2,1)S(1)}, bf16[1024,256]{1,0:T(8,128)(2,1)}, u32[]{:S(2)}) copy-start(bf16[1024,256]{1,0:T(8,128)(2,1)} %get-tuple-element.78.gate_grad) | copy-start | bytes 1572868
  123.9 8.9 %collective-permute-start.16 = (bf16[512,256]{1,0:T(8,128)(2,1)S(1)}, bf16[512,256]{1,0:T(8,128)(2,1)S(1)}, u32[]{:S(2)}, u32[]{:S(2)}) collective-permute-start(bf16[512,256]{1,0:T(8,128)(2,1)S(1)} %get-tuple-element.84), channel_id=1, source_target_pairs={{0,3},{1,0},{2,1},{3,2},{4,7},{5,4},{6,5},{7,6},{8,11},{9,8},{10,9... | collective-permute-start | bytes 786440 | tf_op jit(solution)/shard_map/ppermute | solution.py:370
  126.7 10.0 %collective-permute-start.14 = (bf16[512,256]{1,0:T(8,128)(2,1)S(1)}, bf16[512,256]{1,0:T(8,128)(2,1)S(1)}, u32[]{:S(2)}, u32[]{:S(2)}) collective-permute-start(bf16[512,256]{1,0:T(8,128)(2,1)S(1)} %get-tuple-element.82), channel_id=1, source_target_pairs={{0,1},{1,2},{2,3},{3,0},{4,5},{5,6},{6,7},{7,4},{8,9},{9,10},{10,1... | collective-permute-start | bytes 786440 | tf_op jit(solution)/shard_map/ppermute | solution.py:370
  132.9 14.6 %collective-permute-start.17 = (bf16[1024,256]{1,0:T(8,128)(2,1)S(1)}, bf16[1024,256]{1,0:T(8,128)(2,1)S(1)}, u32[]{:S(2)}, u32[]{:S(2)}) collective-permute-start(bf16[1024,256]{1,0:T(8,128)(2,1)S(1)} %pad_maximum_fusion.7), channel_id=1, source_target_pairs={{0,3},{1,0},{2,1},{3,2},{4,7},{5,4},{6,5},{7,6},{8,11},{9,8},{10,9... | collective-permute-start | bytes 1572872 | tf_op jit(solution)/shard_map/ppermute | solution.py:370
  136.8 14.3 %collective-permute-start.15 = (bf16[1024,256]{1,0:T(8,128)(2,1)S(1)}, bf16[1024,256]{1,0:T(8,128)(2,1)S(1)}, u32[]{:S(2)}, u32[]{:S(2)}) collective-permute-start(bf16[1024,256]{1,0:T(8,128)(2,1)S(1)} %pad_maximum_fusion.6), channel_id=1, source_target_pairs={{0,1},{1,2},{2,3},{3,0},{4,5},{5,6},{6,7},{7,4},{8,9},{9,10},{10,1... | collective-permute-start | bytes 1572872 | tf_op jit(solution)/shard_map/ppermute | solution.py:370

commit v7 on v5

--- a/solution.py
+++ b/solution.py
@@ -71,7 +71,7 @@
 
 
 def by_rows(kernel, outputs, core, *arrays):
-    rows = 256
+    rows = 512
     wide = pl.BlockSpec((rows, 2 * HEAD_DIM), lambda i, c: (i, 0))
     return pl.pallas_call(
         kernel,
@@ -352,16 +352,18 @@
     dq1b, *dkv1b = pairs(
         "pairs_one", core_at, [next_a, next_b], [USERS_ONLY, LATE], key, BF16, late, area // 2
     )
+    query_far, dq1b = lax.optimization_barrier((query_far, dq1b))
+    dq3_same, dq3_cross, *dkv3 = pairs(
+        "pairs_three", core_at, [query_far], [WHOLE], key, BF16, every, area // 8
+    )
+    far_same, far_cross = give(dq3_same, dq3_cross, lambda i: i + 6)
     same, cross = in_order(dq1a, dq1b)
     same, cross = total(same, dq2_same).astype(BF16), total(cross, dq2_cross).astype(BF16)
     back_same, back_cross = give(same, cross, lambda i: i + 2)
-    query_far, dq1b = lax.optimization_barrier((query_far, dq1b))
-    dq3_same, dq3_cross, *dkv3 = pairs(
-        "pairs_three", core_at, [query_far], [WHOLE], key, BF16, every, area // 8
-    )
-    far_same, far_cross = give(dq3_same, dq3_cross, lambda i: i + 6)
-    mine, other = (total(*terms) for terms in zip(dkv0, dkv1a, dkv1b, dkv3))
-    other = swap(jnp.concatenate([dq0_other, other], axis=1).astype(BF16))
+    mine = total(dkv0[0], dkv1a[0], dkv1b[0], dkv3[0])
+    other = total(dkv0[1], dkv1a[1], dkv1b[1], dkv3[1])
+    other = jnp.concatenate([dq0_other, other], axis=1).astype(BF16)
+    other = swap(other)
     place = jnp.stack([core, head]).astype(jnp.int32)
     left, low, high = collect(
         place, dq0, mine, other, back_same, back_cross, far_same, far_cross, key_same, key_cross,

time: 152 us -> 134 us (0.88)
  the two profiles are of different devices: /device:TPU:16 before, /device:TPU:80 now
where the time goes in v7:
time: 134 us; the launch traced here: 133 us
  starting transfers between devices  52 us (39%)
  waiting for transfers between devices  38.6 us (29%)
  Pallas kernels  32.9 us (25%)
  other arithmetic  6.06 us (5%)
  local copies, waits for them, and re-layouts  3.11 us (2%)
    ppermute x10, starting transfers between devices, move(): return lax.ppermute(block, 'seq', route)  44.6 us
    pallas_call x5, Pallas kernels, pairs(): pl.pallas_call(lambda *refs: pairs_kernel(name == 'pairs_own', parts, til...  25.4 us
    ppermute x10, waiting for transfers between devices, move(): return lax.ppermute(block, 'seq', route)  20.4 us
    ppermute x4, waiting for transfers between devices, turn(): return lax.ppermute(block, 'head', [(i, (i + by) % 4) for i in range(4)])  18.2 us
    ppermute x4, starting transfers between devices, turn(): return lax.ppermute(block, 'head', [(i, (i + by) % 4) for i in range(4)])  6.67 us
    pallas_call x1, Pallas kernels, by_rows(): pl.pallas_call(kernel, grid_spec=pltpu.PrefetchScalarGridSpec(num_scalar_...  3.53 us
    unnamed x32, local copies, waits for them, and re-layouts  3.03 us
  transfers between devices with their start and end apart: 18, of which 9 were waited for; matrix products, arithmetic and copies ran while one was open for 3% of the time, Pallas kernels for 24%

profile of v7, /device:TPU:80, one launch (start us, length us, event | category | flops | bytes accessed | tf_op | source)
XLA Modules:
  0.0 133.2 jit_solution(8102931249495194877)
XLA Ops:
  0.0 1.3 broadcast_select_fusion.6
  1.3 0.1 pad_maximum_fusion.5
  1.3 0.1 collective-permute-start.1
  1.5 0.5 collective-permute-start.2
  1.9 3.5 %shard_map.82 = (bf16[1024,256]{1,0:T(8,128)(2,1)}, bf16[1024,256]{1,0:T(8,128)(2,1)}, bf16[1024,256]{1,0:T(8,128)(2,1)}) custom-call(s32[1]{0:T(128)} %bitcast.core.refs_0_, bf16[1024,256]{1,0:T(8,128)(2,1)} %q.1, bf16[1024,256]{1,0:T(8,128)(2,1)} %o.1, bf16[1024,256]{1,0:T(8,128)(2,1)} %gate.1, bf16[1024,256]{1,0:T(8,128)(2,1)} %grad.1), custom_call_target="tpu_custom_call" | custom-call | flops 7864320 | bytes 4194304 | tf_op jit(solution)/shard_map/pallas_call | solution.py:76
  5.5 0.1 collective-permute-start
  5.6 0.0 collective-permute-done.2
  5.6 0.0 collective-permute-done.1
  5.6 0.2 broadcast_select_fusion.3
  5.9 0.0 copy-start.14
  5.9 0.1 pad_maximum_fusion.refs_2_.refs_3_
  6.0 3.7 %collective-permute-start.5 = (bf16[2064,256]{1,0:T(8,128)(2,1)S(1)}, bf16[2064,256]{1,0:T(8,128)(2,1)S(1)}, u32[]{:S(2)}, u32[]{:S(2)}) collective-permute-start(bf16[2064,256]{1,0:T(8,128)(2,1)S(1)} %pad_maximum_fusion.refs_2_.refs_3_), channel_id=1, source_target_pairs={{0,8},{4,12},{8,16},{12,20},{16,24},{20,28},{24,32},{28,36},{32,40... | collective-permute-start | bytes 3170312 | tf_op jit(solution)/shard_map/ppermute | solution.py:32
  9.6 0.1 broadcast_select_fusion
  9.8 2.3 %collective-permute-start.3 = (bf16[1040,256]{1,0:T(8,128)(2,1)S(1)}, bf16[1040,256]{1,0:T(8,128)(2,1)S(1)}, u32[]{:S(2)}, u32[]{:S(2)}) collective-permute-start(bf16[1040,256]{1,0:T(8,128)(2,1)S(1)} %pad_maximum_fusion.3), channel_id=1, source_target_pairs={{8,0},{12,4},{16,8},{20,12},{24,16},{28,20},{32,24},{36,28},{40,32... | collective-permute-start | bytes 1597448 | tf_op jit(solution)/shard_map/ppermute | solution.py:32
  12.1 0.1 pad_maximum_fusion.1.refs_1_
  12.2 2.0 %collective-permute-start.4 = (bf16[1024,256]{1,0:T(8,128)(2,1)S(1)}, bf16[1024,256]{1,0:T(8,128)(2,1)S(1)}, u32[]{:S(2)}, u32[]{:S(2)}) collective-permute-start(bf16[1024,256]{1,0:T(8,128)(2,1)S(1)} %get-tuple-element.87), channel_id=1, source_target_pairs={{8,0},{12,4},{16,8},{20,12},{24,16},{28,20},{32,24},{36,28},{40,32... | collective-permute-start | bytes 1572872 | tf_op jit(solution)/shard_map/ppermute | solution.py:32
  14.2 11.5 %shard_map.83 = (f32[1024,128]{1,0:T(8,128)S(1)}, f32[1024,128]{1,0:T(8,128)S(1)}, f32[1024,256]{1,0:T(8,128)S(1)}, f32[1024,256]{1,0:T(8,128)S(1)}) custom-call(s32[1]{0:T(128)} %bitcast.core.refs_0_, bf16[2064,256]{1,0:T(8,128)(2,1)S(1)} %pad_maximum_fusion.1.refs_1_, bf16[2064,256]{1,0:T(8,128)(2,1)S(1)} %pad_maximum_fusion.refs_2_.refs_3_), custom_call_target="tpu_custom_call" | custom-call | flops 5368709120 | bytes 4194304 | tf_op jit(solution)/shard_map/pallas_call | solution.py:206
  25.7 0.9 collective-permute-done.3.refs_1_
  26.6 5.2 %shard_map.84 = (bf16[1024,128]{1,0:T(8,128)(2,1)S(1)}, bf16[1024,256]{1,0:T(8,128)(2,1)S(1)}, bf16[1024,256]{1,0:T(8,128)(2,1)S(1)}) custom-call(s32[1]{0:T(128)} %bitcast.core.refs_0_, bf16[1040,256]{1,0:T(8,128)(2,1)S(1)} %collective-permute-done.3.refs_1_, bf16[2064,256]{1,0:T(8,128)(2,1)S(1)} %pad_maximum_fusion.refs_2_.refs_3_), custom_call_target="tpu_custom_call" | custom-call | flops 5368709120 | bytes 4194304 | tf_op jit(solution)/shard_map/pallas_call | solution.py:206
  31.9 0.8 copy-done.2
  32.7 0.7 copy-done.8
  33.4 3.6 %collective-permute-done.4.refs_2_ = bf16[1024,256]{1,0:T(8,128)(2,1)S(1)} collective-permute-done((bf16[1024,256]{1,0:T(8,128)(2,1)S(1)}, bf16[1024,256]{1,0:T(8,128)(2,1)S(1)}, u32[]{:S(2)}, u32[]{:S(2)}) %collective-permute-start.4) | collective-permute-done | bytes 524320 | tf_op jit(solution)/shard_map/ppermute | solution.py:32
  37.0 0.0 collective-permute-done.5.refs_3_
  37.0 4.2 %collective-permute-start.6 = (bf16[2064,256]{1,0:T(8,128)(2,1)S(1)}, bf16[2064,256]{1,0:T(8,128)(2,1)S(1)}, u32[]{:S(2)}, u32[]{:S(2)}) collective-permute-start(bf16[2064,256]{1,0:T(8,128)(2,1)S(1)} %pad_maximum_fusion.1.refs_1_), channel_id=1, source_target_pairs={{24,0},{28,4},{32,8},{36,12},{40,16},{44,20},{48,24},{52,28},{56,3... | collective-permute-start | bytes 3170312 | tf_op jit(solution)/shard_map/ppermute | solution.py:32
  41.3 6.5 %shard_map.85 = (bf16[1024,128]{1,0:T(8,128)(2,1)S(1)}, bf16[1024,128]{1,0:T(8,128)(2,1)S(1)}, bf16[1024,256]{1,0:T(8,128)(2,1)}, bf16[1024,256]{1,0:T(8,128)(2,1)}) custom-call(s32[1]{0:T(128)} %bitcast.core.refs_0_, bf16[1040,256]{1,0:T(8,128)(2,1)S(1)} %collective-permute-done.3.refs_1_, bf16[1024,256]{1,0:T(8,128)(2,1)S(1)} %collective-permute-done.4.refs_2_, ...), custom_call_target="tpu_custom_call" | custom-call | flops 5368709120 | bytes 4194304 | tf_op jit(solution)/shard_map/pallas_call | solution.py:206
  47.8 12.4 %collective-permute-start.12 = (bf16[1024,256]{1,0:T(8,128)(2,1)}, bf16[1024,256]{1,0:T(8,128)(2,1)S(1)}, u32[]{:S(2)}, u32[]{:S(2)}) collective-permute-start(bf16[1024,256]{1,0:T(8,128)(2,1)} %get-tuple-element.78), channel_id=1, source_target_pairs={{8,0},{12,4},{16,8},{20,12},{24,16},{28,20},{32,24},{36,28},{40,32... | collective-permute-start | bytes 1572872 | tf_op jit(solution)/shard_map/ppermute | solution.py:32
  60.2 1.9 %collective-permute-start.13 = (bf16[1024,256]{1,0:T(8,128)(2,1)}, bf16[1024,256]{1,0:T(8,128)(2,1)S(1)}, u32[]{:S(2)}, u32[]{:S(2)}) collective-permute-start(bf16[1024,256]{1,0:T(8,128)(2,1)} %get-tuple-element.79), channel_id=1, source_target_pairs={{8,4},{12,0},{16,12},{20,8},{24,20},{28,16},{32,28},{36,24},{40,36... | collective-permute-start | bytes 1572872 | tf_op jit(solution)/shard_map/ppermute | solution.py:32
  62.2 1.0 shard_map.86
  63.2 0.8 copy-done.4
  64.1 0.3 collective-permute-done.6.refs_1_
  64.3 1.1 shard_map.87
  65.5 0.0 copy-start.6
  65.5 0.3 add_convert_fusion.1
  65.8 0.5 copy-done.6
  66.3 0.1 copy-done.12
  66.3 0.1 copy-done.13
  66.5 1.0 pad_maximum_fusion.2
  67.4 0.0 collective-permute-start.7
  67.5 0.1 pad_add_fusion.place
  67.5 1.5 %add_convert_fusion.4 = (bf16[1024,128]{1,0:T(8,128)(2,1)S(1)}, bf16[1024,128]{1,0:T(8,128)(2,1)S(1)}) fusion(bf16[1024,128]{1,0:T(8,128)(2,1)} %copy-done.10, bf16[1024,128]{1,0:T(8,128)(2,1)} %copy-done.11, bf16[1024,128]{1,0:T(8,128)(2,1)} %copy-done.8, pred[]{:T(512)S(6)} %eq.5, bf16[1024,128]{1,0:T(8,128)(2,1)} %copy-done.9), kind=kLoop, calls=%fused_computation.15 | loop fusion | flops 1310720 | bytes 1572865 | tf_op jit(solution)/shard_map/convert_element_type | solution.py:361
  69.0 4.7 %collective-permute-start.9 = (bf16[1024,128]{1,0:T(8,128)(2,1)S(1)}, bf16[1024,128]{1,0:T(8,128)(2,1)S(1)}, u32[]{:S(2)}, u32[]{:S(2)}) collective-permute-start(bf16[1024,128]{1,0:T(8,128)(2,1)S(1)} %get-tuple-element.91), channel_id=1, source_target_pairs={{0,12},{4,8},{8,20},{12,16},{16,28},{20,24},{24,36},{28,32},{32,44... | collective-permute-start | bytes 786440 | tf_op jit(solution)/shard_map/ppermute | solution.py:32
  73.7 4.6 %collective-permute-start.8 = (bf16[1024,128]{1,0:T(8,128)(2,1)S(1)}, bf16[1024,128]{1,0:T(8,128)(2,1)S(1)}, u32[]{:S(2)}, u32[]{:S(2)}) collective-permute-start(bf16[1024,128]{1,0:T(8,128)(2,1)S(1)} %get-tuple-element.92), channel_id=1, source_target_pairs={{0,8},{4,12},{8,16},{12,20},{16,24},{20,28},{24,32},{28,36},{32,40... | collective-permute-start | bytes 786440 | tf_op jit(solution)/shard_map/ppermute | solution.py:32
  78.3 0.0 collective-permute-done.12.key_same
  78.3 5.1 %collective-permute-start.10 = (bf16[1024,128]{1,0:T(8,128)(2,1)}, bf16[1024,128]{1,0:T(8,128)(2,1)S(1)}, u32[]{:S(2)}, u32[]{:S(2)}) collective-permute-start(bf16[1024,128]{1,0:T(8,128)(2,1)} %copy-done.13), channel_id=1, source_target_pairs={{0,24},{4,28},{8,32},{12,36},{16,40},{20,44},{24,48},{28,52},{32,5... | collective-permute-start | bytes 786440 | tf_op jit(solution)/shard_map/ppermute | solution.py:32
  83.4 0.0 collective-permute-done.13.key_cross
  83.5 3.7 %collective-permute-start.11 = (bf16[1024,128]{1,0:T(8,128)(2,1)}, bf16[1024,128]{1,0:T(8,128)(2,1)S(1)}, u32[]{:S(2)}, u32[]{:S(2)}) collective-permute-start(bf16[1024,128]{1,0:T(8,128)(2,1)} %copy-done.12), channel_id=1, source_target_pairs={{0,28},{4,24},{8,36},{12,32},{16,44},{20,40},{24,52},{28,48},{32,6... | collective-permute-start | bytes 786440 | tf_op jit(solution)/shard_map/ppermute | solution.py:32
  87.2 0.0 copy-start
  87.2 0.2 convert_add_fusion.dkv
  87.5 0.0 collective-permute-done.9.back_cross
  87.5 3.6 %collective-permute-done.8.back_same = bf16[1024,128]{1,0:T(8,128)(2,1)S(1)} collective-permute-done((bf16[1024,128]{1,0:T(8,128)(2,1)S(1)}, bf16[1024,128]{1,0:T(8,128)(2,1)S(1)}, u32[]{:S(2)}, u32[]{:S(2)}) %collective-permute-start.8) | collective-permute-done | bytes 262176 | tf_op jit(solution)/shard_map/ppermute | solution.py:32
  91.1 7.8 %collective-permute-done.10.far_same = bf16[1024,128]{1,0:T(8,128)(2,1)S(1)} collective-permute-done((bf16[1024,128]{1,0:T(8,128)(2,1)}, bf16[1024,128]{1,0:T(8,128)(2,1)S(1)}, u32[]{:S(2)}, u32[]{:S(2)}) %collective-permute-start.10) | collective-permute-done | bytes 262176 | tf_op jit(solution)/shard_map/ppermute | solution.py:32
  98.8 4.3 %collective-permute-done.11.far_cross = bf16[1024,128]{1,0:T(8,128)(2,1)S(1)} collective-permute-done((bf16[1024,128]{1,0:T(8,128)(2,1)}, bf16[1024,128]{1,0:T(8,128)(2,1)S(1)}, u32[]{:S(2)}, u32[]{:S(2)}) %collective-permute-start.11) | collective-permute-done | bytes 262176 | tf_op jit(solution)/shard_map/ppermute | solution.py:32
  103.1 0.0 collective-permute-done.7.other
  103.1 1.5 %collect.1 = (bf16[1024,1024]{1,0:T(8,128)(2,1)S(1)}, bf16[512,256]{1,0:T(8,128)(2,1)S(1)}, bf16[512,256]{1,0:T(8,128)(2,1)S(1)}) custom-call(s32[2]{0:T(128)S(1)} %pad_add_fusion.place, f32[1024,128]{1,0:T(8,128)S(1)} %get-tuple-element.52.dq, f32[1024,256]{1,0:T(8,128)S(1)} %convert_add_fusion.dkv, bf16[1024,384]{1,0:T(8,128)(2,1)S(1)} %collective-permute-done.7.other, ...), custom_call_target="tpu_custom_call" | custom-call | flops 536870912 | bytes 8388608 | tf_op jit(solution)/shard_map/collect/pallas_call | solution.py:277
  104.6 2.8 %collective-permute-start.16 = (bf16[512,256]{1,0:T(8,128)(2,1)S(1)}, bf16[512,256]{1,0:T(8,128)(2,1)S(1)}, u32[]{:S(2)}, u32[]{:S(2)}) collective-permute-start(bf16[512,256]{1,0:T(8,128)(2,1)S(1)} %get-tuple-element.86), channel_id=1, source_target_pairs={{0,3},{1,0},{2,1},{3,2},{4,7},{5,4},{6,5},{7,6},{8,11},{9,8},{10,9... | collective-permute-start | bytes 786440 | tf_op jit(solution)/shard_map/ppermute | solution.py:374
  107.5 2.4 %project.1 = (f32[1024,256]{1,0:T(8,128)S(1)}, f32[1024,256]{1,0:T(8,128)S(1)}, f32[1024,256]{1,0:T(8,128)S(1)}) custom-call(s32[2]{0:T(128)S(1)} %pad_add_fusion.place, bf16[1024,1024]{1,0:T(8,128)(2,1)S(1)} %get-tuple-element.81.left, bf16[4,1024,256]{2,1,0:T(8,128)(2,1)S(1)} %copy-done), custom_call_target="tpu_custom_call" | custom-call | flops 1610612736 | bytes 8388608 | tf_op jit(solution)/shard_map/project/pallas_call | solution.py:289
  109.9 3.8 %collective-permute-done.16 = bf16[512,256]{1,0:T(8,128)(2,1)S(1)} collective-permute-done((bf16[512,256]{1,0:T(8,128)(2,1)S(1)}, bf16[512,256]{1,0:T(8,128)(2,1)S(1)}, u32[]{:S(2)}, u32[]{:S(2)}) %collective-permute-start.16) | collective-permute-done | bytes 262176 | tf_op jit(solution)/shard_map/ppermute | solution.py:374
  113.7 0.1 add_convert_fusion.2
  113.8 3.8 %collective-permute-start.17 = (bf16[1024,256]{1,0:T(8,128)(2,1)S(1)}, bf16[1024,256]{1,0:T(8,128)(2,1)S(1)}, u32[]{:S(2)}, u32[]{:S(2)}) collective-permute-start(bf16[1024,256]{1,0:T(8,128)(2,1)S(1)} %pad_maximum_fusion.7), channel_id=1, source_target_pairs={{0,3},{1,0},{2,1},{3,2},{4,7},{5,4},{6,5},{7,6},{8,11},{9,8},{10,9... | collective-permute-start | bytes 1572872 | tf_op jit(solution)/shard_map/ppermute | solution.py:374
  117.6 0.1 add_convert_fusion.3
  117.7 0.1 collective-permute-start.15
  117.8 10.8 %collective-permute-done.17 = bf16[1024,256]{1,0:T(8,128)(2,1)S(1)} collective-permute-done((bf16[1024,256]{1,0:T(8,128)(2,1)S(1)}, bf16[1024,256]{1,0:T(8,128)(2,1)S(1)}, u32[]{:S(2)}, u32[]{:S(2)}) %collective-permute-start.17) | collective-permute-done | bytes 524320 | tf_op jit(solution)/shard_map/ppermute | solution.py:374
  128.6 3.6 %collective-permute-done.15 = bf16[1024,256]{1,0:T(8,128)(2,1)S(1)} collective-permute-done((bf16[1024,256]{1,0:T(8,128)(2,1)S(1)}, bf16[1024,256]{1,0:T(8,128)(2,1)S(1)}, u32[]{:S(2)}, u32[]{:S(2)}) %collective-permute-start.15) | collective-permute-done | bytes 524320 | tf_op jit(solution)/shard_map/ppermute | solution.py:374
  132.2 0.9 add_convert_fusion
  (37 shorter events, 0.3 us)
Async XLA Ops:
  0.0 1.4 %copy-start.15 = (s32[1024]{0:T(1024)S(1)}, s32[1024]{0:T(1024)}, u32[]{:S(2)}) copy-start(s32[1024]{0:T(1024)} %param.14) | copy-start | bytes 12292
  1.3 4.3 %collective-permute-start.1 = (bf16[1024,256]{1,0:T(8,128)(2,1)S(1)}, bf16[1024,256]{1,0:T(8,128)(2,1)S(1)}, u32[]{:S(2)}, u32[]{:S(2)}) collective-permute-start(bf16[1024,256]{1,0:T(8,128)(2,1)S(1)} %pad_maximum_fusion.5), channel_id=1, source_target_pairs={{0,4},{4,0},{8,12},{12,8},{16,20},{20,16},{24,28},{28,24},{32,36},... | collective-permute-start | bytes 1572872 | tf_op jit(solution)/shard_map/ppermute | solution.py:40
  1.5 4.1 %collective-permute-start.2 = (bf16[1024]{0:T(1024)(128)(2,1)S(1)}, bf16[1024]{0:T(1024)(128)(2,1)S(1)}, u32[]{:S(2)}, u32[]{:S(2)}) collective-permute-start(bf16[1024]{0:T(1024)(128)(2,1)S(1)} %add_convert_fusion.6), channel_id=1, source_target_pairs={{0,4},{4,0},{8,12},{12,8},{16,20},{20,16},{24,28},{28,24},{32,36},... | collective-permute-start | bytes 6152 | tf_op jit(solution)/shard_map/ppermute | solution.py:40
  5.5 4.2 %collective-permute-start = (bf16[1024,256]{1,0:T(8,128)(2,1)}, bf16[1024,256]{1,0:T(8,128)(2,1)S(1)}, u32[]{:S(2)}, u32[]{:S(2)}) collective-permute-start(bf16[1024,256]{1,0:T(8,128)(2,1)} %get-tuple-element.47), channel_id=1, source_target_pairs={{0,4},{4,0},{8,12},{12,8},{16,20},{20,16},{24,28},{28,24},{32,36},... | collective-permute-start | bytes 1572872 | tf_op jit(solution)/shard_map/ppermute | solution.py:40
  5.9 3.8 %copy-start.14 = (bf16[1024,256]{1,0:T(8,128)(2,1)S(1)}, bf16[1024,256]{1,0:T(8,128)(2,1)}, u32[]{:S(2)}) copy-start(bf16[1024,256]{1,0:T(8,128)(2,1)} %get-tuple-element.46) | copy-start | bytes 1572868
  6.0 31.1 %collective-permute-start.5 = (bf16[2064,256]{1,0:T(8,128)(2,1)S(1)}, bf16[2064,256]{1,0:T(8,128)(2,1)S(1)}, u32[]{:S(2)}, u32[]{:S(2)}) collective-permute-start(bf16[2064,256]{1,0:T(8,128)(2,1)S(1)} %pad_maximum_fusion.refs_2_.refs_3_), channel_id=1, source_target_pairs={{0,8},{4,12},{8,16},{12,20},{16,24},{20,28},{24,32},{28,36},{32,40... | collective-permute-start | bytes 3170312 | tf_op jit(solution)/shard_map/ppermute | solution.py:32
  9.8 16.9 %collective-permute-start.3 = (bf16[1040,256]{1,0:T(8,128)(2,1)S(1)}, bf16[1040,256]{1,0:T(8,128)(2,1)S(1)}, u32[]{:S(2)}, u32[]{:S(2)}) collective-permute-start(bf16[1040,256]{1,0:T(8,128)(2,1)S(1)} %pad_maximum_fusion.3), channel_id=1, source_target_pairs={{8,0},{12,4},{16,8},{20,12},{24,16},{28,20},{32,24},{36,28},{40,32... | collective-permute-start | bytes 1597448 | tf_op jit(solution)/shard_map/ppermute | solution.py:32
  12.2 24.9 %collective-permute-start.4 = (bf16[1024,256]{1,0:T(8,128)(2,1)S(1)}, bf16[1024,256]{1,0:T(8,128)(2,1)S(1)}, u32[]{:S(2)}, u32[]{:S(2)}) collective-permute-start(bf16[1024,256]{1,0:T(8,128)(2,1)S(1)} %get-tuple-element.87), channel_id=1, source_target_pairs={{8,0},{12,4},{16,8},{20,12},{24,16},{28,20},{32,24},{36,28},{40,32... | collective-permute-start | bytes 1572872 | tf_op jit(solution)/shard_map/ppermute | solution.py:32
  31.9 0.8 copy-start.2
  32.7 0.7 copy-start.8
  37.0 27.3 %collective-permute-start.6 = (bf16[2064,256]{1,0:T(8,128)(2,1)S(1)}, bf16[2064,256]{1,0:T(8,128)(2,1)S(1)}, u32[]{:S(2)}, u32[]{:S(2)}) collective-permute-start(bf16[2064,256]{1,0:T(8,128)(2,1)S(1)} %pad_maximum_fusion.1.refs_1_), channel_id=1, source_target_pairs={{24,0},{28,4},{32,8},{36,12},{40,16},{44,20},{48,24},{52,28},{56,3... | collective-permute-start | bytes 3170312 | tf_op jit(solution)/shard_map/ppermute | solution.py:32
  47.8 15.4 %copy-start.9 = (bf16[1024,128]{1,0:T(8,128)(2,1)}, bf16[1024,128]{1,0:T(8,128)(2,1)S(1)}, u32[]{:S(2)}) copy-start(bf16[1024,128]{1,0:T(8,128)(2,1)S(1)} %get-tuple-element.74) | copy-start | bytes 786436
  47.8 15.4 %copy-start.10 = (bf16[1024,128]{1,0:T(8,128)(2,1)}, bf16[1024,128]{1,0:T(8,128)(2,1)S(1)}, u32[]{:S(2)}) copy-start(bf16[1024,128]{1,0:T(8,128)(2,1)S(1)} %get-tuple-element.75) | copy-start | bytes 786436
  47.8 30.5 %collective-permute-start.12 = (bf16[1024,256]{1,0:T(8,128)(2,1)}, bf16[1024,256]{1,0:T(8,128)(2,1)S(1)}, u32[]{:S(2)}, u32[]{:S(2)}) collective-permute-start(bf16[1024,256]{1,0:T(8,128)(2,1)} %get-tuple-element.78), channel_id=1, source_target_pairs={{8,0},{12,4},{16,8},{20,12},{24,16},{28,20},{32,24},{36,28},{40,32... | collective-permute-start | bytes 1572872 | tf_op jit(solution)/shard_map/ppermute | solution.py:32
  60.2 23.2 %collective-permute-start.13 = (bf16[1024,256]{1,0:T(8,128)(2,1)}, bf16[1024,256]{1,0:T(8,128)(2,1)S(1)}, u32[]{:S(2)}, u32[]{:S(2)}) collective-permute-start(bf16[1024,256]{1,0:T(8,128)(2,1)} %get-tuple-element.79), channel_id=1, source_target_pairs={{8,4},{12,0},{16,12},{20,8},{24,20},{28,16},{32,28},{36,24},{40,36... | collective-permute-start | bytes 1572872 | tf_op jit(solution)/shard_map/ppermute | solution.py:32
  63.2 0.8 copy-start.4
  64.0 1.4 %copy-start.11 = (bf16[1024,128]{1,0:T(8,128)(2,1)}, bf16[1024,128]{1,0:T(8,128)(2,1)S(1)}, u32[]{:S(2)}) copy-start(bf16[1024,128]{1,0:T(8,128)(2,1)S(1)} %get-tuple-element.73) | copy-start | bytes 786436
  65.5 0.8 copy-start.6
  65.5 0.9 copy-start.12
  65.5 1.0 copy-start.13
  67.4 35.6 %collective-permute-start.7 = (bf16[1024,384]{1,0:T(8,128)(2,1)}, bf16[1024,384]{1,0:T(8,128)(2,1)S(1)}, u32[]{:S(2)}, u32[]{:S(2)}) collective-permute-start(bf16[1024,384]{1,0:T(8,128)(2,1)} %pad_maximum_fusion.2), channel_id=1, source_target_pairs={{0,4},{4,0},{8,12},{12,8},{16,20},{20,16},{24,28},{28,24},{32,36},... | collective-permute-start | bytes 2359304 | tf_op jit(solution)/shard_map/ppermute | solution.py:40
  67.5 19.7 %copy-start.3 = (bf16[1024,256]{1,0:T(8,128)(2,1)S(1)}, bf16[1024,256]{1,0:T(8,128)(2,1)}, u32[]{:S(2)}) copy-start(bf16[1024,256]{1,0:T(8,128)(2,1)} %copy-done.2) | copy-start | bytes 1572868
  67.5 19.7 %copy-start.5 = (bf16[1024,256]{1,0:T(8,128)(2,1)S(1)}, bf16[1024,256]{1,0:T(8,128)(2,1)}, u32[]{:S(2)}) copy-start(bf16[1024,256]{1,0:T(8,128)(2,1)} %copy-done.4) | copy-start | bytes 1572868
  67.5 19.8 %copy-start.7 = (bf16[1024,256]{1,0:T(8,128)(2,1)S(1)}, bf16[1024,256]{1,0:T(8,128)(2,1)}, u32[]{:S(2)}) copy-start(bf16[1024,256]{1,0:T(8,128)(2,1)} %copy-done.6) | copy-start | bytes 1572868
  69.0 18.5 %collective-permute-start.9 = (bf16[1024,128]{1,0:T(8,128)(2,1)S(1)}, bf16[1024,128]{1,0:T(8,128)(2,1)S(1)}, u32[]{:S(2)}, u32[]{:S(2)}) collective-permute-start(bf16[1024,128]{1,0:T(8,128)(2,1)S(1)} %get-tuple-element.91), channel_id=1, source_target_pairs={{0,12},{4,8},{8,20},{12,16},{16,28},{20,24},{24,36},{28,32},{32,44... | collective-permute-start | bytes 786440 | tf_op jit(solution)/shard_map/ppermute | solution.py:32
  73.7 17.4 %collective-permute-start.8 = (bf16[1024,128]{1,0:T(8,128)(2,1)S(1)}, bf16[1024,128]{1,0:T(8,128)(2,1)S(1)}, u32[]{:S(2)}, u32[]{:S(2)}) collective-permute-start(bf16[1024,128]{1,0:T(8,128)(2,1)S(1)} %get-tuple-element.92), channel_id=1, source_target_pairs={{0,8},{4,12},{8,16},{12,20},{16,24},{20,28},{24,32},{28,36},{32,40... | collective-permute-start | bytes 786440 | tf_op jit(solution)/shard_map/ppermute | solution.py:32
  78.3 20.5 %collective-permute-start.10 = (bf16[1024,128]{1,0:T(8,128)(2,1)}, bf16[1024,128]{1,0:T(8,128)(2,1)S(1)}, u32[]{:S(2)}, u32[]{:S(2)}) collective-permute-start(bf16[1024,128]{1,0:T(8,128)(2,1)} %copy-done.13), channel_id=1, source_target_pairs={{0,24},{4,28},{8,32},{12,36},{16,40},{20,44},{24,48},{28,52},{32,5... | collective-permute-start | bytes 786440 | tf_op jit(solution)/shard_map/ppermute | solution.py:32
  83.5 19.6 %collective-permute-start.11 = (bf16[1024,128]{1,0:T(8,128)(2,1)}, bf16[1024,128]{1,0:T(8,128)(2,1)S(1)}, u32[]{:S(2)}, u32[]{:S(2)}) collective-permute-start(bf16[1024,128]{1,0:T(8,128)(2,1)} %copy-done.12), channel_id=1, source_target_pairs={{0,28},{4,24},{8,36},{12,32},{16,44},{20,40},{24,52},{28,48},{32,6... | collective-permute-start | bytes 786440 | tf_op jit(solution)/shard_map/ppermute | solution.py:32
  87.2 15.9 %copy-start = (bf16[4,1024,256]{2,1,0:T(8,128)(2,1)S(1)}, bf16[4,1024,256]{2,1,0:T(8,128)(2,1)}, u32[]{:S(2)}) copy-start(bf16[4,1024,256]{2,1,0:T(8,128)(2,1)} %weights.3) | copy-start | bytes 6291460
  87.2 15.9 %copy-start.1 = (bf16[1024,256]{1,0:T(8,128)(2,1)S(1)}, bf16[1024,256]{1,0:T(8,128)(2,1)}, u32[]{:S(2)}) copy-start(bf16[1024,256]{1,0:T(8,128)(2,1)} %get-tuple-element.80.gate_grad) | copy-start | bytes 1572868
  104.6 9.1 %collective-permute-start.16 = (bf16[512,256]{1,0:T(8,128)(2,1)S(1)}, bf16[512,256]{1,0:T(8,128)(2,1)S(1)}, u32[]{:S(2)}, u32[]{:S(2)}) collective-permute-start(bf16[512,256]{1,0:T(8,128)(2,1)S(1)} %get-tuple-element.86), channel_id=1, source_target_pairs={{0,3},{1,0},{2,1},{3,2},{4,7},{5,4},{6,5},{7,6},{8,11},{9,8},{10,9... | collective-permute-start | bytes 786440 | tf_op jit(solution)/shard_map/ppermute | solution.py:374
  107.5 10.1 %collective-permute-start.14 = (bf16[512,256]{1,0:T(8,128)(2,1)S(1)}, bf16[512,256]{1,0:T(8,128)(2,1)S(1)}, u32[]{:S(2)}, u32[]{:S(2)}) collective-permute-start(bf16[512,256]{1,0:T(8,128)(2,1)S(1)} %get-tuple-element.84), channel_id=1, source_target_pairs={{0,1},{1,2},{2,3},{3,0},{4,5},{5,6},{6,7},{7,4},{8,9},{9,10},{10,1... | collective-permute-start | bytes 786440 | tf_op jit(solution)/shard_map/ppermute | solution.py:374
  113.8 14.8 %collective-permute-start.17 = (bf16[1024,256]{1,0:T(8,128)(2,1)S(1)}, bf16[1024,256]{1,0:T(8,128)(2,1)S(1)}, u32[]{:S(2)}, u32[]{:S(2)}) collective-permute-start(bf16[1024,256]{1,0:T(8,128)(2,1)S(1)} %pad_maximum_fusion.7), channel_id=1, source_target_pairs={{0,3},{1,0},{2,1},{3,2},{4,7},{5,4},{6,5},{7,6},{8,11},{9,8},{10,9... | collective-permute-start | bytes 1572872 | tf_op jit(solution)/shard_map/ppermute | solution.py:374
  117.7 14.5 %collective-permute-start.15 = (bf16[1024,256]{1,0:T(8,128)(2,1)S(1)}, bf16[1024,256]{1,0:T(8,128)(2,1)S(1)}, u32[]{:S(2)}, u32[]{:S(2)}) collective-permute-start(bf16[1024,256]{1,0:T(8,128)(2,1)S(1)} %pad_maximum_fusion.6), channel_id=1, source_target_pairs={{0,1},{1,2},{2,3},{3,0},{4,5},{5,6},{6,7},{7,4},{8,9},{9,10},{10,1... | collective-permute-start | bytes 1572872 | tf_op jit(solution)/shard_map/ppermute | solution.py:374

commit v8 on v5

--- a/solution.py
+++ b/solution.py
@@ -71,7 +71,7 @@
 
 
 def by_rows(kernel, outputs, core, *arrays):
-    rows = 256
+    rows = 512
     wide = pl.BlockSpec((rows, 2 * HEAD_DIM), lambda i, c: (i, 0))
     return pl.pallas_call(
         kernel,
@@ -87,7 +87,7 @@
     )(core, *arrays)
 
 
-def pairs_kernel(own, parts, tiles, *refs):
+def pairs_kernel(own, apart, parts, tiles, *refs):
     core, q_in, k_in = refs[0], refs[1:1 + len(parts)], refs[1 + len(parts)]
     *outs, q, k, dq, dk, dv, row_q, col_k, bound, todo, w0, d0, w1, d1, sem = refs[2 + len(parts):]
     copies = [pltpu.make_async_copy(k_in, k, sem.at[0])]
@@ -182,8 +182,8 @@
 
         lax.fori_loop(0, (count + 1) // 2, two, 0)
 
-    for out, half in zip(outs[-2:], (core[0], 1 - core[0])):
-        at = pl.ds(pl.multiple_of(half * ROWS, ROWS), ROWS)
+    for out, half in zip(outs[-2:] if apart else outs[-1:], (core[0], 1 - core[0])):
+        at = pl.ds(pl.multiple_of(half * ROWS, ROWS), ROWS) if apart else pl.ds(0, PAIR)
         out[:, 0:128] = (dk[at, :] * HALF_SCALE).astype(out.dtype)
         out[:, 128:256] = dv[at, :].astype(out.dtype)
     if len(tiles) == TILES:
@@ -203,12 +203,14 @@
 
 def pairs(name, core, queries, parts, key, kind, tiles, area):
     anywhere = pl.BlockSpec(memory_space=pl.ANY)
+    apart = name != "pairs_two"
+    key_shapes = [(ROWS, 256)] * 2 if apart else [(PAIR, 256)]
     return pl.pallas_call(
-        lambda *refs: pairs_kernel(name == "pairs_own", parts, tiles, *refs),
+        lambda *refs: pairs_kernel(name == "pairs_own", apart, parts, tiles, *refs),
         in_specs=[SMEM] + [anywhere] * (len(queries) + 1),
-        out_specs=[VMEM] * (len(tiles) * TILE // ROWS + 2),
+        out_specs=[VMEM] * (len(tiles) * TILE // ROWS + len(key_shapes)),
         out_shape=[jax.ShapeDtypeStruct((ROWS, 128), kind)] * (len(tiles) * TILE // ROWS)
-        + [jax.ShapeDtypeStruct((ROWS, 256), kind)] * 2,
+        + [jax.ShapeDtypeStruct(shape, kind) for shape in key_shapes],
         scratch_shapes=[
             pltpu.VMEM((PAIR + SEG_ROWS, 256), BF16),
             pltpu.VMEM((PAIR + SEG_ROWS, 256), BF16),
@@ -230,7 +232,7 @@
     )(core, *queries, key)
 
 
-def collect_kernel(place, dq, dkv, other, back_same, back_cross, far_same, far_cross, key_same, key_cross,
+def collect_kernel(place, dq, dkv, other, back_same, back_cross, far_same, far_cross, key_back,
                    gate_grad, weights,
                    left, low, high):
     core, x = place[0], place[1]
@@ -243,7 +245,8 @@
             b = b + total(back_cross[...], far_cross[...])
         else:
             part = slice((p - 1) * 128, p * 128)
-            a, b = dkv[:, part] + key_same[:, part].astype(F32), b + key_cross[:, part].astype(F32)
+            at = pl.ds(pl.multiple_of(core * ROWS, ROWS), ROWS)
+            a = dkv[:, part] + key_back[at, part].astype(F32)
         a, b = a.astype(BF16), b.astype(BF16)
         left[:, p * 256:p * 256 + 128] = jnp.where(front, a, b)
         left[:, p * 256 + 128:p * 256 + 256] = jnp.where(front, b, a)
@@ -276,7 +279,7 @@
     half = jax.ShapeDtypeStruct((ROWS // 2, 256), BF16)
     return pl.pallas_call(
         collect_kernel,
-        in_specs=[SMEM] + [VMEM] * 11,
+        in_specs=[SMEM] + [VMEM] * 10,
         out_specs=[VMEM] * 3,
         out_shape=[jax.ShapeDtypeStruct((ROWS, 1024), BF16), half, half],
         compiler_params=params(24),
@@ -340,14 +343,15 @@
     )
     next_a, dq0 = lax.optimization_barrier((next_a, dq0))
     dq1a, *dkv1a = pairs("pairs_one", core_at, [next_a], [EARLY], key, BF16, early, area // 2)
-    query, next_a, next_b, key_prev, dq1a = lax.optimization_barrier(
-        (query, next_a, next_b, key_prev, dq1a)
+    dkv0 = [total(*terms) for terms in zip(dkv0, dkv1a)]
+    query, next_a, next_b, key_prev, dq1a, dkv0 = lax.optimization_barrier(
+        (query, next_a, next_b, key_prev, dq1a, dkv0)
     )
     query_far = shift(query, -6)
-    dq2_same, dq2_cross, *dkv2 = pairs(
+    dq2_same, dq2_cross, dkv2 = pairs(
         "pairs_two", core_at, [next_a, next_b], [EARLY, LATE], key_prev, BF16, every, area // 2
     )
-    key_same, key_cross = give(*dkv2, lambda i: i - 2)
+    key_back = shift(dkv2, -2)
     next_b, dq2_same = lax.optimization_barrier((next_b, dq2_same))
     dq1b, *dkv1b = pairs(
         "pairs_one", core_at, [next_a, next_b], [USERS_ONLY, LATE], key, BF16, late, area // 2
@@ -360,11 +364,14 @@
         "pairs_three", core_at, [query_far], [WHOLE], key, BF16, every, area // 8
     )
     far_same, far_cross = give(dq3_same, dq3_cross, lambda i: i + 6)
-    mine, other = (total(*terms) for terms in zip(dkv0, dkv1a, dkv1b, dkv3))
-    other = swap(jnp.concatenate([dq0_other, other], axis=1).astype(BF16))
+    mine = total(dkv0[0], dkv1b[0], dkv3[0])
+    back_other = jnp.where(front, key_back[ROWS:], key_back[:ROWS])
+    other = total(dkv0[1], dkv1b[1], dkv3[1], back_other)
+    other = jnp.concatenate([dq0_other, other], axis=1).astype(BF16)
+    other = swap(other)
     place = jnp.stack([core, head]).astype(jnp.int32)
     left, low, high = collect(
-        place, dq0, mine, other, back_same, back_cross, far_same, far_cross, key_same, key_cross,
+        place, dq0, mine, other, back_same, back_cross, far_same, far_cross, key_back,
         gate_grad, projections,
     )
 

time: 152 us -> 151 us (level)
  the two profiles are of different devices: /device:TPU:16 before, /device:TPU:94 now
where the time goes in v8:
time: 151 us
  waiting for transfers between devices  74.5 us (49%)
  starting transfers between devices  40.2 us (27%)
  Pallas kernels  28 us (19%)
  other arithmetic  7.2 us (5%)
    ppermute x9, waiting for transfers between devices, move(): return lax.ppermute(block, 'seq', route)  53.4 us
    ppermute x9, starting transfers between devices, move(): return lax.ppermute(block, 'seq', route)  35.2 us
    pallas_call x5, Pallas kernels, pairs(): pl.pallas_call(lambda *refs: pairs_kernel(name == 'pairs_own', apart, par...  20.8 us
    ppermute x4, waiting for transfers between devices, turn(): return lax.ppermute(block, 'head', [(i, (i + by) % 4) for i in range(4)])  19.5 us
    ppermute x4, starting transfers between devices, turn(): return lax.ppermute(block, 'head', [(i, (i + by) % 4) for i in range(4)])  4.33 us
    pallas_call x1, Pallas kernels, by_rows(): pl.pallas_call(kernel, grid_spec=pltpu.PrefetchScalarGridSpec(num_scalar_...  3.51 us
  transfers between devices with their start and end apart: 17, of which 12 were waited for; matrix products, arithmetic and copies ran while one was open for 2% of the time, Pallas kernels for 18%

profile of v8, /device:TPU:94, one launch (start us, length us, event | category | flops | bytes accessed | tf_op | source)
XLA Modules:
  0.0 150.5 jit_solution(5780440772613652849)
XLA Ops:
  0.0 1.3 broadcast_select_fusion.6
  1.3 0.1 pad_maximum_fusion.5
  1.3 0.1 collective-permute-start.1
  1.4 0.0 copy-done.12
  1.5 0.5 collective-permute-start.2
  1.9 3.5 %shard_map.82 = (bf16[1024,256]{1,0:T(8,128)(2,1)}, bf16[1024,256]{1,0:T(8,128)(2,1)}, bf16[1024,256]{1,0:T(8,128)(2,1)}) custom-call(s32[1]{0:T(128)} %bitcast.core.refs_0_, bf16[1024,256]{1,0:T(8,128)(2,1)} %q.1, bf16[1024,256]{1,0:T(8,128)(2,1)} %o.1, bf16[1024,256]{1,0:T(8,128)(2,1)} %gate.1, bf16[1024,256]{1,0:T(8,128)(2,1)} %grad.1), custom_call_target="tpu_custom_call" | custom-call | flops 7864320 | bytes 4194304 | tf_op jit(solution)/shard_map/pallas_call | solution.py:76
  5.5 0.1 collective-permute-start
  5.6 0.0 collective-permute-done.2
  5.6 0.0 collective-permute-done.1
  5.6 0.2 broadcast_select_fusion.3
  5.8 0.0 copy-start.11
  5.9 0.1 pad_maximum_fusion.refs_2_.refs_3_
  5.9 1.6 %collective-permute-done = bf16[1024,256]{1,0:T(8,128)(2,1)S(1)} collective-permute-done((bf16[1024,256]{1,0:T(8,128)(2,1)}, bf16[1024,256]{1,0:T(8,128)(2,1)S(1)}, u32[]{:S(2)}, u32[]{:S(2)}) %collective-permute-start) | collective-permute-done | bytes 524320 | tf_op jit(solution)/shard_map/ppermute | solution.py:40
  7.6 0.1 broadcast_select_fusion
  7.7 2.0 %collective-permute-start.3 = (bf16[1040,256]{1,0:T(8,128)(2,1)S(1)}, bf16[1040,256]{1,0:T(8,128)(2,1)S(1)}, u32[]{:S(2)}, u32[]{:S(2)}) collective-permute-start(bf16[1040,256]{1,0:T(8,128)(2,1)S(1)} %pad_maximum_fusion.3), channel_id=1, source_target_pairs={{8,0},{12,4},{16,8},{20,12},{24,16},{28,20},{32,24},{36,28},{40,32... | collective-permute-start | bytes 1597448 | tf_op jit(solution)/shard_map/ppermute | solution.py:32
  9.7 0.1 pad_maximum_fusion.1.refs_1_
  9.8 2.0 %collective-permute-start.4 = (bf16[1024,256]{1,0:T(8,128)(2,1)S(1)}, bf16[1024,256]{1,0:T(8,128)(2,1)S(1)}, u32[]{:S(2)}, u32[]{:S(2)}) collective-permute-start(bf16[1024,256]{1,0:T(8,128)(2,1)S(1)} %get-tuple-element.87), channel_id=1, source_target_pairs={{8,0},{12,4},{16,8},{20,12},{24,16},{28,20},{32,24},{36,28},{40,32... | collective-permute-start | bytes 1572872 | tf_op jit(solution)/shard_map/ppermute | solution.py:32
  11.8 3.9 %collective-permute-start.5 = (bf16[2064,256]{1,0:T(8,128)(2,1)S(1)}, bf16[2064,256]{1,0:T(8,128)(2,1)S(1)}, u32[]{:S(2)}, u32[]{:S(2)}) collective-permute-start(bf16[2064,256]{1,0:T(8,128)(2,1)S(1)} %pad_maximum_fusion.refs_2_.refs_3_), channel_id=1, source_target_pairs={{0,8},{4,12},{8,16},{12,20},{16,24},{20,28},{24,32},{28,36},{32,40... | collective-permute-start | bytes 3170312 | tf_op jit(solution)/shard_map/ppermute | solution.py:32
  15.7 11.5 %shard_map.83 = (f32[1024,128]{1,0:T(8,128)S(1)}, f32[1024,128]{1,0:T(8,128)S(1)}, f32[1024,256]{1,0:T(8,128)S(1)}, f32[1024,256]{1,0:T(8,128)S(1)}) custom-call(s32[1]{0:T(128)} %bitcast.core.refs_0_, bf16[2064,256]{1,0:T(8,128)(2,1)S(1)} %pad_maximum_fusion.1.refs_1_, bf16[2064,256]{1,0:T(8,128)(2,1)S(1)} %pad_maximum_fusion.refs_2_.refs_3_), custom_call_target="tpu_custom_call" | custom-call | flops 5368709120 | bytes 4194304 | tf_op jit(solution)/shard_map/pallas_call | solution.py:208
  27.2 0.0 collective-permute-done.3.refs_1_
  27.2 3.4 %shard_map.84 = (bf16[1024,128]{1,0:T(8,128)(2,1)S(1)}, bf16[1024,256]{1,0:T(8,128)(2,1)S(1)}, bf16[1024,256]{1,0:T(8,128)(2,1)S(1)}) custom-call(s32[1]{0:T(128)} %bitcast.core.refs_0_, bf16[1040,256]{1,0:T(8,128)(2,1)S(1)} %collective-permute-done.3.refs_1_, bf16[2064,256]{1,0:T(8,128)(2,1)S(1)} %pad_maximum_fusion.refs_2_.refs_3_), custom_call_target="tpu_custom_call" | custom-call | flops 5368709120 | bytes 4194304 | tf_op jit(solution)/shard_map/pallas_call | solution.py:208
  30.7 0.1 convert_add_fusion.1
  30.8 1.1 convert_add_fusion.2
  31.9 3.1 %collective-permute-done.4.refs_2_ = bf16[1024,256]{1,0:T(8,128)(2,1)S(1)} collective-permute-done((bf16[1024,256]{1,0:T(8,128)(2,1)S(1)}, bf16[1024,256]{1,0:T(8,128)(2,1)S(1)}, u32[]{:S(2)}, u32[]{:S(2)}) %collective-permute-start.4) | collective-permute-done | bytes 524320 | tf_op jit(solution)/shard_map/ppermute | solution.py:32
  35.0 6.1 %collective-permute-done.5.refs_3_ = bf16[2064,256]{1,0:T(8,128)(2,1)S(1)} collective-permute-done((bf16[2064,256]{1,0:T(8,128)(2,1)S(1)}, bf16[2064,256]{1,0:T(8,128)(2,1)S(1)}, u32[]{:S(2)}, u32[]{:S(2)}) %collective-permute-start.5) | collective-permute-done | bytes 1056800 | tf_op jit(solution)/shard_map/ppermute | solution.py:32
  41.0 3.1 %collective-permute-start.6 = (bf16[2064,256]{1,0:T(8,128)(2,1)S(1)}, bf16[2064,256]{1,0:T(8,128)(2,1)S(1)}, u32[]{:S(2)}, u32[]{:S(2)}) collective-permute-start(bf16[2064,256]{1,0:T(8,128)(2,1)S(1)} %pad_maximum_fusion.1.refs_1_), channel_id=1, source_target_pairs={{24,0},{28,4},{32,8},{36,12},{40,16},{44,20},{48,24},{52,28},{56,3... | collective-permute-start | bytes 3170312 | tf_op jit(solution)/shard_map/ppermute | solution.py:32
  44.2 1.3 shard_map.85
  45.5 0.0 copy-start.4
  45.5 17.8 %collective-permute-start.7 = (bf16[2048,256]{1,0:T(8,128)(2,1)S(1)}, bf16[2048,256]{1,0:T(8,128)(2,1)S(1)}, u32[]{:S(2)}, u32[]{:S(2)}) collective-permute-start(bf16[2048,256]{1,0:T(8,128)(2,1)S(1)} %get-tuple-element.74), channel_id=1, source_target_pairs={{8,0},{12,4},{16,8},{20,12},{24,16},{28,20},{32,24},{36,28},{40,32... | collective-permute-start | bytes 3145736 | tf_op jit(solution)/shard_map/ppermute | solution.py:32
  63.3 3.4 %shard_map.86 = (bf16[1024,128]{1,0:T(8,128)(2,1)S(1)}, bf16[1024,256]{1,0:T(8,128)(2,1)S(1)}, bf16[1024,256]{1,0:T(8,128)(2,1)S(1)}) custom-call(s32[1]{0:T(128)} %bitcast.core.refs_0_, bf16[1040,256]{1,0:T(8,128)(2,1)S(1)} %collective-permute-done.3.refs_1_, bf16[1024,256]{1,0:T(8,128)(2,1)S(1)} %collective-permute-done.4.refs_2_, ...), custom_call_target="tpu_custom_call" | custom-call | flops 5368709120 | bytes 4194304 | tf_op jit(solution)/shard_map/pallas_call | solution.py:208
  66.7 0.0 copy-done.3
  66.7 0.0 copy-done.4
  66.8 0.0 collective-permute-done.6.refs_1_
  66.8 1.1 shard_map.87
  68.0 16.6 %collective-permute-done.7.key_back = bf16[2048,256]{1,0:T(8,128)(2,1)S(1)} collective-permute-done((bf16[2048,256]{1,0:T(8,128)(2,1)S(1)}, bf16[2048,256]{1,0:T(8,128)(2,1)S(1)}, u32[]{:S(2)}, u32[]{:S(2)}) %collective-permute-start.7) | collective-permute-done | bytes 1048608 | tf_op jit(solution)/shard_map/ppermute | solution.py:32
  84.5 0.3 add_convert_fusion.1
  84.9 1.0 pad_maximum_fusion.2
  85.9 0.0 collective-permute-start.8
  85.9 0.1 pad_add_fusion.place
  86.0 1.5 add_convert_fusion.4
  87.4 1.9 %collective-permute-start.10 = (bf16[1024,128]{1,0:T(8,128)(2,1)S(1)}, bf16[1024,128]{1,0:T(8,128)(2,1)S(1)}, u32[]{:S(2)}, u32[]{:S(2)}) collective-permute-start(bf16[1024,128]{1,0:T(8,128)(2,1)S(1)} %get-tuple-element.91), channel_id=1, source_target_pairs={{0,12},{4,8},{8,20},{12,16},{16,28},{20,24},{24,36},{28,32},{32,44... | collective-permute-start | bytes 786440 | tf_op jit(solution)/shard_map/ppermute | solution.py:32
  89.4 1.9 %collective-permute-start.9 = (bf16[1024,128]{1,0:T(8,128)(2,1)S(1)}, bf16[1024,128]{1,0:T(8,128)(2,1)S(1)}, u32[]{:S(2)}, u32[]{:S(2)}) collective-permute-start(bf16[1024,128]{1,0:T(8,128)(2,1)S(1)} %get-tuple-element.92), channel_id=1, source_target_pairs={{0,8},{4,12},{8,16},{12,20},{16,24},{20,28},{24,32},{28,36},{32,40... | collective-permute-start | bytes 786440 | tf_op jit(solution)/shard_map/ppermute | solution.py:32
  91.3 1.3 collective-permute-start.11
  92.6 1.3 collective-permute-start.12
  93.9 0.0 copy-start
  94.0 0.1 convert_add_fusion.dkv
  94.1 4.5 %collective-permute-done.10.back_cross = bf16[1024,128]{1,0:T(8,128)(2,1)S(1)} collective-permute-done((bf16[1024,128]{1,0:T(8,128)(2,1)S(1)}, bf16[1024,128]{1,0:T(8,128)(2,1)S(1)}, u32[]{:S(2)}, u32[]{:S(2)}) %collective-permute-start.10) | collective-permute-done | bytes 262176 | tf_op jit(solution)/shard_map/ppermute | solution.py:32
  98.6 5.8 %collective-permute-done.9.back_same = bf16[1024,128]{1,0:T(8,128)(2,1)S(1)} collective-permute-done((bf16[1024,128]{1,0:T(8,128)(2,1)S(1)}, bf16[1024,128]{1,0:T(8,128)(2,1)S(1)}, u32[]{:S(2)}, u32[]{:S(2)}) %collective-permute-start.9) | collective-permute-done | bytes 262176 | tf_op jit(solution)/shard_map/ppermute | solution.py:32
  104.4 12.1 %collective-permute-done.11.far_same = bf16[1024,128]{1,0:T(8,128)(2,1)S(1)} collective-permute-done((bf16[1024,128]{1,0:T(8,128)(2,1)S(1)}, bf16[1024,128]{1,0:T(8,128)(2,1)S(1)}, u32[]{:S(2)}, u32[]{:S(2)}) %collective-permute-start.11) | collective-permute-done | bytes 262176 | tf_op jit(solution)/shard_map/ppermute | solution.py:32
  116.5 5.2 %collective-permute-done.12.far_cross = bf16[1024,128]{1,0:T(8,128)(2,1)S(1)} collective-permute-done((bf16[1024,128]{1,0:T(8,128)(2,1)S(1)}, bf16[1024,128]{1,0:T(8,128)(2,1)S(1)}, u32[]{:S(2)}, u32[]{:S(2)}) %collective-permute-start.12) | collective-permute-done | bytes 262176 | tf_op jit(solution)/shard_map/ppermute | solution.py:32
  121.8 0.0 collective-permute-done.8.other
  121.8 1.3 collect.1
  123.1 0.5 collective-permute-start.13
  123.7 2.4 %project.1 = (f32[1024,256]{1,0:T(8,128)S(1)}, f32[1024,256]{1,0:T(8,128)S(1)}, f32[1024,256]{1,0:T(8,128)S(1)}) custom-call(s32[2]{0:T(128)S(1)} %pad_add_fusion.place, bf16[1024,1024]{1,0:T(8,128)(2,1)S(1)} %get-tuple-element.81.left, bf16[4,1024,256]{2,1,0:T(8,128)(2,1)S(1)} %copy-done), custom_call_target="tpu_custom_call" | custom-call | flops 1610612736 | bytes 8388608 | tf_op jit(solution)/shard_map/project/pallas_call | solution.py:292
  126.1 1.6 %collective-permute-start.15 = (bf16[512,256]{1,0:T(8,128)(2,1)S(1)}, bf16[512,256]{1,0:T(8,128)(2,1)S(1)}, u32[]{:S(2)}, u32[]{:S(2)}) collective-permute-start(bf16[512,256]{1,0:T(8,128)(2,1)S(1)} %get-tuple-element.86), channel_id=1, source_target_pairs={{0,3},{1,0},{2,1},{3,2},{4,7},{5,4},{6,5},{7,6},{8,11},{9,8},{10,9... | collective-permute-start | bytes 786440 | tf_op jit(solution)/shard_map/ppermute | solution.py:379
  127.7 3.8 %collective-permute-done.13 = bf16[512,256]{1,0:T(8,128)(2,1)S(1)} collective-permute-done((bf16[512,256]{1,0:T(8,128)(2,1)S(1)}, bf16[512,256]{1,0:T(8,128)(2,1)S(1)}, u32[]{:S(2)}, u32[]{:S(2)}) %collective-permute-start.13) | collective-permute-done | bytes 262176 | tf_op jit(solution)/shard_map/ppermute | solution.py:379
  131.5 0.1 add_convert_fusion.3
  131.6 1.8 %collective-permute-start.14 = (bf16[1024,256]{1,0:T(8,128)(2,1)S(1)}, bf16[1024,256]{1,0:T(8,128)(2,1)S(1)}, u32[]{:S(2)}, u32[]{:S(2)}) collective-permute-start(bf16[1024,256]{1,0:T(8,128)(2,1)S(1)} %pad_maximum_fusion.6), channel_id=1, source_target_pairs={{0,1},{1,2},{2,3},{3,0},{4,5},{5,6},{6,7},{7,4},{8,9},{9,10},{10,1... | collective-permute-start | bytes 1572872 | tf_op jit(solution)/shard_map/ppermute | solution.py:379
  133.4 2.0 %collective-permute-done.15 = bf16[512,256]{1,0:T(8,128)(2,1)S(1)} collective-permute-done((bf16[512,256]{1,0:T(8,128)(2,1)S(1)}, bf16[512,256]{1,0:T(8,128)(2,1)S(1)}, u32[]{:S(2)}, u32[]{:S(2)}) %collective-permute-start.15) | collective-permute-done | bytes 262176 | tf_op jit(solution)/shard_map/ppermute | solution.py:379
  135.4 0.1 add_convert_fusion.2
  135.5 0.4 collective-permute-start.16
  135.9 8.9 %collective-permute-done.14 = bf16[1024,256]{1,0:T(8,128)(2,1)S(1)} collective-permute-done((bf16[1024,256]{1,0:T(8,128)(2,1)S(1)}, bf16[1024,256]{1,0:T(8,128)(2,1)S(1)}, u32[]{:S(2)}, u32[]{:S(2)}) %collective-permute-start.14) | collective-permute-done | bytes 524320 | tf_op jit(solution)/shard_map/ppermute | solution.py:379
  144.8 4.8 %collective-permute-done.16 = bf16[1024,256]{1,0:T(8,128)(2,1)S(1)} collective-permute-done((bf16[1024,256]{1,0:T(8,128)(2,1)S(1)}, bf16[1024,256]{1,0:T(8,128)(2,1)S(1)}, u32[]{:S(2)}, u32[]{:S(2)}) %collective-permute-start.16) | collective-permute-done | bytes 524320 | tf_op jit(solution)/shard_map/ppermute | solution.py:379
  149.6 0.9 add_convert_fusion
  (31 shorter events, 0.3 us)
Async XLA Ops:
  0.0 1.4 copy-start.12
  1.3 4.3 %collective-permute-start.1 = (bf16[1024,256]{1,0:T(8,128)(2,1)S(1)}, bf16[1024,256]{1,0:T(8,128)(2,1)S(1)}, u32[]{:S(2)}, u32[]{:S(2)}) collective-permute-start(bf16[1024,256]{1,0:T(8,128)(2,1)S(1)} %pad_maximum_fusion.5), channel_id=1, source_target_pairs={{0,4},{4,0},{8,12},{12,8},{16,20},{20,16},{24,28},{28,24},{32,36},... | collective-permute-start | bytes 1572872 | tf_op jit(solution)/shard_map/ppermute | solution.py:40
  1.5 4.1 %collective-permute-start.2 = (bf16[1024]{0:T(1024)(128)(2,1)S(1)}, bf16[1024]{0:T(1024)(128)(2,1)S(1)}, u32[]{:S(2)}, u32[]{:S(2)}) collective-permute-start(bf16[1024]{0:T(1024)(128)(2,1)S(1)} %add_convert_fusion.6), channel_id=1, source_target_pairs={{0,4},{4,0},{8,12},{12,8},{16,20},{20,16},{24,28},{28,24},{32,36},... | collective-permute-start | bytes 6152 | tf_op jit(solution)/shard_map/ppermute | solution.py:40
  5.5 2.1 %collective-permute-start = (bf16[1024,256]{1,0:T(8,128)(2,1)}, bf16[1024,256]{1,0:T(8,128)(2,1)S(1)}, u32[]{:S(2)}, u32[]{:S(2)}) collective-permute-start(bf16[1024,256]{1,0:T(8,128)(2,1)} %get-tuple-element.47), channel_id=1, source_target_pairs={{0,4},{4,0},{8,12},{12,8},{16,20},{20,16},{24,28},{28,24},{32,36},... | collective-permute-start | bytes 1572872 | tf_op jit(solution)/shard_map/ppermute | solution.py:40
  5.8 1.7 %copy-start.11 = (bf16[1024,256]{1,0:T(8,128)(2,1)S(1)}, bf16[1024,256]{1,0:T(8,128)(2,1)}, u32[]{:S(2)}) copy-start(bf16[1024,256]{1,0:T(8,128)(2,1)} %get-tuple-element.46) | copy-start | bytes 1572868
  7.7 19.5 %collective-permute-start.3 = (bf16[1040,256]{1,0:T(8,128)(2,1)S(1)}, bf16[1040,256]{1,0:T(8,128)(2,1)S(1)}, u32[]{:S(2)}, u32[]{:S(2)}) collective-permute-start(bf16[1040,256]{1,0:T(8,128)(2,1)S(1)} %pad_maximum_fusion.3), channel_id=1, source_target_pairs={{8,0},{12,4},{16,8},{20,12},{24,16},{28,20},{32,24},{36,28},{40,32... | collective-permute-start | bytes 1597448 | tf_op jit(solution)/shard_map/ppermute | solution.py:32
  9.8 25.2 %collective-permute-start.4 = (bf16[1024,256]{1,0:T(8,128)(2,1)S(1)}, bf16[1024,256]{1,0:T(8,128)(2,1)S(1)}, u32[]{:S(2)}, u32[]{:S(2)}) collective-permute-start(bf16[1024,256]{1,0:T(8,128)(2,1)S(1)} %get-tuple-element.87), channel_id=1, source_target_pairs={{8,0},{12,4},{16,8},{20,12},{24,16},{28,20},{32,24},{36,28},{40,32... | collective-permute-start | bytes 1572872 | tf_op jit(solution)/shard_map/ppermute | solution.py:32
  11.8 29.2 %collective-permute-start.5 = (bf16[2064,256]{1,0:T(8,128)(2,1)S(1)}, bf16[2064,256]{1,0:T(8,128)(2,1)S(1)}, u32[]{:S(2)}, u32[]{:S(2)}) collective-permute-start(bf16[2064,256]{1,0:T(8,128)(2,1)S(1)} %pad_maximum_fusion.refs_2_.refs_3_), channel_id=1, source_target_pairs={{0,8},{4,12},{8,16},{12,20},{16,24},{20,28},{24,32},{28,36},{32,40... | collective-permute-start | bytes 3170312 | tf_op jit(solution)/shard_map/ppermute | solution.py:32
  30.7 1.2 copy-start.2
  41.0 25.7 %collective-permute-start.6 = (bf16[2064,256]{1,0:T(8,128)(2,1)S(1)}, bf16[2064,256]{1,0:T(8,128)(2,1)S(1)}, u32[]{:S(2)}, u32[]{:S(2)}) collective-permute-start(bf16[2064,256]{1,0:T(8,128)(2,1)S(1)} %pad_maximum_fusion.1.refs_1_), channel_id=1, source_target_pairs={{24,0},{28,4},{32,8},{36,12},{40,16},{44,20},{48,24},{52,28},{56,3... | collective-permute-start | bytes 3170312 | tf_op jit(solution)/shard_map/ppermute | solution.py:32
  45.5 21.2 %copy-start.3 = (bf16[1024,128]{1,0:T(8,128)(2,1)}, bf16[1024,128]{1,0:T(8,128)(2,1)S(1)}, u32[]{:S(2)}) copy-start(bf16[1024,128]{1,0:T(8,128)(2,1)S(1)} %get-tuple-element.76) | copy-start | bytes 786436
  45.5 21.2 %copy-start.4 = (bf16[1024,128]{1,0:T(8,128)(2,1)}, bf16[1024,128]{1,0:T(8,128)(2,1)S(1)}, u32[]{:S(2)}) copy-start(bf16[1024,128]{1,0:T(8,128)(2,1)S(1)} %get-tuple-element.77) | copy-start | bytes 786436
  45.5 39.0 %collective-permute-start.7 = (bf16[2048,256]{1,0:T(8,128)(2,1)S(1)}, bf16[2048,256]{1,0:T(8,128)(2,1)S(1)}, u32[]{:S(2)}, u32[]{:S(2)}) collective-permute-start(bf16[2048,256]{1,0:T(8,128)(2,1)S(1)} %get-tuple-element.74), channel_id=1, source_target_pairs={{8,0},{12,4},{16,8},{20,12},{24,16},{28,20},{32,24},{36,28},{40,32... | collective-permute-start | bytes 3145736 | tf_op jit(solution)/shard_map/ppermute | solution.py:32
  66.8 1.2 copy-start.5
  67.9 17.0 %copy-start.6 = (bf16[1024,128]{1,0:T(8,128)(2,1)}, bf16[1024,128]{1,0:T(8,128)(2,1)S(1)}, u32[]{:S(2)}) copy-start(bf16[1024,128]{1,0:T(8,128)(2,1)S(1)} %get-tuple-element.79) | copy-start | bytes 786436
  67.9 17.0 %copy-start.8 = (bf16[1024,128]{1,0:T(8,128)(2,1)}, bf16[1024,128]{1,0:T(8,128)(2,1)S(1)}, u32[]{:S(2)}) copy-start(bf16[1024,128]{1,0:T(8,128)(2,1)S(1)} %get-tuple-element.78) | copy-start | bytes 786436
  85.9 35.9 %collective-permute-start.8 = (bf16[1024,384]{1,0:T(8,128)(2,1)}, bf16[1024,384]{1,0:T(8,128)(2,1)S(1)}, u32[]{:S(2)}, u32[]{:S(2)}) collective-permute-start(bf16[1024,384]{1,0:T(8,128)(2,1)} %pad_maximum_fusion.2), channel_id=1, source_target_pairs={{0,4},{4,0},{8,12},{12,8},{16,20},{20,16},{24,28},{28,24},{32,36},... | collective-permute-start | bytes 2359304 | tf_op jit(solution)/shard_map/ppermute | solution.py:40
  85.9 5.4 %copy-start.9 = (bf16[1024,128]{1,0:T(8,128)(2,1)S(1)}, bf16[1024,128]{1,0:T(8,128)(2,1)}, u32[]{:S(2)}) copy-start(bf16[1024,128]{1,0:T(8,128)(2,1)} %copy-done.8) | copy-start | bytes 786436
  85.9 6.7 %copy-start.7 = (bf16[1024,128]{1,0:T(8,128)(2,1)S(1)}, bf16[1024,128]{1,0:T(8,128)(2,1)}, u32[]{:S(2)}) copy-start(bf16[1024,128]{1,0:T(8,128)(2,1)} %copy-done.6) | copy-start | bytes 786436
  85.9 8.0 %copy-start.10 = (f32[1024,256]{1,0:T(8,128)S(1)}, f32[1024,256]{1,0:T(8,128)}, u32[]{:S(2)}) copy-start(f32[1024,256]{1,0:T(8,128)} %convert_add_fusion.2) | copy-start | bytes 3145732
  87.4 11.2 %collective-permute-start.10 = (bf16[1024,128]{1,0:T(8,128)(2,1)S(1)}, bf16[1024,128]{1,0:T(8,128)(2,1)S(1)}, u32[]{:S(2)}, u32[]{:S(2)}) collective-permute-start(bf16[1024,128]{1,0:T(8,128)(2,1)S(1)} %get-tuple-element.91), channel_id=1, source_target_pairs={{0,12},{4,8},{8,20},{12,16},{16,28},{20,24},{24,36},{28,32},{32,44... | collective-permute-start | bytes 786440 | tf_op jit(solution)/shard_map/ppermute | solution.py:32
  89.4 15.0 %collective-permute-start.9 = (bf16[1024,128]{1,0:T(8,128)(2,1)S(1)}, bf16[1024,128]{1,0:T(8,128)(2,1)S(1)}, u32[]{:S(2)}, u32[]{:S(2)}) collective-permute-start(bf16[1024,128]{1,0:T(8,128)(2,1)S(1)} %get-tuple-element.92), channel_id=1, source_target_pairs={{0,8},{4,12},{8,16},{12,20},{16,24},{20,28},{24,32},{28,36},{32,40... | collective-permute-start | bytes 786440 | tf_op jit(solution)/shard_map/ppermute | solution.py:32
  91.3 25.2 %collective-permute-start.11 = (bf16[1024,128]{1,0:T(8,128)(2,1)S(1)}, bf16[1024,128]{1,0:T(8,128)(2,1)S(1)}, u32[]{:S(2)}, u32[]{:S(2)}) collective-permute-start(bf16[1024,128]{1,0:T(8,128)(2,1)S(1)} %copy-done.9), channel_id=1, source_target_pairs={{0,24},{4,28},{8,32},{12,36},{16,40},{20,44},{24,48},{28,52},{32,5... | collective-permute-start | bytes 786440 | tf_op jit(solution)/shard_map/ppermute | solution.py:32
  92.6 29.2 %collective-permute-start.12 = (bf16[1024,128]{1,0:T(8,128)(2,1)S(1)}, bf16[1024,128]{1,0:T(8,128)(2,1)S(1)}, u32[]{:S(2)}, u32[]{:S(2)}) collective-permute-start(bf16[1024,128]{1,0:T(8,128)(2,1)S(1)} %copy-done.7), channel_id=1, source_target_pairs={{0,28},{4,24},{8,36},{12,32},{16,44},{20,40},{24,52},{28,48},{32,6... | collective-permute-start | bytes 786440 | tf_op jit(solution)/shard_map/ppermute | solution.py:32
  93.9 27.9 %copy-start = (bf16[4,1024,256]{2,1,0:T(8,128)(2,1)S(1)}, bf16[4,1024,256]{2,1,0:T(8,128)(2,1)}, u32[]{:S(2)}) copy-start(bf16[4,1024,256]{2,1,0:T(8,128)(2,1)} %weights.3) | copy-start | bytes 6291460
  93.9 27.9 %copy-start.1 = (bf16[1024,256]{1,0:T(8,128)(2,1)S(1)}, bf16[1024,256]{1,0:T(8,128)(2,1)}, u32[]{:S(2)}) copy-start(bf16[1024,256]{1,0:T(8,128)(2,1)} %get-tuple-element.80.gate_grad) | copy-start | bytes 1572868
  123.1 8.4 %collective-permute-start.13 = (bf16[512,256]{1,0:T(8,128)(2,1)S(1)}, bf16[512,256]{1,0:T(8,128)(2,1)S(1)}, u32[]{:S(2)}, u32[]{:S(2)}) collective-permute-start(bf16[512,256]{1,0:T(8,128)(2,1)S(1)} %get-tuple-element.84), channel_id=1, source_target_pairs={{0,1},{1,2},{2,3},{3,0},{4,5},{5,6},{6,7},{7,4},{8,9},{9,10},{10,1... | collective-permute-start | bytes 786440 | tf_op jit(solution)/shard_map/ppermute | solution.py:379
  126.1 9.3 %collective-permute-start.15 = (bf16[512,256]{1,0:T(8,128)(2,1)S(1)}, bf16[512,256]{1,0:T(8,128)(2,1)S(1)}, u32[]{:S(2)}, u32[]{:S(2)}) collective-permute-start(bf16[512,256]{1,0:T(8,128)(2,1)S(1)} %get-tuple-element.86), channel_id=1, source_target_pairs={{0,3},{1,0},{2,1},{3,2},{4,7},{5,4},{6,5},{7,6},{8,11},{9,8},{10,9... | collective-permute-start | bytes 786440 | tf_op jit(solution)/shard_map/ppermute | solution.py:379
  131.6 13.2 %collective-permute-start.14 = (bf16[1024,256]{1,0:T(8,128)(2,1)S(1)}, bf16[1024,256]{1,0:T(8,128)(2,1)S(1)}, u32[]{:S(2)}, u32[]{:S(2)}) collective-permute-start(bf16[1024,256]{1,0:T(8,128)(2,1)S(1)} %pad_maximum_fusion.6), channel_id=1, source_target_pairs={{0,1},{1,2},{2,3},{3,0},{4,5},{5,6},{6,7},{7,4},{8,9},{9,10},{10,1... | collective-permute-start | bytes 1572872 | tf_op jit(solution)/shard_map/ppermute | solution.py:379
  135.5 14.1 %collective-permute-start.16 = (bf16[1024,256]{1,0:T(8,128)(2,1)S(1)}, bf16[1024,256]{1,0:T(8,128)(2,1)S(1)}, u32[]{:S(2)}, u32[]{:S(2)}) collective-permute-start(bf16[1024,256]{1,0:T(8,128)(2,1)S(1)} %pad_maximum_fusion.7), channel_id=1, source_target_pairs={{0,3},{1,0},{2,1},{3,2},{4,7},{5,4},{6,5},{7,6},{8,11},{9,8},{10,9... | collective-permute-start | bytes 1572872 | tf_op jit(solution)/shard_map/ppermute | solution.py:379

commit v9 on v8

--- a/solution.py
+++ b/solution.py
@@ -87,9 +87,10 @@
     )(core, *arrays)
 
 
-def pairs_kernel(own, apart, parts, tiles, *refs):
+def pairs_kernel(own, apart, bases, parts, tiles, *refs):
     core, q_in, k_in = refs[0], refs[1:1 + len(parts)], refs[1 + len(parts)]
-    *outs, q, k, dq, dk, dv, row_q, col_k, bound, todo, w0, d0, w1, d1, sem = refs[2 + len(parts):]
+    base = refs[2 + len(parts):2 + len(parts) + bases]
+    *outs, q, k, dq, dk, dv, row_q, col_k, bound, todo, w0, d0, w1, d1, sem = refs[2 + len(parts) + bases:]
     copies = [pltpu.make_async_copy(k_in, k, sem.at[0])]
     for ref, moves in zip(q_in, parts):
         for source, target, size in moves:
@@ -182,10 +183,13 @@
 
         lax.fori_loop(0, (count + 1) // 2, two, 0)
 
-    for out, half in zip(outs[-2:] if apart else outs[-1:], (core[0], 1 - core[0])):
+    for i, (out, half) in enumerate(zip(outs[-2:] if apart else outs[-1:], (core[0], 1 - core[0]))):
         at = pl.ds(pl.multiple_of(half * ROWS, ROWS), ROWS) if apart else pl.ds(0, PAIR)
-        out[:, 0:128] = (dk[at, :] * HALF_SCALE).astype(out.dtype)
-        out[:, 128:256] = dv[at, :].astype(out.dtype)
+        key_grad, value_grad = dk[at, :] * HALF_SCALE, dv[at, :]
+        if bases:
+            key_grad, value_grad = key_grad + base[i][:, 0:128], value_grad + base[i][:, 128:256]
+        out[:, 0:128] = key_grad.astype(out.dtype)
+        out[:, 128:256] = value_grad.astype(out.dtype)
     if len(tiles) == TILES:
         for out, half in zip(outs[:2], (core[0], 1 - core[0])):
             at = pl.ds(pl.multiple_of(half * ROWS, ROWS), ROWS)
@@ -201,16 +205,16 @@
 LATE = [(0, ROWS, ROWS)]
 
 
-def pairs(name, core, queries, parts, key, kind, tiles, area):
+def pairs(name, core, queries, parts, key, kind, tiles, area, base=()):
     anywhere = pl.BlockSpec(memory_space=pl.ANY)
     apart = name != "pairs_two"
     key_shapes = [(ROWS, 256)] * 2 if apart else [(PAIR, 256)]
     return pl.pallas_call(
-        lambda *refs: pairs_kernel(name == "pairs_own", apart, parts, tiles, *refs),
-        in_specs=[SMEM] + [anywhere] * (len(queries) + 1),
+        lambda *refs: pairs_kernel(name == "pairs_own", apart, len(base), parts, tiles, *refs),
+        in_specs=[SMEM] + [anywhere] * (len(queries) + 1) + [VMEM] * len(base),
         out_specs=[VMEM] * (len(tiles) * TILE // ROWS + len(key_shapes)),
         out_shape=[jax.ShapeDtypeStruct((ROWS, 128), kind)] * (len(tiles) * TILE // ROWS)
-        + [jax.ShapeDtypeStruct(shape, kind) for shape in key_shapes],
+        + [jax.ShapeDtypeStruct(shape, F32 if base else kind) for shape in key_shapes],
         scratch_shapes=[
             pltpu.VMEM((PAIR + SEG_ROWS, 256), BF16),
             pltpu.VMEM((PAIR + SEG_ROWS, 256), BF16),
@@ -229,7 +233,7 @@
         ],
         compiler_params=params(28),
         cost_estimate=cost(20 * area * 128, area, 8 * PAIR * 256),
-    )(core, *queries, key)
+    )(core, *queries, key, *base)
 
 
 def collect_kernel(place, dq, dkv, other, back_same, back_cross, far_same, far_cross, key_back,
@@ -342,10 +346,9 @@
         "pairs_own", core_at, [query], [WHOLE], key, F32, every, area // 2
     )
     next_a, dq0 = lax.optimization_barrier((next_a, dq0))
-    dq1a, *dkv1a = pairs("pairs_one", core_at, [next_a], [EARLY], key, BF16, early, area // 2)
-    dkv0 = [total(*terms) for terms in zip(dkv0, dkv1a)]
-    query, next_a, next_b, key_prev, dq1a, dkv0 = lax.optimization_barrier(
-        (query, next_a, next_b, key_prev, dq1a, dkv0)
+    dq1a, *dkv0 = pairs("pairs_one", core_at, [next_a], [EARLY], key, BF16, early, area // 2, dkv0)
+    query, next_a, next_b, key_prev, dq1a = lax.optimization_barrier(
+        (query, next_a, next_b, key_prev, dq1a)
     )
     query_far = shift(query, -6)
     dq2_same, dq2_cross, dkv2 = pairs(

time: 151 us -> 146 us (0.967)
  waiting for transfers between devices: 74.5 us -> 69 us
    ppermute x9, waiting for transfers between devices: 53.4 us -> 49.6 us  [move(): return lax.ppermute(block, 'seq', route)]
    ppermute x4, waiting for transfers between devices: 1.65 us -> 0.01 us  [swap(): lax.ppermute(block, 'seq', [(i, i ^ 1) for i in range(lax.axis_size('seq'...]
  transfers between devices with their start and end apart: 17 -> 17, of which waited for: 12 -> 11; matrix products, arithmetic and copies ran while one was open for 2% -> 2% of each run, Pallas kernels for 18% -> 18%
where the time goes in v9:
time: 146 us
  waiting for transfers between devices  69 us (47%)
  starting transfers between devices  40.6 us (28%)
  Pallas kernels  28.1 us (19%)
  other arithmetic  6.04 us (4%)
  local copies, waits for them, and re-layouts  1.64 us (1%)
    ppermute x9, waiting for transfers between devices, move(): return lax.ppermute(block, 'seq', route)  49.6 us
    ppermute x9, starting transfers between devices, move(): return lax.ppermute(block, 'seq', route)  35.6 us
    pallas_call x5, Pallas kernels, pairs(): pl.pallas_call(lambda *refs: pairs_kernel(name == 'pairs_own', apart, len...  20.9 us
    ppermute x4, waiting for transfers between devices, turn(): return lax.ppermute(block, 'head', [(i, (i + by) % 4) for i in range(4)])  19.5 us
    ppermute x4, starting transfers between devices, turn(): return lax.ppermute(block, 'head', [(i, (i + by) % 4) for i in range(4)])  4.33 us
    pallas_call x1, Pallas kernels, by_rows(): pl.pallas_call(kernel, grid_spec=pltpu.PrefetchScalarGridSpec(num_scalar_...  3.52 us
  transfers between devices with their start and end apart: 17, of which 11 were waited for; matrix products, arithmetic and copies ran while one was open for 2% of the time, Pallas kernels for 18%

profile of v9, /device:TPU:94, one launch (start us, length us, event | category | flops | bytes accessed | tf_op | source)
XLA Modules:
  0.0 145.9 jit_solution(7329339372845952892)
XLA Ops:
  0.0 1.3 broadcast_select_fusion.6
  1.3 0.1 pad_maximum_fusion.5
  1.3 0.1 collective-permute-start.1
  1.4 0.0 copy-done.15
  1.5 0.5 collective-permute-start.2
  1.9 3.5 %shard_map.82 = (bf16[1024,256]{1,0:T(8,128)(2,1)}, bf16[1024,256]{1,0:T(8,128)(2,1)}, bf16[1024,256]{1,0:T(8,128)(2,1)}) custom-call(s32[1]{0:T(128)} %bitcast.core.refs_0_, bf16[1024,256]{1,0:T(8,128)(2,1)} %q.1, bf16[1024,256]{1,0:T(8,128)(2,1)} %o.1, bf16[1024,256]{1,0:T(8,128)(2,1)} %gate.1, bf16[1024,256]{1,0:T(8,128)(2,1)} %grad.1), custom_call_target="tpu_custom_call" | custom-call | flops 7864320 | bytes 4194304 | tf_op jit(solution)/shard_map/pallas_call | solution.py:76
  5.5 0.1 collective-permute-start
  5.6 0.0 collective-permute-done.2
  5.6 0.0 collective-permute-done.1
  5.6 0.2 broadcast_select_fusion.3
  5.9 0.0 copy-start.14
  5.9 0.1 pad_maximum_fusion.refs_2_.refs_3_
  5.9 3.7 %collective-permute-start.5 = (bf16[2064,256]{1,0:T(8,128)(2,1)S(1)}, bf16[2064,256]{1,0:T(8,128)(2,1)S(1)}, u32[]{:S(2)}, u32[]{:S(2)}) collective-permute-start(bf16[2064,256]{1,0:T(8,128)(2,1)S(1)} %pad_maximum_fusion.refs_2_.refs_3_), channel_id=1, source_target_pairs={{0,8},{4,12},{8,16},{12,20},{16,24},{20,28},{24,32},{28,36},{32,40... | collective-permute-start | bytes 3170312 | tf_op jit(solution)/shard_map/ppermute | solution.py:32
  9.6 0.0 collective-permute-done
  9.6 0.1 broadcast_select_fusion
  9.8 2.3 %collective-permute-start.3 = (bf16[1040,256]{1,0:T(8,128)(2,1)S(1)}, bf16[1040,256]{1,0:T(8,128)(2,1)S(1)}, u32[]{:S(2)}, u32[]{:S(2)}) collective-permute-start(bf16[1040,256]{1,0:T(8,128)(2,1)S(1)} %pad_maximum_fusion.3), channel_id=1, source_target_pairs={{8,0},{12,4},{16,8},{20,12},{24,16},{28,20},{32,24},{36,28},{40,32... | collective-permute-start | bytes 1597448 | tf_op jit(solution)/shard_map/ppermute | solution.py:32
  12.1 0.1 pad_maximum_fusion.1.refs_1_
  12.2 2.0 %collective-permute-start.4 = (bf16[1024,256]{1,0:T(8,128)(2,1)S(1)}, bf16[1024,256]{1,0:T(8,128)(2,1)S(1)}, u32[]{:S(2)}, u32[]{:S(2)}) collective-permute-start(bf16[1024,256]{1,0:T(8,128)(2,1)S(1)} %get-tuple-element.83), channel_id=1, source_target_pairs={{8,0},{12,4},{16,8},{20,12},{24,16},{28,20},{32,24},{36,28},{40,32... | collective-permute-start | bytes 1572872 | tf_op jit(solution)/shard_map/ppermute | solution.py:32
  14.2 11.5 %shard_map.83 = (f32[1024,128]{1,0:T(8,128)S(1)}, f32[1024,128]{1,0:T(8,128)S(1)}, f32[1024,256]{1,0:T(8,128)S(1)}, f32[1024,256]{1,0:T(8,128)S(1)}) custom-call(s32[1]{0:T(128)} %bitcast.core.refs_0_, bf16[2064,256]{1,0:T(8,128)(2,1)S(1)} %pad_maximum_fusion.1.refs_1_, bf16[2064,256]{1,0:T(8,128)(2,1)S(1)} %pad_maximum_fusion.refs_2_.refs_3_), custom_call_target="tpu_custom_call" | custom-call | flops 5368709120 | bytes 4194304 | tf_op jit(solution)/shard_map/pallas_call | solution.py:212
  25.8 0.9 collective-permute-done.3.refs_1_
  26.7 3.5 %shard_map.84 = (bf16[1024,128]{1,0:T(8,128)(2,1)S(1)}, f32[1024,256]{1,0:T(8,128)S(1)}, f32[1024,256]{1,0:T(8,128)S(1)}) custom-call(s32[1]{0:T(128)} %bitcast.core.refs_0_, bf16[1040,256]{1,0:T(8,128)(2,1)S(1)} %collective-permute-done.3.refs_1_, bf16[2064,256]{1,0:T(8,128)(2,1)S(1)} %pad_maximum_fusion.refs_2_.refs_3_, ...), custom_call_target="tpu_custom_call" | custom-call | flops 5368709120 | bytes 4194304 | tf_op jit(solution)/shard_map/pallas_call | solution.py:212
  30.2 0.7 copy-done.6
  30.9 6.2 %collective-permute-done.4.refs_2_ = bf16[1024,256]{1,0:T(8,128)(2,1)S(1)} collective-permute-done((bf16[1024,256]{1,0:T(8,128)(2,1)S(1)}, bf16[1024,256]{1,0:T(8,128)(2,1)S(1)}, u32[]{:S(2)}, u32[]{:S(2)}) %collective-permute-start.4) | collective-permute-done | bytes 524320 | tf_op jit(solution)/shard_map/ppermute | solution.py:32
  37.1 0.0 collective-permute-done.5.refs_3_
  37.1 4.5 %collective-permute-start.6 = (bf16[2064,256]{1,0:T(8,128)(2,1)S(1)}, bf16[2064,256]{1,0:T(8,128)(2,1)S(1)}, u32[]{:S(2)}, u32[]{:S(2)}) collective-permute-start(bf16[2064,256]{1,0:T(8,128)(2,1)S(1)} %pad_maximum_fusion.1.refs_1_), channel_id=1, source_target_pairs={{24,0},{28,4},{32,8},{36,12},{40,16},{44,20},{48,24},{52,28},{56,3... | collective-permute-start | bytes 3170312 | tf_op jit(solution)/shard_map/ppermute | solution.py:32
  41.6 1.3 shard_map.85
  43.0 16.6 %collective-permute-start.7 = (bf16[2048,256]{1,0:T(8,128)(2,1)S(1)}, bf16[2048,256]{1,0:T(8,128)(2,1)S(1)}, u32[]{:S(2)}, u32[]{:S(2)}) collective-permute-start(bf16[2048,256]{1,0:T(8,128)(2,1)S(1)} %get-tuple-element.70), channel_id=1, source_target_pairs={{8,0},{12,4},{16,8},{20,12},{24,16},{28,20},{32,24},{36,28},{40,32... | collective-permute-start | bytes 3145736 | tf_op jit(solution)/shard_map/ppermute | solution.py:32
  59.7 3.4 %shard_map.86 = (bf16[1024,128]{1,0:T(8,128)(2,1)S(1)}, bf16[1024,256]{1,0:T(8,128)(2,1)S(1)}, bf16[1024,256]{1,0:T(8,128)(2,1)S(1)}) custom-call(s32[1]{0:T(128)} %bitcast.core.refs_0_, bf16[1040,256]{1,0:T(8,128)(2,1)S(1)} %collective-permute-done.3.refs_1_, bf16[1024,256]{1,0:T(8,128)(2,1)S(1)} %collective-permute-done.4.refs_2_, ...), custom_call_target="tpu_custom_call" | custom-call | flops 5368709120 | bytes 4194304 | tf_op jit(solution)/shard_map/pallas_call | solution.py:212
  63.1 0.0 copy-done.7
  63.1 0.8 copy-done.2
  63.9 0.0 collective-permute-done.6.refs_1_
  63.9 1.1 shard_map.87
  65.1 0.0 copy-start.4
  65.1 16.1 %collective-permute-done.7.key_back = bf16[2048,256]{1,0:T(8,128)(2,1)S(1)} collective-permute-done((bf16[2048,256]{1,0:T(8,128)(2,1)S(1)}, bf16[2048,256]{1,0:T(8,128)(2,1)S(1)}, u32[]{:S(2)}, u32[]{:S(2)}) %collective-permute-start.7) | collective-permute-done | bytes 1048608 | tf_op jit(solution)/shard_map/ppermute | solution.py:32
  81.2 0.3 add_convert_fusion.1
  81.5 1.0 pad_maximum_fusion.2
  82.5 0.0 collective-permute-start.8
  82.5 0.0 copy-start.5
  82.5 0.1 pad_add_fusion.place
  82.6 1.5 %add_convert_fusion.4 = (bf16[1024,128]{1,0:T(8,128)(2,1)S(1)}, bf16[1024,128]{1,0:T(8,128)(2,1)S(1)}) fusion(bf16[1024,128]{1,0:T(8,128)(2,1)} %copy-done.8, bf16[1024,128]{1,0:T(8,128)(2,1)} %copy-done.9, bf16[1024,128]{1,0:T(8,128)(2,1)} %copy-done.6, pred[]{:T(512)S(6)} %eq.5, bf16[1024,128]{1,0:T(8,128)(2,1)} %copy-done.7), kind=kLoop, calls=%fused_computation.16 | loop fusion | flops 1310720 | bytes 1572865 | tf_op jit(solution)/shard_map/convert_element_type | solution.py:363
  84.1 1.9 %collective-permute-start.10 = (bf16[1024,128]{1,0:T(8,128)(2,1)S(1)}, bf16[1024,128]{1,0:T(8,128)(2,1)S(1)}, u32[]{:S(2)}, u32[]{:S(2)}) collective-permute-start(bf16[1024,128]{1,0:T(8,128)(2,1)S(1)} %get-tuple-element.87), channel_id=1, source_target_pairs={{0,12},{4,8},{8,20},{12,16},{16,28},{20,24},{24,36},{28,32},{32,44... | collective-permute-start | bytes 786440 | tf_op jit(solution)/shard_map/ppermute | solution.py:32
  86.0 1.9 %collective-permute-start.9 = (bf16[1024,128]{1,0:T(8,128)(2,1)S(1)}, bf16[1024,128]{1,0:T(8,128)(2,1)S(1)}, u32[]{:S(2)}, u32[]{:S(2)}) collective-permute-start(bf16[1024,128]{1,0:T(8,128)(2,1)S(1)} %get-tuple-element.88), channel_id=1, source_target_pairs={{0,8},{4,12},{8,16},{12,20},{16,24},{20,28},{24,32},{28,36},{32,40... | collective-permute-start | bytes 786440 | tf_op jit(solution)/shard_map/ppermute | solution.py:32
  88.0 1.3 collective-permute-start.11
  89.3 1.3 collective-permute-start.12
  90.6 0.0 copy-start
  90.6 0.1 convert_add_fusion.dkv
  90.8 4.5 %collective-permute-done.10.back_cross = bf16[1024,128]{1,0:T(8,128)(2,1)S(1)} collective-permute-done((bf16[1024,128]{1,0:T(8,128)(2,1)S(1)}, bf16[1024,128]{1,0:T(8,128)(2,1)S(1)}, u32[]{:S(2)}, u32[]{:S(2)}) %collective-permute-start.10) | collective-permute-done | bytes 262176 | tf_op jit(solution)/shard_map/ppermute | solution.py:32
  95.2 5.8 %collective-permute-done.9.back_same = bf16[1024,128]{1,0:T(8,128)(2,1)S(1)} collective-permute-done((bf16[1024,128]{1,0:T(8,128)(2,1)S(1)}, bf16[1024,128]{1,0:T(8,128)(2,1)S(1)}, u32[]{:S(2)}, u32[]{:S(2)}) %collective-permute-start.9) | collective-permute-done | bytes 262176 | tf_op jit(solution)/shard_map/ppermute | solution.py:32
  101.1 10.8 %collective-permute-done.11.far_same = bf16[1024,128]{1,0:T(8,128)(2,1)S(1)} collective-permute-done((bf16[1024,128]{1,0:T(8,128)(2,1)S(1)}, bf16[1024,128]{1,0:T(8,128)(2,1)S(1)}, u32[]{:S(2)}, u32[]{:S(2)}) %collective-permute-start.11) | collective-permute-done | bytes 262176 | tf_op jit(solution)/shard_map/ppermute | solution.py:32
  111.9 5.2 %collective-permute-done.12.far_cross = bf16[1024,128]{1,0:T(8,128)(2,1)S(1)} collective-permute-done((bf16[1024,128]{1,0:T(8,128)(2,1)S(1)}, bf16[1024,128]{1,0:T(8,128)(2,1)S(1)}, u32[]{:S(2)}, u32[]{:S(2)}) %collective-permute-start.12) | collective-permute-done | bytes 262176 | tf_op jit(solution)/shard_map/ppermute | solution.py:32
  117.1 0.0 collective-permute-done.8.other
  117.1 1.3 collect.1
  118.4 0.5 collective-permute-start.13
  119.0 2.4 %project.1 = (f32[1024,256]{1,0:T(8,128)S(1)}, f32[1024,256]{1,0:T(8,128)S(1)}, f32[1024,256]{1,0:T(8,128)S(1)}) custom-call(s32[2]{0:T(128)S(1)} %pad_add_fusion.place, bf16[1024,1024]{1,0:T(8,128)(2,1)S(1)} %get-tuple-element.77.left, bf16[4,1024,256]{2,1,0:T(8,128)(2,1)S(1)} %copy-done), custom_call_target="tpu_custom_call" | custom-call | flops 1610612736 | bytes 8388608 | tf_op jit(solution)/shard_map/project/pallas_call | solution.py:296
  121.4 1.6 %collective-permute-start.15 = (bf16[512,256]{1,0:T(8,128)(2,1)S(1)}, bf16[512,256]{1,0:T(8,128)(2,1)S(1)}, u32[]{:S(2)}, u32[]{:S(2)}) collective-permute-start(bf16[512,256]{1,0:T(8,128)(2,1)S(1)} %get-tuple-element.82), channel_id=1, source_target_pairs={{0,3},{1,0},{2,1},{3,2},{4,7},{5,4},{6,5},{7,6},{8,11},{9,8},{10,9... | collective-permute-start | bytes 786440 | tf_op jit(solution)/shard_map/ppermute | solution.py:382
  123.0 3.8 %collective-permute-done.13 = bf16[512,256]{1,0:T(8,128)(2,1)S(1)} collective-permute-done((bf16[512,256]{1,0:T(8,128)(2,1)S(1)}, bf16[512,256]{1,0:T(8,128)(2,1)S(1)}, u32[]{:S(2)}, u32[]{:S(2)}) %collective-permute-start.13) | collective-permute-done | bytes 262176 | tf_op jit(solution)/shard_map/ppermute | solution.py:382
  126.8 0.1 add_convert_fusion.3
  126.9 1.8 %collective-permute-start.14 = (bf16[1024,256]{1,0:T(8,128)(2,1)S(1)}, bf16[1024,256]{1,0:T(8,128)(2,1)S(1)}, u32[]{:S(2)}, u32[]{:S(2)}) collective-permute-start(bf16[1024,256]{1,0:T(8,128)(2,1)S(1)} %pad_maximum_fusion.6), channel_id=1, source_target_pairs={{0,1},{1,2},{2,3},{3,0},{4,5},{5,6},{6,7},{7,4},{8,9},{9,10},{10,1... | collective-permute-start | bytes 1572872 | tf_op jit(solution)/shard_map/ppermute | solution.py:382
  128.7 2.0 %collective-permute-done.15 = bf16[512,256]{1,0:T(8,128)(2,1)S(1)} collective-permute-done((bf16[512,256]{1,0:T(8,128)(2,1)S(1)}, bf16[512,256]{1,0:T(8,128)(2,1)S(1)}, u32[]{:S(2)}, u32[]{:S(2)}) %collective-permute-start.15) | collective-permute-done | bytes 262176 | tf_op jit(solution)/shard_map/ppermute | solution.py:382
  130.7 0.1 add_convert_fusion.2
  130.8 0.4 collective-permute-start.16
  131.2 8.9 %collective-permute-done.14 = bf16[1024,256]{1,0:T(8,128)(2,1)S(1)} collective-permute-done((bf16[1024,256]{1,0:T(8,128)(2,1)S(1)}, bf16[1024,256]{1,0:T(8,128)(2,1)S(1)}, u32[]{:S(2)}, u32[]{:S(2)}) %collective-permute-start.14) | collective-permute-done | bytes 524320 | tf_op jit(solution)/shard_map/ppermute | solution.py:382
  140.1 4.8 %collective-permute-done.16 = bf16[1024,256]{1,0:T(8,128)(2,1)S(1)} collective-permute-done((bf16[1024,256]{1,0:T(8,128)(2,1)S(1)}, bf16[1024,256]{1,0:T(8,128)(2,1)S(1)}, u32[]{:S(2)}, u32[]{:S(2)}) %collective-permute-start.16) | collective-permute-done | bytes 524320 | tf_op jit(solution)/shard_map/ppermute | solution.py:382
  144.9 0.9 add_convert_fusion
  (35 shorter events, 0.3 us)
Async XLA Ops:
  0.0 1.4 copy-start.15
  1.3 4.3 %collective-permute-start.1 = (bf16[1024,256]{1,0:T(8,128)(2,1)S(1)}, bf16[1024,256]{1,0:T(8,128)(2,1)S(1)}, u32[]{:S(2)}, u32[]{:S(2)}) collective-permute-start(bf16[1024,256]{1,0:T(8,128)(2,1)S(1)} %pad_maximum_fusion.5), channel_id=1, source_target_pairs={{0,4},{4,0},{8,12},{12,8},{16,20},{20,16},{24,28},{28,24},{32,36},... | collective-permute-start | bytes 1572872 | tf_op jit(solution)/shard_map/ppermute | solution.py:40
  1.5 4.1 %collective-permute-start.2 = (bf16[1024]{0:T(1024)(128)(2,1)S(1)}, bf16[1024]{0:T(1024)(128)(2,1)S(1)}, u32[]{:S(2)}, u32[]{:S(2)}) collective-permute-start(bf16[1024]{0:T(1024)(128)(2,1)S(1)} %add_convert_fusion.6), channel_id=1, source_target_pairs={{0,4},{4,0},{8,12},{12,8},{16,20},{20,16},{24,28},{28,24},{32,36},... | collective-permute-start | bytes 6152 | tf_op jit(solution)/shard_map/ppermute | solution.py:40
  5.5 4.2 %collective-permute-start = (bf16[1024,256]{1,0:T(8,128)(2,1)}, bf16[1024,256]{1,0:T(8,128)(2,1)S(1)}, u32[]{:S(2)}, u32[]{:S(2)}) collective-permute-start(bf16[1024,256]{1,0:T(8,128)(2,1)} %get-tuple-element.45), channel_id=1, source_target_pairs={{0,4},{4,0},{8,12},{12,8},{16,20},{20,16},{24,28},{28,24},{32,36},... | collective-permute-start | bytes 1572872 | tf_op jit(solution)/shard_map/ppermute | solution.py:40
  5.9 3.8 %copy-start.14 = (bf16[1024,256]{1,0:T(8,128)(2,1)S(1)}, bf16[1024,256]{1,0:T(8,128)(2,1)}, u32[]{:S(2)}) copy-start(bf16[1024,256]{1,0:T(8,128)(2,1)} %get-tuple-element.44) | copy-start | bytes 1572868
  5.9 31.1 %collective-permute-start.5 = (bf16[2064,256]{1,0:T(8,128)(2,1)S(1)}, bf16[2064,256]{1,0:T(8,128)(2,1)S(1)}, u32[]{:S(2)}, u32[]{:S(2)}) collective-permute-start(bf16[2064,256]{1,0:T(8,128)(2,1)S(1)} %pad_maximum_fusion.refs_2_.refs_3_), channel_id=1, source_target_pairs={{0,8},{4,12},{8,16},{12,20},{16,24},{20,28},{24,32},{28,36},{32,40... | collective-permute-start | bytes 3170312 | tf_op jit(solution)/shard_map/ppermute | solution.py:32
  9.8 16.9 %collective-permute-start.3 = (bf16[1040,256]{1,0:T(8,128)(2,1)S(1)}, bf16[1040,256]{1,0:T(8,128)(2,1)S(1)}, u32[]{:S(2)}, u32[]{:S(2)}) collective-permute-start(bf16[1040,256]{1,0:T(8,128)(2,1)S(1)} %pad_maximum_fusion.3), channel_id=1, source_target_pairs={{8,0},{12,4},{16,8},{20,12},{24,16},{28,20},{32,24},{36,28},{40,32... | collective-permute-start | bytes 1597448 | tf_op jit(solution)/shard_map/ppermute | solution.py:32
  12.2 24.9 %collective-permute-start.4 = (bf16[1024,256]{1,0:T(8,128)(2,1)S(1)}, bf16[1024,256]{1,0:T(8,128)(2,1)S(1)}, u32[]{:S(2)}, u32[]{:S(2)}) collective-permute-start(bf16[1024,256]{1,0:T(8,128)(2,1)S(1)} %get-tuple-element.83), channel_id=1, source_target_pairs={{8,0},{12,4},{16,8},{20,12},{24,16},{28,20},{32,24},{36,28},{40,32... | collective-permute-start | bytes 1572872 | tf_op jit(solution)/shard_map/ppermute | solution.py:32
  30.2 0.7 copy-start.6
  37.1 26.9 %collective-permute-start.6 = (bf16[2064,256]{1,0:T(8,128)(2,1)S(1)}, bf16[2064,256]{1,0:T(8,128)(2,1)S(1)}, u32[]{:S(2)}, u32[]{:S(2)}) collective-permute-start(bf16[2064,256]{1,0:T(8,128)(2,1)S(1)} %pad_maximum_fusion.1.refs_1_), channel_id=1, source_target_pairs={{24,0},{28,4},{32,8},{36,12},{40,16},{44,20},{48,24},{52,28},{56,3... | collective-permute-start | bytes 3170312 | tf_op jit(solution)/shard_map/ppermute | solution.py:32
  43.0 20.1 %copy-start.7 = (bf16[1024,128]{1,0:T(8,128)(2,1)}, bf16[1024,128]{1,0:T(8,128)(2,1)S(1)}, u32[]{:S(2)}) copy-start(bf16[1024,128]{1,0:T(8,128)(2,1)S(1)} %get-tuple-element.72) | copy-start | bytes 786436
  43.0 20.1 %copy-start.8 = (bf16[1024,128]{1,0:T(8,128)(2,1)}, bf16[1024,128]{1,0:T(8,128)(2,1)S(1)}, u32[]{:S(2)}) copy-start(bf16[1024,128]{1,0:T(8,128)(2,1)S(1)} %get-tuple-element.73) | copy-start | bytes 786436
  43.0 38.2 %collective-permute-start.7 = (bf16[2048,256]{1,0:T(8,128)(2,1)S(1)}, bf16[2048,256]{1,0:T(8,128)(2,1)S(1)}, u32[]{:S(2)}, u32[]{:S(2)}) collective-permute-start(bf16[2048,256]{1,0:T(8,128)(2,1)S(1)} %get-tuple-element.70), channel_id=1, source_target_pairs={{8,0},{12,4},{16,8},{20,12},{24,16},{28,20},{32,24},{36,28},{40,32... | collective-permute-start | bytes 3145736 | tf_op jit(solution)/shard_map/ppermute | solution.py:32
  63.1 0.8 copy-start.2
  63.9 1.2 copy-start.9
  65.1 16.4 %copy-start.4 = (bf16[1024,256]{1,0:T(8,128)(2,1)}, bf16[1024,256]{1,0:T(8,128)(2,1)S(1)}, u32[]{:S(2)}) copy-start(bf16[1024,256]{1,0:T(8,128)(2,1)S(1)} %get-tuple-element.65) | copy-start | bytes 1572868
  65.1 16.4 %copy-start.10 = (bf16[1024,128]{1,0:T(8,128)(2,1)}, bf16[1024,128]{1,0:T(8,128)(2,1)S(1)}, u32[]{:S(2)}) copy-start(bf16[1024,128]{1,0:T(8,128)(2,1)S(1)} %get-tuple-element.75) | copy-start | bytes 786436
  65.1 16.4 %copy-start.12 = (bf16[1024,128]{1,0:T(8,128)(2,1)}, bf16[1024,128]{1,0:T(8,128)(2,1)S(1)}, u32[]{:S(2)}) copy-start(bf16[1024,128]{1,0:T(8,128)(2,1)S(1)} %get-tuple-element.74) | copy-start | bytes 786436
  82.5 34.6 %collective-permute-start.8 = (bf16[1024,384]{1,0:T(8,128)(2,1)}, bf16[1024,384]{1,0:T(8,128)(2,1)S(1)}, u32[]{:S(2)}, u32[]{:S(2)}) collective-permute-start(bf16[1024,384]{1,0:T(8,128)(2,1)} %pad_maximum_fusion.2), channel_id=1, source_target_pairs={{0,4},{4,0},{8,12},{12,8},{16,20},{20,16},{24,28},{28,24},{32,36},... | collective-permute-start | bytes 2359304 | tf_op jit(solution)/shard_map/ppermute | solution.py:40
  82.5 5.4 %copy-start.13 = (bf16[1024,128]{1,0:T(8,128)(2,1)S(1)}, bf16[1024,128]{1,0:T(8,128)(2,1)}, u32[]{:S(2)}) copy-start(bf16[1024,128]{1,0:T(8,128)(2,1)} %copy-done.12) | copy-start | bytes 786436
  82.5 6.7 %copy-start.11 = (bf16[1024,128]{1,0:T(8,128)(2,1)S(1)}, bf16[1024,128]{1,0:T(8,128)(2,1)}, u32[]{:S(2)}) copy-start(bf16[1024,128]{1,0:T(8,128)(2,1)} %copy-done.10) | copy-start | bytes 786436
  82.5 8.0 %copy-start.3 = (bf16[1024,256]{1,0:T(8,128)(2,1)S(1)}, bf16[1024,256]{1,0:T(8,128)(2,1)}, u32[]{:S(2)}) copy-start(bf16[1024,256]{1,0:T(8,128)(2,1)} %copy-done.2) | copy-start | bytes 1572868
  82.5 8.0 %copy-start.5 = (bf16[1024,256]{1,0:T(8,128)(2,1)S(1)}, bf16[1024,256]{1,0:T(8,128)(2,1)}, u32[]{:S(2)}) copy-start(bf16[1024,256]{1,0:T(8,128)(2,1)} %copy-done.4) | copy-start | bytes 1572868
  84.1 11.2 %collective-permute-start.10 = (bf16[1024,128]{1,0:T(8,128)(2,1)S(1)}, bf16[1024,128]{1,0:T(8,128)(2,1)S(1)}, u32[]{:S(2)}, u32[]{:S(2)}) collective-permute-start(bf16[1024,128]{1,0:T(8,128)(2,1)S(1)} %get-tuple-element.87), channel_id=1, source_target_pairs={{0,12},{4,8},{8,20},{12,16},{16,28},{20,24},{24,36},{28,32},{32,44... | collective-permute-start | bytes 786440 | tf_op jit(solution)/shard_map/ppermute | solution.py:32
  86.0 15.0 %collective-permute-start.9 = (bf16[1024,128]{1,0:T(8,128)(2,1)S(1)}, bf16[1024,128]{1,0:T(8,128)(2,1)S(1)}, u32[]{:S(2)}, u32[]{:S(2)}) collective-permute-start(bf16[1024,128]{1,0:T(8,128)(2,1)S(1)} %get-tuple-element.88), channel_id=1, source_target_pairs={{0,8},{4,12},{8,16},{12,20},{16,24},{20,28},{24,32},{28,36},{32,40... | collective-permute-start | bytes 786440 | tf_op jit(solution)/shard_map/ppermute | solution.py:32
  88.0 23.9 %collective-permute-start.11 = (bf16[1024,128]{1,0:T(8,128)(2,1)S(1)}, bf16[1024,128]{1,0:T(8,128)(2,1)S(1)}, u32[]{:S(2)}, u32[]{:S(2)}) collective-permute-start(bf16[1024,128]{1,0:T(8,128)(2,1)S(1)} %copy-done.13), channel_id=1, source_target_pairs={{0,24},{4,28},{8,32},{12,36},{16,40},{20,44},{24,48},{28,52},{32,5... | collective-permute-start | bytes 786440 | tf_op jit(solution)/shard_map/ppermute | solution.py:32
  89.3 27.8 %collective-permute-start.12 = (bf16[1024,128]{1,0:T(8,128)(2,1)S(1)}, bf16[1024,128]{1,0:T(8,128)(2,1)S(1)}, u32[]{:S(2)}, u32[]{:S(2)}) collective-permute-start(bf16[1024,128]{1,0:T(8,128)(2,1)S(1)} %copy-done.11), channel_id=1, source_target_pairs={{0,28},{4,24},{8,36},{12,32},{16,44},{20,40},{24,52},{28,48},{32,6... | collective-permute-start | bytes 786440 | tf_op jit(solution)/shard_map/ppermute | solution.py:32
  90.6 26.5 %copy-start = (bf16[4,1024,256]{2,1,0:T(8,128)(2,1)S(1)}, bf16[4,1024,256]{2,1,0:T(8,128)(2,1)}, u32[]{:S(2)}) copy-start(bf16[4,1024,256]{2,1,0:T(8,128)(2,1)} %weights.3) | copy-start | bytes 6291460
  90.6 26.5 %copy-start.1 = (bf16[1024,256]{1,0:T(8,128)(2,1)S(1)}, bf16[1024,256]{1,0:T(8,128)(2,1)}, u32[]{:S(2)}) copy-start(bf16[1024,256]{1,0:T(8,128)(2,1)} %get-tuple-element.76.gate_grad) | copy-start | bytes 1572868
  118.4 8.4 %collective-permute-start.13 = (bf16[512,256]{1,0:T(8,128)(2,1)S(1)}, bf16[512,256]{1,0:T(8,128)(2,1)S(1)}, u32[]{:S(2)}, u32[]{:S(2)}) collective-permute-start(bf16[512,256]{1,0:T(8,128)(2,1)S(1)} %get-tuple-element.80), channel_id=1, source_target_pairs={{0,1},{1,2},{2,3},{3,0},{4,5},{5,6},{6,7},{7,4},{8,9},{9,10},{10,1... | collective-permute-start | bytes 786440 | tf_op jit(solution)/shard_map/ppermute | solution.py:382
  121.4 9.3 %collective-permute-start.15 = (bf16[512,256]{1,0:T(8,128)(2,1)S(1)}, bf16[512,256]{1,0:T(8,128)(2,1)S(1)}, u32[]{:S(2)}, u32[]{:S(2)}) collective-permute-start(bf16[512,256]{1,0:T(8,128)(2,1)S(1)} %get-tuple-element.82), channel_id=1, source_target_pairs={{0,3},{1,0},{2,1},{3,2},{4,7},{5,4},{6,5},{7,6},{8,11},{9,8},{10,9... | collective-permute-start | bytes 786440 | tf_op jit(solution)/shard_map/ppermute | solution.py:382
  126.9 13.2 %collective-permute-start.14 = (bf16[1024,256]{1,0:T(8,128)(2,1)S(1)}, bf16[1024,256]{1,0:T(8,128)(2,1)S(1)}, u32[]{:S(2)}, u32[]{:S(2)}) collective-permute-start(bf16[1024,256]{1,0:T(8,128)(2,1)S(1)} %pad_maximum_fusion.6), channel_id=1, source_target_pairs={{0,1},{1,2},{2,3},{3,0},{4,5},{5,6},{6,7},{7,4},{8,9},{9,10},{10,1... | collective-permute-start | bytes 1572872 | tf_op jit(solution)/shard_map/ppermute | solution.py:382
  130.8 14.1 %collective-permute-start.16 = (bf16[1024,256]{1,0:T(8,128)(2,1)S(1)}, bf16[1024,256]{1,0:T(8,128)(2,1)S(1)}, u32[]{:S(2)}, u32[]{:S(2)}) collective-permute-start(bf16[1024,256]{1,0:T(8,128)(2,1)S(1)} %pad_maximum_fusion.7), channel_id=1, source_target_pairs={{0,3},{1,0},{2,1},{3,2},{4,7},{5,4},{6,5},{7,6},{8,11},{9,8},{10,9... | collective-permute-start | bytes 1572872 | tf_op jit(solution)/shard_map/ppermute | solution.py:382
